TPU v7x, 32 devices: a whole 2x2x4 slice. The times are simulated.
32 devices in a mesh: groups: 2 (over y), seq: 8 (over z, x), chan: 2 (over core).
Axes of the slice: x: 2, y: 2, z: 4, core: 2. Of those that a mesh axis runs over, the one named last changes fastest.
Arguments:
- signal: bfloat16 [4096, 1024], P(('groups', 'seq'), 'chan'), parts along dimension 0, may hold values from -6 to 6
- tangent: bfloat16 [4096, 1024], P(('groups', 'seq'), 'chan'), parts along dimension 0, may hold values from -6 to 6
- gains: float32 [2, 1024], P(None, 'chan'), may hold values from 0.5 to 2
- convolution_kernel: bfloat16 [2, 3072, 2, 512], P(None, 'seq', None, 'chan'), may hold values from -0.109375 to 0.109375
- mixing_kernel: bfloat16 [2, 512, 1024], P(None, 'seq', 'chan'), may hold values from -0.25 to 0.25
Outputs:
- out_signal: bfloat16 [4096, 1024], P(('groups', 'seq'), 'chan'), parts along dimension 0
- out_tangent: bfloat16 [4096, 1024], P(('groups', 'seq'), 'chan'), parts along dimension 0
There are 2 independent parts, one for each index of `groups`. A program takes and returns all parts, laid end to end along the dimension named above; an argument that names none is the same for every part. Nothing has to cross between parts.
All inputs are finite; a program needn't handle non-finite values.
Results may differ from a plain program's by a relative error of at most 0.0063.
Values may be sent and summed in bfloat16 or wider, within the bound.
No kernel may reach another device: no remote copies, remote signals or barrier semaphores. Data moves between devices by JAX's collectives and lax.ppermute only.
A program may use at most 64 MiB of HBM per device.

v0:
```python
import jax
import jax.numpy as jnp
from jax import lax
from jax.sharding import PartitionSpec as P

LAYERS = 2


def from_behind(block, axis, distance):
    devices = range(lax.axis_size(axis))
    route = [(i - distance, i) for i in devices if i - distance in devices]
    return lax.ppermute(block, axis, route)


def delayed_rows(block, delay_offset, mover):
    rows = block.shape[1]
    whole, rest = divmod(delay_offset, rows)
    parts = []
    if rest:
        parts.append(mover(block[:, rows - rest :], whole + 1))
    parts.append(mover(block[:, : rows - rest], whole))
    return jnp.concatenate(parts, 1)


def on_device(signal, tangent, gains, convolution_kernel, mixing_kernel):
    rows = signal.shape[0]
    half = signal.shape[1]
    width = half * lax.axis_size("chan")
    branch = convolution_kernel.shape[3]
    base = rows * lax.axis_size("seq") // 16
    state = signal
    dstate = tangent

    def move_half(piece, by):
        return from_behind(piece, "seq", by)

    for layer_number in range(LAYERS):
        dilation_step = base * 2**layer_number
        xval = state.astype(jnp.float32)
        dxval = dstate.astype(jnp.float32)
        partial_value = jnp.stack([jnp.sum(xval * xval, axis=1), jnp.sum(xval * dxval, axis=1)], 0)
        totals = lax.psum(partial_value, "chan")
        mean_sq = (totals[0] / width)[:, None]
        mean_cross = (totals[1] / width)[:, None]
        scale = lax.rsqrt(mean_sq + 1e-05)
        gain = gains[layer_number][None, :]
        normed = (gain * xval * scale).astype(jnp.bfloat16)
        dnormed = (gain * (dxval * scale - xval * scale * scale * scale * mean_cross)).astype(
            jnp.bfloat16
        )
        paired = jnp.stack([normed, dnormed], 0)
        taps = jnp.stack(
            [
                paired,
                delayed_rows(paired, dilation_step, move_half),
                delayed_rows(paired, 2 * dilation_step, move_half),
            ],
            2,
        )
        stacked = lax.all_gather(taps, "chan", axis=3, tiled=True)
        left = stacked.reshape(2 * rows, 3 * width)
        conv_local = convolution_kernel[layer_number].reshape(
            convolution_kernel.shape[1], 2 * branch
        )
        conv_whole = lax.all_gather(conv_local, "seq", axis=0, tiled=True)
        full = jnp.dot(left, conv_whole, preferred_element_type=jnp.float32)
        filt, gate = (full[:rows, :branch], full[:rows, branch:])
        dfilt, dgate = (full[rows:, :branch], full[rows:, branch:])
        tanh_f = jnp.tanh(filt)
        sig_g = jax.nn.sigmoid(gate)
        gated = (tanh_f * sig_g).astype(jnp.bfloat16)
        dgated = (
            (1.0 - tanh_f * tanh_f) * sig_g * dfilt + tanh_f * sig_g * (1.0 - sig_g) * dgate
        ).astype(jnp.bfloat16)
        branch_all = lax.all_gather(jnp.concatenate([gated, dgated], 0), "chan", axis=1, tiled=True)
        mix_whole = lax.all_gather(mixing_kernel[layer_number], "seq", axis=0, tiled=True)
        mixed = jnp.dot(branch_all, mix_whole, preferred_element_type=jnp.float32)
        state = (xval + mixed[:rows]).astype(jnp.bfloat16)
        dstate = (dxval + mixed[rows:]).astype(jnp.bfloat16)
    return (state, dstate)


def solution(mesh):
    return jax.shard_map(
        on_device,
        mesh=mesh,
        in_specs=(
            P(("groups", "seq"), "chan"),
            P(("groups", "seq"), "chan"),
            P(None, "chan"),
            P(None, "seq", None, "chan"),
            P(None, "seq", "chan"),
        ),
        out_specs=(P(("groups", "seq"), "chan"), P(("groups", "seq"), "chan")),
        check_vma=False,
    )
```

profile of v0, /device:TPU:0, one launch (start us, length us, event | category | flops | bytes accessed | tf_op | source)
XLA Modules:
  0.0 246.1 jit_solution(518207839076454163)
XLA Ops:
  7.2 0.0 all-gather.7.cloned.1.call-start
  7.2 1.1 copy.13
  8.3 1.1 copy.14
  9.4 0.1 fusion.10
  9.5 2.6 %psum.14 = f32[2,256]{1,0:T(2,128)S(1)} all-reduce(f32[2,256]{1,0:T(2,128)S(1)} %pad_maximum_fusion.6), channel_id=1, replica_groups=mesh['groups'=2,'seq'=8,'chan'=2] {'chan'}, use_global_device_ids=true, to_apply=%region_2.0 | all-reduce | flops 512 | bytes 4096 | tf_op jit(solution)/shard_map/psum | solution.py:42
  12.1 0.8 fusion.58
  12.9 0.2 fusion.29
  13.1 0.1 fusion.53
  13.2 4.8 %collective-permute-start.2 = (bf16[2,256,512]{1,2,0:T(8,128)(2,1)S(1)}, bf16[2,256,512]{1,2,0:T(8,128)(2,1)S(1)}, u32[]{:S(2)}, u32[]{:S(2)}) collective-permute-start(bf16[2,256,512]{1,2,0:T(8,128)(2,1)S(1)} %get-tuple-element.23), channel_id=1, source_target_pairs={{0,2},{2,4},{4,6},{6,8},{8,10},{10,12},{12,14},{1,3},{3,5},{5,7},{... | collective-permute-start | bytes 1572872 | tf_op jit(solution)/shard_map/ppermute | solution.py:12
  18.0 0.1 fusion.32
  18.1 3.6 %collective-permute-start = (bf16[2,128,512]{1,2,0:T(8,128)(2,1)S(1)}, bf16[2,128,512]{1,2,0:T(8,128)(2,1)S(1)}, u32[]{:S(2)}, u32[]{:S(2)}) collective-permute-start(bf16[2,128,512]{1,2,0:T(8,128)(2,1)S(1)} %get-tuple-element.24), channel_id=1, source_target_pairs={{0,2},{2,4},{4,6},{6,8},{8,10},{10,12},{12,14},{1,3},{3,5},{5,7},{... | collective-permute-start | bytes 786440 | tf_op jit(solution)/shard_map/ppermute | solution.py:12
  21.7 13.4 %collective-permute-done = bf16[2,128,512]{1,2,0:T(8,128)(2,1)S(1)} collective-permute-done((bf16[2,128,512]{1,2,0:T(8,128)(2,1)S(1)}, bf16[2,128,512]{1,2,0:T(8,128)(2,1)S(1)}, u32[]{:S(2)}, u32[]{:S(2)}) %collective-permute-start) | collective-permute-done | bytes 262176 | tf_op jit(solution)/shard_map/ppermute | solution.py:12
  35.1 0.1 maximum_bitcast_fusion
  35.2 1.3 pad_maximum_fusion
  36.5 0.0 all-gather.9.cloned.1.call-start
  36.6 0.5 fusion.56
  37.1 0.9 copy.23
  38.0 0.0 all-gather.11.cloned.1.call-start
  38.1 34.5 %all-gather = bf16[1,512,512]{2,1,0:T(8,128)(2,1)S(1)} all-gather(bf16[1,64,512]{2,1,0:T(8,128)(2,1)S(1)} %get-tuple-element.31), channel_id=2, replica_groups=mesh['groups'=2,'seq'=8,'chan'=2] {'seq'}, dimensions={1}, use_global_device_ids=true | all-gather | bytes 589824 | tf_op jit(solution)/shard_map/all_gather | solution.py:76
  72.6 5.1 %copy.15 = bf16[2,256,3,1024]{1,0,3,2:T(2,128)(2,1)S(1)} copy(bf16[2,256,3,1024]{1,3,0,2:T(8,128)(2,1)} %all-gather.7.cloned.1.call-done) | data formatting | bytes 6291456 | tf_op jit(solution)/shard_map/all_gather | solution.py:60
  77.7 2.2 copy.22
  79.9 35.4 %all-gather.9.cloned.1.call-done = bf16[3072,512]{1,0:T(8,128)(2,1)} async-done(((bf16[384,512]{1,0:T(8,128)(2,1)}), bf16[3072,512]{1,0:T(8,128)(2,1)}) %all-gather.9.cloned.1.call-update) | async-done | bytes 3145744 | tf_op jit(solution)/shard_map/all_gather | solution.py:65
  115.4 4.6 %fusion.59 = f32[512,512]{1,0:T(8,128)S(1)} fusion(bf16[512,3072]{0,1:T(8,128)(2,1)} %bitcast.57, bf16[3072,512]{1,0:T(8,128)(2,1)} %all-gather.9.cloned.1.call-done), kind=kOutput, calls=%fused_computation.96 | convolution fusion | flops 1610612736 | bytes 7340032 | tf_op jit(solution)/shard_map/dot_general | solution.py:66
  120.0 0.1 fusion.47
  120.2 2.2 all_gather.26
  122.4 0.5 fusion.26
  122.9 0.2 fusion.18
  123.0 2.5 %psum.15 = f32[2,256]{1,0:T(2,128)S(1)} all-reduce(f32[2,256]{1,0:T(2,128)S(1)} %pad_maximum_fusion.7), channel_id=1, replica_groups=mesh['groups'=2,'seq'=8,'chan'=2] {'chan'}, use_global_device_ids=true, to_apply=%region_5.0 | all-reduce | flops 512 | bytes 4096 | tf_op jit(solution)/shard_map/psum | solution.py:42
  125.5 0.2 fusion.28
  125.8 0.1 fusion.52
  125.8 2.5 %collective-permute-start.3 = (bf16[2,256,512]{1,2,0:T(8,128)(2,1)S(1)}, bf16[2,256,512]{1,2,0:T(8,128)(2,1)S(1)}, u32[]{:S(2)}, u32[]{:S(2)}) collective-permute-start(bf16[2,256,512]{1,2,0:T(8,128)(2,1)S(1)} %get-tuple-element.21), channel_id=1, source_target_pairs={{0,2},{2,4},{4,6},{6,8},{8,10},{10,12},{12,14},{1,3},{3,5},{5,7},{... | collective-permute-start | bytes 1572872 | tf_op jit(solution)/shard_map/ppermute | solution.py:12
  128.4 3.3 %collective-permute-start.4 = (bf16[2,256,512]{1,2,0:T(8,128)(2,1)S(1)}, bf16[2,256,512]{1,2,0:T(8,128)(2,1)S(1)}, u32[]{:S(2)}, u32[]{:S(2)}) collective-permute-start(bf16[2,256,512]{1,2,0:T(8,128)(2,1)S(1)} %get-tuple-element.21), channel_id=1, source_target_pairs={{0,4},{2,6},{4,8},{6,10},{8,12},{10,14},{1,5},{3,7},{5,9},{7,11},{... | collective-permute-start | bytes 1572872 | tf_op jit(solution)/shard_map/ppermute | solution.py:12
  131.7 8.1 %collective-permute-done.3 = bf16[2,256,512]{1,2,0:T(8,128)(2,1)S(1)} collective-permute-done((bf16[2,256,512]{1,2,0:T(8,128)(2,1)S(1)}, bf16[2,256,512]{1,2,0:T(8,128)(2,1)S(1)}, u32[]{:S(2)}, u32[]{:S(2)}) %collective-permute-start.3) | collective-permute-done | bytes 524320 | tf_op jit(solution)/shard_map/ppermute | solution.py:12
  139.8 3.1 %collective-permute-done.4 = bf16[2,256,512]{1,2,0:T(8,128)(2,1)S(1)} collective-permute-done((bf16[2,256,512]{1,2,0:T(8,128)(2,1)S(1)}, bf16[2,256,512]{1,2,0:T(8,128)(2,1)S(1)}, u32[]{:S(2)}, u32[]{:S(2)}) %collective-permute-start.4) | collective-permute-done | bytes 524320 | tf_op jit(solution)/shard_map/ppermute | solution.py:12
  142.9 1.3 pad_maximum_fusion.1
  144.2 0.0 all-gather.13.cloned.1.call-start
  144.3 0.9 copy.25
  145.2 40.1 %all-gather.1 = bf16[1,512,512]{2,1,0:T(8,128)(2,1)S(1)} all-gather(bf16[1,64,512]{2,1,0:T(8,128)(2,1)S(1)} %get-tuple-element.30), channel_id=3, replica_groups=mesh['groups'=2,'seq'=8,'chan'=2] {'seq'}, dimensions={1}, use_global_device_ids=true | all-gather | bytes 589824 | tf_op jit(solution)/shard_map/all_gather | solution.py:76
  185.3 5.1 %copy.16 = bf16[2,256,3,1024]{1,0,3,2:T(2,128)(2,1)S(1)} copy(bf16[2,256,3,1024]{1,3,0,2:T(8,128)(2,1)} %all-gather.11.cloned.1.call-done) | data formatting | bytes 6291456 | tf_op jit(solution)/shard_map/all_gather | solution.py:60
  190.4 2.2 copy.24
  192.7 37.5 %all-gather.13.cloned.1.call-done = bf16[3072,512]{1,0:T(8,128)(2,1)} async-done(((bf16[384,512]{1,0:T(8,128)(2,1)}), bf16[3072,512]{1,0:T(8,128)(2,1)}) %all-gather.13.cloned.1.call-update) | async-done | bytes 3145744 | tf_op jit(solution)/shard_map/all_gather | solution.py:65
  230.2 4.6 %fusion.60 = f32[512,512]{1,0:T(8,128)S(1)} fusion(bf16[512,3072]{0,1:T(8,128)(2,1)} %bitcast.58, bf16[3072,512]{1,0:T(8,128)(2,1)} %all-gather.13.cloned.1.call-done), kind=kOutput, calls=%fused_computation.97 | convolution fusion | flops 1610612736 | bytes 7340032 | tf_op jit(solution)/shard_map/dot_general | solution.py:66
  234.9 0.1 fusion.46
  235.1 2.2 all_gather.30
  237.2 0.5 fusion.24
  237.7 0.1 fusion.7
  237.8 0.8 copy.19
  238.7 0.8 copy.20
  (20 shorter events, 0.2 us)
Async XLA Ops:
  7.2 65.4 %all-gather.7.cloned.1.call-start = ((), (), s32[]{:S(2)}) async-start(), calls=%async_computation | async-start | bytes 4718592 | tf_op jit(solution)/shard_map/all_gather | solution.py:60
  13.2 21.9 %collective-permute-start.2 = (bf16[2,256,512]{1,2,0:T(8,128)(2,1)S(1)}, bf16[2,256,512]{1,2,0:T(8,128)(2,1)S(1)}, u32[]{:S(2)}, u32[]{:S(2)}) collective-permute-start(bf16[2,256,512]{1,2,0:T(8,128)(2,1)S(1)} %get-tuple-element.23), channel_id=1, source_target_pairs={{0,2},{2,4},{4,6},{6,8},{8,10},{10,12},{12,14},{1,3},{3,5},{5,7},{... | collective-permute-start | bytes 1572872 | tf_op jit(solution)/shard_map/ppermute | solution.py:12
  18.1 18.5 %copy-start = (bf16[2,384,2,256]{3,2,1,0:T(2,128)(2,1)S(1)}, bf16[2,384,2,256]{3,2,1,0:T(2,128)(2,1)}, u32[]{:S(2)}) copy-start(bf16[2,384,2,256]{3,2,1,0:T(2,128)(2,1)} %param.8) | copy-start | bytes 2359300
  18.1 17.0 %collective-permute-start = (bf16[2,128,512]{1,2,0:T(8,128)(2,1)S(1)}, bf16[2,128,512]{1,2,0:T(8,128)(2,1)S(1)}, u32[]{:S(2)}, u32[]{:S(2)}) collective-permute-start(bf16[2,128,512]{1,2,0:T(8,128)(2,1)S(1)} %get-tuple-element.24), channel_id=1, source_target_pairs={{0,2},{2,4},{4,6},{6,8},{8,10},{10,12},{12,14},{1,3},{3,5},{5,7},{... | collective-permute-start | bytes 786440 | tf_op jit(solution)/shard_map/ppermute | solution.py:12
  21.6 13.4 %collective-permute-start.1 = (bf16[2,128,512]{1,2,0:T(8,128)(2,1)S(1)}, bf16[2,128,512]{1,2,0:T(8,128)(2,1)S(1)}, u32[]{:S(2)}, u32[]{:S(2)}) collective-permute-start(bf16[2,128,512]{1,2,0:T(8,128)(2,1)S(1)} %get-tuple-element.25), channel_id=1, source_target_pairs={{0,0},{2,2},{4,4},{6,6},{8,8},{10,10},{12,12},{14,14},{1,1},{3,3},... | collective-permute-start | bytes 786440 | tf_op jit(solution)/shard_map/ppermute | solution.py:12
  35.1 2.9 %copy-start.1 = (bf16[2,64,512]{2,1,0:T(8,128)(2,1)S(1)}, bf16[2,64,512]{2,1,0:T(8,128)(2,1)}, u32[]{:S(2)}) copy-start(bf16[2,64,512]{2,1,0:T(8,128)(2,1)} %param.9) | copy-start | bytes 393220
  36.5 78.9 %all-gather.9.cloned.1.call-start = ((), (), s32[]{:S(2)}) async-start(), calls=%async_computation.1 | async-start | bytes 3538944 | tf_op jit(solution)/shard_map/all_gather | solution.py:65
  38.0 147.3 %all-gather.11.cloned.1.call-start = ((), (), s32[]{:S(2)}) async-start(), calls=%async_computation.2 | async-start | bytes 4718592 | tf_op jit(solution)/shard_map/all_gather | solution.py:60
  125.8 14.0 %collective-permute-start.3 = (bf16[2,256,512]{1,2,0:T(8,128)(2,1)S(1)}, bf16[2,256,512]{1,2,0:T(8,128)(2,1)S(1)}, u32[]{:S(2)}, u32[]{:S(2)}) collective-permute-start(bf16[2,256,512]{1,2,0:T(8,128)(2,1)S(1)} %get-tuple-element.21), channel_id=1, source_target_pairs={{0,2},{2,4},{4,6},{6,8},{8,10},{10,12},{12,14},{1,3},{3,5},{5,7},{... | collective-permute-start | bytes 1572872 | tf_op jit(solution)/shard_map/ppermute | solution.py:12
  128.4 14.5 %collective-permute-start.4 = (bf16[2,256,512]{1,2,0:T(8,128)(2,1)S(1)}, bf16[2,256,512]{1,2,0:T(8,128)(2,1)S(1)}, u32[]{:S(2)}, u32[]{:S(2)}) collective-permute-start(bf16[2,256,512]{1,2,0:T(8,128)(2,1)S(1)} %get-tuple-element.21), channel_id=1, source_target_pairs={{0,4},{2,6},{4,8},{6,10},{8,12},{10,14},{1,5},{3,7},{5,9},{7,11},{... | collective-permute-start | bytes 1572872 | tf_op jit(solution)/shard_map/ppermute | solution.py:12
  144.2 86.0 %all-gather.13.cloned.1.call-start = ((), (), s32[]{:S(2)}) async-start(), calls=%async_computation.3 | async-start | bytes 3538944 | tf_op jit(solution)/shard_map/all_gather | solution.py:65
Sparse Core Ops, SparseCore 0:
  36.6 14.3 all-gather.6
  53.2 62.1 all-gather.8
  144.4 21.7 all-gather.10
  168.2 62.0 all-gather.12
where the time goes:
time: 247 us; the launch traced here: 246 us
  waiting for transfers between devices  97.6 us (40%)
  blocking collectives  84 us (34%)
  local copies, waits for them, and re-layouts  21.7 us (9%)
  starting transfers between devices  14.4 us (6%)
  between operations  14 us (6%)
  matrix products  10.3 us (4%)
  other arithmetic  4.16 us (2%)
    all_gather x2, blocking collectives, on_device(): lax.all_gather(mixing_kernel[layer_number], 'seq', axis=0, tiled=True)  74.6 us
    all_gather x2, waiting for transfers between devices, on_device(): conv_whole = lax.all_gather(conv_local, 'seq', axis=0, tiled=True)  73 us
    ppermute x5, waiting for transfers between devices, from_behind(): return lax.ppermute(block, axis, route)  24.6 us
    ppermute x5, starting transfers between devices, from_behind(): return lax.ppermute(block, axis, route)  14.2 us
    all_gather x2, local copies, waits for them, and re-layouts, on_device(): stacked = lax.all_gather(taps, 'chan', axis=3, tiled=True)  10.3 us
    unnamed x12, local copies, waits for them, and re-layouts  10.1 us
    dot_general x2, matrix products, on_device(): full = jnp.dot(left, conv_whole, preferred_element_type=jnp.float32)  9.3 us
    psum x2, blocking collectives, on_device(): totals = lax.psum(partial_value, 'chan')  5.06 us
  transfers between devices with their start and end apart: 9, of which 5 were waited for; matrix products, arithmetic and copies ran while one was open for 7% of the time, Pallas kernels for 0%

commit v1 on v0

v1 whole, which is shorter than its diff:
```python
import functools

import jax
import jax.numpy as jnp
from jax import lax
from jax.experimental import pallas as pl
from jax.experimental.pallas import tpu as pltpu
from jax.sharding import PartitionSpec as P

TAPS = 3
EPS = 1e-05
F32 = jnp.float32
BF16 = jnp.bfloat16
VMEM = pl.BlockSpec(memory_space=pltpu.VMEM)
SMEM = pl.BlockSpec(memory_space=pltpu.SMEM)
ANY = pl.BlockSpec(memory_space=pl.ANY)
PARAMS = pltpu.CompilerParams(vmem_limit_bytes=56 * 2**20)


def swap_chan(block):
    return lax.ppermute(block, "chan", [(0, 1), (1, 0)])


def swap_groups(block):
    return lax.ppermute(block, "groups", [(0, 1), (1, 0)])


def swap_pair(block, seq):
    return lax.ppermute(block, "seq", [(s, s ^ 1) for s in range(seq)])


def ring(block, seq, by):
    return lax.ppermute(block, "seq", [(s, (s + by) % seq) for s in range(seq)])


def from_behind(block, seq, by):
    return lax.ppermute(block, "seq", [(s - by, s) for s in range(by, seq)])


def weight_copies(place, convs, conv_rows, mix_rows, pairs, wide, mix, sems):
    copies = []

    def add(src, dst):
        copies.append(pltpu.make_async_copy(src, dst, sems.at[len(copies)]))

    if pairs is None:
        add(convs[0], wide)
        add(convs[1], mix)
        return copies
    s, g = place[0], place[1]
    seq = pairs[0]
    for ref, (by, dx, dy) in zip(convs, pairs[1]):
        owner = lax.rem(s + (seq - by), seq)
        if dx:
            owner = owner + 1 - 2 * lax.rem(owner, 2)
        half = (1 - g) if dy else g
        unit = owner * 2 + half
        add(
            ref.at[pl.ds(0, conv_rows)],
            wide.at[pl.ds(pl.multiple_of(unit * conv_rows, conv_rows), conv_rows)],
        )
        add(
            ref.at[pl.ds(conv_rows, mix_rows)],
            mix.at[pl.ds(pl.multiple_of(unit * mix_rows, mix_rows), mix_rows)],
        )
    return copies


def normalise(xm, xp, dxm, dxp, gm, gp, width):
    total = jnp.sum(xm * xm, axis=1, keepdims=True) + jnp.sum(xp * xp, axis=1, keepdims=True)
    cross = jnp.sum(xm * dxm, axis=1, keepdims=True) + jnp.sum(xp * dxp, axis=1, keepdims=True)
    scale = lax.rsqrt(total / width + EPS)
    factor = scale * scale * scale * (cross / width)
    return (
        (gm * xm * scale).astype(BF16),
        (gp * xp * scale).astype(BF16),
        (gm * (dxm * scale - xm * factor)).astype(BF16),
        (gp * (dxp * scale - xp * factor)).astype(BF16),
    )


def gate_into(out, full, dfull, branch):
    tanh_f = jnp.tanh(full[:, :branch])
    sig_g = jax.nn.sigmoid(full[:, branch:])
    out[0][...] = (tanh_f * sig_g).astype(BF16)
    out[1][...] = (
        (1.0 - tanh_f * tanh_f) * sig_g * dfull[:, :branch]
        + tanh_f * sig_g * (1.0 - sig_g) * dfull[:, branch:]
    ).astype(BF16)


def conv0_kernel(cfg, place, gm_ref, gp_ref, *refs):
    rows, half, branch, blocks, starts, slabs, conv_rows, mix_rows, pairs = cfg
    mine = refs[:blocks]
    theirs = refs[blocks : 2 * blocks]
    n_in = 2 * blocks + (2 if pairs is None else len(pairs[1]))
    convs = refs[2 * blocks : n_in]
    z_ref, mix_ref, wide, hm, hp, acc, sems = refs[n_in:]
    copies = weight_copies(place, convs, conv_rows, mix_rows, pairs, wide, mix_ref, sems)
    for copy in copies:
        copy.start()
    gm = gm_ref[0:1, :]
    gp = gp_ref[0:1, :]
    step = 64

    for b in range(blocks):
        base = (blocks - 1 - b) * rows

        def body(i, carry, b=b, base=base):
            at = pl.multiple_of(i * step, step)
            to = pl.multiple_of(base + i * step, step)
            xm = mine[b][0, pl.ds(at, step), :].astype(F32)
            dxm = mine[b][1, pl.ds(at, step), :].astype(F32)
            xp = theirs[b][0, pl.ds(at, step), :].astype(F32)
            dxp = theirs[b][1, pl.ds(at, step), :].astype(F32)
            a, c, d, e = normalise(xm, xp, dxm, dxp, gm, gp, 2 * half)
            hm[0, pl.ds(to, step), :] = a
            hp[0, pl.ds(to, step), :] = c
            hm[1, pl.ds(to, step), :] = d
            hp[1, pl.ds(to, step), :] = e
            return carry

        lax.fori_loop(0, rows // step, body, 0)
    for copy in copies:
        copy.wait()
    c = place[2]
    at_m = pl.multiple_of(c * half, half)
    at_p = pl.multiple_of((1 - c) * half, half)
    for begin, size, lags in slabs:
        for v in range(2):
            for k in range(TAPS):
                row = starts[lags + k]
                part = jnp.dot(
                    hm[v, row : row + size, :],
                    wide[pl.ds(2 * half * k + at_m, half), :],
                    preferred_element_type=F32,
                ) + jnp.dot(
                    hp[v, row : row + size, :],
                    wide[pl.ds(2 * half * k + at_p, half), :],
                    preferred_element_type=F32,
                )
                if k == 0:
                    acc[v, 0:size, :] = part
                else:
                    acc[v, 0:size, :] += part
        for r in range(0, size, rows):
            gate_into(
                (
                    z_ref.at[0, begin + r : begin + r + rows, :],
                    z_ref.at[1, begin + r : begin + r + rows, :],
                ),
                acc[0, r : r + rows, :],
                acc[1, r : r + rows, :],
                branch,
            )


def mix0_kernel(cfg, place, gm_ref, gp_ref, zm_ref, zp_ref, mixm_ref, mixp_ref, *refs):
    rows, half, branch, layer = cfg
    mine = refs[:TAPS]
    theirs = refs[TAPS : 2 * TAPS]
    hm_ref, hp_ref, state_ref = refs[2 * TAPS :]
    c = place[2]
    at_m = pl.ds(pl.multiple_of(c * branch, branch), branch)
    at_p = pl.ds(pl.multiple_of((1 - c) * branch, branch), branch)
    gm = gm_ref[layer : layer + 1, :]
    gp = gp_ref[layer : layer + 1, :]
    step = min(128, rows)
    for j in range(TAPS):
        base = (TAPS - 1 - j) * rows

        def body(i, carry, j=j, base=base):
            at = pl.multiple_of(i * step, step)
            to = pl.multiple_of(base + i * step, step)
            new = []
            for v in range(2):
                zm = zm_ref[v, pl.ds(to, step), :]
                zp = zp_ref[v, pl.ds(to, step), :]
                for x_ref, mix in ((mine[j], mixm_ref), (theirs[j], mixp_ref)):
                    y = jnp.dot(zm, mix[at_m, :], preferred_element_type=F32)
                    y = y + jnp.dot(zp, mix[at_p, :], preferred_element_type=F32)
                    new.append((x_ref[v, pl.ds(at, step), :].astype(F32) + y).astype(BF16))
            if j == 0:
                state_ref[0, pl.ds(at, step), :] = new[0]
                state_ref[1, pl.ds(at, step), :] = new[2]
            xm, xp, dxm, dxp = (t.astype(F32) for t in new)
            a, b, d, e = normalise(xm, xp, dxm, dxp, gm, gp, 2 * half)
            hm_ref[0, pl.ds(to, step), :] = a
            hp_ref[0, pl.ds(to, step), :] = b
            hm_ref[1, pl.ds(to, step), :] = d
            hp_ref[1, pl.ds(to, step), :] = e
            return carry

        lax.fori_loop(0, rows // step, body, 0)


def conv1_kernel(cfg, place, hm, hp, *refs):
    rows, half, branch, conv_rows, mix_rows, pairs = cfg
    n_in = 2 if pairs is None else len(pairs[1])
    convs = refs[:n_in]
    z_ref, mix_ref, wide, acc, sems = refs[n_in:]
    copies = weight_copies(place, convs, conv_rows, mix_rows, pairs, wide, mix_ref, sems)
    for copy in copies:
        copy.start()
    for copy in copies:
        copy.wait()
    c = place[2]
    at_m = pl.multiple_of(c * half, half)
    at_p = pl.multiple_of((1 - c) * half, half)
    for v in range(2):
        for k in range(TAPS):
            row = (TAPS - 1 - k) * rows
            part = jnp.dot(
                hm[v, row : row + rows, :],
                wide[pl.ds(2 * half * k + at_m, half), :],
                preferred_element_type=F32,
            ) + jnp.dot(
                hp[v, row : row + rows, :],
                wide[pl.ds(2 * half * k + at_p, half), :],
                preferred_element_type=F32,
            )
            if k == 0:
                acc[v, :, :] = part
            else:
                acc[v, :, :] += part
    gate_into((z_ref.at[0], z_ref.at[1]), acc[0], acc[1], branch)


def mix1_kernel(cfg, place, zm_ref, zp_ref, mix_ref, state_ref, out_ref, dout_ref):
    (branch,) = cfg
    c = place[2]
    at_m = pl.ds(pl.multiple_of(c * branch, branch), branch)
    at_p = pl.ds(pl.multiple_of((1 - c) * branch, branch), branch)
    for v, out in ((0, out_ref), (1, dout_ref)):
        y = jnp.dot(zm_ref[v], mix_ref[at_m, :], preferred_element_type=F32)
        y = y + jnp.dot(zp_ref[v], mix_ref[at_p, :], preferred_element_type=F32)
        out[...] = (state_ref[v].astype(F32) + y).astype(BF16)


def gather_weights(chunks, seq, share):
    order = []
    layers = []
    hops = seq // 2
    for chunk, across in zip(chunks, share):
        pieces = []
        order = []
        for k in range(hops):
            own = chunk if k == 0 else ring(chunk, seq, 2 * k)
            by_x = swap_pair(own, seq)
            by_y = swap_groups(own)
            both = swap_groups(by_x) if k < across else swap_pair(by_y, seq)
            for piece, dx, dy in ((own, 0, 0), (by_x, 1, 0), (by_y, 0, 1), (both, 1, 1)):
                pieces.append(piece)
                order.append((2 * k, dx, dy))
        layers.append(pieces)
    return layers, (seq, tuple(order))


def on_device(signal, tangent, gains, convolution_kernel, mixing_kernel):
    rows, half = signal.shape
    seq = lax.axis_size("seq")
    layers = gains.shape[0]
    branch = convolution_kernel.shape[3]
    shard = convolution_kernel.shape[1]
    mix_shard = mixing_kernel.shape[1]
    lag = rows * seq // 16
    place = jnp.stack([lax.axis_index("seq"), lax.axis_index("groups"), lax.axis_index("chan")])
    place = place.astype(jnp.int32)
    wide_rows, mix_whole = shard * seq, mix_shard * seq

    conv_local = convolution_kernel.reshape(layers, shard, 2 * branch)
    small = seq <= 8
    if small:
        conv_rows, mix_rows = shard // 2, mix_shard // 2
        g = lax.axis_index("groups")
        chunks = [
            jnp.concatenate(
                [
                    lax.dynamic_slice_in_dim(conv_local[l], g * conv_rows, conv_rows, 0),
                    lax.dynamic_slice_in_dim(mixing_kernel[l], g * mix_rows, mix_rows, 0),
                ],
                0,
            )
            for l in range(layers)
        ]
        weights, pairs = gather_weights(chunks, seq, (3, 2))
    else:
        conv_rows, mix_rows, pairs = shard, mix_shard, None
        weights = [
            [
                lax.all_gather(conv_local[l], "seq", axis=0, tiled=True),
                lax.all_gather(mixing_kernel[l], "seq", axis=0, tiled=True),
            ]
            for l in range(layers)
        ]

    own = jnp.stack([signal, tangent], 0)
    joined = 2 * lag == rows
    if joined:
        two = from_behind(own, seq, 2)
        odd = lax.rem(lax.axis_index("seq"), 2) == 1
        one = swap_pair(jnp.where(odd, two, own), seq)
        three = from_behind(one, seq, 2)
        mine = [own, one, two, three]
        step, used = lag, (0, 1, 2)
    else:
        mine = [own] + [from_behind(own, seq, k * (lag // rows)) for k in range(1, 7)]
        step, used = rows, (0, 2, 4)
    theirs = [swap_chan(block) for block in mine]
    gains_p = swap_chan(gains)
    blocks = len(mine)
    tall = blocks * rows
    starts = tuple(tall - rows - m * step for m in range(7))
    if joined:
        slabs = ((0, TAPS * rows, 4),)
    else:
        slabs = tuple(((TAPS - 1 - j) * rows, rows, 2 * j) for j in range(TAPS))
    slab = slabs[0][1]

    n_copies = 2 if pairs is None else 2 * len(pairs[1])
    cfg = (rows, half, branch, blocks, starts, slabs, conv_rows, mix_rows, pairs)
    z_mine, mix_mine = pl.pallas_call(
        functools.partial(conv0_kernel, cfg),
        out_shape=(
            jax.ShapeDtypeStruct((2, TAPS * rows, branch), BF16),
            jax.ShapeDtypeStruct((mix_whole, half), BF16),
        ),
        in_specs=[SMEM, VMEM, VMEM] + [VMEM] * (2 * blocks) + [ANY] * len(weights[0]),
        out_specs=(VMEM, VMEM),
        scratch_shapes=[
            pltpu.VMEM((wide_rows, 2 * branch), BF16),
            pltpu.VMEM((2, tall, half), BF16),
            pltpu.VMEM((2, tall, half), BF16),
            pltpu.VMEM((2, slab, 2 * branch), F32),
            pltpu.SemaphoreType.DMA((n_copies,)),
        ],
        compiler_params=PARAMS,
        name="conv0",
    )(place, gains, gains_p, *mine, *theirs, *weights[0])
    mix_theirs = swap_chan(mix_mine)
    z_theirs = swap_chan(z_mine)
    hm, hp, state = pl.pallas_call(
        functools.partial(mix0_kernel, (rows, half, branch, 1)),
        out_shape=(
            jax.ShapeDtypeStruct((2, TAPS * rows, half), BF16),
            jax.ShapeDtypeStruct((2, TAPS * rows, half), BF16),
            jax.ShapeDtypeStruct((2, rows, half), BF16),
        ),
        in_specs=[SMEM] + [VMEM] * (6 + 2 * TAPS),
        out_specs=(VMEM, VMEM, VMEM),
        compiler_params=PARAMS,
        name="mix0",
    )(
        place,
        gains,
        gains_p,
        z_mine,
        z_theirs,
        mix_mine,
        mix_theirs,
        *[mine[b] for b in used],
        *[theirs[b] for b in used],
    )
    z_mine, mix_mine = pl.pallas_call(
        functools.partial(conv1_kernel, (rows, half, branch, conv_rows, mix_rows, pairs)),
        out_shape=(
            jax.ShapeDtypeStruct((2, rows, branch), BF16),
            jax.ShapeDtypeStruct((mix_whole, half), BF16),
        ),
        in_specs=[SMEM, VMEM, VMEM] + [ANY] * len(weights[1]),
        out_specs=(VMEM, VMEM),
        scratch_shapes=[
            pltpu.VMEM((wide_rows, 2 * branch), BF16),
            pltpu.VMEM((2, rows, 2 * branch), F32),
            pltpu.SemaphoreType.DMA((n_copies,)),
        ],
        compiler_params=PARAMS,
        name="conv1",
    )(place, hm, hp, *weights[1])
    z_theirs = swap_chan(z_mine)
    return pl.pallas_call(
        functools.partial(mix1_kernel, (branch,)),
        out_shape=(
            jax.ShapeDtypeStruct((rows, half), BF16),
            jax.ShapeDtypeStruct((rows, half), BF16),
        ),
        in_specs=[SMEM] + [VMEM] * 4,
        out_specs=(VMEM, VMEM),
        compiler_params=PARAMS,
        name="mix1",
    )(place, z_mine, z_theirs, mix_mine, state)


def solution(mesh):
    return jax.shard_map(
        on_device,
        mesh=mesh,
        in_specs=(
            P(("groups", "seq"), "chan"),
            P(("groups", "seq"), "chan"),
            P(None, "chan"),
            P(None, "seq", None, "chan"),
            P(None, "seq", "chan"),
        ),
        out_specs=(P(("groups", "seq"), "chan"), P(("groups", "seq"), "chan")),
        check_vma=False,
    )
```

time: 247 us -> 162 us (0.66)
  blocking collectives: 84 us -> 0 us
  starting transfers between devices: 14.4 us -> 50.9 us
  Pallas kernels: 0 us -> 28.7 us
  waiting for transfers between devices: 97.6 us -> 72.1 us
  local copies, waits for them, and re-layouts: 21.7 us -> 5.28 us
  between operations: 14 us -> 1.1 us
  matrix products: 10.3 us -> 0 us
    all_gather x4 -> x0, blocking collectives: 79 us -> none  [the longest x2 74.6 us: on_device(): lax.all_gather(mixing_kernel[layer_number], 'seq', axis=0, tiled=True)]
    all_gather x4 -> x0, waiting for transfers between devices: 73 us -> none  [the longest x2 73 us: on_device(): conv_whole = lax.all_gather(conv_local, 'seq', axis=0, tiled=True)]
    ppermute x5 -> x41, waiting for transfers between devices: 24.6 us -> 72.1 us  [the longest x13 33.6 us: swap_groups(): return lax.ppermute(block, 'groups', [(0, 1), (1, 0)])]
    ppermute x5 -> x41, starting transfers between devices: 14.2 us -> 50.9 us  [the longest x2 15.7 us: from_behind(): return lax.ppermute(block, 'seq', [(s - by, s) for s in range(by, seq)])]
    pallas_call x0 -> x4, Pallas kernels: none -> 28.7 us  [the longest x1 11.2 us: on_device(): pl.pallas_call(functools.partial(conv0_kernel, cfg), out_shape=(jax.Shape...]
    all_gather x2 -> x0, local copies, waits for them, and re-layouts: 10.3 us -> none  [on_device(): stacked = lax.all_gather(taps, 'chan', axis=3, tiled=True)]
    dot_general x4 -> x0, matrix products: 10.3 us -> none  [the longest x2 9.3 us: on_device(): full = jnp.dot(left, conv_whole, preferred_element_type=jnp.float32)]
    unnamed x12 -> x92, local copies, waits for them, and re-layouts: 10.1 us -> 3.3 us
  transfers between devices with their start and end apart: 9 -> 41, of which waited for: 5 -> 19; matrix products, arithmetic and copies ran while one was open for 7% -> 2% of each run, Pallas kernels for 0% -> 5%
where the time goes in v1:
time: 162 us; the launch traced here: 160 us
  waiting for transfers between devices  72.1 us (45%)
  starting transfers between devices  50.9 us (31%)
  Pallas kernels  28.7 us (18%)
  local copies, waits for them, and re-layouts  5.28 us (3%)
  other arithmetic  1.84 us (1%)
    ppermute x13, waiting for transfers between devices, swap_groups(): return lax.ppermute(block, 'groups', [(0, 1), (1, 0)])  33.6 us
    ppermute x6, waiting for transfers between devices, ring(): return lax.ppermute(block, 'seq', [(s, (s + by) % seq) for s in range(seq)])  16.6 us
    ppermute x2, starting transfers between devices, from_behind(): return lax.ppermute(block, 'seq', [(s - by, s) for s in range(by, seq)])  15.7 us
    ppermute x13, starting transfers between devices, swap_groups(): return lax.ppermute(block, 'groups', [(0, 1), (1, 0)])  12.7 us
    ppermute x6, starting transfers between devices, ring(): return lax.ppermute(block, 'seq', [(s, (s + by) % seq) for s in range(seq)])  12.5 us
    pallas_call x1, Pallas kernels, on_device(): pl.pallas_call(functools.partial(conv0_kernel, cfg), out_shape=(jax.Shape...  11.2 us
    ppermute x12, waiting for transfers between devices, swap_pair(): return lax.ppermute(block, 'seq', [(s, s ^ 1) for s in range(seq)])  10.3 us
    ppermute x2, waiting for transfers between devices, from_behind(): return lax.ppermute(block, 'seq', [(s - by, s) for s in range(by, seq)])  9.82 us
  transfers between devices with their start and end apart: 41, of which 19 were waited for; matrix products, arithmetic and copies ran while one was open for 2% of the time, Pallas kernels for 5%

profile of v1, /device:TPU:0, one launch (start us, length us, event | category | flops | bytes accessed | tf_op | source)
XLA Modules:
  0.0 159.9 jit_solution(17577896865106531211)
XLA Ops:
  0.6 1.2 pad_maximum_fusion.refs_0_
  1.8 5.1 %collective-permute-start.1 = (bf16[2,256,512]{2,1,0:T(8,128)(2,1)S(1)}, bf16[2,256,512]{2,1,0:T(8,128)(2,1)S(1)}, u32[]{:S(2)}, u32[]{:S(2)}) collective-permute-start(bf16[2,256,512]{2,1,0:T(8,128)(2,1)S(1)} %pad_maximum_fusion.refs_0_), channel_id=1, source_target_pairs={{0,4},{2,6},{4,8},{6,10},{8,12},{10,14},{1,5},{3,7},{5,9},{7,11},{... | collective-permute-start | bytes 1572872 | tf_op jit(solution)/shard_map/ppermute | solution.py:37
  7.6 0.6 fusion.1
  8.3 9.8 %collective-permute-done.1.refs_2_ = bf16[2,256,512]{2,1,0:T(8,128)(2,1)S(1)} collective-permute-done((bf16[2,256,512]{2,1,0:T(8,128)(2,1)S(1)}, bf16[2,256,512]{2,1,0:T(8,128)(2,1)S(1)}, u32[]{:S(2)}, u32[]{:S(2)}) %collective-permute-start.1) | collective-permute-done | bytes 524320 | tf_op jit(solution)/shard_map/ppermute | solution.py:37
  18.2 1.6 collective-permute-start.2
  19.7 2.5 %collective-permute-start.11 = (bf16[224,512]{1,0:T(8,128)(2,1)S(1)}, bf16[224,512]{1,0:T(8,128)(2,1)S(1)}, u32[]{:S(2)}, u32[]{:S(2)}) collective-permute-start(bf16[224,512]{1,0:T(8,128)(2,1)S(1)} %pad_maximum_fusion.1.refs_8_), channel_id=1, source_target_pairs={{0,4},{2,6},{4,8},{6,10},{8,12},{10,14},{12,0},{14,2},{1,5},{3,7},... | collective-permute-start | bytes 688136 | tf_op jit(solution)/shard_map/ppermute | solution.py:33
  22.3 2.6 %collective-permute-start.15 = (bf16[224,512]{1,0:T(8,128)(2,1)S(1)}, bf16[224,512]{1,0:T(8,128)(2,1)S(1)}, u32[]{:S(2)}, u32[]{:S(2)}) collective-permute-start(bf16[224,512]{1,0:T(8,128)(2,1)S(1)} %pad_maximum_fusion.1.refs_8_), channel_id=1, source_target_pairs={{0,8},{2,10},{4,12},{6,14},{8,0},{10,2},{12,4},{14,6},{1,9},{3,11}... | collective-permute-start | bytes 688136 | tf_op jit(solution)/shard_map/ppermute | solution.py:33
  24.9 1.3 collective-permute-start.19
  26.8 3.5 %collective-permute-done.11.refs_12_ = bf16[224,512]{1,0:T(8,128)(2,1)S(1)} collective-permute-done((bf16[224,512]{1,0:T(8,128)(2,1)S(1)}, bf16[224,512]{1,0:T(8,128)(2,1)S(1)}, u32[]{:S(2)}, u32[]{:S(2)}) %collective-permute-start.11) | collective-permute-done | bytes 229408 | tf_op jit(solution)/shard_map/ppermute | solution.py:33
  30.3 1.5 collective-permute-start.9
  31.8 1.3 collective-permute-done.2.refs_1_
  33.1 10.6 %collective-permute-start.3 = (bf16[2,256,512]{2,1,0:T(8,128)(2,1)S(1)}, bf16[2,256,512]{2,1,0:T(8,128)(2,1)}, u32[]{:S(2)}, u32[]{:S(2)}) collective-permute-start(bf16[2,256,512]{2,1,0:T(8,128)(2,1)S(1)} %collective-permute-done.2.refs_1_), channel_id=1, source_target_pairs={{0,4},{2,6},{4,8},{6,10},{8,12},{10,14},{1,5},{3,7},{5,9},{7,11},{... | collective-permute-start | bytes 1572872 | tf_op jit(solution)/shard_map/ppermute | solution.py:37
  44.2 1.5 collective-permute-start.16
  46.3 1.5 collective-permute-start.13
  47.8 2.0 %collective-permute-done.12.refs_13_ = bf16[224,512]{1,0:T(8,128)(2,1)} collective-permute-done((bf16[224,512]{1,0:T(8,128)(2,1)S(1)}, bf16[224,512]{1,0:T(8,128)(2,1)}, u32[]{:S(2)}, u32[]{:S(2)}) %collective-permute-start.12) | collective-permute-done | bytes 229408 | tf_op jit(solution)/shard_map/ppermute | solution.py:29
  49.9 2.3 %collective-permute-done.16.refs_17_ = bf16[224,512]{1,0:T(8,128)(2,1)S(1)} collective-permute-done((bf16[224,512]{1,0:T(8,128)(2,1)S(1)}, bf16[224,512]{1,0:T(8,128)(2,1)S(1)}, u32[]{:S(2)}, u32[]{:S(2)}) %collective-permute-start.16) | collective-permute-done | bytes 229408 | tf_op jit(solution)/shard_map/ppermute | solution.py:29
  53.2 2.2 %collective-permute-done.13.refs_14_ = bf16[224,512]{1,0:T(8,128)(2,1)S(1)} collective-permute-done((bf16[224,512]{1,0:T(8,128)(2,1)S(1)}, bf16[224,512]{1,0:T(8,128)(2,1)S(1)}, u32[]{:S(2)}, u32[]{:S(2)}) %collective-permute-start.13) | collective-permute-done | bytes 229408 | tf_op jit(solution)/shard_map/ppermute | solution.py:25
  56.0 4.8 %collective-permute-done.17.refs_18_ = bf16[224,512]{1,0:T(8,128)(2,1)S(1)} collective-permute-done((bf16[224,512]{1,0:T(8,128)(2,1)S(1)}, bf16[224,512]{1,0:T(8,128)(2,1)S(1)}, u32[]{:S(2)}, u32[]{:S(2)}) %collective-permute-start.17) | collective-permute-done | bytes 229408 | tf_op jit(solution)/shard_map/ppermute | solution.py:25
  61.4 2.7 %collective-permute-done.10.refs_11_ = bf16[224,512]{1,0:T(8,128)(2,1)S(1)} collective-permute-done((bf16[224,512]{1,0:T(8,128)(2,1)S(1)}, bf16[224,512]{1,0:T(8,128)(2,1)S(1)}, u32[]{:S(2)}, u32[]{:S(2)}) %collective-permute-start.10) | collective-permute-done | bytes 229408 | tf_op jit(solution)/shard_map/ppermute | solution.py:25
  64.1 0.7 copy-done.31
  65.3 0.8 dynamic-slice_bitcast_fusion
  66.1 1.5 collective-permute-start.18
  67.6 6.0 %collective-permute-done.14.refs_15_ = bf16[224,512]{1,0:T(8,128)(2,1)} collective-permute-done((bf16[224,512]{1,0:T(8,128)(2,1)}, bf16[224,512]{1,0:T(8,128)(2,1)}, u32[]{:S(2)}, u32[]{:S(2)}) %collective-permute-start.14) | collective-permute-done | bytes 229408 | tf_op jit(solution)/shard_map/ppermute | solution.py:25
  74.8 1.2 collective-permute-done.18.refs_19_
  76.0 3.9 %collective-permute-done.22.refs_23_ = bf16[224,512]{1,0:T(8,128)(2,1)S(1)} collective-permute-done((bf16[224,512]{1,0:T(8,128)(2,1)}, bf16[224,512]{1,0:T(8,128)(2,1)S(1)}, u32[]{:S(2)}, u32[]{:S(2)}) %collective-permute-start.22) | collective-permute-done | bytes 229408 | tf_op jit(solution)/shard_map/ppermute | solution.py:29
  79.9 0.6 copy-done.41
  81.0 11.2 %conv0.1 = (bf16[2,768,256]{2,1,0:T(8,128)(2,1)}, bf16[512,512]{1,0:T(8,128)(2,1)}) custom-call(s32[3]{0:T(128)} %pad_add_fusion.place, f32[2,512]{1,0:T(2,128)} %gm_ref.3, f32[2,512]{1,0:T(2,128)} %copy-done.44, bf16[2,256,512]{2,1,0:T(8,128)(2,1)} %copy-done, bf16[2,256,512]{2,1,0:T(8,128)(2,1)} %copy-done.2, bf16[2,256,512]{2,1,0:T(8,128)(2,1)} %copy-done.1, ...), custom_call_target="tpu_custom_call" | custom-call | tf_op jit(solution)/shard_map/conv0/pallas_call | solution.py:322
  92.3 2.4 %collective-permute-start.28 = (bf16[224,512]{1,0:T(8,128)(2,1)S(1)}, bf16[224,512]{1,0:T(8,128)(2,1)S(1)}, u32[]{:S(2)}, u32[]{:S(2)}) collective-permute-start(bf16[224,512]{1,0:T(8,128)(2,1)S(1)} %pad_maximum_fusion.2.refs_0_), channel_id=1, source_target_pairs={{0,4},{2,6},{4,8},{6,10},{8,12},{10,14},{12,0},{14,2},{1,5},{3,7},... | collective-permute-start | bytes 688136 | tf_op jit(solution)/shard_map/ppermute | solution.py:33
  94.7 1.7 %collective-permute-start.32 = (bf16[224,512]{1,0:T(8,128)(2,1)S(1)}, bf16[224,512]{1,0:T(8,128)(2,1)S(1)}, u32[]{:S(2)}, u32[]{:S(2)}) collective-permute-start(bf16[224,512]{1,0:T(8,128)(2,1)S(1)} %pad_maximum_fusion.2.refs_0_), channel_id=1, source_target_pairs={{0,8},{2,10},{4,12},{6,14},{8,0},{10,2},{12,4},{14,6},{1,9},{3,11}... | collective-permute-start | bytes 688136 | tf_op jit(solution)/shard_map/ppermute | solution.py:33
  96.4 2.0 %collective-permute-start.36 = (bf16[224,512]{1,0:T(8,128)(2,1)S(1)}, bf16[224,512]{1,0:T(8,128)(2,1)S(1)}, u32[]{:S(2)}, u32[]{:S(2)}) collective-permute-start(bf16[224,512]{1,0:T(8,128)(2,1)S(1)} %pad_maximum_fusion.2.refs_0_), channel_id=1, source_target_pairs={{0,12},{2,14},{4,0},{6,2},{8,4},{10,6},{12,8},{14,10},{1,13},{3,15... | collective-permute-start | bytes 688136 | tf_op jit(solution)/shard_map/ppermute | solution.py:33
  98.3 0.7 collective-permute-start.25
  99.0 3.7 %collective-permute-done.28.refs_4_ = bf16[224,512]{1,0:T(8,128)(2,1)S(1)} collective-permute-done((bf16[224,512]{1,0:T(8,128)(2,1)S(1)}, bf16[224,512]{1,0:T(8,128)(2,1)S(1)}, u32[]{:S(2)}, u32[]{:S(2)}) %collective-permute-start.28) | collective-permute-done | bytes 229408 | tf_op jit(solution)/shard_map/ppermute | solution.py:33
  102.7 9.4 %collective-permute-done.32.refs_8_ = bf16[224,512]{1,0:T(8,128)(2,1)S(1)} collective-permute-done((bf16[224,512]{1,0:T(8,128)(2,1)S(1)}, bf16[224,512]{1,0:T(8,128)(2,1)S(1)}, u32[]{:S(2)}, u32[]{:S(2)}) %collective-permute-start.32) | collective-permute-done | bytes 229408 | tf_op jit(solution)/shard_map/ppermute | solution.py:33
  112.1 1.4 collective-permute-start.26
  114.7 5.9 %collective-permute-done.26.refs_2_ = bf16[224,512]{1,0:T(8,128)(2,1)S(1)} collective-permute-done((bf16[224,512]{1,0:T(8,128)(2,1)S(1)}, bf16[224,512]{1,0:T(8,128)(2,1)S(1)}, u32[]{:S(2)}, u32[]{:S(2)}) %collective-permute-start.26) | collective-permute-done | bytes 229408 | tf_op jit(solution)/shard_map/ppermute | solution.py:25
  120.6 1.4 collective-permute-start.38
  122.0 0.6 collective-permute-start.30
  122.6 2.9 %collective-permute-done.34.refs_10_ = bf16[224,512]{1,0:T(8,128)(2,1)S(1)} collective-permute-done((bf16[224,512]{1,0:T(8,128)(2,1)S(1)}, bf16[224,512]{1,0:T(8,128)(2,1)S(1)}, u32[]{:S(2)}, u32[]{:S(2)}) %collective-permute-start.34) | collective-permute-done | bytes 229408 | tf_op jit(solution)/shard_map/ppermute | solution.py:25
  126.0 4.4 %collective-permute-done.38.refs_14_ = bf16[224,512]{1,0:T(8,128)(2,1)S(1)} collective-permute-done((bf16[224,512]{1,0:T(8,128)(2,1)S(1)}, bf16[224,512]{1,0:T(8,128)(2,1)S(1)}, u32[]{:S(2)}, u32[]{:S(2)}) %collective-permute-start.38) | collective-permute-done | bytes 229408 | tf_op jit(solution)/shard_map/ppermute | solution.py:25
  130.9 3.4 %collective-permute-done.30.refs_6_ = bf16[224,512]{1,0:T(8,128)(2,1)S(1)} collective-permute-done((bf16[224,512]{1,0:T(8,128)(2,1)S(1)}, bf16[224,512]{1,0:T(8,128)(2,1)S(1)}, u32[]{:S(2)}, u32[]{:S(2)}) %collective-permute-start.30) | collective-permute-done | bytes 229408 | tf_op jit(solution)/shard_map/ppermute | solution.py:25
  134.4 1.4 collective-permute-start.27
  136.9 1.5 collective-permute-start.39
  138.4 8.2 %mix0.1 = (bf16[2,768,512]{2,1,0:T(8,128)(2,1)}, bf16[2,768,512]{2,1,0:T(8,128)(2,1)}, bf16[2,256,512]{2,1,0:T(8,128)(2,1)}) custom-call(s32[3]{0:T(128)} %pad_add_fusion.place, f32[2,512]{1,0:T(2,128)} %gm_ref.3, f32[2,512]{1,0:T(2,128)} %copy-done.44, bf16[2,768,256]{2,1,0:T(8,128)(2,1)} %get-tuple-element.9.zm_ref, bf16[2,768,256]{2,1,0:T(8,128)(2,1)} %copy-done.11, ...), custom_call_target="tpu_custom_call" | custom-call | tf_op jit(solution)/shard_map/mix0/pallas_call | solution.py:342
  146.7 0.7 collective-permute-done.39.refs_15_
  148.1 6.8 %conv1.1 = (bf16[2,256,256]{2,1,0:T(8,128)(2,1)}, bf16[512,512]{1,0:T(8,128)(2,1)}) custom-call(s32[3]{0:T(128)} %pad_add_fusion.place, bf16[2,768,512]{2,1,0:T(8,128)(2,1)} %get-tuple-element.11.hm, bf16[2,768,512]{2,1,0:T(8,128)(2,1)} %get-tuple-element.12.hp, bf16[224,512]{1,0:T(8,128)(2,1)} %copy-done.9, bf16[224,512]{1,0:T(8,128)(2,1)} %copy-done.24, ...), custom_call_target="tpu_custom_call" | custom-call | tf_op jit(solution)/shard_map/conv1/pallas_call | solution.py:364
  155.0 1.7 %collective-permute-done.40.zp_ref = bf16[2,256,256]{2,1,0:T(8,128)(2,1)S(1)} collective-permute-done((bf16[2,256,256]{2,1,0:T(8,128)(2,1)}, bf16[2,256,256]{2,1,0:T(8,128)(2,1)S(1)}, u32[]{:S(2)}, u32[]{:S(2)}) %collective-permute-start.40) | collective-permute-done | bytes 262176 | tf_op jit(solution)/shard_map/ppermute | solution.py:21
  156.7 0.7 copy-done.13
  157.4 2.5 %mix1.1 = (bf16[256,512]{1,0:T(8,128)(2,1)}, bf16[256,512]{1,0:T(8,128)(2,1)}) custom-call(s32[3]{0:T(128)} %pad_add_fusion.place, bf16[2,256,256]{2,1,0:T(8,128)(2,1)} %get-tuple-element.13.zm_ref, bf16[2,256,256]{2,1,0:T(8,128)(2,1)} %copy-done.13, bf16[512,512]{1,0:T(8,128)(2,1)} %get-tuple-element.14.mix_ref, ...), custom_call_target="tpu_custom_call" | custom-call | tf_op jit(solution)/shard_map/mix1/pallas_call | solution.py:381
  (141 shorter events, 10.6 us)
Async XLA Ops:
  1.8 48.1 %copy-start = (bf16[2,256,512]{2,1,0:T(8,128)(2,1)}, bf16[2,256,512]{2,1,0:T(8,128)(2,1)S(1)}, u32[]{:S(2)}) copy-start(bf16[2,256,512]{2,1,0:T(8,128)(2,1)S(1)} %pad_maximum_fusion.refs_0_) | copy-start | bytes 1572868
  1.8 16.2 %collective-permute-start.1 = (bf16[2,256,512]{2,1,0:T(8,128)(2,1)S(1)}, bf16[2,256,512]{2,1,0:T(8,128)(2,1)S(1)}, u32[]{:S(2)}, u32[]{:S(2)}) collective-permute-start(bf16[2,256,512]{2,1,0:T(8,128)(2,1)S(1)} %pad_maximum_fusion.refs_0_), channel_id=1, source_target_pairs={{0,4},{2,6},{4,8},{6,10},{8,12},{10,14},{1,5},{3,7},{5,9},{7,11},{... | collective-permute-start | bytes 1572872 | tf_op jit(solution)/shard_map/ppermute | solution.py:37
  18.1 56.7 %copy-start.1 = (bf16[2,256,512]{2,1,0:T(8,128)(2,1)}, bf16[2,256,512]{2,1,0:T(8,128)(2,1)S(1)}, u32[]{:S(2)}) copy-start(bf16[2,256,512]{2,1,0:T(8,128)(2,1)S(1)} %collective-permute-done.1.refs_2_) | copy-start | bytes 1572868
  18.2 14.9 %collective-permute-start.2 = (bf16[2,256,512]{2,1,0:T(8,128)(2,1)S(1)}, bf16[2,256,512]{2,1,0:T(8,128)(2,1)S(1)}, u32[]{:S(2)}, u32[]{:S(2)}) collective-permute-start(bf16[2,256,512]{2,1,0:T(8,128)(2,1)S(1)} %broadcast_select_fusion), channel_id=1, source_target_pairs={{0,2},{2,0},{4,6},{6,4},{8,10},{10,8},{12,14},{14,12},{1,3},{3,1},... | collective-permute-start | bytes 1572872 | tf_op jit(solution)/shard_map/ppermute | solution.py:29
  19.7 10.5 %collective-permute-start.11 = (bf16[224,512]{1,0:T(8,128)(2,1)S(1)}, bf16[224,512]{1,0:T(8,128)(2,1)S(1)}, u32[]{:S(2)}, u32[]{:S(2)}) collective-permute-start(bf16[224,512]{1,0:T(8,128)(2,1)S(1)} %pad_maximum_fusion.1.refs_8_), channel_id=1, source_target_pairs={{0,4},{2,6},{4,8},{6,10},{8,12},{10,14},{12,0},{14,2},{1,5},{3,7},... | collective-permute-start | bytes 688136 | tf_op jit(solution)/shard_map/ppermute | solution.py:33
  22.3 3.9 %collective-permute-start = (f32[2,512]{1,0:T(2,128)S(1)}, f32[2,512]{1,0:T(2,128)S(1)}, u32[]{:S(2)}, u32[]{:S(2)}) collective-permute-start(f32[2,512]{1,0:T(2,128)S(1)} %copy-done.43), channel_id=1, source_target_pairs={{0,1},{1,0},{2,3},{3,2},{4,5},{5,4},{6,7},{7,6},{8,9},{9,8},{10,11... | collective-permute-start | bytes 12296 | tf_op jit(solution)/shard_map/ppermute | solution.py:21
  22.3 21.4 %collective-permute-start.15 = (bf16[224,512]{1,0:T(8,128)(2,1)S(1)}, bf16[224,512]{1,0:T(8,128)(2,1)S(1)}, u32[]{:S(2)}, u32[]{:S(2)}) collective-permute-start(bf16[224,512]{1,0:T(8,128)(2,1)S(1)} %pad_maximum_fusion.1.refs_8_), channel_id=1, source_target_pairs={{0,8},{2,10},{4,12},{6,14},{8,0},{10,2},{12,4},{14,6},{1,9},{3,11}... | collective-permute-start | bytes 688136 | tf_op jit(solution)/shard_map/ppermute | solution.py:33
  24.9 19.4 %collective-permute-start.19 = (bf16[224,512]{1,0:T(8,128)(2,1)S(1)}, bf16[224,512]{1,0:T(8,128)(2,1)S(1)}, u32[]{:S(2)}, u32[]{:S(2)}) collective-permute-start(bf16[224,512]{1,0:T(8,128)(2,1)S(1)} %pad_maximum_fusion.1.refs_8_), channel_id=1, source_target_pairs={{0,12},{2,14},{4,0},{6,2},{8,4},{10,6},{12,8},{14,10},{1,13},{3,15... | collective-permute-start | bytes 688136 | tf_op jit(solution)/shard_map/ppermute | solution.py:33
  26.2 53.6 %copy-start.44 = (f32[2,512]{1,0:T(2,128)}, f32[2,512]{1,0:T(2,128)S(1)}, u32[]{:S(2)}) copy-start(f32[2,512]{1,0:T(2,128)S(1)} %collective-permute-done.gp_ref) | copy-start | bytes 12292
  26.2 19.5 %collective-permute-start.8 = (bf16[224,512]{1,0:T(8,128)(2,1)S(1)}, bf16[224,512]{1,0:T(8,128)(2,1)S(1)}, u32[]{:S(2)}, u32[]{:S(2)}) collective-permute-start(bf16[224,512]{1,0:T(8,128)(2,1)S(1)} %pad_maximum_fusion.1.refs_8_), channel_id=1, source_target_pairs={{0,2},{2,0},{4,6},{6,4},{8,10},{10,8},{12,14},{14,12},{1,3},{3,1},... | collective-permute-start | bytes 688136 | tf_op jit(solution)/shard_map/ppermute | solution.py:29
  30.3 16.0 %collective-permute-start.9 = (bf16[224,512]{1,0:T(8,128)(2,1)S(1)}, bf16[224,512]{1,0:T(8,128)(2,1)S(1)}, u32[]{:S(2)}, u32[]{:S(2)}) collective-permute-start(bf16[224,512]{1,0:T(8,128)(2,1)S(1)} %pad_maximum_fusion.1.refs_8_), channel_id=1, source_target_pairs={{0,16},{16,0},{1,17},{17,1},{2,18},{18,2},{3,19},{19,3},{4,20},{20... | collective-permute-start | bytes 688136 | tf_op jit(solution)/shard_map/ppermute | solution.py:25
  33.1 46.8 %copy-start.2 = (bf16[2,256,512]{2,1,0:T(8,128)(2,1)}, bf16[2,256,512]{2,1,0:T(8,128)(2,1)S(1)}, u32[]{:S(2)}) copy-start(bf16[2,256,512]{2,1,0:T(8,128)(2,1)S(1)} %collective-permute-done.2.refs_1_) | copy-start | bytes 1572868
  33.1 28.2 %collective-permute-start.3 = (bf16[2,256,512]{2,1,0:T(8,128)(2,1)S(1)}, bf16[2,256,512]{2,1,0:T(8,128)(2,1)}, u32[]{:S(2)}, u32[]{:S(2)}) collective-permute-start(bf16[2,256,512]{2,1,0:T(8,128)(2,1)S(1)} %collective-permute-done.2.refs_1_), channel_id=1, source_target_pairs={{0,4},{2,6},{4,8},{6,10},{8,12},{10,14},{1,5},{3,7},{5,9},{7,11},{... | collective-permute-start | bytes 1572872 | tf_op jit(solution)/shard_map/ppermute | solution.py:37
  43.7 6.1 %collective-permute-start.12 = (bf16[224,512]{1,0:T(8,128)(2,1)S(1)}, bf16[224,512]{1,0:T(8,128)(2,1)}, u32[]{:S(2)}, u32[]{:S(2)}) collective-permute-start(bf16[224,512]{1,0:T(8,128)(2,1)S(1)} %collective-permute-done.11.refs_12_), channel_id=1, source_target_pairs={{0,2},{2,0},{4,6},{6,4},{8,10},{10,8},{12,14},{14,12},{1,3},{3,1},... | collective-permute-start | bytes 688136 | tf_op jit(solution)/shard_map/ppermute | solution.py:29
  44.2 8.0 %collective-permute-start.16 = (bf16[224,512]{1,0:T(8,128)(2,1)S(1)}, bf16[224,512]{1,0:T(8,128)(2,1)S(1)}, u32[]{:S(2)}, u32[]{:S(2)}) collective-permute-start(bf16[224,512]{1,0:T(8,128)(2,1)S(1)} %collective-permute-done.15.refs_16_), channel_id=1, source_target_pairs={{0,2},{2,0},{4,6},{6,4},{8,10},{10,8},{12,14},{14,12},{1,3},{3,1},... | collective-permute-start | bytes 688136 | tf_op jit(solution)/shard_map/ppermute | solution.py:29
  45.8 7.0 %collective-permute-start.21 = (bf16[224,512]{1,0:T(8,128)(2,1)S(1)}, bf16[224,512]{1,0:T(8,128)(2,1)S(1)}, u32[]{:S(2)}, u32[]{:S(2)}) collective-permute-start(bf16[224,512]{1,0:T(8,128)(2,1)S(1)} %collective-permute-done.19.refs_20_), channel_id=1, source_target_pairs={{0,16},{16,0},{1,17},{17,1},{2,18},{18,2},{3,19},{19,3},{4,20},{20... | collective-permute-start | bytes 688136 | tf_op jit(solution)/shard_map/ppermute | solution.py:25
  46.3 9.2 %collective-permute-start.13 = (bf16[224,512]{1,0:T(8,128)(2,1)S(1)}, bf16[224,512]{1,0:T(8,128)(2,1)S(1)}, u32[]{:S(2)}, u32[]{:S(2)}) collective-permute-start(bf16[224,512]{1,0:T(8,128)(2,1)S(1)} %collective-permute-done.11.refs_12_), channel_id=1, source_target_pairs={{0,16},{16,0},{1,17},{17,1},{2,18},{18,2},{3,19},{19,3},{4,20},{20... | collective-permute-start | bytes 688136 | tf_op jit(solution)/shard_map/ppermute | solution.py:25
  49.9 16.2 %collective-permute-start.4 = (bf16[2,256,512]{2,1,0:T(8,128)(2,1)S(1)}, bf16[2,256,512]{2,1,0:T(8,128)(2,1)S(1)}, u32[]{:S(2)}, u32[]{:S(2)}) collective-permute-start(bf16[2,256,512]{2,1,0:T(8,128)(2,1)S(1)} %pad_maximum_fusion.refs_0_), channel_id=1, source_target_pairs={{0,1},{1,0},{2,3},{3,2},{4,5},{5,4},{6,7},{7,6},{8,9},{9,8},{10,11... | collective-permute-start | bytes 1572872 | tf_op jit(solution)/shard_map/ppermute | solution.py:21
  52.2 8.5 %collective-permute-start.17 = (bf16[224,512]{1,0:T(8,128)(2,1)S(1)}, bf16[224,512]{1,0:T(8,128)(2,1)S(1)}, u32[]{:S(2)}, u32[]{:S(2)}) collective-permute-start(bf16[224,512]{1,0:T(8,128)(2,1)S(1)} %collective-permute-done.15.refs_16_), channel_id=1, source_target_pairs={{0,16},{16,0},{1,17},{17,1},{2,18},{18,2},{3,19},{19,3},{4,20},{20... | collective-permute-start | bytes 688136 | tf_op jit(solution)/shard_map/ppermute | solution.py:25
  52.7 8.0 %collective-permute-start.20 = (bf16[224,512]{1,0:T(8,128)(2,1)S(1)}, bf16[224,512]{1,0:T(8,128)(2,1)S(1)}, u32[]{:S(2)}, u32[]{:S(2)}) collective-permute-start(bf16[224,512]{1,0:T(8,128)(2,1)S(1)} %collective-permute-done.19.refs_20_), channel_id=1, source_target_pairs={{0,2},{2,0},{4,6},{6,4},{8,10},{10,8},{12,14},{14,12},{1,3},{3,1},... | collective-permute-start | bytes 688136 | tf_op jit(solution)/shard_map/ppermute | solution.py:29
  55.5 8.6 %collective-permute-start.10 = (bf16[224,512]{1,0:T(8,128)(2,1)S(1)}, bf16[224,512]{1,0:T(8,128)(2,1)S(1)}, u32[]{:S(2)}, u32[]{:S(2)}) collective-permute-start(bf16[224,512]{1,0:T(8,128)(2,1)S(1)} %collective-permute-done.8.refs_9_), channel_id=1, source_target_pairs={{0,16},{16,0},{1,17},{17,1},{2,18},{18,2},{3,19},{19,3},{4,20},{20... | collective-permute-start | bytes 688136 | tf_op jit(solution)/shard_map/ppermute | solution.py:25
  60.8 19.1 %collective-permute-start.6 = (bf16[2,256,512]{2,1,0:T(8,128)(2,1)S(1)}, bf16[2,256,512]{2,1,0:T(8,128)(2,1)S(1)}, u32[]{:S(2)}, u32[]{:S(2)}) collective-permute-start(bf16[2,256,512]{2,1,0:T(8,128)(2,1)S(1)} %collective-permute-done.1.refs_2_), channel_id=1, source_target_pairs={{0,1},{1,0},{2,3},{3,2},{4,5},{5,4},{6,7},{7,6},{8,9},{9,8},{10,11... | collective-permute-start | bytes 1572872 | tf_op jit(solution)/shard_map/ppermute | solution.py:21
  60.8 19.1 %collective-permute-start.5 = (bf16[2,256,512]{2,1,0:T(8,128)(2,1)S(1)}, bf16[2,256,512]{2,1,0:T(8,128)(2,1)S(1)}, u32[]{:S(2)}, u32[]{:S(2)}) collective-permute-start(bf16[2,256,512]{2,1,0:T(8,128)(2,1)S(1)} %collective-permute-done.2.refs_1_), channel_id=1, source_target_pairs={{0,1},{1,0},{2,3},{3,2},{4,5},{5,4},{6,7},{7,6},{8,9},{9,8},{10,11... | collective-permute-start | bytes 1572872 | tf_op jit(solution)/shard_map/ppermute | solution.py:21
  61.3 18.6 %collective-permute-start.7 = (bf16[2,256,512]{2,1,0:T(8,128)(2,1)}, bf16[2,256,512]{2,1,0:T(8,128)(2,1)}, u32[]{:S(2)}, u32[]{:S(2)}) collective-permute-start(bf16[2,256,512]{2,1,0:T(8,128)(2,1)} %collective-permute-done.3.refs_3_), channel_id=1, source_target_pairs={{0,1},{1,0},{2,3},{3,2},{4,5},{5,4},{6,7},{7,6},{8,9},{9,8},{10,11... | collective-permute-start | bytes 1572872 | tf_op jit(solution)/shard_map/ppermute | solution.py:21
  64.8 8.8 %collective-permute-start.14 = (bf16[224,512]{1,0:T(8,128)(2,1)}, bf16[224,512]{1,0:T(8,128)(2,1)}, u32[]{:S(2)}, u32[]{:S(2)}) collective-permute-start(bf16[224,512]{1,0:T(8,128)(2,1)} %collective-permute-done.12.refs_13_), channel_id=1, source_target_pairs={{0,16},{16,0},{1,17},{17,1},{2,18},{18,2},{3,19},{19,3},{4,20},{20... | collective-permute-start | bytes 688136 | tf_op jit(solution)/shard_map/ppermute | solution.py:25
  66.1 9.9 %collective-permute-start.18 = (bf16[224,512]{1,0:T(8,128)(2,1)}, bf16[224,512]{1,0:T(8,128)(2,1)S(1)}, u32[]{:S(2)}, u32[]{:S(2)}) collective-permute-start(bf16[224,512]{1,0:T(8,128)(2,1)} %copy-done.20), channel_id=1, source_target_pairs={{0,16},{16,0},{1,17},{17,1},{2,18},{18,2},{3,19},{19,3},{4,20},{20... | collective-permute-start | bytes 688136 | tf_op jit(solution)/shard_map/ppermute | solution.py:25
  73.6 6.2 %collective-permute-start.22 = (bf16[224,512]{1,0:T(8,128)(2,1)}, bf16[224,512]{1,0:T(8,128)(2,1)S(1)}, u32[]{:S(2)}, u32[]{:S(2)}) collective-permute-start(bf16[224,512]{1,0:T(8,128)(2,1)} %copy-done.23), channel_id=1, source_target_pairs={{0,2},{2,0},{4,6},{6,4},{8,10},{10,8},{12,14},{14,12},{1,3},{3,1},... | collective-permute-start | bytes 688136 | tf_op jit(solution)/shard_map/ppermute | solution.py:29
  92.2 44.7 %collective-permute-start.23 = (bf16[2,768,256]{2,1,0:T(8,128)(2,1)}, bf16[2,768,256]{2,1,0:T(8,128)(2,1)S(1)}, u32[]{:S(2)}, u32[]{:S(2)}) collective-permute-start(bf16[2,768,256]{2,1,0:T(8,128)(2,1)} %get-tuple-element.9.zm_ref), channel_id=1, source_target_pairs={{0,1},{1,0},{2,3},{3,2},{4,5},{5,4},{6,7},{7,6},{8,9},{9,8},{10,11... | collective-permute-start | bytes 2359304 | tf_op jit(solution)/shard_map/ppermute | solution.py:21
  92.3 54.3 %copy-start.9 = (bf16[224,512]{1,0:T(8,128)(2,1)}, bf16[224,512]{1,0:T(8,128)(2,1)S(1)}, u32[]{:S(2)}) copy-start(bf16[224,512]{1,0:T(8,128)(2,1)S(1)} %pad_maximum_fusion.2.refs_0_) | copy-start | bytes 688132
  92.3 10.4 %collective-permute-start.28 = (bf16[224,512]{1,0:T(8,128)(2,1)S(1)}, bf16[224,512]{1,0:T(8,128)(2,1)S(1)}, u32[]{:S(2)}, u32[]{:S(2)}) collective-permute-start(bf16[224,512]{1,0:T(8,128)(2,1)S(1)} %pad_maximum_fusion.2.refs_0_), channel_id=1, source_target_pairs={{0,4},{2,6},{4,8},{6,10},{8,12},{10,14},{12,0},{14,2},{1,5},{3,7},... | collective-permute-start | bytes 688136 | tf_op jit(solution)/shard_map/ppermute | solution.py:33
  94.7 17.4 %collective-permute-start.32 = (bf16[224,512]{1,0:T(8,128)(2,1)S(1)}, bf16[224,512]{1,0:T(8,128)(2,1)S(1)}, u32[]{:S(2)}, u32[]{:S(2)}) collective-permute-start(bf16[224,512]{1,0:T(8,128)(2,1)S(1)} %pad_maximum_fusion.2.refs_0_), channel_id=1, source_target_pairs={{0,8},{2,10},{4,12},{6,14},{8,0},{10,2},{12,4},{14,6},{1,9},{3,11}... | collective-permute-start | bytes 688136 | tf_op jit(solution)/shard_map/ppermute | solution.py:33
  96.4 17.2 %collective-permute-start.36 = (bf16[224,512]{1,0:T(8,128)(2,1)S(1)}, bf16[224,512]{1,0:T(8,128)(2,1)S(1)}, u32[]{:S(2)}, u32[]{:S(2)}) collective-permute-start(bf16[224,512]{1,0:T(8,128)(2,1)S(1)} %pad_maximum_fusion.2.refs_0_), channel_id=1, source_target_pairs={{0,12},{2,14},{4,0},{6,2},{8,4},{10,6},{12,8},{14,10},{1,13},{3,15... | collective-permute-start | bytes 688136 | tf_op jit(solution)/shard_map/ppermute | solution.py:33
  98.3 15.7 %collective-permute-start.25 = (bf16[224,512]{1,0:T(8,128)(2,1)S(1)}, bf16[224,512]{1,0:T(8,128)(2,1)S(1)}, u32[]{:S(2)}, u32[]{:S(2)}) collective-permute-start(bf16[224,512]{1,0:T(8,128)(2,1)S(1)} %pad_maximum_fusion.2.refs_0_), channel_id=1, source_target_pairs={{0,2},{2,0},{4,6},{6,4},{8,10},{10,8},{12,14},{14,12},{1,3},{3,1},... | collective-permute-start | bytes 688136 | tf_op jit(solution)/shard_map/ppermute | solution.py:29
  102.7 44.7 %copy-start.19 = (bf16[224,512]{1,0:T(8,128)(2,1)}, bf16[224,512]{1,0:T(8,128)(2,1)S(1)}, u32[]{:S(2)}) copy-start(bf16[224,512]{1,0:T(8,128)(2,1)S(1)} %collective-permute-done.28.refs_4_) | copy-start | bytes 688132
  102.7 33.7 %collective-permute-start.24 = (bf16[512,512]{1,0:T(8,128)(2,1)}, bf16[512,512]{1,0:T(8,128)(2,1)S(1)}, u32[]{:S(2)}, u32[]{:S(2)}) collective-permute-start(bf16[512,512]{1,0:T(8,128)(2,1)} %get-tuple-element.10.mixm_ref), channel_id=1, source_target_pairs={{0,1},{1,0},{2,3},{3,2},{4,5},{5,4},{6,7},{7,6},{8,9},{9,8},{10,11... | collective-permute-start | bytes 1572872 | tf_op jit(solution)/shard_map/ppermute | solution.py:21
  112.1 35.3 %copy-start.21 = (bf16[224,512]{1,0:T(8,128)(2,1)}, bf16[224,512]{1,0:T(8,128)(2,1)S(1)}, u32[]{:S(2)}) copy-start(bf16[224,512]{1,0:T(8,128)(2,1)S(1)} %collective-permute-done.32.refs_8_) | copy-start | bytes 688132
  112.1 8.5 %collective-permute-start.26 = (bf16[224,512]{1,0:T(8,128)(2,1)S(1)}, bf16[224,512]{1,0:T(8,128)(2,1)S(1)}, u32[]{:S(2)}, u32[]{:S(2)}) collective-permute-start(bf16[224,512]{1,0:T(8,128)(2,1)S(1)} %pad_maximum_fusion.2.refs_0_), channel_id=1, source_target_pairs={{0,16},{16,0},{1,17},{17,1},{2,18},{18,2},{3,19},{19,3},{4,20},{20... | collective-permute-start | bytes 688136 | tf_op jit(solution)/shard_map/ppermute | solution.py:25
  113.6 8.5 %collective-permute-start.29 = (bf16[224,512]{1,0:T(8,128)(2,1)S(1)}, bf16[224,512]{1,0:T(8,128)(2,1)S(1)}, u32[]{:S(2)}, u32[]{:S(2)}) collective-permute-start(bf16[224,512]{1,0:T(8,128)(2,1)S(1)} %collective-permute-done.28.refs_4_), channel_id=1, source_target_pairs={{0,2},{2,0},{4,6},{6,4},{8,10},{10,8},{12,14},{14,12},{1,3},{3,1},... | collective-permute-start | bytes 688136 | tf_op jit(solution)/shard_map/ppermute | solution.py:29
  114.1 11.4 %collective-permute-start.34 = (bf16[224,512]{1,0:T(8,128)(2,1)S(1)}, bf16[224,512]{1,0:T(8,128)(2,1)S(1)}, u32[]{:S(2)}, u32[]{:S(2)}) collective-permute-start(bf16[224,512]{1,0:T(8,128)(2,1)S(1)} %collective-permute-done.32.refs_8_), channel_id=1, source_target_pairs={{0,16},{16,0},{1,17},{17,1},{2,18},{18,2},{3,19},{19,3},{4,20},{20... | collective-permute-start | bytes 688136 | tf_op jit(solution)/shard_map/ppermute | solution.py:25
  120.6 9.8 %collective-permute-start.38 = (bf16[224,512]{1,0:T(8,128)(2,1)S(1)}, bf16[224,512]{1,0:T(8,128)(2,1)S(1)}, u32[]{:S(2)}, u32[]{:S(2)}) collective-permute-start(bf16[224,512]{1,0:T(8,128)(2,1)S(1)} %collective-permute-done.36.refs_12_), channel_id=1, source_target_pairs={{0,16},{16,0},{1,17},{17,1},{2,18},{18,2},{3,19},{19,3},{4,20},{20... | collective-permute-start | bytes 688136 | tf_op jit(solution)/shard_map/ppermute | solution.py:25
  122.0 12.3 %collective-permute-start.30 = (bf16[224,512]{1,0:T(8,128)(2,1)S(1)}, bf16[224,512]{1,0:T(8,128)(2,1)S(1)}, u32[]{:S(2)}, u32[]{:S(2)}) collective-permute-start(bf16[224,512]{1,0:T(8,128)(2,1)S(1)} %collective-permute-done.28.refs_4_), channel_id=1, source_target_pairs={{0,16},{16,0},{1,17},{17,1},{2,18},{18,2},{3,19},{19,3},{4,20},{20... | collective-permute-start | bytes 688136 | tf_op jit(solution)/shard_map/ppermute | solution.py:25
  125.5 10.3 %collective-permute-start.33 = (bf16[224,512]{1,0:T(8,128)(2,1)S(1)}, bf16[224,512]{1,0:T(8,128)(2,1)S(1)}, u32[]{:S(2)}, u32[]{:S(2)}) collective-permute-start(bf16[224,512]{1,0:T(8,128)(2,1)S(1)} %collective-permute-done.32.refs_8_), channel_id=1, source_target_pairs={{0,2},{2,0},{4,6},{6,4},{8,10},{10,8},{12,14},{14,12},{1,3},{3,1},... | collective-permute-start | bytes 688136 | tf_op jit(solution)/shard_map/ppermute | solution.py:29
  130.4 16.2 %collective-permute-start.37 = (bf16[224,512]{1,0:T(8,128)(2,1)S(1)}, bf16[224,512]{1,0:T(8,128)(2,1)S(1)}, u32[]{:S(2)}, u32[]{:S(2)}) collective-permute-start(bf16[224,512]{1,0:T(8,128)(2,1)S(1)} %collective-permute-done.36.refs_12_), channel_id=1, source_target_pairs={{0,2},{2,0},{4,6},{6,4},{8,10},{10,8},{12,14},{14,12},{1,3},{3,1},... | collective-permute-start | bytes 688136 | tf_op jit(solution)/shard_map/ppermute | solution.py:29
  134.4 12.3 %collective-permute-start.27 = (bf16[224,512]{1,0:T(8,128)(2,1)S(1)}, bf16[224,512]{1,0:T(8,128)(2,1)S(1)}, u32[]{:S(2)}, u32[]{:S(2)}) collective-permute-start(bf16[224,512]{1,0:T(8,128)(2,1)S(1)} %collective-permute-done.25.refs_1_), channel_id=1, source_target_pairs={{0,16},{16,0},{1,17},{17,1},{2,18},{18,2},{3,19},{19,3},{4,20},{20... | collective-permute-start | bytes 688136 | tf_op jit(solution)/shard_map/ppermute | solution.py:25
  135.8 10.9 %collective-permute-start.31 = (bf16[224,512]{1,0:T(8,128)(2,1)S(1)}, bf16[224,512]{1,0:T(8,128)(2,1)S(1)}, u32[]{:S(2)}, u32[]{:S(2)}) collective-permute-start(bf16[224,512]{1,0:T(8,128)(2,1)S(1)} %collective-permute-done.29.refs_5_), channel_id=1, source_target_pairs={{0,16},{16,0},{1,17},{17,1},{2,18},{18,2},{3,19},{19,3},{4,20},{20... | collective-permute-start | bytes 688136 | tf_op jit(solution)/shard_map/ppermute | solution.py:25
  136.4 10.3 %collective-permute-start.35 = (bf16[224,512]{1,0:T(8,128)(2,1)S(1)}, bf16[224,512]{1,0:T(8,128)(2,1)S(1)}, u32[]{:S(2)}, u32[]{:S(2)}) collective-permute-start(bf16[224,512]{1,0:T(8,128)(2,1)S(1)} %collective-permute-done.34.refs_10_), channel_id=1, source_target_pairs={{0,2},{2,0},{4,6},{6,4},{8,10},{10,8},{12,14},{14,12},{1,3},{3,1},... | collective-permute-start | bytes 688136 | tf_op jit(solution)/shard_map/ppermute | solution.py:29
  136.9 10.5 %collective-permute-start.39 = (bf16[224,512]{1,0:T(8,128)(2,1)S(1)}, bf16[224,512]{1,0:T(8,128)(2,1)S(1)}, u32[]{:S(2)}, u32[]{:S(2)}) collective-permute-start(bf16[224,512]{1,0:T(8,128)(2,1)S(1)} %collective-permute-done.38.refs_14_), channel_id=1, source_target_pairs={{0,2},{2,0},{4,6},{6,4},{8,10},{10,8},{12,14},{14,12},{1,3},{3,1},... | collective-permute-start | bytes 688136 | tf_op jit(solution)/shard_map/ppermute | solution.py:29
  154.9 1.8 %collective-permute-start.40 = (bf16[2,256,256]{2,1,0:T(8,128)(2,1)}, bf16[2,256,256]{2,1,0:T(8,128)(2,1)S(1)}, u32[]{:S(2)}, u32[]{:S(2)}) collective-permute-start(bf16[2,256,256]{2,1,0:T(8,128)(2,1)} %get-tuple-element.13.zm_ref), channel_id=1, source_target_pairs={{0,1},{1,0},{2,3},{3,2},{4,5},{5,4},{6,7},{7,6},{8,9},{9,8},{10,11... | collective-permute-start | bytes 786440 | tf_op jit(solution)/shard_map/ppermute | solution.py:21
  (38 other events, 410.9 us)

commit v2 on v1

v2 whole, which is shorter than its diff:
```python
import functools

import jax
import jax.numpy as jnp
from jax import lax
from jax.experimental import pallas as pl
from jax.experimental.pallas import tpu as pltpu
from jax.sharding import PartitionSpec as P

TAPS = 3
EPS = 1e-05
F32 = jnp.float32
BF16 = jnp.bfloat16
VMEM = pl.BlockSpec(memory_space=pltpu.VMEM)
SMEM = pl.BlockSpec(memory_space=pltpu.SMEM)
ANY = pl.BlockSpec(memory_space=pltpu.HBM)


def scoped(mebibytes):
    return pltpu.CompilerParams(vmem_limit_bytes=mebibytes * 2**20)


def near(block):
    return pltpu.with_memory_space_constraint(block, pltpu.VMEM)


def far(block):
    return pltpu.with_memory_space_constraint(block, pltpu.HBM)


def near_out(*shape):
    return pltpu.VMEM(shape, BF16)


def cost(flops, bytes_moved):
    return pl.CostEstimate(flops=flops, bytes_accessed=bytes_moved, transcendentals=0)


def swap_chan(block):
    return lax.ppermute(block, "chan", [(0, 1), (1, 0)])


def swap_groups(block):
    return lax.ppermute(block, "groups", [(0, 1), (1, 0)])


def swap_pair(block, seq):
    return lax.ppermute(block, "seq", [(s, s ^ 1) for s in range(seq)])


def ring(block, seq, by):
    return lax.ppermute(block, "seq", [(s, (s + by) % seq) for s in range(seq)])


def from_behind(block, seq, by):
    return lax.ppermute(block, "seq", [(s - by, s) for s in range(by, seq)])


def weight_moves(place, refs, conv_rows, mix_rows, pairs, wide, mix):
    if pairs is None:
        return [(refs[0], wide), (refs[1], mix)]
    s, g = place[0], place[1]
    seq, order = pairs
    moves = []
    for index, begin, skip, count, by, dx, dy in order:
        owner = lax.rem(s + (seq - by), seq)
        if dx:
            owner = owner + 1 - 2 * lax.rem(owner, 2)
        half = (1 - g) if dy else g
        unit = owner * 2 + half
        n_conv = min(conv_rows - skip, count)
        to = pl.multiple_of(unit * conv_rows + skip, 16)
        moves.append((refs[index].at[pl.ds(begin, n_conv)], wide.at[pl.ds(to, n_conv)]))
        if count > n_conv:
            to = pl.multiple_of(unit * mix_rows, 16)
            moves.append(
                (refs[index].at[pl.ds(begin + n_conv, mix_rows)], mix.at[pl.ds(to, mix_rows)])
            )
    return moves


def normalise(xm, xp, dxm, dxp, gm, gp, width):
    total = jnp.sum(xm * xm, axis=1, keepdims=True) + jnp.sum(xp * xp, axis=1, keepdims=True)
    cross = jnp.sum(xm * dxm, axis=1, keepdims=True) + jnp.sum(xp * dxp, axis=1, keepdims=True)
    scale = lax.rsqrt(total / width + EPS)
    factor = scale * scale * scale * (cross / width)
    return (
        (gm * xm * scale).astype(BF16),
        (gp * xp * scale).astype(BF16),
        (gm * (dxm * scale - xm * factor)).astype(BF16),
        (gp * (dxp * scale - xp * factor)).astype(BF16),
    )


def gate_into(out, full, dfull, branch):
    tanh_f = jnp.tanh(full[:, :branch])
    sig_g = jax.nn.sigmoid(full[:, branch:])
    out[0][...] = (tanh_f * sig_g).astype(BF16)
    out[1][...] = (
        (1.0 - tanh_f * tanh_f) * sig_g * dfull[:, :branch]
        + tanh_f * sig_g * (1.0 - sig_g) * dfull[:, branch:]
    ).astype(BF16)


def conv0_kernel(cfg, place, gm_ref, gp_ref, *refs):
    rows, half, branch, blocks, starts, slabs, conv_rows, mix_rows, pairs, n_conv = cfg
    convs = refs[2 * blocks : 2 * blocks + n_conv]
    z_ref, mix_ref, wide, raw, hm, hp, acc, sems, wsems = refs[2 * blocks + n_conv :]
    copies = [
        [
            pltpu.make_async_copy(refs[b + i * blocks], raw.at[i, b], sems.at[i, b])
            for i in range(2)
        ]
        for b in range(blocks)
    ]
    for pair in copies:
        for copy in pair:
            copy.start()
    moves = weight_moves(place, convs, conv_rows, mix_rows, pairs, wide, mix_ref)
    moves = [pltpu.make_async_copy(*move, wsems.at[i]) for i, move in enumerate(moves)]
    for copy in moves:
        copy.start()
    gm = gm_ref[0:1, :]
    gp = gp_ref[0:1, :]
    step = 64
    for b in range(blocks):
        base = (blocks - 1 - b) * rows
        for copy in copies[b]:
            copy.wait()

        def body(i, carry, b=b, base=base):
            at = pl.ds(pl.multiple_of(i * step, step), step)
            to = pl.ds(pl.multiple_of(base + i * step, step), step)
            xm = raw[0, b, 0, at, :].astype(F32)
            dxm = raw[0, b, 1, at, :].astype(F32)
            xp = raw[1, b, 0, at, :].astype(F32)
            dxp = raw[1, b, 1, at, :].astype(F32)
            hm[0, to, :], hp[0, to, :], hm[1, to, :], hp[1, to, :] = normalise(
                xm, xp, dxm, dxp, gm, gp, 2 * half
            )
            return carry

        lax.fori_loop(0, rows // step, body, 0)
    for copy in moves:
        copy.wait()
    c = place[2]
    at_m = pl.multiple_of(c * half, half)
    at_p = pl.multiple_of((1 - c) * half, half)
    for begin, size, lags in slabs:
        for k in range(TAPS):
            row = starts[lags + k]
            for v in range(2):
                part = jnp.dot(
                    hm[v, row : row + size, :],
                    wide[pl.ds(2 * half * k + at_m, half), :],
                    preferred_element_type=F32,
                ) + jnp.dot(
                    hp[v, row : row + size, :],
                    wide[pl.ds(2 * half * k + at_p, half), :],
                    preferred_element_type=F32,
                )
                if k == 0:
                    acc[v, 0:size, :] = part
                else:
                    acc[v, 0:size, :] += part
        for r in range(0, size, rows):
            gate_into(
                (
                    z_ref.at[0, begin + r : begin + r + rows, :],
                    z_ref.at[1, begin + r : begin + r + rows, :],
                ),
                acc[0, r : r + rows, :],
                acc[1, r : r + rows, :],
                branch,
            )


def mix0_kernel(cfg, place, gm_ref, gp_ref, zm_ref, zp_ref, mixm_ref, mixp_ref, *refs):
    rows, half, branch, layer = cfg
    mine = refs[:TAPS]
    theirs = refs[TAPS : 2 * TAPS]
    hm_ref, hp_ref, state_ref = refs[2 * TAPS :]
    c = place[2]
    at_m = pl.ds(pl.multiple_of(c * branch, branch), branch)
    at_p = pl.ds(pl.multiple_of((1 - c) * branch, branch), branch)
    gm = gm_ref[layer : layer + 1, :]
    gp = gp_ref[layer : layer + 1, :]
    step = min(128, rows)
    for j in range(TAPS):
        base = (TAPS - 1 - j) * rows

        def body(i, carry, j=j, base=base):
            at = pl.multiple_of(i * step, step)
            to = pl.multiple_of(base + i * step, step)
            new = []
            for v in range(2):
                zm = zm_ref[v, pl.ds(to, step), :]
                zp = zp_ref[v, pl.ds(to, step), :]
                for x_ref, mix in ((mine[j], mixm_ref), (theirs[j], mixp_ref)):
                    y = jnp.dot(zm, mix[at_m, :], preferred_element_type=F32)
                    y = y + jnp.dot(zp, mix[at_p, :], preferred_element_type=F32)
                    new.append((x_ref[v, pl.ds(at, step), :].astype(F32) + y).astype(BF16))
            if j == 0:
                state_ref[0, pl.ds(at, step), :] = new[0]
                state_ref[1, pl.ds(at, step), :] = new[2]
            xm, xp, dxm, dxp = (t.astype(F32) for t in new)
            a, b, d, e = normalise(xm, xp, dxm, dxp, gm, gp, 2 * half)
            hm_ref[j, 0, pl.ds(at, step), :] = a
            hp_ref[j, 0, pl.ds(at, step), :] = b
            hm_ref[j, 1, pl.ds(at, step), :] = d
            hp_ref[j, 1, pl.ds(at, step), :] = e
            return carry

        lax.fori_loop(0, rows // step, body, 0)


def conv1_kernel(cfg, place, hm, hp, *refs):
    rows, half, branch, conv_rows, mix_rows, pairs, n_conv = cfg
    convs = refs[:n_conv]
    z_ref, mix_ref, wide, acc = refs[n_conv:]
    for src, dst in weight_moves(place, convs, conv_rows, mix_rows, pairs, wide, mix_ref):
        dst[...] = src[...]
    c = place[2]
    at_m = pl.multiple_of(c * half, half)
    at_p = pl.multiple_of((1 - c) * half, half)
    for k in range(TAPS):
        part = jnp.dot(
            hm[k].reshape(2 * rows, half),
            wide[pl.ds(2 * half * k + at_m, half), :],
            preferred_element_type=F32,
        ) + jnp.dot(
            hp[k].reshape(2 * rows, half),
            wide[pl.ds(2 * half * k + at_p, half), :],
            preferred_element_type=F32,
        )
        if k == 0:
            acc[...] = part
        else:
            acc[...] += part
    gate_into((z_ref.at[0], z_ref.at[1]), acc[0:rows, :], acc[rows : 2 * rows, :], branch)


def mix1_kernel(cfg, place, zm_ref, zp_ref, mix_ref, state_ref, out_ref, dout_ref):
    (branch,) = cfg
    c = place[2]
    at_m = pl.ds(pl.multiple_of(c * branch, branch), branch)
    at_p = pl.ds(pl.multiple_of((1 - c) * branch, branch), branch)
    for v, out in ((0, out_ref), (1, dout_ref)):
        y = jnp.dot(zm_ref[v], mix_ref[at_m, :], preferred_element_type=F32)
        y = y + jnp.dot(zp_ref[v], mix_ref[at_p, :], preferred_element_type=F32)
        out[...] = (state_ref[v].astype(F32) + y).astype(BF16)


def exchange(own, chunks, seq):
    c0, c1 = chunks
    rows = own.shape[1]
    half = own.shape[2]
    unit = c0.shape[0]
    pieces = ([], [])
    order = ([], [])

    def keep(layer, array, *slots):
        for begin, skip, count, k, dx, dy in slots:
            order[layer].append((len(pieces[layer]), begin, skip, count, 2 * k, dx, dy))
        pieces[layer].append(array)

    def whole(layer, array, *slots):
        keep(layer, array, *[(i * unit, 0, unit, *slot) for i, slot in enumerate(slots)])

    def part(array, i):
        return array[i * unit : (i + 1) * unit]

    def cat(*arrays):
        return jnp.concatenate(arrays, 0)

    def flat(block):
        return block.reshape(2 * rows, half)

    def together(*blocks):
        return lax.optimization_barrier(blocks)

    def x(block):
        return swap_pair(block, seq)

    def y(block):
        return swap_groups(block)

    def z(block, by=1):
        return ring(block, seq, 2 * by)

    whole(0, c0, (0, 0, 0))
    whole(1, c1, (0, 0, 0))
    z1a, z1b = z(c0), z(c0, 3)
    c01 = cat(c0, c1)
    z1a, z1b, x1, y1, own, c1 = together(z1a, z1b, x(c01), y(c01), own, c1)
    whole(0, z1a, (1, 0, 0))
    whole(0, z1b, (3, 0, 0))
    x0, y0 = part(x1, 0), part(y1, 1)
    whole(0, x1, (0, 1, 0))
    keep(1, x1, (unit, 0, unit, 0, 1, 0))
    whole(0, y1, (0, 0, 1))
    keep(1, y1, (unit, 0, unit, 0, 0, 1))
    z2 = z(cat(z1a, flat(own)))
    x2 = x(cat(z1a, z1b, y0))
    y2 = y(cat(z1a, z1b, x0))
    z2, x2, y2, own, c1 = together(z2, x2, y2, own, c1)
    q2 = part(z2, 0)
    two = from_first(z2[unit:].reshape(own.shape), seq, 1)
    keep(0, z2, (0, 0, unit, 2, 0, 0))
    whole(0, x2, (1, 1, 0), (3, 1, 0))
    keep(1, x2, (2 * unit, 0, unit, 0, 1, 1))
    whole(0, y2, (1, 0, 1), (3, 0, 1), (0, 1, 1))
    z3a, z3b = z(c1), z(c1, 3)
    odd = lax.rem(lax.axis_index("seq"), 2) == 1
    x3 = x(cat(q2, flat(jnp.where(odd, two, own))))
    y3 = y(cat(q2, x2[: 2 * unit]))
    z3a, z3b, x3, y3 = together(z3a, z3b, x3, y3)
    one = from_first(x3[unit:].reshape(own.shape), seq, 0)
    whole(1, z3a, (1, 0, 0))
    whole(1, z3b, (3, 0, 0))
    keep(0, x3, (0, 0, unit, 2, 1, 0))
    whole(0, y3, (2, 0, 1), (1, 1, 1), (3, 1, 1))
    z4 = z(cat(z3a, flat(one)))
    x4 = x(cat(z3a, z3b))
    y4 = y(cat(z3a, z3b, part(x3, 0)))
    z4, x4, y4 = together(z4, x4, y4)
    p2 = part(z4, 0)
    three = from_first(z4[unit:].reshape(own.shape), seq, 1)
    keep(1, z4, (0, 0, unit, 2, 0, 0))
    whole(1, x4, (1, 1, 0), (3, 1, 0))
    whole(1, y4, (1, 0, 1), (3, 0, 1))
    keep(0, y4, (2 * unit, 0, unit, 2, 1, 1))
    x5 = x(cat(p2, part(y4, 0)))
    y5 = y(cat(p2, part(x4, 1)))
    whole(1, x5, (2, 1, 0), (1, 1, 1))
    whole(1, y5, (2, 0, 1), (3, 1, 1))
    cut = unit // 2
    x6 = x(y5[:cut])
    y6 = y(x5[cut:unit])
    keep(1, x6, (0, 0, cut, 2, 1, 1))
    keep(1, y6, (0, cut, unit - cut, 2, 1, 1))
    return (one, two, three), (x5, y5), pieces, tuple((seq, tuple(o)) for o in order)


def from_first(block, seq, planes):
    s = lax.axis_index("seq")
    first = s < 2 if planes else s < 1
    return jnp.where(first, jnp.zeros_like(block), block)


def on_device(signal, tangent, gains, convolution_kernel, mixing_kernel):
    rows, half = signal.shape
    seq = lax.axis_size("seq")
    layers = gains.shape[0]
    branch = convolution_kernel.shape[3]
    shard = convolution_kernel.shape[1]
    mix_shard = mixing_kernel.shape[1]
    lag = rows * seq // 16
    place = jnp.stack([lax.axis_index("seq"), lax.axis_index("groups"), lax.axis_index("chan")])
    place = place.astype(jnp.int32)
    wide_rows, mix_whole = shard * seq, mix_shard * seq

    conv_local = convolution_kernel.reshape(layers, shard, 2 * branch)
    own = jnp.stack([signal, tangent], 0)
    if 2 * lag == rows:
        conv_rows, mix_rows = shard // 2, mix_shard // 2
        g = lax.axis_index("groups")
        both = jnp.concatenate(
            [
                lax.dynamic_slice_in_dim(conv_local, g * conv_rows, conv_rows, 1),
                lax.dynamic_slice_in_dim(mixing_kernel, g * mix_rows, mix_rows, 1),
            ],
            1,
        )
        chunks = [both[l] for l in range(layers)]
        pairs = None
        step, used = lag, (0, 1, 2)
        blocks = 4
    else:
        conv_rows, mix_rows, pairs = shard, mix_shard, (None, None)
        weights = [
            [
                lax.all_gather(conv_local[l], "seq", axis=0, tiled=True),
                lax.all_gather(mixing_kernel[l], "seq", axis=0, tiled=True),
            ]
            for l in range(layers)
        ]
        step, used = rows, (0, 2, 4)
        blocks = 7
    gains_p = swap_chan(gains)
    tall = blocks * rows
    starts = tuple(tall - rows - m * step for m in range(7))
    if 2 * lag == rows:
        slabs = ((0, TAPS * rows, 4),)
    else:
        slabs = tuple(((TAPS - 1 - j) * rows, rows, 2 * j) for j in range(TAPS))
    slab = slabs[0][1]

    if pairs is None:
        halo, beside, weights, pairs = exchange(own, chunks, seq)
        mine = [own, *halo]
    else:
        beside = ()
        mine = [own] + [from_behind(own, seq, k * (lag // rows)) for k in range(1, 7)]
    theirs = [swap_chan(block) for block in mine]

    n_conv = [len(w) for w in weights]
    cfg = (rows, half, branch, blocks, starts, slabs, conv_rows, mix_rows, pairs[0], n_conv[0])
    z_mine, mix_mine = pl.pallas_call(
        functools.partial(conv0_kernel, cfg),
        out_shape=(near_out(2, TAPS * rows, branch), near_out(mix_whole, half)),
        in_specs=[SMEM, VMEM, VMEM] + [ANY] * (2 * blocks + n_conv[0]),
        out_specs=(VMEM, VMEM),
        scratch_shapes=[
            pltpu.VMEM((wide_rows, 2 * branch), BF16),
            pltpu.VMEM((2, blocks, 2, rows, half), BF16),
            pltpu.VMEM((2, tall, half), BF16),
            pltpu.VMEM((2, tall, half), BF16),
            pltpu.VMEM((2, slab, 2 * branch), F32),
            pltpu.SemaphoreType.DMA((2, blocks)),
            pltpu.SemaphoreType.DMA((2 if pairs[0] is None else 2 * len(pairs[0][1]),)),
        ],
        compiler_params=scoped(28),
        cost_estimate=cost(0, 32 * 2**20),
        name="conv0",
    )(
        place,
        near(gains),
        near(gains_p),
        *[far(block) for block in (*mine, *theirs, *weights[0])],
    )
    z_mine, mix_mine = lax.optimization_barrier((z_mine, mix_mine, *beside))[:2]
    mix_theirs = swap_chan(mix_mine)
    z_theirs = swap_chan(z_mine)
    hm, hp, state = pl.pallas_call(
        functools.partial(mix0_kernel, (rows, half, branch, 1)),
        out_shape=(
            near_out(TAPS, 2, rows, half),
            near_out(TAPS, 2, rows, half),
            near_out(2, rows, half),
        ),
        in_specs=[SMEM] + [VMEM] * (6 + 2 * TAPS),
        out_specs=(VMEM, VMEM, VMEM),
        compiler_params=scoped(6),
        cost_estimate=cost(0, 20 * 2**20),
        name="mix0",
    )(
        place,
        near(gains),
        near(gains_p),
        z_mine,
        near(z_theirs),
        mix_mine,
        near(mix_theirs),
        *[near(mine[b]) for b in used],
        *[near(theirs[b]) for b in used],
    )
    cfg = (rows, half, branch, conv_rows, mix_rows, pairs[1], n_conv[1])
    z_mine, mix_mine = pl.pallas_call(
        functools.partial(conv1_kernel, cfg),
        out_shape=(near_out(2, rows, branch), near_out(mix_whole, half)),
        in_specs=[SMEM] + [VMEM] * (2 + n_conv[1]),
        out_specs=(VMEM, VMEM),
        scratch_shapes=[
            pltpu.VMEM((wide_rows, 2 * branch), BF16),
            pltpu.VMEM((2 * rows, 2 * branch), F32),
        ],
        compiler_params=scoped(8),
        name="conv1",
    )(place, hm, hp, *[near(w) for w in weights[1]])
    z_theirs = swap_chan(z_mine)
    return pl.pallas_call(
        functools.partial(mix1_kernel, (branch,)),
        out_shape=(
            jax.ShapeDtypeStruct((rows, half), BF16),
            jax.ShapeDtypeStruct((rows, half), BF16),
        ),
        in_specs=[SMEM] + [VMEM] * 4,
        out_specs=(VMEM, VMEM),
        compiler_params=scoped(4),
        name="mix1",
    )(place, z_mine, near(z_theirs), mix_mine, state)


def solution(mesh):
    return jax.shard_map(
        on_device,
        mesh=mesh,
        in_specs=(
            P(("groups", "seq"), "chan"),
            P(("groups", "seq"), "chan"),
            P(None, "chan"),
            P(None, "seq", None, "chan"),
            P(None, "seq", "chan"),
        ),
        out_specs=(P(("groups", "seq"), "chan"), P(("groups", "seq"), "chan")),
        check_vma=False,
    )
```

time: 162 us -> 115 us (0.71); the launches traced: 160 us -> 115 us
  starting transfers between devices: 50.9 us -> 22.8 us
  waiting for transfers between devices: 72.1 us -> 54 us
  Pallas kernels: 28.7 us -> 21.4 us
  other arithmetic: 1.84 us -> 7.26 us
  local copies, waits for them, and re-layouts: 5.28 us -> 7.91 us
    ppermute x13 -> x6, waiting for transfers between devices: 33.6 us -> 9.75 us  [swap_groups(): return lax.ppermute(block, 'groups', [(0, 1), (1, 0)])]
    ppermute x2 -> x0, starting transfers between devices: 15.7 us -> none  [from_behind(): return lax.ppermute(block, 'seq', [(s - by, s) for s in range(by, seq)])]
    ppermute x12 -> x6, waiting for transfers between devices: 10.3 us -> 24.6 us  [swap_pair(): return lax.ppermute(block, 'seq', [(s, s ^ 1) for s in range(seq)])]
    ppermute x2 -> x0, waiting for transfers between devices: 9.82 us -> none  [from_behind(): return lax.ppermute(block, 'seq', [(s - by, s) for s in range(by, seq)])]
    ppermute x13 -> x6, starting transfers between devices: 12.7 us -> 4.52 us  [swap_groups(): return lax.ppermute(block, 'groups', [(0, 1), (1, 0)])]
    concatenate x2 -> x9, other arithmetic: 0.03 us -> 6.08 us  [cat(): return jnp.concatenate(arrays, 0)]
    ppermute x6, starting transfers between devices: 12.5 us -> 8.88 us  [ring(): return lax.ppermute(block, 'seq', [(s, (s + by) % seq) for s in range(seq)])]
    pallas_call x1, Pallas kernels: 8.17 us -> 4.93 us  [on_device(): pl.pallas_call(functools.partial(mix0_kernel, (rows, half, branch, 1)), o...]
  transfers between devices with their start and end apart: 41 -> 26, of which waited for: 19 -> 13; matrix products, arithmetic and copies ran while one was open for 2% -> 6% of each run, Pallas kernels for 5% -> 14%
where the time goes in v2:
time: 115 us
  waiting for transfers between devices  54 us (47%)
  starting transfers between devices  22.8 us (20%)
  Pallas kernels  21.4 us (19%)
  local copies, waits for them, and re-layouts  7.91 us (7%)
  other arithmetic  7.26 us (6%)
    ppermute x6, waiting for transfers between devices, swap_pair(): return lax.ppermute(block, 'seq', [(s, s ^ 1) for s in range(seq)])  24.6 us
    ppermute x6, waiting for transfers between devices, ring(): return lax.ppermute(block, 'seq', [(s, (s + by) % seq) for s in range(seq)])  18.1 us
    pallas_call x1, Pallas kernels, on_device(): pl.pallas_call(functools.partial(conv0_kernel, cfg), out_shape=(near_out(...  11.6 us
    ppermute x6, waiting for transfers between devices, swap_groups(): return lax.ppermute(block, 'groups', [(0, 1), (1, 0)])  9.75 us
    ppermute x6, starting transfers between devices, ring(): return lax.ppermute(block, 'seq', [(s, (s + by) % seq) for s in range(seq)])  8.88 us
    ppermute x6, starting transfers between devices, swap_pair(): return lax.ppermute(block, 'seq', [(s, s ^ 1) for s in range(seq)])  8.34 us
    concatenate x9, other arithmetic, cat(): return jnp.concatenate(arrays, 0)  6.08 us
    pallas_call x1, Pallas kernels, on_device(): pl.pallas_call(functools.partial(mix0_kernel, (rows, half, branch, 1)), o...  4.93 us
  transfers between devices with their start and end apart: 26, of which 13 were waited for; matrix products, arithmetic and copies ran while one was open for 6% of the time, Pallas kernels for 14%

profile of v2, /device:TPU:0, one launch (start us, length us, event | category | flops | bytes accessed | tf_op | source)
XLA Modules:
  0.0 114.6 jit_solution(17300244140238818123)
XLA Ops:
  0.7 2.5 %reshape.26 = bf16[2,384,512]{2,1,0:T(8,128)(2,1)S(1)} reshape(bf16[2,384,2,256]{3,2,1,0:T(2,128)(2,1)} %param.8) | data formatting | bytes 1572864 | tf_op jit(solution)/shard_map/reshape | solution.py:363
  3.3 3.0 %collective-permute-start.3 = (bf16[448,512]{1,0:T(8,128)(2,1)S(1)}, bf16[448,512]{1,0:T(8,128)(2,1)S(1)}, u32[]{:S(2)}, u32[]{:S(2)}) collective-permute-start(bf16[448,512]{1,0:T(8,128)(2,1)S(1)} %pad_maximum_fusion.11), channel_id=1, source_target_pairs={{0,2},{2,0},{4,6},{6,4},{8,10},{10,8},{12,14},{14,12},{1,3},{3,1},... | collective-permute-start | bytes 1376264 | tf_op jit(solution)/shard_map/ppermute | solution.py:48
  6.3 1.5 %collective-permute-start.4 = (bf16[448,512]{1,0:T(8,128)(2,1)S(1)}, bf16[448,512]{1,0:T(8,128)(2,1)S(1)}, u32[]{:S(2)}, u32[]{:S(2)}) collective-permute-start(bf16[448,512]{1,0:T(8,128)(2,1)S(1)} %pad_maximum_fusion.11), channel_id=1, source_target_pairs={{0,16},{16,0},{1,17},{17,1},{2,18},{18,2},{3,19},{19,3},{4,20},{20... | collective-permute-start | bytes 1376264 | tf_op jit(solution)/shard_map/ppermute | solution.py:44
  7.9 1.6 %collective-permute-start.1 = (bf16[224,512]{1,0:T(8,128)(2,1)S(1)}, bf16[224,512]{1,0:T(8,128)(2,1)S(1)}, u32[]{:S(2)}, u32[]{:S(2)}) collective-permute-start(bf16[224,512]{1,0:T(8,128)(2,1)S(1)} %get-tuple-element.59.refs_8_), channel_id=1, source_target_pairs={{0,4},{2,6},{4,8},{6,10},{8,12},{10,14},{12,0},{14,2},{1,5},{3,7},... | collective-permute-start | bytes 688136 | tf_op jit(solution)/shard_map/ppermute | solution.py:52
  9.4 2.2 %collective-permute-start.2 = (bf16[224,512]{1,0:T(8,128)(2,1)S(1)}, bf16[224,512]{1,0:T(8,128)(2,1)S(1)}, u32[]{:S(2)}, u32[]{:S(2)}) collective-permute-start(bf16[224,512]{1,0:T(8,128)(2,1)S(1)} %get-tuple-element.59.refs_8_), channel_id=1, source_target_pairs={{0,12},{2,14},{4,0},{6,2},{8,4},{10,6},{12,8},{14,10},{1,13},{3,15... | collective-permute-start | bytes 688136 | tf_op jit(solution)/shard_map/ppermute | solution.py:52
  11.8 6.5 %collective-permute-done.1.refs_9_ = bf16[224,512]{1,0:T(8,128)(2,1)S(1)} collective-permute-done((bf16[224,512]{1,0:T(8,128)(2,1)S(1)}, bf16[224,512]{1,0:T(8,128)(2,1)S(1)}, u32[]{:S(2)}, u32[]{:S(2)}) %collective-permute-start.1) | collective-permute-done | bytes 229408 | tf_op jit(solution)/shard_map/ppermute | solution.py:52
  18.3 2.6 %collective-permute-done.2.refs_10_ = bf16[224,512]{1,0:T(8,128)(2,1)S(1)} collective-permute-done((bf16[224,512]{1,0:T(8,128)(2,1)S(1)}, bf16[224,512]{1,0:T(8,128)(2,1)S(1)}, u32[]{:S(2)}, u32[]{:S(2)}) %collective-permute-start.2) | collective-permute-done | bytes 229408 | tf_op jit(solution)/shard_map/ppermute | solution.py:52
  20.9 0.8 copy-done.11
  21.9 1.0 pad_maximum_fusion
  22.8 1.1 collective-permute-start.5
  24.0 1.2 %pad_maximum_fusion.5 = (bf16[672,512]{1,0:T(8,128)(2,1)}, bf16[672,512]{1,0:T(8,128)(2,1)}) fusion(bf16[224,512]{1,0:T(8,128)(2,1)S(1)} %slice.48, bf16[224,512]{1,0:T(8,128)(2,1)S(1)} %collective-permute-done.2.refs_10_, bf16[224,512]{1,0:T(8,128)(2,1)S(1)} %collective-permute-done.1.refs_9_, bf16[224,512]{1,0:T(8,128)(2,1)S(1)} %slice.47), kind=kLoop, calls=%fused_computation.5 | loop fusion | flops 3096576 | bytes 2293760 | tf_op jit(solution)/shard_map/concatenate | solution.py:274
  25.2 0.5 collective-permute-start.6
  25.7 0.5 collective-permute-start.7
  26.2 16.2 %collective-permute-done.6.refs_14_.refs_3_ = bf16[672,512]{1,0:T(8,128)(2,1)S(1)} collective-permute-done((bf16[672,512]{1,0:T(8,128)(2,1)}, bf16[672,512]{1,0:T(8,128)(2,1)S(1)}, u32[]{:S(2)}, u32[]{:S(2)}) %collective-permute-start.6) | collective-permute-done | bytes 688160 | tf_op jit(solution)/shard_map/ppermute | solution.py:48
  42.5 0.4 collective-permute-done.7.refs_15_
  43.3 0.5 copy-done.24
  43.9 0.9 pad_maximum_fusion.1
  44.8 1.4 %collective-permute-start.10 = (bf16[736,512]{1,0:T(8,128)(2,1)}, bf16[736,512]{1,0:T(8,128)(2,1)S(1)}, u32[]{:S(2)}, u32[]{:S(2)}) collective-permute-start(bf16[736,512]{1,0:T(8,128)(2,1)} %pad_maximum_fusion.1), channel_id=1, source_target_pairs={{0,2},{2,0},{4,6},{6,4},{8,10},{10,8},{12,14},{14,12},{1,3},{3,1},... | collective-permute-start | bytes 2261000 | tf_op jit(solution)/shard_map/ppermute | solution.py:48
  46.2 0.9 pad_maximum_fusion.6
  47.0 0.5 collective-permute-start.11
  47.8 3.5 %collective-permute-start.9 = (bf16[224,512]{1,0:T(8,128)(2,1)S(1)}, bf16[224,512]{1,0:T(8,128)(2,1)S(1)}, u32[]{:S(2)}, u32[]{:S(2)}) collective-permute-start(bf16[224,512]{1,0:T(8,128)(2,1)S(1)} %get-tuple-element.35.refs_0_), channel_id=1, source_target_pairs={{0,12},{2,14},{4,0},{6,2},{8,4},{10,6},{12,8},{14,10},{1,13},{3,15... | collective-permute-start | bytes 688136 | tf_op jit(solution)/shard_map/ppermute | solution.py:52
  51.4 6.1 %collective-permute-done.8.refs_4_ = bf16[224,512]{1,0:T(8,128)(2,1)S(1)} collective-permute-done((bf16[224,512]{1,0:T(8,128)(2,1)S(1)}, bf16[224,512]{1,0:T(8,128)(2,1)S(1)}, u32[]{:S(2)}, u32[]{:S(2)}) %collective-permute-start.8) | collective-permute-done | bytes 229408 | tf_op jit(solution)/shard_map/ppermute | solution.py:52
  57.5 0.5 collective-permute-done.9.refs_5_
  58.0 5.0 %collective-permute-done.11.refs_17_ = bf16[672,512]{1,0:T(8,128)(2,1)} collective-permute-done((bf16[672,512]{1,0:T(8,128)(2,1)}, bf16[672,512]{1,0:T(8,128)(2,1)}, u32[]{:S(2)}, u32[]{:S(2)}) %collective-permute-start.11) | collective-permute-done | bytes 688160 | tf_op jit(solution)/shard_map/ppermute | solution.py:44
  63.0 0.8 copy-done.25
  64.1 0.6 collective-permute-start.14
  64.6 1.0 pad_maximum_fusion.12
  65.6 1.4 %collective-permute-start.13 = (bf16[448,512]{1,0:T(8,128)(2,1)S(1)}, bf16[448,512]{1,0:T(8,128)(2,1)S(1)}, u32[]{:S(2)}, u32[]{:S(2)}) collective-permute-start(bf16[448,512]{1,0:T(8,128)(2,1)S(1)} %pad_maximum_fusion.12), channel_id=1, source_target_pairs={{0,2},{2,0},{4,6},{6,4},{8,10},{10,8},{12,14},{14,12},{1,3},{3,1},... | collective-permute-start | bytes 1376264 | tf_op jit(solution)/shard_map/ppermute | solution.py:48
  67.0 0.5 collective-permute-start
  67.5 8.3 %collective-permute-done.13.refs_7_ = bf16[448,512]{1,0:T(8,128)(2,1)S(1)} collective-permute-done((bf16[448,512]{1,0:T(8,128)(2,1)S(1)}, bf16[448,512]{1,0:T(8,128)(2,1)S(1)}, u32[]{:S(2)}, u32[]{:S(2)}) %collective-permute-start.13) | collective-permute-done | bytes 458784 | tf_op jit(solution)/shard_map/ppermute | solution.py:48
  75.8 3.6 %collective-permute-done.14.refs_18_.refs_8_ = bf16[672,512]{1,0:T(8,128)(2,1)S(1)} collective-permute-done((bf16[672,512]{1,0:T(8,128)(2,1)S(1)}, bf16[672,512]{1,0:T(8,128)(2,1)S(1)}, u32[]{:S(2)}, u32[]{:S(2)}) %collective-permute-start.14) | collective-permute-done | bytes 688160 | tf_op jit(solution)/shard_map/ppermute | solution.py:44
  79.5 2.3 %collective-permute-done.12.refs_6_ = bf16[736,512]{1,0:T(8,128)(2,1)S(1)} collective-permute-done((bf16[736,512]{1,0:T(8,128)(2,1)S(1)}, bf16[736,512]{1,0:T(8,128)(2,1)S(1)}, u32[]{:S(2)}, u32[]{:S(2)}) %collective-permute-start.12) | collective-permute-done | bytes 753696 | tf_op jit(solution)/shard_map/ppermute | solution.py:52
  81.9 0.9 slice_select_fusion
  82.8 1.0 pad_maximum_fusion.9
  83.8 1.1 collective-permute-start.19
  84.9 0.8 copy-done.15
  85.7 0.5 collective-permute-start.20
  86.4 11.6 %conv0.1 = (bf16[2,768,256]{2,1,0:T(8,128)(2,1)S(1)}, bf16[512,512]{1,0:T(8,128)(2,1)S(1)}) custom-call(s32[3]{0:T(128)S(1)} %pad_add_fusion.place, f32[2,512]{1,0:T(2,128)S(1)} %copy-done.23, f32[2,512]{1,0:T(2,128)S(1)} %collective-permute-done.gp_ref, bf16[2,256,512]{2,1,0:T(8,128)(2,1)} %copy-done.1, bf16[2,256,512]{2,1,0:T(8,128)(2,1)} %bitcast.20, ...), custom_call_target="tpu_custom_call" | custom-call | bytes 33554432 | tf_op jit(solution)/shard_map/conv0/pallas_call | solution.py:409
  98.0 0.7 collective-permute-done.20.refs_10_
  98.7 0.5 collective-permute-start.22
  99.2 0.9 slice.62
  100.1 0.9 collective-permute-start.23
  101.1 0.9 slice.63
  102.0 0.9 collective-permute-start.24
  103.0 4.9 %mix0.1 = (bf16[3,2,256,512]{3,2,1,0:T(8,128)(2,1)S(1)}, bf16[3,2,256,512]{3,2,1,0:T(8,128)(2,1)S(1)}, bf16[2,256,512]{2,1,0:T(8,128)(2,1)S(1)}) custom-call(s32[3]{0:T(128)S(1)} %pad_add_fusion.place, f32[2,512]{1,0:T(2,128)S(1)} %copy-done.23, f32[2,512]{1,0:T(2,128)S(1)} %collective-permute-done.gp_ref, ...), custom_call_target="tpu_custom_call" | custom-call | bytes 20971520 | tf_op jit(solution)/shard_map/mix0/pallas_call | solution.py:435
  108.0 3.3 %conv1.1 = (bf16[2,256,256]{2,1,0:T(8,128)(2,1)S(1)}, bf16[512,512]{1,0:T(8,128)(2,1)S(1)}) custom-call(s32[3]{0:T(128)S(1)} %pad_add_fusion.place, bf16[3,2,256,512]{3,2,1,0:T(8,128)(2,1)S(1)} %get-tuple-element.51.hm, bf16[3,2,256,512]{3,2,1,0:T(8,128)(2,1)S(1)} %get-tuple-element.52.hp, bf16[224,512]{1,0:T(8,128)(2,1)S(1)} %copy-done.18, ...), custom_call_target="tpu_custom_call" | custom-call | tf_op jit(solution)/shard_map/conv1/pallas_call | solution.py:459
  111.4 1.5 %collective-permute-done.25.zp_ref = bf16[2,256,256]{2,1,0:T(8,128)(2,1)S(1)} collective-permute-done((bf16[2,256,256]{2,1,0:T(8,128)(2,1)S(1)}, bf16[2,256,256]{2,1,0:T(8,128)(2,1)S(1)}, u32[]{:S(2)}, u32[]{:S(2)}) %collective-permute-start.25) | collective-permute-done | bytes 262176 | tf_op jit(solution)/shard_map/ppermute | solution.py:40
  112.9 1.7 %mix1.1 = (bf16[256,512]{1,0:T(8,128)(2,1)}, bf16[256,512]{1,0:T(8,128)(2,1)}) custom-call(s32[3]{0:T(128)S(1)} %pad_add_fusion.place, bf16[2,256,256]{2,1,0:T(8,128)(2,1)S(1)} %get-tuple-element.53.zm_ref, bf16[2,256,256]{2,1,0:T(8,128)(2,1)S(1)} %collective-permute-done.25.zp_ref, bf16[512,512]{1,0:T(8,128)(2,1)S(1)} %get-tuple-element.54.mix_ref, ...), custom_call_target="tpu_custom_call" | custom-call | tf_op jit(solution)/shard_map/mix1/pallas_call | solution.py:472
  (100 shorter events, 1.7 us)
Async XLA Ops:
  3.1 8.6 %copy-start.29 = (bf16[256,512]{1,0:T(8,128)(2,1)S(1)}, bf16[256,512]{1,0:T(8,128)(2,1)}, u32[]{:S(2)}) copy-start(bf16[256,512]{1,0:T(8,128)(2,1)} %param.6) | copy-start | bytes 786436
  3.2 8.5 %copy-start.30 = (bf16[256,512]{1,0:T(8,128)(2,1)S(1)}, bf16[256,512]{1,0:T(8,128)(2,1)}, u32[]{:S(2)}) copy-start(bf16[256,512]{1,0:T(8,128)(2,1)} %param.5) | copy-start | bytes 786436
  3.3 18.4 %copy-start.26 = (bf16[224,512]{1,0:T(8,128)(2,1)}, bf16[224,512]{1,0:T(8,128)(2,1)S(1)}, u32[]{:S(2)}) copy-start(bf16[224,512]{1,0:T(8,128)(2,1)S(1)} %get-tuple-element.59.refs_8_) | copy-start | bytes 688132
  3.3 44.5 %copy-start.17 = (bf16[224,512]{1,0:T(8,128)(2,1)}, bf16[224,512]{1,0:T(8,128)(2,1)S(1)}, u32[]{:S(2)}) copy-start(bf16[224,512]{1,0:T(8,128)(2,1)S(1)} %get-tuple-element.35.refs_0_) | copy-start | bytes 688132
  3.3 17.5 %collective-permute-start.3 = (bf16[448,512]{1,0:T(8,128)(2,1)S(1)}, bf16[448,512]{1,0:T(8,128)(2,1)S(1)}, u32[]{:S(2)}, u32[]{:S(2)}) collective-permute-start(bf16[448,512]{1,0:T(8,128)(2,1)S(1)} %pad_maximum_fusion.11), channel_id=1, source_target_pairs={{0,2},{2,0},{4,6},{6,4},{8,10},{10,8},{12,14},{14,12},{1,3},{3,1},... | collective-permute-start | bytes 1376264 | tf_op jit(solution)/shard_map/ppermute | solution.py:48
  6.3 14.5 %collective-permute-start.4 = (bf16[448,512]{1,0:T(8,128)(2,1)S(1)}, bf16[448,512]{1,0:T(8,128)(2,1)S(1)}, u32[]{:S(2)}, u32[]{:S(2)}) collective-permute-start(bf16[448,512]{1,0:T(8,128)(2,1)S(1)} %pad_maximum_fusion.11), channel_id=1, source_target_pairs={{0,16},{16,0},{1,17},{17,1},{2,18},{18,2},{3,19},{19,3},{4,20},{20... | collective-permute-start | bytes 1376264 | tf_op jit(solution)/shard_map/ppermute | solution.py:44
  7.9 10.4 %collective-permute-start.1 = (bf16[224,512]{1,0:T(8,128)(2,1)S(1)}, bf16[224,512]{1,0:T(8,128)(2,1)S(1)}, u32[]{:S(2)}, u32[]{:S(2)}) collective-permute-start(bf16[224,512]{1,0:T(8,128)(2,1)S(1)} %get-tuple-element.59.refs_8_), channel_id=1, source_target_pairs={{0,4},{2,6},{4,8},{6,10},{8,12},{10,14},{12,0},{14,2},{1,5},{3,7},... | collective-permute-start | bytes 688136 | tf_op jit(solution)/shard_map/ppermute | solution.py:52
  9.4 11.4 %collective-permute-start.2 = (bf16[224,512]{1,0:T(8,128)(2,1)S(1)}, bf16[224,512]{1,0:T(8,128)(2,1)S(1)}, u32[]{:S(2)}, u32[]{:S(2)}) collective-permute-start(bf16[224,512]{1,0:T(8,128)(2,1)S(1)} %get-tuple-element.59.refs_8_), channel_id=1, source_target_pairs={{0,12},{2,14},{4,0},{6,2},{8,4},{10,6},{12,8},{14,10},{1,13},{3,15... | collective-permute-start | bytes 688136 | tf_op jit(solution)/shard_map/ppermute | solution.py:52
  11.7 55.2 %copy-start.1 = (bf16[2,256,512]{2,1,0:T(8,128)(2,1)}, bf16[2,256,512]{2,1,0:T(8,128)(2,1)S(1)}, u32[]{:S(2)}) copy-start(bf16[2,256,512]{2,1,0:T(8,128)(2,1)S(1)} %pad_maximum_fusion.8.refs_0_) | copy-start | bytes 1572868
  18.2 24.7 %copy-start.27 = (bf16[224,512]{1,0:T(8,128)(2,1)}, bf16[224,512]{1,0:T(8,128)(2,1)S(1)}, u32[]{:S(2)}) copy-start(bf16[224,512]{1,0:T(8,128)(2,1)S(1)} %collective-permute-done.1.refs_9_) | copy-start | bytes 688132
  22.8 20.1 %collective-permute-start.5 = (bf16[736,512]{1,0:T(8,128)(2,1)}, bf16[736,512]{1,0:T(8,128)(2,1)S(1)}, u32[]{:S(2)}, u32[]{:S(2)}) collective-permute-start(bf16[736,512]{1,0:T(8,128)(2,1)} %pad_maximum_fusion), channel_id=1, source_target_pairs={{0,4},{2,6},{4,8},{6,10},{8,12},{10,14},{12,0},{14,2},{1,5},{3,7},... | collective-permute-start | bytes 2261000 | tf_op jit(solution)/shard_map/ppermute | solution.py:52
  25.2 17.3 %collective-permute-start.6 = (bf16[672,512]{1,0:T(8,128)(2,1)}, bf16[672,512]{1,0:T(8,128)(2,1)S(1)}, u32[]{:S(2)}, u32[]{:S(2)}) collective-permute-start(bf16[672,512]{1,0:T(8,128)(2,1)} %get-tuple-element.57), channel_id=1, source_target_pairs={{0,2},{2,0},{4,6},{6,4},{8,10},{10,8},{12,14},{14,12},{1,3},{3,1},... | collective-permute-start | bytes 2064392 | tf_op jit(solution)/shard_map/ppermute | solution.py:48
  25.7 17.1 %collective-permute-start.7 = (bf16[672,512]{1,0:T(8,128)(2,1)}, bf16[672,512]{1,0:T(8,128)(2,1)}, u32[]{:S(2)}, u32[]{:S(2)}) collective-permute-start(bf16[672,512]{1,0:T(8,128)(2,1)} %get-tuple-element.56), channel_id=1, source_target_pairs={{0,16},{16,0},{1,17},{17,1},{2,18},{18,2},{3,19},{19,3},{4,20},{20... | collective-permute-start | bytes 2064392 | tf_op jit(solution)/shard_map/ppermute | solution.py:44
  43.0 32.8 %copy-start.3 = (bf16[512,512]{1,0:T(8,128)(2,1)}, bf16[512,512]{1,0:T(8,128)(2,1)S(1)}, u32[]{:S(2)}) copy-start(bf16[512,512]{1,0:T(8,128)(2,1)S(1)} %slice_select_fusion.2) | copy-start | bytes 1572868
  44.8 18.2 %collective-permute-start.10 = (bf16[736,512]{1,0:T(8,128)(2,1)}, bf16[736,512]{1,0:T(8,128)(2,1)S(1)}, u32[]{:S(2)}, u32[]{:S(2)}) collective-permute-start(bf16[736,512]{1,0:T(8,128)(2,1)} %pad_maximum_fusion.1), channel_id=1, source_target_pairs={{0,2},{2,0},{4,6},{6,4},{8,10},{10,8},{12,14},{14,12},{1,3},{3,1},... | collective-permute-start | bytes 2261000 | tf_op jit(solution)/shard_map/ppermute | solution.py:48
  47.0 15.9 %collective-permute-start.11 = (bf16[672,512]{1,0:T(8,128)(2,1)}, bf16[672,512]{1,0:T(8,128)(2,1)}, u32[]{:S(2)}, u32[]{:S(2)}) collective-permute-start(bf16[672,512]{1,0:T(8,128)(2,1)} %pad_maximum_fusion.6), channel_id=1, source_target_pairs={{0,16},{16,0},{1,17},{17,1},{2,18},{18,2},{3,19},{19,3},{4,20},{20... | collective-permute-start | bytes 2064392 | tf_op jit(solution)/shard_map/ppermute | solution.py:44
  47.5 9.9 %collective-permute-start.8 = (bf16[224,512]{1,0:T(8,128)(2,1)S(1)}, bf16[224,512]{1,0:T(8,128)(2,1)S(1)}, u32[]{:S(2)}, u32[]{:S(2)}) collective-permute-start(bf16[224,512]{1,0:T(8,128)(2,1)S(1)} %get-tuple-element.35.refs_0_), channel_id=1, source_target_pairs={{0,4},{2,6},{4,8},{6,10},{8,12},{10,14},{12,0},{14,2},{1,5},{3,7},... | collective-permute-start | bytes 688136 | tf_op jit(solution)/shard_map/ppermute | solution.py:52
  47.8 10.1 %collective-permute-start.9 = (bf16[224,512]{1,0:T(8,128)(2,1)S(1)}, bf16[224,512]{1,0:T(8,128)(2,1)S(1)}, u32[]{:S(2)}, u32[]{:S(2)}) collective-permute-start(bf16[224,512]{1,0:T(8,128)(2,1)S(1)} %get-tuple-element.35.refs_0_), channel_id=1, source_target_pairs={{0,12},{2,14},{4,0},{6,2},{8,4},{10,6},{12,8},{14,10},{1,13},{3,15... | collective-permute-start | bytes 688136 | tf_op jit(solution)/shard_map/ppermute | solution.py:52
  58.0 6.0 %copy-start.19 = (bf16[224,512]{1,0:T(8,128)(2,1)}, bf16[224,512]{1,0:T(8,128)(2,1)S(1)}, u32[]{:S(2)}) copy-start(bf16[224,512]{1,0:T(8,128)(2,1)S(1)} %collective-permute-done.9.refs_5_) | copy-start | bytes 688132
  63.8 15.6 %copy-start.5 = (bf16[512,512]{1,0:T(8,128)(2,1)}, bf16[512,512]{1,0:T(8,128)(2,1)S(1)}, u32[]{:S(2)}) copy-start(bf16[512,512]{1,0:T(8,128)(2,1)S(1)} %slice_select_fusion.1) | copy-start | bytes 1572868
  63.9 17.9 %collective-permute-start.12 = (bf16[736,512]{1,0:T(8,128)(2,1)S(1)}, bf16[736,512]{1,0:T(8,128)(2,1)S(1)}, u32[]{:S(2)}, u32[]{:S(2)}) collective-permute-start(bf16[736,512]{1,0:T(8,128)(2,1)S(1)} %pad_maximum_fusion.2), channel_id=1, source_target_pairs={{0,4},{2,6},{4,8},{6,10},{8,12},{10,14},{12,0},{14,2},{1,5},{3,7},... | collective-permute-start | bytes 2261000 | tf_op jit(solution)/shard_map/ppermute | solution.py:52
  64.1 15.4 %collective-permute-start.14 = (bf16[672,512]{1,0:T(8,128)(2,1)S(1)}, bf16[672,512]{1,0:T(8,128)(2,1)S(1)}, u32[]{:S(2)}, u32[]{:S(2)}) collective-permute-start(bf16[672,512]{1,0:T(8,128)(2,1)S(1)} %pad_maximum_fusion.7), channel_id=1, source_target_pairs={{0,16},{16,0},{1,17},{17,1},{2,18},{18,2},{3,19},{19,3},{4,20},{20... | collective-permute-start | bytes 2064392 | tf_op jit(solution)/shard_map/ppermute | solution.py:44
  65.6 10.2 %collective-permute-start.13 = (bf16[448,512]{1,0:T(8,128)(2,1)S(1)}, bf16[448,512]{1,0:T(8,128)(2,1)S(1)}, u32[]{:S(2)}, u32[]{:S(2)}) collective-permute-start(bf16[448,512]{1,0:T(8,128)(2,1)S(1)} %pad_maximum_fusion.12), channel_id=1, source_target_pairs={{0,2},{2,0},{4,6},{6,4},{8,10},{10,8},{12,14},{14,12},{1,3},{3,1},... | collective-permute-start | bytes 1376264 | tf_op jit(solution)/shard_map/ppermute | solution.py:48
  67.0 17.9 %collective-permute-start.15 = (bf16[2,256,512]{2,1,0:T(8,128)(2,1)S(1)}, bf16[2,256,512]{2,1,0:T(8,128)(2,1)S(1)}, u32[]{:S(2)}, u32[]{:S(2)}) collective-permute-start(bf16[2,256,512]{2,1,0:T(8,128)(2,1)S(1)} %pad_maximum_fusion.8.refs_0_), channel_id=1, source_target_pairs={{0,1},{1,0},{2,3},{3,2},{4,5},{5,4},{6,7},{7,6},{8,9},{9,8},{10,11... | collective-permute-start | bytes 1572872 | tf_op jit(solution)/shard_map/ppermute | solution.py:40
  67.0 16.8 %collective-permute-start = (f32[2,512]{1,0:T(2,128)S(1)}, f32[2,512]{1,0:T(2,128)S(1)}, u32[]{:S(2)}, u32[]{:S(2)}) collective-permute-start(f32[2,512]{1,0:T(2,128)S(1)} %copy-done.23), channel_id=1, source_target_pairs={{0,1},{1,0},{2,3},{3,2},{4,5},{5,4},{6,7},{7,6},{8,9},{9,8},{10,11... | collective-permute-start | bytes 12296 | tf_op jit(solution)/shard_map/ppermute | solution.py:40
  75.8 6.1 %copy-start.21 = (bf16[448,512]{1,0:T(8,128)(2,1)}, bf16[448,512]{1,0:T(8,128)(2,1)S(1)}, u32[]{:S(2)}) copy-start(bf16[448,512]{1,0:T(8,128)(2,1)S(1)} %collective-permute-done.13.refs_7_) | copy-start | bytes 1376260
  75.8 10.5 %collective-permute-start.17 = (bf16[2,256,512]{2,1,0:T(8,128)(2,1)S(1)}, bf16[2,256,512]{2,1,0:T(8,128)(2,1)}, u32[]{:S(2)}, u32[]{:S(2)}) collective-permute-start(bf16[2,256,512]{2,1,0:T(8,128)(2,1)S(1)} %bitcast.16), channel_id=1, source_target_pairs={{0,1},{1,0},{2,3},{3,2},{4,5},{5,4},{6,7},{7,6},{8,9},{9,8},{10,11... | collective-permute-start | bytes 1572872 | tf_op jit(solution)/shard_map/ppermute | solution.py:40
  79.5 4.3 %copy-start.9 = (bf16[672,512]{1,0:T(8,128)(2,1)}, bf16[672,512]{1,0:T(8,128)(2,1)S(1)}, u32[]{:S(2)}) copy-start(bf16[672,512]{1,0:T(8,128)(2,1)S(1)} %collective-permute-done.14.refs_18_.refs_8_) | copy-start | bytes 2064388
  79.5 6.9 %collective-permute-start.16 = (bf16[2,256,512]{2,1,0:T(8,128)(2,1)S(1)}, bf16[2,256,512]{2,1,0:T(8,128)(2,1)}, u32[]{:S(2)}, u32[]{:S(2)}) collective-permute-start(bf16[2,256,512]{2,1,0:T(8,128)(2,1)S(1)} %bitcast.19), channel_id=1, source_target_pairs={{0,1},{1,0},{2,3},{3,2},{4,5},{5,4},{6,7},{7,6},{8,9},{9,8},{10,11... | collective-permute-start | bytes 1572872 | tf_op jit(solution)/shard_map/ppermute | solution.py:40
  82.8 3.6 %collective-permute-start.18 = (bf16[2,256,512]{2,1,0:T(8,128)(2,1)}, bf16[2,256,512]{2,1,0:T(8,128)(2,1)}, u32[]{:S(2)}, u32[]{:S(2)}) collective-permute-start(bf16[2,256,512]{2,1,0:T(8,128)(2,1)} %bitcast.11.refs_3_), channel_id=1, source_target_pairs={{0,1},{1,0},{2,3},{3,2},{4,5},{5,4},{6,7},{7,6},{8,9},{9,8},{10,11... | collective-permute-start | bytes 1572872 | tf_op jit(solution)/shard_map/ppermute | solution.py:40
  83.8 14.1 %collective-permute-start.19 = (bf16[448,512]{1,0:T(8,128)(2,1)}, bf16[448,512]{1,0:T(8,128)(2,1)}, u32[]{:S(2)}, u32[]{:S(2)}) collective-permute-start(bf16[448,512]{1,0:T(8,128)(2,1)} %get-tuple-element.61), channel_id=1, source_target_pairs={{0,2},{2,0},{4,6},{6,4},{8,10},{10,8},{12,14},{14,12},{1,3},{3,1},... | collective-permute-start | bytes 1376264 | tf_op jit(solution)/shard_map/ppermute | solution.py:48
  85.7 13.0 %collective-permute-start.20 = (bf16[448,512]{1,0:T(8,128)(2,1)}, bf16[448,512]{1,0:T(8,128)(2,1)}, u32[]{:S(2)}, u32[]{:S(2)}) collective-permute-start(bf16[448,512]{1,0:T(8,128)(2,1)} %get-tuple-element.60), channel_id=1, source_target_pairs={{0,16},{16,0},{1,17},{17,1},{2,18},{18,2},{3,19},{19,3},{4,20},{20... | collective-permute-start | bytes 1376264 | tf_op jit(solution)/shard_map/ppermute | solution.py:44
  86.3 16.6 %copy-start.2 = (bf16[2,256,512]{2,1,0:T(8,128)(2,1)S(1)}, bf16[2,256,512]{2,1,0:T(8,128)(2,1)}, u32[]{:S(2)}) copy-start(bf16[2,256,512]{2,1,0:T(8,128)(2,1)} %copy-done.1) | copy-start | bytes 1572868
  86.3 16.6 %copy-start.4 = (bf16[512,512]{1,0:T(8,128)(2,1)S(1)}, bf16[512,512]{1,0:T(8,128)(2,1)}, u32[]{:S(2)}) copy-start(bf16[512,512]{1,0:T(8,128)(2,1)} %copy-done.3) | copy-start | bytes 1572868
  86.3 16.7 %copy-start.6 = (bf16[512,512]{1,0:T(8,128)(2,1)S(1)}, bf16[512,512]{1,0:T(8,128)(2,1)}, u32[]{:S(2)}) copy-start(bf16[512,512]{1,0:T(8,128)(2,1)} %copy-done.5) | copy-start | bytes 1572868
  86.3 16.7 %copy-start.16 = (bf16[2,256,512]{2,1,0:T(8,128)(2,1)S(1)}, bf16[2,256,512]{2,1,0:T(8,128)(2,1)}, u32[]{:S(2)}) copy-start(bf16[2,256,512]{2,1,0:T(8,128)(2,1)} %copy-done.15) | copy-start | bytes 1572868
  98.7 4.3 %collective-permute-start.21 = (bf16[2,768,256]{2,1,0:T(8,128)(2,1)S(1)}, bf16[2,768,256]{2,1,0:T(8,128)(2,1)S(1)}, u32[]{:S(2)}, u32[]{:S(2)}) collective-permute-start(bf16[2,768,256]{2,1,0:T(8,128)(2,1)S(1)} %get-tuple-element.49.zm_ref), channel_id=1, source_target_pairs={{0,1},{1,0},{2,3},{3,2},{4,5},{5,4},{6,7},{7,6},{8,9},{9,8},{10,11... | collective-permute-start | bytes 2359304 | tf_op jit(solution)/shard_map/ppermute | solution.py:40
  98.7 4.2 %collective-permute-start.22 = (bf16[512,512]{1,0:T(8,128)(2,1)S(1)}, bf16[512,512]{1,0:T(8,128)(2,1)S(1)}, u32[]{:S(2)}, u32[]{:S(2)}) collective-permute-start(bf16[512,512]{1,0:T(8,128)(2,1)S(1)} %get-tuple-element.50.mixm_ref), channel_id=1, source_target_pairs={{0,1},{1,0},{2,3},{3,2},{4,5},{5,4},{6,7},{7,6},{8,9},{9,8},{10,11... | collective-permute-start | bytes 1572872 | tf_op jit(solution)/shard_map/ppermute | solution.py:40
  100.1 7.8 %collective-permute-start.23 = (bf16[112,512]{1,0:T(8,128)(2,1)S(1)}, bf16[112,512]{1,0:T(8,128)(2,1)S(1)}, u32[]{:S(2)}, u32[]{:S(2)}) collective-permute-start(bf16[112,512]{1,0:T(8,128)(2,1)S(1)} %slice.62), channel_id=1, source_target_pairs={{0,2},{2,0},{4,6},{6,4},{8,10},{10,8},{12,14},{14,12},{1,3},{3,1},... | collective-permute-start | bytes 344072 | tf_op jit(solution)/shard_map/ppermute | solution.py:48
  102.0 6.0 %copy-start.8 = (bf16[672,512]{1,0:T(8,128)(2,1)S(1)}, bf16[672,512]{1,0:T(8,128)(2,1)}, u32[]{:S(2)}) copy-start(bf16[672,512]{1,0:T(8,128)(2,1)} %copy-done.7) | copy-start | bytes 2064388
  102.0 6.0 %copy-start.10 = (bf16[672,512]{1,0:T(8,128)(2,1)S(1)}, bf16[672,512]{1,0:T(8,128)(2,1)}, u32[]{:S(2)}) copy-start(bf16[672,512]{1,0:T(8,128)(2,1)} %copy-done.9) | copy-start | bytes 2064388
  102.0 6.0 %copy-start.12 = (bf16[448,512]{1,0:T(8,128)(2,1)S(1)}, bf16[448,512]{1,0:T(8,128)(2,1)}, u32[]{:S(2)}) copy-start(bf16[448,512]{1,0:T(8,128)(2,1)} %copy-done.11) | copy-start | bytes 1376260
  102.0 6.0 %copy-start.14 = (bf16[448,512]{1,0:T(8,128)(2,1)S(1)}, bf16[448,512]{1,0:T(8,128)(2,1)}, u32[]{:S(2)}) copy-start(bf16[448,512]{1,0:T(8,128)(2,1)} %copy-done.13) | copy-start | bytes 1376260
  102.0 6.0 %copy-start.18 = (bf16[224,512]{1,0:T(8,128)(2,1)S(1)}, bf16[224,512]{1,0:T(8,128)(2,1)}, u32[]{:S(2)}) copy-start(bf16[224,512]{1,0:T(8,128)(2,1)} %copy-done.17) | copy-start | bytes 688132
  102.0 6.0 %copy-start.20 = (bf16[224,512]{1,0:T(8,128)(2,1)S(1)}, bf16[224,512]{1,0:T(8,128)(2,1)}, u32[]{:S(2)}) copy-start(bf16[224,512]{1,0:T(8,128)(2,1)} %copy-done.19) | copy-start | bytes 688132
  102.0 6.0 %copy-start.22 = (bf16[448,512]{1,0:T(8,128)(2,1)S(1)}, bf16[448,512]{1,0:T(8,128)(2,1)}, u32[]{:S(2)}) copy-start(bf16[448,512]{1,0:T(8,128)(2,1)} %copy-done.21) | copy-start | bytes 1376260
  102.0 5.9 %collective-permute-start.24 = (bf16[112,512]{1,0:T(8,128)(2,1)S(1)}, bf16[112,512]{1,0:T(8,128)(2,1)S(1)}, u32[]{:S(2)}, u32[]{:S(2)}) collective-permute-start(bf16[112,512]{1,0:T(8,128)(2,1)S(1)} %slice.63), channel_id=1, source_target_pairs={{0,16},{16,0},{1,17},{17,1},{2,18},{18,2},{3,19},{19,3},{4,20},{20... | collective-permute-start | bytes 344072 | tf_op jit(solution)/shard_map/ppermute | solution.py:44
  111.3 1.6 %collective-permute-start.25 = (bf16[2,256,256]{2,1,0:T(8,128)(2,1)S(1)}, bf16[2,256,256]{2,1,0:T(8,128)(2,1)S(1)}, u32[]{:S(2)}, u32[]{:S(2)}) collective-permute-start(bf16[2,256,256]{2,1,0:T(8,128)(2,1)S(1)} %get-tuple-element.53.zm_ref), channel_id=1, source_target_pairs={{0,1},{1,0},{2,3},{3,2},{4,5},{5,4},{6,7},{7,6},{8,9},{9,8},{10,11... | collective-permute-start | bytes 786440 | tf_op jit(solution)/shard_map/ppermute | solution.py:40
  (10 other events, 17.6 us)

commit v3 on v2

--- a/solution.py
+++ b/solution.py
@@ -105,44 +105,29 @@
 def conv0_kernel(cfg, place, gm_ref, gp_ref, *refs):
     rows, half, branch, blocks, starts, slabs, conv_rows, mix_rows, pairs, n_conv = cfg
     convs = refs[2 * blocks : 2 * blocks + n_conv]
-    z_ref, mix_ref, wide, raw, hm, hp, acc, sems, wsems = refs[2 * blocks + n_conv :]
-    copies = [
-        [
-            pltpu.make_async_copy(refs[b + i * blocks], raw.at[i, b], sems.at[i, b])
-            for i in range(2)
-        ]
-        for b in range(blocks)
-    ]
-    for pair in copies:
-        for copy in pair:
-            copy.start()
+    z_ref, mix_ref, wide, hm, hp, acc = refs[2 * blocks + n_conv :]
     moves = weight_moves(place, convs, conv_rows, mix_rows, pairs, wide, mix_ref)
-    moves = [pltpu.make_async_copy(*move, wsems.at[i]) for i, move in enumerate(moves)]
-    for copy in moves:
-        copy.start()
+    for src, dst in moves:
+        dst[...] = src[...]
     gm = gm_ref[0:1, :]
     gp = gp_ref[0:1, :]
     step = 64
     for b in range(blocks):
         base = (blocks - 1 - b) * rows
-        for copy in copies[b]:
-            copy.wait()
 
         def body(i, carry, b=b, base=base):
             at = pl.ds(pl.multiple_of(i * step, step), step)
             to = pl.ds(pl.multiple_of(base + i * step, step), step)
-            xm = raw[0, b, 0, at, :].astype(F32)
-            dxm = raw[0, b, 1, at, :].astype(F32)
-            xp = raw[1, b, 0, at, :].astype(F32)
-            dxp = raw[1, b, 1, at, :].astype(F32)
+            xm = refs[b][0, at, :].astype(F32)
+            dxm = refs[b][1, at, :].astype(F32)
+            xp = refs[b + blocks][0, at, :].astype(F32)
+            dxp = refs[b + blocks][1, at, :].astype(F32)
             hm[0, to, :], hp[0, to, :], hm[1, to, :], hp[1, to, :] = normalise(
                 xm, xp, dxm, dxp, gm, gp, 2 * half
             )
             return carry
 
         lax.fori_loop(0, rows // step, body, 0)
-    for copy in moves:
-        copy.wait()
     c = place[2]
     at_m = pl.multiple_of(c * half, half)
     at_p = pl.multiple_of((1 - c) * half, half)
@@ -185,7 +170,7 @@
     at_p = pl.ds(pl.multiple_of((1 - c) * branch, branch), branch)
     gm = gm_ref[layer : layer + 1, :]
     gp = gp_ref[layer : layer + 1, :]
-    step = min(128, rows)
+    step = min(256, rows)
     for j in range(TAPS):
         base = (TAPS - 1 - j) * rows
 
@@ -251,11 +236,54 @@
         out[...] = (state_ref[v].astype(F32) + y).astype(BF16)
 
 
-def exchange(own, chunks, seq):
-    c0, c1 = chunks
-    rows = own.shape[1]
-    half = own.shape[2]
-    unit = c0.shape[0]
+def pack(seq, place, *buffers):
+    arrays = []
+
+    def index(array):
+        for i, known in enumerate(arrays):
+            if known is array:
+                return i
+        arrays.append(array)
+        return len(arrays) - 1
+
+    plan = []
+    for buffer in buffers:
+        parts = []
+        for array, begin, count, *mark in buffer:
+            planes, even = (mark + [None, None])[:2] if mark else (None, None)
+            parts.append(
+                (index(array), begin, count, planes, None if even is None else index(even))
+            )
+        plan.append(parts)
+    width = arrays[0].shape[-1]
+
+    def kernel(place_ref, *refs):
+        s = place_ref[0]
+        for out, parts in zip(refs[len(arrays) :], plan):
+            to = 0
+            for i, begin, count, planes, even in parts:
+                value = refs[i][begin : begin + count, :]
+                if planes is not None:
+                    value = jnp.where(s < max(2 * planes, 1), jnp.zeros_like(value), value)
+                if even is not None:
+                    value = jnp.where(lax.rem(s, 2) == 1, value, refs[even][...])
+                out[to : to + count, :] = value
+                to += count
+
+    return pl.pallas_call(
+        kernel,
+        out_shape=tuple(near_out(sum(part[2] for part in buf), width) for buf in buffers),
+        in_specs=[SMEM] + [VMEM] * len(arrays),
+        out_specs=(VMEM,) * len(buffers),
+        compiler_params=scoped(4),
+        name="pack",
+    )(place, *[near(array) for array in arrays])
+
+
+def exchange(place, own, chunks, gains, seq):
+    both = chunks
+    unit = both.shape[0] // 2
+    tall = own.shape[0]
     pieces = ([], [])
     order = ([], [])
 
@@ -267,15 +295,6 @@
     def whole(layer, array, *slots):
         keep(layer, array, *[(i * unit, 0, unit, *slot) for i, slot in enumerate(slots)])
 
-    def part(array, i):
-        return array[i * unit : (i + 1) * unit]
-
-    def cat(*arrays):
-        return jnp.concatenate(arrays, 0)
-
-    def flat(block):
-        return block.reshape(2 * rows, half)
-
     def together(*blocks):
         return lax.optimization_barrier(blocks)
 
@@ -288,64 +307,68 @@
     def z(block, by=1):
         return ring(block, seq, 2 * by)
 
-    whole(0, c0, (0, 0, 0))
-    whole(1, c1, (0, 0, 0))
-    z1a, z1b = z(c0), z(c0, 3)
-    c01 = cat(c0, c1)
-    z1a, z1b, x1, y1, own, c1 = together(z1a, z1b, x(c01), y(c01), own, c1)
+    c0, c1 = both[:unit], both[unit:]
+    whole(0, both, (0, 0, 0))
+    keep(1, both, (unit, 0, unit, 0, 0, 0))
+    z1a, z1b, x1, y1, own, c1 = together(z(c0), z(c0, 3), x(both), y(both), own, c1)
     whole(0, z1a, (1, 0, 0))
     whole(0, z1b, (3, 0, 0))
-    x0, y0 = part(x1, 0), part(y1, 1)
     whole(0, x1, (0, 1, 0))
     keep(1, x1, (unit, 0, unit, 0, 1, 0))
     whole(0, y1, (0, 0, 1))
     keep(1, y1, (unit, 0, unit, 0, 0, 1))
-    z2 = z(cat(z1a, flat(own)))
-    x2 = x(cat(z1a, z1b, y0))
-    y2 = y(cat(z1a, z1b, x0))
-    z2, x2, y2, own, c1 = together(z2, x2, y2, own, c1)
-    q2 = part(z2, 0)
-    two = from_first(z2[unit:].reshape(own.shape), seq, 1)
+    to_z, to_x, to_y = pack(
+        seq,
+        place,
+        [(z1a, 0, unit), (own, 0, tall)],
+        [(z1a, 0, unit), (z1b, 0, unit), (y1, unit, unit)],
+        [(z1a, 0, unit), (z1b, 0, unit), (x1, 0, unit)],
+    )
+    z2, x2, y2, own, c1, gains_p = together(z(to_z), x(to_x), y(to_y), own, c1, swap_chan(gains))
     keep(0, z2, (0, 0, unit, 2, 0, 0))
     whole(0, x2, (1, 1, 0), (3, 1, 0))
     keep(1, x2, (2 * unit, 0, unit, 0, 1, 1))
     whole(0, y2, (1, 0, 1), (3, 0, 1), (0, 1, 1))
-    z3a, z3b = z(c1), z(c1, 3)
-    odd = lax.rem(lax.axis_index("seq"), 2) == 1
-    x3 = x(cat(q2, flat(jnp.where(odd, two, own))))
-    y3 = y(cat(q2, x2[: 2 * unit]))
-    z3a, z3b, x3, y3 = together(z3a, z3b, x3, y3)
-    one = from_first(x3[unit:].reshape(own.shape), seq, 0)
-    whole(1, z3a, (1, 0, 0))
+    to_z, to_x, to_y, two = pack(
+        seq,
+        place,
+        [(both, unit, unit), (x2, 2 * unit, unit)],
+        [(z2, 0, unit), (z2, unit, tall, 1, own)],
+        [(z2, 0, unit), (x2, 0, 2 * unit)],
+        [(z2, unit, tall, 1)],
+    )
+    z3a, z3b, x3, y3 = together(z(to_z), z(c1, 3), x(to_x), y(to_y))
+    whole(1, z3a, (1, 0, 0), (1, 1, 1))
     whole(1, z3b, (3, 0, 0))
     keep(0, x3, (0, 0, unit, 2, 1, 0))
     whole(0, y3, (2, 0, 1), (1, 1, 1), (3, 1, 1))
-    z4 = z(cat(z3a, flat(one)))
-    x4 = x(cat(z3a, z3b))
-    y4 = y(cat(z3a, z3b, part(x3, 0)))
-    z4, x4, y4 = together(z4, x4, y4)
-    p2 = part(z4, 0)
-    three = from_first(z4[unit:].reshape(own.shape), seq, 1)
+    to_z, to_x, to_y, one = pack(
+        seq,
+        place,
+        [(z3a, 0, unit), (x3, unit, tall, 0)],
+        [(z3a, 0, unit), (z3b, 0, unit)],
+        [(z3a, 0, unit), (z3b, 0, unit), (x3, 0, unit)],
+        [(x3, unit, tall, 0)],
+    )
+    z4, x4, y4 = together(z(to_z), x(to_x), y(to_y))
     keep(1, z4, (0, 0, unit, 2, 0, 0))
     whole(1, x4, (1, 1, 0), (3, 1, 0))
     whole(1, y4, (1, 0, 1), (3, 0, 1))
     keep(0, y4, (2 * unit, 0, unit, 2, 1, 1))
-    x5 = x(cat(p2, part(y4, 0)))
-    y5 = y(cat(p2, part(x4, 1)))
-    whole(1, x5, (2, 1, 0), (1, 1, 1))
-    whole(1, y5, (2, 0, 1), (3, 1, 1))
     cut = unit // 2
-    x6 = x(y5[:cut])
-    y6 = y(x5[cut:unit])
-    keep(1, x6, (0, 0, cut, 2, 1, 1))
-    keep(1, y6, (0, cut, unit - cut, 2, 1, 1))
-    return (one, two, three), (x5, y5), pieces, tuple((seq, tuple(o)) for o in order)
-
-
-def from_first(block, seq, planes):
-    s = lax.axis_index("seq")
-    first = s < 2 if planes else s < 1
-    return jnp.where(first, jnp.zeros_like(block), block)
+    to_z, to_x, to_y, three = pack(
+        seq,
+        place,
+        [(z3a, unit, unit)],
+        [(z4, 0, unit), (y4, unit, cut)],
+        [(z4, 0, unit), (x4, unit + cut, unit - cut)],
+        [(z4, unit, tall, 1)],
+    )
+    x5, y5, z5 = x(to_x), y(to_y), z(to_z)
+    whole(1, z5, (2, 1, 1))
+    keep(1, x5, (0, 0, unit, 2, 1, 0), (unit, 0, cut, 3, 1, 1))
+    keep(1, y5, (0, 0, unit, 2, 0, 1), (unit, cut, unit - cut, 3, 1, 1))
+    return gains_p, (one, two, three), (x5, y5, z5), pieces, tuple((seq, tuple(o)) for o in order)
 
 
 def on_device(signal, tangent, gains, convolution_kernel, mixing_kernel):
@@ -365,14 +388,13 @@
     if 2 * lag == rows:
         conv_rows, mix_rows = shard // 2, mix_shard // 2
         g = lax.axis_index("groups")
-        both = jnp.concatenate(
+        chunks = jnp.concatenate(
             [
                 lax.dynamic_slice_in_dim(conv_local, g * conv_rows, conv_rows, 1),
                 lax.dynamic_slice_in_dim(mixing_kernel, g * mix_rows, mix_rows, 1),
             ],
             1,
-        )
-        chunks = [both[l] for l in range(layers)]
+        ).reshape(layers * (conv_rows + mix_rows), 2 * branch)
         pairs = None
         step, used = lag, (0, 1, 2)
         blocks = 4
@@ -387,7 +409,6 @@
         ]
         step, used = rows, (0, 2, 4)
         blocks = 7
-    gains_p = swap_chan(gains)
     tall = blocks * rows
     starts = tuple(tall - rows - m * step for m in range(7))
     if 2 * lag == rows:
@@ -397,10 +418,13 @@
     slab = slabs[0][1]
 
     if pairs is None:
-        halo, beside, weights, pairs = exchange(own, chunks, seq)
-        mine = [own, *halo]
+        gains_p, halo, beside, weights, pairs = exchange(
+            place, own.reshape(2 * rows, half), chunks, gains, seq
+        )
+        mine = [own, *[block.reshape(own.shape) for block in halo]]
     else:
         beside = ()
+        gains_p = swap_chan(gains)
         mine = [own] + [from_behind(own, seq, k * (lag // rows)) for k in range(1, 7)]
     theirs = [swap_chan(block) for block in mine]
 
@@ -409,25 +433,23 @@
     z_mine, mix_mine = pl.pallas_call(
         functools.partial(conv0_kernel, cfg),
         out_shape=(near_out(2, TAPS * rows, branch), near_out(mix_whole, half)),
-        in_specs=[SMEM, VMEM, VMEM] + [ANY] * (2 * blocks + n_conv[0]),
+        in_specs=[SMEM] + [VMEM] * (2 + 2 * blocks + n_conv[0]),
         out_specs=(VMEM, VMEM),
         scratch_shapes=[
             pltpu.VMEM((wide_rows, 2 * branch), BF16),
-            pltpu.VMEM((2, blocks, 2, rows, half), BF16),
             pltpu.VMEM((2, tall, half), BF16),
             pltpu.VMEM((2, tall, half), BF16),
             pltpu.VMEM((2, slab, 2 * branch), F32),
-            pltpu.SemaphoreType.DMA((2, blocks)),
-            pltpu.SemaphoreType.DMA((2 if pairs[0] is None else 2 * len(pairs[0][1]),)),
         ],
-        compiler_params=scoped(28),
+        compiler_params=scoped(20),
         cost_estimate=cost(0, 32 * 2**20),
         name="conv0",
     )(
         place,
         near(gains),
         near(gains_p),
-        *[far(block) for block in (*mine, *theirs, *weights[0])],
+        *[near(block) for block in (*mine, *theirs)],
+        *[near(w) for w in weights[0]],
     )
     z_mine, mix_mine = lax.optimization_barrier((z_mine, mix_mine, *beside))[:2]
     mix_theirs = swap_chan(mix_mine)

time: 115 us -> 101 us (0.88)
  other arithmetic: 7.26 us -> 0.19 us
  local copies, waits for them, and re-layouts: 7.91 us -> 2.56 us
  waiting for transfers between devices: 54 us -> 56.2 us
  Pallas kernels: 21.4 us -> 19.2 us
    ppermute x6 -> x7, waiting for transfers between devices: 18.1 us -> 25.6 us  [ring(): return lax.ppermute(block, 'seq', [(s, (s + by) % seq) for s in range(seq)])]
    concatenate x9 -> x1, other arithmetic: 6.08 us -> 0.03 us  [on_device(): jnp.concatenate([lax.dynamic_slice_in_dim(conv_local, g * conv_rows, conv...]
    ppermute x6 -> x5, waiting for transfers between devices: 9.75 us -> 4.87 us  [swap_groups(): return lax.ppermute(block, 'groups', [(0, 1), (1, 0)])]
    ppermute x6 -> x5, waiting for transfers between devices: 24.6 us -> 20.6 us  [swap_pair(): return lax.ppermute(block, 'seq', [(s, s ^ 1) for s in range(seq)])]
    ppermute x8, waiting for transfers between devices: 1.54 us -> 5.11 us  [swap_chan(): return lax.ppermute(block, 'chan', [(0, 1), (1, 0)])]
    ppermute x6 -> x5, starting transfers between devices: 8.34 us -> 4.9 us  [swap_pair(): return lax.ppermute(block, 'seq', [(s, s ^ 1) for s in range(seq)])]
    unnamed x62 -> x8, local copies, waits for them, and re-layouts: 3.46 us -> 0.03 us
    pallas_call x1, Pallas kernels: 11.6 us -> 8.6 us  [on_device(): pl.pallas_call(functools.partial(conv0_kernel, cfg), out_shape=(near_out(...]
  transfers between devices with their start and end apart: 26 -> 25, of which waited for: 13 -> 14; matrix products, arithmetic and copies ran while one was open for 6% -> 0% of each run, Pallas kernels for 14% -> 9%
where the time goes in v3:
time: 101 us
  waiting for transfers between devices  56.2 us (56%)
  starting transfers between devices  21.8 us (22%)
  Pallas kernels  19.2 us (19%)
  local copies, waits for them, and re-layouts  2.56 us (3%)
    ppermute x7, waiting for transfers between devices, ring(): return lax.ppermute(block, 'seq', [(s, (s + by) % seq) for s in range(seq)])  25.6 us
    ppermute x5, waiting for transfers between devices, swap_pair(): return lax.ppermute(block, 'seq', [(s, s ^ 1) for s in range(seq)])  20.6 us
    ppermute x7, starting transfers between devices, ring(): return lax.ppermute(block, 'seq', [(s, (s + by) % seq) for s in range(seq)])  9.22 us
    pallas_call x1, Pallas kernels, on_device(): pl.pallas_call(functools.partial(conv0_kernel, cfg), out_shape=(near_out(...  8.6 us
    ppermute x5, starting transfers between devices, swap_groups(): return lax.ppermute(block, 'groups', [(0, 1), (1, 0)])  6.38 us
    ppermute x8, waiting for transfers between devices, swap_chan(): return lax.ppermute(block, 'chan', [(0, 1), (1, 0)])  5.11 us
    ppermute x5, starting transfers between devices, swap_pair(): return lax.ppermute(block, 'seq', [(s, s ^ 1) for s in range(seq)])  4.9 us
    ppermute x5, waiting for transfers between devices, swap_groups(): return lax.ppermute(block, 'groups', [(0, 1), (1, 0)])  4.87 us
  transfers between devices with their start and end apart: 25, of which 14 were waited for; matrix products, arithmetic and copies ran while one was open for 0% of the time, Pallas kernels for 9%

profile of v3, /device:TPU:0, one launch (start us, length us, event | category | flops | bytes accessed | tf_op | source)
XLA Modules:
  0.0 100.8 jit_solution(13350705784447530800)
XLA Ops:
  0.6 0.0 copy-start
  0.7 2.5 %reshape.24 = bf16[2,384,512]{2,1,0:T(8,128)(2,1)S(1)} reshape(bf16[2,384,2,256]{3,2,1,0:T(2,128)(2,1)} %param.8) | data formatting | bytes 1572864 | tf_op jit(solution)/shard_map/reshape | solution.py:386
  3.1 0.0 copy-start.2
  3.1 0.0 copy-start.3
  3.3 3.0 %collective-permute-start.3 = (bf16[448,512]{1,0:T(8,128)(2,1)S(1)}, bf16[448,512]{1,0:T(8,128)(2,1)S(1)}, u32[]{:S(2)}, u32[]{:S(2)}) collective-permute-start(bf16[448,512]{1,0:T(8,128)(2,1)S(1)} %bitcast.16), channel_id=1, source_target_pairs={{0,16},{16,0},{1,17},{17,1},{2,18},{18,2},{3,19},{19,3},{4,20},{20... | collective-permute-start | bytes 1376264 | tf_op jit(solution)/shard_map/ppermute | solution.py:44
  6.3 1.5 %collective-permute-start.2 = (bf16[448,512]{1,0:T(8,128)(2,1)S(1)}, bf16[448,512]{1,0:T(8,128)(2,1)S(1)}, u32[]{:S(2)}, u32[]{:S(2)}) collective-permute-start(bf16[448,512]{1,0:T(8,128)(2,1)S(1)} %bitcast.17), channel_id=1, source_target_pairs={{0,2},{2,0},{4,6},{6,4},{8,10},{10,8},{12,14},{14,12},{1,3},{3,1},... | collective-permute-start | bytes 1376264 | tf_op jit(solution)/shard_map/ppermute | solution.py:48
  7.8 0.0 copy-start.1
  7.8 3.7 %collective-permute-start.1 = (bf16[224,512]{1,0:T(8,128)(2,1)S(1)}, bf16[224,512]{1,0:T(8,128)(2,1)S(1)}, u32[]{:S(2)}, u32[]{:S(2)}) collective-permute-start(bf16[224,512]{1,0:T(8,128)(2,1)S(1)} %get-tuple-element.89), channel_id=1, source_target_pairs={{0,12},{2,14},{4,0},{6,2},{8,4},{10,6},{12,8},{14,10},{1,13},{3,15... | collective-permute-start | bytes 688136 | tf_op jit(solution)/shard_map/ppermute | solution.py:52
  11.5 0.1 pad_add_fusion.place_ref.place
  11.6 0.1 pad_maximum_fusion.1.refs_0_
  11.6 5.9 %collective-permute-done.1.refs_2_.refs_10_ = bf16[224,512]{1,0:T(8,128)(2,1)S(1)} collective-permute-done((bf16[224,512]{1,0:T(8,128)(2,1)S(1)}, bf16[224,512]{1,0:T(8,128)(2,1)S(1)}, u32[]{:S(2)}, u32[]{:S(2)}) %collective-permute-start.1) | collective-permute-done | bytes 229408 | tf_op jit(solution)/shard_map/ppermute | solution.py:52
  17.6 4.1 %collective-permute-done.refs_0_.refs_9_ = bf16[224,512]{1,0:T(8,128)(2,1)S(1)} collective-permute-done((bf16[224,512]{1,0:T(8,128)(2,1)S(1)}, bf16[224,512]{1,0:T(8,128)(2,1)S(1)}, u32[]{:S(2)}, u32[]{:S(2)}) %collective-permute-start) | collective-permute-done | bytes 229408 | tf_op jit(solution)/shard_map/ppermute | solution.py:52
  21.6 0.7 pack.4
  22.3 1.7 %collective-permute-start.4 = (bf16[736,512]{1,0:T(8,128)(2,1)S(1)}, bf16[736,512]{1,0:T(8,128)(2,1)S(1)}, u32[]{:S(2)}, u32[]{:S(2)}) collective-permute-start(bf16[736,512]{1,0:T(8,128)(2,1)S(1)} %get-tuple-element.50), channel_id=1, source_target_pairs={{0,4},{2,6},{4,8},{6,10},{8,12},{10,14},{12,0},{14,2},{1,5},{3,7},... | collective-permute-start | bytes 2261000 | tf_op jit(solution)/shard_map/ppermute | solution.py:52
  24.0 0.5 collective-permute-start.5
  24.5 0.5 collective-permute-start.6
  25.0 1.2 %collective-permute-done.7.gp_ref = f32[2,512]{1,0:T(2,128)S(1)} collective-permute-done((f32[2,512]{1,0:T(2,128)S(1)}, f32[2,512]{1,0:T(2,128)S(1)}, u32[]{:S(2)}, u32[]{:S(2)}) %collective-permute-start.7) | collective-permute-done | bytes 4128 | tf_op jit(solution)/shard_map/ppermute | solution.py:40
  26.2 13.2 %collective-permute-done.5.refs_1_.refs_14_.refs_3_ = bf16[672,512]{1,0:T(8,128)(2,1)S(1)} collective-permute-done((bf16[672,512]{1,0:T(8,128)(2,1)S(1)}, bf16[672,512]{1,0:T(8,128)(2,1)S(1)}, u32[]{:S(2)}, u32[]{:S(2)}) %collective-permute-start.5) | collective-permute-done | bytes 688160 | tf_op jit(solution)/shard_map/ppermute | solution.py:48
  39.5 0.3 collective-permute-done.6.refs_15_
  39.7 1.6 %collective-permute-done.4.refs_2_.refs_13_ = bf16[736,512]{1,0:T(8,128)(2,1)S(1)} collective-permute-done((bf16[736,512]{1,0:T(8,128)(2,1)S(1)}, bf16[736,512]{1,0:T(8,128)(2,1)S(1)}, u32[]{:S(2)}, u32[]{:S(2)}) %collective-permute-start.4) | collective-permute-done | bytes 753696 | tf_op jit(solution)/shard_map/ppermute | solution.py:52
  41.3 0.8 pack.5
  42.0 0.6 collective-permute-start.10
  42.6 0.5 collective-permute-start.11
  43.2 3.8 %collective-permute-start.9 = (bf16[224,512]{1,0:T(8,128)(2,1)S(1)}, bf16[224,512]{1,0:T(8,128)(2,1)S(1)}, u32[]{:S(2)}, u32[]{:S(2)}) collective-permute-start(bf16[224,512]{1,0:T(8,128)(2,1)S(1)} %get-tuple-element.59), channel_id=1, source_target_pairs={{0,12},{2,14},{4,0},{6,2},{8,4},{10,6},{12,8},{14,10},{1,13},{3,15... | collective-permute-start | bytes 688136 | tf_op jit(solution)/shard_map/ppermute | solution.py:52
  47.0 10.4 %collective-permute-done.9.refs_2_.refs_5_ = bf16[224,512]{1,0:T(8,128)(2,1)S(1)} collective-permute-done((bf16[224,512]{1,0:T(8,128)(2,1)S(1)}, bf16[224,512]{1,0:T(8,128)(2,1)S(1)}, u32[]{:S(2)}, u32[]{:S(2)}) %collective-permute-start.9) | collective-permute-done | bytes 229408 | tf_op jit(solution)/shard_map/ppermute | solution.py:52
  57.4 0.9 collective-permute-done.10.refs_1_.refs_16_
  58.3 0.7 pack.6
  59.0 0.1 collective-permute-start.12
  59.1 0.8 collective-permute-start.14
  59.9 1.5 %collective-permute-start.13 = (bf16[448,512]{1,0:T(8,128)(2,1)S(1)}, bf16[448,512]{1,0:T(8,128)(2,1)S(1)}, u32[]{:S(2)}, u32[]{:S(2)}) collective-permute-start(bf16[448,512]{1,0:T(8,128)(2,1)S(1)} %get-tuple-element.68), channel_id=1, source_target_pairs={{0,2},{2,0},{4,6},{6,4},{8,10},{10,8},{12,14},{14,12},{1,3},{3,1},... | collective-permute-start | bytes 1376264 | tf_op jit(solution)/shard_map/ppermute | solution.py:48
  61.4 0.5 collective-permute-start.17
  61.9 6.5 %collective-permute-done.13.refs_3_.refs_7_ = bf16[448,512]{1,0:T(8,128)(2,1)S(1)} collective-permute-done((bf16[448,512]{1,0:T(8,128)(2,1)S(1)}, bf16[448,512]{1,0:T(8,128)(2,1)S(1)}, u32[]{:S(2)}, u32[]{:S(2)}) %collective-permute-start.13) | collective-permute-done | bytes 458784 | tf_op jit(solution)/shard_map/ppermute | solution.py:48
  68.4 4.6 %collective-permute-done.14.refs_2_.refs_18_.refs_8_ = bf16[672,512]{1,0:T(8,128)(2,1)S(1)} collective-permute-done((bf16[672,512]{1,0:T(8,128)(2,1)S(1)}, bf16[672,512]{1,0:T(8,128)(2,1)S(1)}, u32[]{:S(2)}, u32[]{:S(2)}) %collective-permute-start.14) | collective-permute-done | bytes 688160 | tf_op jit(solution)/shard_map/ppermute | solution.py:44
  73.0 3.1 %collective-permute-done.12.refs_1_.refs_6_ = bf16[736,512]{1,0:T(8,128)(2,1)S(1)} collective-permute-done((bf16[736,512]{1,0:T(8,128)(2,1)S(1)}, bf16[736,512]{1,0:T(8,128)(2,1)S(1)}, u32[]{:S(2)}, u32[]{:S(2)}) %collective-permute-start.12) | collective-permute-done | bytes 753696 | tf_op jit(solution)/shard_map/ppermute | solution.py:52
  76.1 0.7 pack.7
  76.8 0.1 collective-permute-start.18
  76.9 0.8 collective-permute-start.19
  77.7 1.5 %collective-permute-start.20 = (bf16[336,512]{1,0:T(8,128)(2,1)S(1)}, bf16[336,512]{1,0:T(8,128)(2,1)S(1)}, u32[]{:S(2)}, u32[]{:S(2)}) collective-permute-start(bf16[336,512]{1,0:T(8,128)(2,1)S(1)} %get-tuple-element.79), channel_id=1, source_target_pairs={{0,16},{16,0},{1,17},{17,1},{2,18},{18,2},{3,19},{19,3},{4,20},{20... | collective-permute-start | bytes 1032200 | tf_op jit(solution)/shard_map/ppermute | solution.py:44
  79.2 0.0 collective-permute-start.21
  79.2 8.6 %conv0.1 = (bf16[2,768,256]{2,1,0:T(8,128)(2,1)S(1)}, bf16[512,512]{1,0:T(8,128)(2,1)S(1)}) custom-call(s32[3]{0:T(128)S(1)} %pad_add_fusion.place_ref.place, f32[2,512]{1,0:T(2,128)S(1)} %copy-done.1, f32[2,512]{1,0:T(2,128)S(1)} %collective-permute-done.7.gp_ref, bf16[2,256,512]{2,1,0:T(8,128)(2,1)S(1)} %pad_maximum_fusion.1.refs_0_, ...), custom_call_target="tpu_custom_call" | custom-call | bytes 33554432 | tf_op jit(solution)/shard_map/conv0/pallas_call | solution.py:433
  87.8 0.6 collective-permute-done.21.refs_9_
  88.4 0.5 collective-permute-start.23
  88.9 2.5 %collective-permute-done.23.mixp_ref = bf16[512,512]{1,0:T(8,128)(2,1)S(1)} collective-permute-done((bf16[512,512]{1,0:T(8,128)(2,1)S(1)}, bf16[512,512]{1,0:T(8,128)(2,1)S(1)}, u32[]{:S(2)}, u32[]{:S(2)}) %collective-permute-start.23) | collective-permute-done | bytes 524320 | tf_op jit(solution)/shard_map/ppermute | solution.py:40
  91.4 3.5 %mix0.1 = (bf16[3,2,256,512]{3,2,1,0:T(8,128)(2,1)S(1)}, bf16[3,2,256,512]{3,2,1,0:T(8,128)(2,1)S(1)}, bf16[2,256,512]{2,1,0:T(8,128)(2,1)S(1)}) custom-call(s32[3]{0:T(128)S(1)} %pad_add_fusion.place_ref.place, f32[2,512]{1,0:T(2,128)S(1)} %copy-done.1, f32[2,512]{1,0:T(2,128)S(1)} %collective-permute-done.7.gp_ref, ...), custom_call_target="tpu_custom_call" | custom-call | bytes 20971520 | tf_op jit(solution)/shard_map/mix0/pallas_call | solution.py:457
  94.9 2.6 %conv1.1 = (bf16[2,256,256]{2,1,0:T(8,128)(2,1)S(1)}, bf16[512,512]{1,0:T(8,128)(2,1)S(1)}) custom-call(s32[3]{0:T(128)S(1)} %pad_add_fusion.place_ref.place, bf16[3,2,256,512]{3,2,1,0:T(8,128)(2,1)S(1)} %get-tuple-element.83.hm, bf16[3,2,256,512]{3,2,1,0:T(8,128)(2,1)S(1)} %get-tuple-element.84.hp, bf16[448,512]{1,0:T(8,128)(2,1)S(1)} %bitcast.20, ...), custom_call_target="tpu_custom_call" | custom-call | tf_op jit(solution)/shard_map/conv1/pallas_call | solution.py:481
  97.5 0.2 collective-permute-start.24
  97.7 1.4 %collective-permute-done.24.zp_ref = bf16[2,256,256]{2,1,0:T(8,128)(2,1)S(1)} collective-permute-done((bf16[2,256,256]{2,1,0:T(8,128)(2,1)S(1)}, bf16[2,256,256]{2,1,0:T(8,128)(2,1)S(1)}, u32[]{:S(2)}, u32[]{:S(2)}) %collective-permute-start.24) | collective-permute-done | bytes 262176 | tf_op jit(solution)/shard_map/ppermute | solution.py:40
  99.1 1.7 %mix1.1 = (bf16[256,512]{1,0:T(8,128)(2,1)}, bf16[256,512]{1,0:T(8,128)(2,1)}) custom-call(s32[3]{0:T(128)S(1)} %pad_add_fusion.place_ref.place, bf16[2,256,256]{2,1,0:T(8,128)(2,1)S(1)} %get-tuple-element.85.zm_ref, bf16[2,256,256]{2,1,0:T(8,128)(2,1)S(1)} %collective-permute-done.24.zp_ref, bf16[512,512]{1,0:T(8,128)(2,1)S(1)} %get-tuple-element.86.mix_ref, ...), custom_call_target="tpu_custom_call" | custom-call | tf_op jit(solution)/shard_map/mix1/pallas_call | solution.py:494
  (25 shorter events, 0.2 us)
Async XLA Ops:
  0.6 2.5 %copy-start = (bf16[2,64,512]{2,1,0:T(8,128)(2,1)S(1)}, bf16[2,64,512]{2,1,0:T(8,128)(2,1)}, u32[]{:S(2)}) copy-start(bf16[2,64,512]{2,1,0:T(8,128)(2,1)} %param.9) | copy-start | bytes 393220
  3.1 8.4 %copy-start.2 = (bf16[256,512]{1,0:T(8,128)(2,1)S(1)}, bf16[256,512]{1,0:T(8,128)(2,1)}, u32[]{:S(2)}) copy-start(bf16[256,512]{1,0:T(8,128)(2,1)} %param.6) | copy-start | bytes 786436
  3.1 8.4 %copy-start.3 = (bf16[256,512]{1,0:T(8,128)(2,1)S(1)}, bf16[256,512]{1,0:T(8,128)(2,1)}, u32[]{:S(2)}) copy-start(bf16[256,512]{1,0:T(8,128)(2,1)} %param.5) | copy-start | bytes 786436
  3.3 18.4 %collective-permute-start.3 = (bf16[448,512]{1,0:T(8,128)(2,1)S(1)}, bf16[448,512]{1,0:T(8,128)(2,1)S(1)}, u32[]{:S(2)}, u32[]{:S(2)}) collective-permute-start(bf16[448,512]{1,0:T(8,128)(2,1)S(1)} %bitcast.16), channel_id=1, source_target_pairs={{0,16},{16,0},{1,17},{17,1},{2,18},{18,2},{3,19},{19,3},{4,20},{20... | collective-permute-start | bytes 1376264 | tf_op jit(solution)/shard_map/ppermute | solution.py:44
  6.3 15.3 %collective-permute-start.2 = (bf16[448,512]{1,0:T(8,128)(2,1)S(1)}, bf16[448,512]{1,0:T(8,128)(2,1)S(1)}, u32[]{:S(2)}, u32[]{:S(2)}) collective-permute-start(bf16[448,512]{1,0:T(8,128)(2,1)S(1)} %bitcast.17), channel_id=1, source_target_pairs={{0,2},{2,0},{4,6},{6,4},{8,10},{10,8},{12,14},{14,12},{1,3},{3,1},... | collective-permute-start | bytes 1376264 | tf_op jit(solution)/shard_map/ppermute | solution.py:48
  7.8 17.2 %copy-start.1 = (f32[2,512]{1,0:T(2,128)S(1)}, f32[2,512]{1,0:T(2,128)}, u32[]{:S(2)}) copy-start(f32[2,512]{1,0:T(2,128)} %gm_ref.3) | copy-start | bytes 12292
  7.8 9.7 %collective-permute-start.1 = (bf16[224,512]{1,0:T(8,128)(2,1)S(1)}, bf16[224,512]{1,0:T(8,128)(2,1)S(1)}, u32[]{:S(2)}, u32[]{:S(2)}) collective-permute-start(bf16[224,512]{1,0:T(8,128)(2,1)S(1)} %get-tuple-element.89), channel_id=1, source_target_pairs={{0,12},{2,14},{4,0},{6,2},{8,4},{10,6},{12,8},{14,10},{1,13},{3,15... | collective-permute-start | bytes 688136 | tf_op jit(solution)/shard_map/ppermute | solution.py:52
  11.5 10.1 %collective-permute-start = (bf16[224,512]{1,0:T(8,128)(2,1)S(1)}, bf16[224,512]{1,0:T(8,128)(2,1)S(1)}, u32[]{:S(2)}, u32[]{:S(2)}) collective-permute-start(bf16[224,512]{1,0:T(8,128)(2,1)S(1)} %get-tuple-element.89), channel_id=1, source_target_pairs={{0,4},{2,6},{4,8},{6,10},{8,12},{10,14},{12,0},{14,2},{1,5},{3,7},... | collective-permute-start | bytes 688136 | tf_op jit(solution)/shard_map/ppermute | solution.py:52
  22.3 18.9 %collective-permute-start.4 = (bf16[736,512]{1,0:T(8,128)(2,1)S(1)}, bf16[736,512]{1,0:T(8,128)(2,1)S(1)}, u32[]{:S(2)}, u32[]{:S(2)}) collective-permute-start(bf16[736,512]{1,0:T(8,128)(2,1)S(1)} %get-tuple-element.50), channel_id=1, source_target_pairs={{0,4},{2,6},{4,8},{6,10},{8,12},{10,14},{12,0},{14,2},{1,5},{3,7},... | collective-permute-start | bytes 2261000 | tf_op jit(solution)/shard_map/ppermute | solution.py:52
  24.0 15.5 %collective-permute-start.5 = (bf16[672,512]{1,0:T(8,128)(2,1)S(1)}, bf16[672,512]{1,0:T(8,128)(2,1)S(1)}, u32[]{:S(2)}, u32[]{:S(2)}) collective-permute-start(bf16[672,512]{1,0:T(8,128)(2,1)S(1)} %get-tuple-element.51), channel_id=1, source_target_pairs={{0,2},{2,0},{4,6},{6,4},{8,10},{10,8},{12,14},{14,12},{1,3},{3,1},... | collective-permute-start | bytes 2064392 | tf_op jit(solution)/shard_map/ppermute | solution.py:48
  24.5 15.2 %collective-permute-start.6 = (bf16[672,512]{1,0:T(8,128)(2,1)S(1)}, bf16[672,512]{1,0:T(8,128)(2,1)S(1)}, u32[]{:S(2)}, u32[]{:S(2)}) collective-permute-start(bf16[672,512]{1,0:T(8,128)(2,1)S(1)} %get-tuple-element.52), channel_id=1, source_target_pairs={{0,16},{16,0},{1,17},{17,1},{2,18},{18,2},{3,19},{19,3},{4,20},{20... | collective-permute-start | bytes 2064392 | tf_op jit(solution)/shard_map/ppermute | solution.py:44
  25.0 1.2 %collective-permute-start.7 = (f32[2,512]{1,0:T(2,128)S(1)}, f32[2,512]{1,0:T(2,128)S(1)}, u32[]{:S(2)}, u32[]{:S(2)}) collective-permute-start(f32[2,512]{1,0:T(2,128)S(1)} %copy-done.1), channel_id=1, source_target_pairs={{0,1},{1,0},{2,3},{3,2},{4,5},{5,4},{6,7},{7,6},{8,9},{9,8},{10,11... | collective-permute-start | bytes 12296 | tf_op jit(solution)/shard_map/ppermute | solution.py:40
  42.0 16.2 %collective-permute-start.10 = (bf16[736,512]{1,0:T(8,128)(2,1)S(1)}, bf16[736,512]{1,0:T(8,128)(2,1)S(1)}, u32[]{:S(2)}, u32[]{:S(2)}) collective-permute-start(bf16[736,512]{1,0:T(8,128)(2,1)S(1)} %get-tuple-element.60), channel_id=1, source_target_pairs={{0,2},{2,0},{4,6},{6,4},{8,10},{10,8},{12,14},{14,12},{1,3},{3,1},... | collective-permute-start | bytes 2261000 | tf_op jit(solution)/shard_map/ppermute | solution.py:48
  42.6 14.7 %collective-permute-start.11 = (bf16[672,512]{1,0:T(8,128)(2,1)S(1)}, bf16[672,512]{1,0:T(8,128)(2,1)S(1)}, u32[]{:S(2)}, u32[]{:S(2)}) collective-permute-start(bf16[672,512]{1,0:T(8,128)(2,1)S(1)} %get-tuple-element.61), channel_id=1, source_target_pairs={{0,16},{16,0},{1,17},{17,1},{2,18},{18,2},{3,19},{19,3},{4,20},{20... | collective-permute-start | bytes 2064392 | tf_op jit(solution)/shard_map/ppermute | solution.py:44
  43.1 14.2 %collective-permute-start.8 = (bf16[448,512]{1,0:T(8,128)(2,1)S(1)}, bf16[448,512]{1,0:T(8,128)(2,1)S(1)}, u32[]{:S(2)}, u32[]{:S(2)}) collective-permute-start(bf16[448,512]{1,0:T(8,128)(2,1)S(1)} %get-tuple-element.58), channel_id=1, source_target_pairs={{0,4},{2,6},{4,8},{6,10},{8,12},{10,14},{12,0},{14,2},{1,5},{3,7},... | collective-permute-start | bytes 1376264 | tf_op jit(solution)/shard_map/ppermute | solution.py:52
  43.2 14.2 %collective-permute-start.9 = (bf16[224,512]{1,0:T(8,128)(2,1)S(1)}, bf16[224,512]{1,0:T(8,128)(2,1)S(1)}, u32[]{:S(2)}, u32[]{:S(2)}) collective-permute-start(bf16[224,512]{1,0:T(8,128)(2,1)S(1)} %get-tuple-element.59), channel_id=1, source_target_pairs={{0,12},{2,14},{4,0},{6,2},{8,4},{10,6},{12,8},{14,10},{1,13},{3,15... | collective-permute-start | bytes 688136 | tf_op jit(solution)/shard_map/ppermute | solution.py:52
  59.0 17.1 %collective-permute-start.12 = (bf16[736,512]{1,0:T(8,128)(2,1)S(1)}, bf16[736,512]{1,0:T(8,128)(2,1)S(1)}, u32[]{:S(2)}, u32[]{:S(2)}) collective-permute-start(bf16[736,512]{1,0:T(8,128)(2,1)S(1)} %get-tuple-element.67), channel_id=1, source_target_pairs={{0,4},{2,6},{4,8},{6,10},{8,12},{10,14},{12,0},{14,2},{1,5},{3,7},... | collective-permute-start | bytes 2261000 | tf_op jit(solution)/shard_map/ppermute | solution.py:52
  59.1 13.9 %collective-permute-start.14 = (bf16[672,512]{1,0:T(8,128)(2,1)S(1)}, bf16[672,512]{1,0:T(8,128)(2,1)S(1)}, u32[]{:S(2)}, u32[]{:S(2)}) collective-permute-start(bf16[672,512]{1,0:T(8,128)(2,1)S(1)} %get-tuple-element.69), channel_id=1, source_target_pairs={{0,16},{16,0},{1,17},{17,1},{2,18},{18,2},{3,19},{19,3},{4,20},{20... | collective-permute-start | bytes 2064392 | tf_op jit(solution)/shard_map/ppermute | solution.py:44
  59.9 8.5 %collective-permute-start.13 = (bf16[448,512]{1,0:T(8,128)(2,1)S(1)}, bf16[448,512]{1,0:T(8,128)(2,1)S(1)}, u32[]{:S(2)}, u32[]{:S(2)}) collective-permute-start(bf16[448,512]{1,0:T(8,128)(2,1)S(1)} %get-tuple-element.68), channel_id=1, source_target_pairs={{0,2},{2,0},{4,6},{6,4},{8,10},{10,8},{12,14},{14,12},{1,3},{3,1},... | collective-permute-start | bytes 1376264 | tf_op jit(solution)/shard_map/ppermute | solution.py:48
  61.4 16.3 %collective-permute-start.15 = (bf16[2,256,512]{2,1,0:T(8,128)(2,1)S(1)}, bf16[2,256,512]{2,1,0:T(8,128)(2,1)S(1)}, u32[]{:S(2)}, u32[]{:S(2)}) collective-permute-start(bf16[2,256,512]{2,1,0:T(8,128)(2,1)S(1)} %pad_maximum_fusion.1.refs_0_), channel_id=1, source_target_pairs={{0,1},{1,0},{2,3},{3,2},{4,5},{5,4},{6,7},{7,6},{8,9},{9,8},{10,11... | collective-permute-start | bytes 1572872 | tf_op jit(solution)/shard_map/ppermute | solution.py:40
  61.4 17.8 %collective-permute-start.17 = (bf16[2,256,512]{2,1,0:T(8,128)(2,1)S(1)}, bf16[2,256,512]{2,1,0:T(8,128)(2,1)S(1)}, u32[]{:S(2)}, u32[]{:S(2)}) collective-permute-start(bf16[2,256,512]{2,1,0:T(8,128)(2,1)S(1)} %bitcast.21), channel_id=1, source_target_pairs={{0,1},{1,0},{2,3},{3,2},{4,5},{5,4},{6,7},{7,6},{8,9},{9,8},{10,11... | collective-permute-start | bytes 1572872 | tf_op jit(solution)/shard_map/ppermute | solution.py:40
  68.4 10.8 %collective-permute-start.16 = (bf16[2,256,512]{2,1,0:T(8,128)(2,1)S(1)}, bf16[2,256,512]{2,1,0:T(8,128)(2,1)S(1)}, u32[]{:S(2)}, u32[]{:S(2)}) collective-permute-start(bf16[2,256,512]{2,1,0:T(8,128)(2,1)S(1)} %bitcast.24), channel_id=1, source_target_pairs={{0,1},{1,0},{2,3},{3,2},{4,5},{5,4},{6,7},{7,6},{8,9},{9,8},{10,11... | collective-permute-start | bytes 1572872 | tf_op jit(solution)/shard_map/ppermute | solution.py:40
  76.8 2.4 %collective-permute-start.18 = (bf16[2,256,512]{2,1,0:T(8,128)(2,1)S(1)}, bf16[2,256,512]{2,1,0:T(8,128)(2,1)S(1)}, u32[]{:S(2)}, u32[]{:S(2)}) collective-permute-start(bf16[2,256,512]{2,1,0:T(8,128)(2,1)S(1)} %bitcast.27), channel_id=1, source_target_pairs={{0,1},{1,0},{2,3},{3,2},{4,5},{5,4},{6,7},{7,6},{8,9},{9,8},{10,11... | collective-permute-start | bytes 1572872 | tf_op jit(solution)/shard_map/ppermute | solution.py:40
  76.9 11.5 %collective-permute-start.19 = (bf16[336,512]{1,0:T(8,128)(2,1)S(1)}, bf16[336,512]{1,0:T(8,128)(2,1)S(1)}, u32[]{:S(2)}, u32[]{:S(2)}) collective-permute-start(bf16[336,512]{1,0:T(8,128)(2,1)S(1)} %get-tuple-element.78), channel_id=1, source_target_pairs={{0,2},{2,0},{4,6},{6,4},{8,10},{10,8},{12,14},{14,12},{1,3},{3,1},... | collective-permute-start | bytes 1032200 | tf_op jit(solution)/shard_map/ppermute | solution.py:48
  77.7 10.7 %collective-permute-start.20 = (bf16[336,512]{1,0:T(8,128)(2,1)S(1)}, bf16[336,512]{1,0:T(8,128)(2,1)S(1)}, u32[]{:S(2)}, u32[]{:S(2)}) collective-permute-start(bf16[336,512]{1,0:T(8,128)(2,1)S(1)} %get-tuple-element.79), channel_id=1, source_target_pairs={{0,16},{16,0},{1,17},{17,1},{2,18},{18,2},{3,19},{19,3},{4,20},{20... | collective-permute-start | bytes 1032200 | tf_op jit(solution)/shard_map/ppermute | solution.py:44
  79.2 9.2 %collective-permute-start.21 = (bf16[224,512]{1,0:T(8,128)(2,1)S(1)}, bf16[224,512]{1,0:T(8,128)(2,1)S(1)}, u32[]{:S(2)}, u32[]{:S(2)}) collective-permute-start(bf16[224,512]{1,0:T(8,128)(2,1)S(1)} %get-tuple-element.80), channel_id=1, source_target_pairs={{0,4},{2,6},{4,8},{6,10},{8,12},{10,14},{12,0},{14,2},{1,5},{3,7},... | collective-permute-start | bytes 688136 | tf_op jit(solution)/shard_map/ppermute | solution.py:52
  88.4 3.0 %collective-permute-start.22 = (bf16[2,768,256]{2,1,0:T(8,128)(2,1)S(1)}, bf16[2,768,256]{2,1,0:T(8,128)(2,1)S(1)}, u32[]{:S(2)}, u32[]{:S(2)}) collective-permute-start(bf16[2,768,256]{2,1,0:T(8,128)(2,1)S(1)} %get-tuple-element.81.zm_ref), channel_id=1, source_target_pairs={{0,1},{1,0},{2,3},{3,2},{4,5},{5,4},{6,7},{7,6},{8,9},{9,8},{10,11... | collective-permute-start | bytes 2359304 | tf_op jit(solution)/shard_map/ppermute | solution.py:40
  88.4 3.0 %collective-permute-start.23 = (bf16[512,512]{1,0:T(8,128)(2,1)S(1)}, bf16[512,512]{1,0:T(8,128)(2,1)S(1)}, u32[]{:S(2)}, u32[]{:S(2)}) collective-permute-start(bf16[512,512]{1,0:T(8,128)(2,1)S(1)} %get-tuple-element.82.mixm_ref), channel_id=1, source_target_pairs={{0,1},{1,0},{2,3},{3,2},{4,5},{5,4},{6,7},{7,6},{8,9},{9,8},{10,11... | collective-permute-start | bytes 1572872 | tf_op jit(solution)/shard_map/ppermute | solution.py:40
  97.5 1.6 %collective-permute-start.24 = (bf16[2,256,256]{2,1,0:T(8,128)(2,1)S(1)}, bf16[2,256,256]{2,1,0:T(8,128)(2,1)S(1)}, u32[]{:S(2)}, u32[]{:S(2)}) collective-permute-start(bf16[2,256,256]{2,1,0:T(8,128)(2,1)S(1)} %get-tuple-element.85.zm_ref), channel_id=1, source_target_pairs={{0,1},{1,0},{2,3},{3,2},{4,5},{5,4},{6,7},{7,6},{8,9},{9,8},{10,11... | collective-permute-start | bytes 786440 | tf_op jit(solution)/shard_map/ppermute | solution.py:40

commit v4 on v3

--- a/solution.py
+++ b/solution.py
@@ -69,9 +69,10 @@
         half = (1 - g) if dy else g
         unit = owner * 2 + half
         n_conv = min(conv_rows - skip, count)
-        to = pl.multiple_of(unit * conv_rows + skip, 16)
-        moves.append((refs[index].at[pl.ds(begin, n_conv)], wide.at[pl.ds(to, n_conv)]))
-        if count > n_conv:
+        if wide is not None:
+            to = pl.multiple_of(unit * conv_rows + skip, 16)
+            moves.append((refs[index].at[pl.ds(begin, n_conv)], wide.at[pl.ds(to, n_conv)]))
+        if count > n_conv and mix is not None:
             to = pl.multiple_of(unit * mix_rows, 16)
             moves.append(
                 (refs[index].at[pl.ds(begin + n_conv, mix_rows)], mix.at[pl.ds(to, mix_rows)])
@@ -102,38 +103,57 @@
     ).astype(BF16)
 
 
-def conv0_kernel(cfg, place, gm_ref, gp_ref, *refs):
-    rows, half, branch, blocks, starts, slabs, conv_rows, mix_rows, pairs, n_conv = cfg
-    convs = refs[2 * blocks : 2 * blocks + n_conv]
-    z_ref, mix_ref, wide, hm, hp, acc = refs[2 * blocks + n_conv :]
-    moves = weight_moves(place, convs, conv_rows, mix_rows, pairs, wide, mix_ref)
-    for src, dst in moves:
+def norm_rows(gm, gp, mine, theirs, hm, hp, base):
+    rows, half = mine.shape[1:]
+    step = 64
+
+    def body(i, carry):
+        at = pl.ds(pl.multiple_of(i * step, step), step)
+        to = pl.ds(pl.multiple_of(base + i * step, step), step)
+        xm = mine[0, at, :].astype(F32)
+        dxm = mine[1, at, :].astype(F32)
+        xp = theirs[0, at, :].astype(F32)
+        dxp = theirs[1, at, :].astype(F32)
+        hm[0, to, :], hp[0, to, :], hm[1, to, :], hp[1, to, :] = normalise(
+            xm, xp, dxm, dxp, gm, gp, 2 * half
+        )
+        return carry
+
+    lax.fori_loop(0, rows // step, body, 0)
+
+
+def ready_kernel(cfg, place, gm_ref, gp_ref, *refs):
+    rows, tall, n_blocks, conv_rows, mix_rows, pairs = cfg
+    wide, mix, hm, hp = refs[-4:]
+    convs = refs[2 * n_blocks : -4]
+    for src, dst in weight_moves(place, convs, conv_rows, mix_rows, pairs, wide, mix):
         dst[...] = src[...]
-    gm = gm_ref[0:1, :]
-    gp = gp_ref[0:1, :]
-    step = 64
-    for b in range(blocks):
-        base = (blocks - 1 - b) * rows
-
-        def body(i, carry, b=b, base=base):
-            at = pl.ds(pl.multiple_of(i * step, step), step)
-            to = pl.ds(pl.multiple_of(base + i * step, step), step)
-            xm = refs[b][0, at, :].astype(F32)
-            dxm = refs[b][1, at, :].astype(F32)
-            xp = refs[b + blocks][0, at, :].astype(F32)
-            dxp = refs[b + blocks][1, at, :].astype(F32)
-            hm[0, to, :], hp[0, to, :], hm[1, to, :], hp[1, to, :] = normalise(
-                xm, xp, dxm, dxp, gm, gp, 2 * half
-            )
-            return carry
-
-        lax.fori_loop(0, rows // step, body, 0)
+    for b in range(n_blocks):
+        norm_rows(
+            gm_ref[0:1, :],
+            gp_ref[0:1, :],
+            refs[b],
+            refs[n_blocks + b],
+            hm,
+            hp,
+            tall - (b + 1) * rows,
+        )
+
+
+def place_kernel(cfg, place, *refs):
+    conv_rows, mix_rows, pairs = cfg
+    wide, mix = refs[-2:]
+    for src, dst in weight_moves(place, refs[:-2], conv_rows, mix_rows, pairs, wide, mix):
+        dst[...] = src[...]
+
+
+def conv_slabs(cfg, place, hm, hp, wide, z_ref, acc):
+    rows, half, branch, slabs = cfg
     c = place[2]
     at_m = pl.multiple_of(c * half, half)
     at_p = pl.multiple_of((1 - c) * half, half)
-    for begin, size, lags in slabs:
-        for k in range(TAPS):
-            row = starts[lags + k]
+    for begin, size, taps in slabs:
+        for k, row in enumerate(taps):
             for v in range(2):
                 part = jnp.dot(
                     hm[v, row : row + size, :],
@@ -160,7 +180,20 @@
             )
 
 
-def mix0_kernel(cfg, place, gm_ref, gp_ref, zm_ref, zp_ref, mixm_ref, mixp_ref, *refs):
+def conv0_near_kernel(cfg, weight_cfg, place, hm, hp, *refs):
+    z_ref, wide, mix, acc = refs[-4:]
+    if weight_cfg[2] is not None:
+        for src, dst in weight_moves(place, refs[:-6], *weight_cfg, wide, mix):
+            dst[...] = src[...]
+    conv_slabs(cfg, place, hm, hp, wide, z_ref, acc)
+
+
+def conv0_far_kernel(cfg, place, gm_ref, gp_ref, mine, theirs, wide, _, __, z_ref, hm, hp, acc):
+    norm_rows(gm_ref[0:1, :], gp_ref[0:1, :], mine, theirs, hm, hp, 0)
+    conv_slabs(cfg, place, hm, hp, wide, z_ref, acc)
+
+
+def mix0_kernel(cfg, place, gm_ref, gp_ref, zma, zpa, zmb, zpb, mixm_ref, mixp_ref, *refs):
     rows, half, branch, layer = cfg
     mine = refs[:TAPS]
     theirs = refs[TAPS : 2 * TAPS]
@@ -172,9 +205,9 @@
     gp = gp_ref[layer : layer + 1, :]
     step = min(256, rows)
     for j in range(TAPS):
-        base = (TAPS - 1 - j) * rows
-
-        def body(i, carry, j=j, base=base):
+        zm_ref, zp_ref, base = (zma, zpa, (1 - j) * rows) if j < 2 else (zmb, zpb, 0)
+
+        def body(i, carry, j=j, base=base, zm_ref=zm_ref, zp_ref=zp_ref):
             at = pl.multiple_of(i * step, step)
             to = pl.multiple_of(base + i * step, step)
             new = []
@@ -199,12 +232,8 @@
         lax.fori_loop(0, rows // step, body, 0)
 
 
-def conv1_kernel(cfg, place, hm, hp, *refs):
-    rows, half, branch, conv_rows, mix_rows, pairs, n_conv = cfg
-    convs = refs[:n_conv]
-    z_ref, mix_ref, wide, acc = refs[n_conv:]
-    for src, dst in weight_moves(place, convs, conv_rows, mix_rows, pairs, wide, mix_ref):
-        dst[...] = src[...]
+def conv1_kernel(cfg, place, hm, hp, wide, z_ref, acc):
+    rows, half, branch = cfg
     c = place[2]
     at_m = pl.multiple_of(c * half, half)
     at_p = pl.multiple_of((1 - c) * half, half)
@@ -280,7 +309,7 @@
     )(place, *[near(array) for array in arrays])
 
 
-def exchange(place, own, chunks, gains, seq):
+def exchange(place, own, chunks, gains, seq, ready, newest):
     both = chunks
     unit = both.shape[0] // 2
     tall = own.shape[0]
@@ -342,33 +371,41 @@
     whole(1, z3b, (3, 0, 0))
     keep(0, x3, (0, 0, unit, 2, 1, 0))
     whole(0, y3, (2, 0, 1), (1, 1, 1), (3, 1, 1))
-    to_z, to_x, to_y, one = pack(
+    cut = unit // 2
+    to_z, to_x, w_x, w_y, one = pack(
         seq,
         place,
         [(z3a, 0, unit), (x3, unit, tall, 0)],
         [(z3a, 0, unit), (z3b, 0, unit)],
-        [(z3a, 0, unit), (z3b, 0, unit), (x3, 0, unit)],
+        [(y3, 0, cut)],
+        [(x3, cut, unit - cut)],
         [(x3, unit, tall, 0)],
     )
-    z4, x4, y4 = together(z(to_z), x(to_x), y(to_y))
+    first = ready(gains_p, (own, one, two), pieces[0], (seq, tuple(order[0])))
+    pieces[0].clear()
+    order[0].clear()
+    x4a, y4a = x(w_x), y(w_y)
+    keep(0, x4a, (0, 0, cut, 2, 1, 1))
+    keep(0, y4a, (0, cut, unit - cut, 2, 1, 1))
+    made = newest(first, pieces[0], (seq, tuple(order[0])))
+    to_x = together(to_x, x4a, y4a)[0]
+    z4, x4, y4, made = together(z(to_z), x(to_x), y(to_x), made)
     keep(1, z4, (0, 0, unit, 2, 0, 0))
     whole(1, x4, (1, 1, 0), (3, 1, 0))
     whole(1, y4, (1, 0, 1), (3, 0, 1))
-    keep(0, y4, (2 * unit, 0, unit, 2, 1, 1))
-    cut = unit // 2
     to_z, to_x, to_y, three = pack(
         seq,
         place,
-        [(z3a, unit, unit)],
+        [(z3a, cut, 2 * unit - cut)],
         [(z4, 0, unit), (y4, unit, cut)],
         [(z4, 0, unit), (x4, unit + cut, unit - cut)],
         [(z4, unit, tall, 1)],
     )
     x5, y5, z5 = x(to_x), y(to_y), z(to_z)
-    whole(1, z5, (2, 1, 1))
+    keep(1, z5, (unit - cut, 0, unit, 2, 1, 1))
     keep(1, x5, (0, 0, unit, 2, 1, 0), (unit, 0, cut, 3, 1, 1))
     keep(1, y5, (0, 0, unit, 2, 0, 1), (unit, cut, unit - cut, 3, 1, 1))
-    return gains_p, (one, two, three), (x5, y5, z5), pieces, tuple((seq, tuple(o)) for o in order)
+    return gains_p, (one, two, three), made, (x5, y5, z5), pieces[1], (seq, tuple(order[1]))
 
 
 def on_device(signal, tangent, gains, convolution_kernel, mixing_kernel):
@@ -383,23 +420,24 @@
     place = place.astype(jnp.int32)
     wide_rows, mix_whole = shard * seq, mix_shard * seq
 
-    conv_local = convolution_kernel.reshape(layers, shard, 2 * branch)
     own = jnp.stack([signal, tangent], 0)
     if 2 * lag == rows:
         conv_rows, mix_rows = shard // 2, mix_shard // 2
         g = lax.axis_index("groups")
         chunks = jnp.concatenate(
             [
-                lax.dynamic_slice_in_dim(conv_local, g * conv_rows, conv_rows, 1),
+                lax.dynamic_slice_in_dim(
+                    convolution_kernel, g * conv_rows, conv_rows, 1
+                ).reshape(layers, conv_rows, 2 * branch),
                 lax.dynamic_slice_in_dim(mixing_kernel, g * mix_rows, mix_rows, 1),
             ],
             1,
         ).reshape(layers * (conv_rows + mix_rows), 2 * branch)
-        pairs = None
         step, used = lag, (0, 1, 2)
         blocks = 4
     else:
-        conv_rows, mix_rows, pairs = shard, mix_shard, (None, None)
+        conv_rows, mix_rows = shard, mix_shard
+        conv_local = convolution_kernel.reshape(layers, shard, 2 * branch)
         weights = [
             [
                 lax.all_gather(conv_local[l], "seq", axis=0, tiled=True),
@@ -412,47 +450,94 @@
     tall = blocks * rows
     starts = tuple(tall - rows - m * step for m in range(7))
     if 2 * lag == rows:
-        slabs = ((0, TAPS * rows, 4),)
+        slabs = ((0, 2 * rows, tuple(starts[2 + k] for k in range(TAPS))),)
     else:
-        slabs = tuple(((TAPS - 1 - j) * rows, rows, 2 * j) for j in range(TAPS))
-    slab = slabs[0][1]
-
-    if pairs is None:
-        gains_p, halo, beside, weights, pairs = exchange(
-            place, own.reshape(2 * rows, half), chunks, gains, seq
+        slabs = tuple(
+            ((1 - j) * rows, rows, tuple(starts[2 * j + k] for k in range(TAPS))) for j in range(2)
         )
-        mine = [own, *[block.reshape(own.shape) for block in halo]]
+    far_slabs = ((0, rows, tuple(starts[4 + k] for k in range(TAPS))),)
+
+    mine, theirs = [], []
+
+    def ready(gains_p, halo, pieces, pairs):
+        for block in halo:
+            mine.append(block.reshape(own.shape))
+            theirs.append(swap_chan(mine[-1]))
+        cfg = (rows, tall, len(halo), conv_rows, mix_rows, pairs)
+        return pl.pallas_call(
+            functools.partial(ready_kernel, cfg),
+            out_shape=(
+                near_out(wide_rows, 2 * branch),
+                near_out(mix_whole, half),
+                near_out(2, tall, half),
+                near_out(2, tall, half),
+            ),
+            in_specs=[SMEM] + [VMEM] * (2 + 2 * len(halo) + len(pieces)),
+            out_specs=(VMEM,) * 4,
+            compiler_params=scoped(4),
+            cost_estimate=cost(0, 2**16),
+            name="ready",
+        )(
+            place,
+            near(gains),
+            near(gains_p),
+            *[near(block) for block in (*mine, *theirs)],
+            *[near(piece) for piece in pieces],
+        )
+
+    def newest(made, pieces, pairs):
+        wide, mix, hm, hp = made
+        n_in = 3 + len(pieces)
+        z, wide, mix = pl.pallas_call(
+            functools.partial(
+                conv0_near_kernel, (rows, half, branch, slabs), (conv_rows, mix_rows, pairs)
+            ),
+            out_shape=(
+                near_out(2, 2 * rows, branch),
+                near_out(wide_rows, 2 * branch),
+                near_out(mix_whole, half),
+            ),
+            in_specs=[SMEM] + [VMEM] * (n_in + 1),
+            out_specs=(VMEM,) * 3,
+            input_output_aliases={n_in: 1, n_in + 1: 2},
+            scratch_shapes=[pltpu.VMEM((2, slabs[0][1], 2 * branch), F32)],
+            compiler_params=scoped(12),
+            cost_estimate=cost(0, 2**16),
+            name="conv0_near",
+        )(place, hm, hp, *[near(piece) for piece in pieces], wide, mix)
+        return z, mix, wide, hm, hp
+
+    if 2 * lag == rows:
+        flat = own.reshape(2 * rows, half)
+        gains_p, halo, made, beside, weights1, pairs1 = exchange(
+            place, flat, chunks, gains, seq, ready, newest
+        )
+        last = halo[-1].reshape(own.shape)
     else:
-        beside = ()
         gains_p = swap_chan(gains)
-        mine = [own] + [from_behind(own, seq, k * (lag // rows)) for k in range(1, 7)]
-    theirs = [swap_chan(block) for block in mine]
-
-    n_conv = [len(w) for w in weights]
-    cfg = (rows, half, branch, blocks, starts, slabs, conv_rows, mix_rows, pairs[0], n_conv[0])
-    z_mine, mix_mine = pl.pallas_call(
-        functools.partial(conv0_kernel, cfg),
-        out_shape=(near_out(2, TAPS * rows, branch), near_out(mix_whole, half)),
-        in_specs=[SMEM] + [VMEM] * (2 + 2 * blocks + n_conv[0]),
-        out_specs=(VMEM, VMEM),
-        scratch_shapes=[
-            pltpu.VMEM((wide_rows, 2 * branch), BF16),
-            pltpu.VMEM((2, tall, half), BF16),
-            pltpu.VMEM((2, tall, half), BF16),
-            pltpu.VMEM((2, slab, 2 * branch), F32),
-        ],
-        compiler_params=scoped(20),
-        cost_estimate=cost(0, 32 * 2**20),
-        name="conv0",
-    )(
-        place,
-        near(gains),
-        near(gains_p),
-        *[near(block) for block in (*mine, *theirs)],
-        *[near(w) for w in weights[0]],
-    )
-    z_mine, mix_mine = lax.optimization_barrier((z_mine, mix_mine, *beside))[:2]
-    mix_theirs = swap_chan(mix_mine)
+        halo = [from_behind(own, seq, k * (lag // rows)) for k in range(1, 7)]
+        made = newest(ready(gains_p, (own, *halo[:-1]), weights[0], None), [], None)
+        last, beside, weights1, pairs1 = halo[-1], (), weights[1], None
+    za_mine, mix_mine, wide, hm, hp = made
+    last_theirs, za_theirs, mix_theirs = lax.optimization_barrier(
+        (swap_chan(last), swap_chan(za_mine), swap_chan(mix_mine))
+    )
+
+    z_mine = pl.pallas_call(
+        functools.partial(conv0_far_kernel, (rows, half, branch, far_slabs)),
+        out_shape=(
+            near_out(2, rows, branch),
+            near_out(2, tall, half),
+            near_out(2, tall, half),
+        ),
+        in_specs=[SMEM] + [VMEM] * 7,
+        out_specs=(VMEM,) * 3,
+        input_output_aliases={6: 1, 7: 2},
+        scratch_shapes=[pltpu.VMEM((2, rows, 2 * branch), F32)],
+        compiler_params=scoped(8),
+        cost_estimate=cost(0, 2**16),
+        name="conv0_far",
+    )(place, near(gains), near(gains_p), near(last), near(last_theirs), wide, hm, hp)[0]
     z_theirs = swap_chan(z_mine)
     hm, hp, state = pl.pallas_call(
         functools.partial(mix0_kernel, (rows, half, branch, 1)),
@@ -461,35 +546,43 @@
             near_out(TAPS, 2, rows, half),
             near_out(2, rows, half),
         ),
-        in_specs=[SMEM] + [VMEM] * (6 + 2 * TAPS),
+        in_specs=[SMEM] + [VMEM] * (8 + 2 * TAPS),
         out_specs=(VMEM, VMEM, VMEM),
         compiler_params=scoped(6),
-        cost_estimate=cost(0, 20 * 2**20),
+        cost_estimate=cost(0, 2**16),
         name="mix0",
     )(
         place,
         near(gains),
         near(gains_p),
+        near(za_mine),
+        near(za_theirs),
         z_mine,
         near(z_theirs),
-        mix_mine,
+        near(mix_mine),
         near(mix_theirs),
         *[near(mine[b]) for b in used],
         *[near(theirs[b]) for b in used],
     )
-    cfg = (rows, half, branch, conv_rows, mix_rows, pairs[1], n_conv[1])
-    z_mine, mix_mine = pl.pallas_call(
-        functools.partial(conv1_kernel, cfg),
-        out_shape=(near_out(2, rows, branch), near_out(mix_whole, half)),
-        in_specs=[SMEM] + [VMEM] * (2 + n_conv[1]),
+    hm, hp, *weights1 = lax.optimization_barrier((hm, hp, *weights1))
+    placed = pl.pallas_call(
+        functools.partial(place_kernel, (conv_rows, mix_rows, pairs1)),
+        out_shape=(near_out(wide_rows, 2 * branch), near_out(mix_whole, half)),
+        in_specs=[SMEM] + [VMEM] * len(weights1),
         out_specs=(VMEM, VMEM),
-        scratch_shapes=[
-            pltpu.VMEM((wide_rows, 2 * branch), BF16),
-            pltpu.VMEM((2 * rows, 2 * branch), F32),
-        ],
+        compiler_params=scoped(2),
+        name="place",
+    )(place, *[near(w) for w in weights1])
+    wide, mix_last = placed
+    z_mine = pl.pallas_call(
+        functools.partial(conv1_kernel, (rows, half, branch)),
+        out_shape=near_out(2, rows, branch),
+        in_specs=[SMEM] + [VMEM] * 3,
+        out_specs=VMEM,
+        scratch_shapes=[pltpu.VMEM((2 * rows, 2 * branch), F32)],
         compiler_params=scoped(8),
         name="conv1",
-    )(place, hm, hp, *[near(w) for w in weights[1]])
+    )(place, hm, hp, wide)
     z_theirs = swap_chan(z_mine)
     return pl.pallas_call(
         functools.partial(mix1_kernel, (branch,)),
@@ -501,7 +594,7 @@
         out_specs=(VMEM, VMEM),
         compiler_params=scoped(4),
         name="mix1",
-    )(place, z_mine, near(z_theirs), mix_mine, state)
+    )(place, z_mine, near(z_theirs), mix_last, state)
 
 
 def solution(mesh):

time: 101 us -> 101 us (level)
  waiting for transfers between devices: 56.2 us -> 49.2 us
  starting transfers between devices: 21.8 us -> 26.7 us
  Pallas kernels: 19.2 us -> 21 us
    ppermute x7, starting transfers between devices: 9.22 us -> 12.9 us  [ring(): return lax.ppermute(block, 'seq', [(s, (s + by) % seq) for s in range(seq)])]
    ppermute x7, waiting for transfers between devices: 25.6 us -> 22.1 us  [ring(): return lax.ppermute(block, 'seq', [(s, (s + by) % seq) for s in range(seq)])]
    ppermute x5 -> x6, waiting for transfers between devices: 20.6 us -> 17.2 us  [swap_pair(): return lax.ppermute(block, 'seq', [(s, s ^ 1) for s in range(seq)])]
    reshape x1, local copies, waits for them, and re-layouts: 2.48 us -> 0.25 us  [on_device(): chunks = jnp.concatenate([lax.dynamic_slice_in_dim(convolution_kernel, g...]
    pallas_call x2 -> x5, Pallas kernels: 11.2 us -> 13 us  [the longest x1 4.02 us: newest(): pl.pallas_call(functools.partial(conv0_near_kernel, (rows, half, branch,...]
    unnamed x8, local copies, waits for them, and re-layouts: 0.03 us -> 1.12 us
    ppermute x5 -> x6, starting transfers between devices: 6.38 us -> 7.43 us  [swap_groups(): return lax.ppermute(block, 'groups', [(0, 1), (1, 0)])]
    ppermute x8 -> x9, waiting for transfers between devices: 5.11 us -> 4.22 us  [swap_chan(): return lax.ppermute(block, 'chan', [(0, 1), (1, 0)])]
  transfers between devices with their start and end apart: 25 -> 28, of which waited for: 14 -> 15; matrix products, arithmetic and copies ran while one was open for 0% -> 1% of each run, Pallas kernels for 9% -> 15%
where the time goes in v4:
time: 101 us
  waiting for transfers between devices  49.2 us (49%)
  starting transfers between devices  26.7 us (26%)
  Pallas kernels  21 us (21%)
  local copies, waits for them, and re-layouts  2.5 us (2%)
    ppermute x7, waiting for transfers between devices, ring(): return lax.ppermute(block, 'seq', [(s, (s + by) % seq) for s in range(seq)])  22.1 us
    ppermute x6, waiting for transfers between devices, swap_pair(): return lax.ppermute(block, 'seq', [(s, s ^ 1) for s in range(seq)])  17.2 us
    ppermute x7, starting transfers between devices, ring(): return lax.ppermute(block, 'seq', [(s, (s + by) % seq) for s in range(seq)])  12.9 us
    ppermute x6, starting transfers between devices, swap_groups(): return lax.ppermute(block, 'groups', [(0, 1), (1, 0)])  7.43 us
    ppermute x6, starting transfers between devices, swap_pair(): return lax.ppermute(block, 'seq', [(s, s ^ 1) for s in range(seq)])  5.69 us
    ppermute x6, waiting for transfers between devices, swap_groups(): return lax.ppermute(block, 'groups', [(0, 1), (1, 0)])  5.65 us
    ppermute x9, waiting for transfers between devices, swap_chan(): return lax.ppermute(block, 'chan', [(0, 1), (1, 0)])  4.22 us
    pallas_call x1, Pallas kernels, newest(): pl.pallas_call(functools.partial(conv0_near_kernel, (rows, half, branch,...  4.02 us
  transfers between devices with their start and end apart: 28, of which 15 were waited for; matrix products, arithmetic and copies ran while one was open for 1% of the time, Pallas kernels for 15%

profile of v4, /device:TPU:0, one launch (start us, length us, event | category | flops | bytes accessed | tf_op | source)
XLA Modules:
  0.0 101.1 jit_solution(16161294412073392897)
XLA Ops:
  0.7 1.1 %copy-done = bf16[2,384,2,256]{3,2,1,0:T(2,128)(2,1)S(1)} copy-done((bf16[2,384,2,256]{3,2,1,0:T(2,128)(2,1)S(1)}, bf16[2,384,2,256]{3,2,1,0:T(2,128)(2,1)}, u32[]{:S(2)}) %copy-start) | copy-done | bytes 786456
  1.8 0.3 constant_dynamic-slice_fusion.1
  2.0 0.3 reshape.27
  2.3 0.9 constant_dynamic-slice_fusion
  3.2 3.0 %collective-permute-start.3 = (bf16[448,512]{1,0:T(8,128)(2,1)S(1)}, bf16[448,512]{1,0:T(8,128)(2,1)S(1)}, u32[]{:S(2)}, u32[]{:S(2)}) collective-permute-start(bf16[448,512]{1,0:T(8,128)(2,1)S(1)} %bitcast.17), channel_id=1, source_target_pairs={{0,16},{16,0},{1,17},{17,1},{2,18},{18,2},{3,19},{19,3},{4,20},{20... | collective-permute-start | bytes 1376264 | tf_op jit(solution)/shard_map/ppermute | solution.py:44
  6.2 1.5 %collective-permute-start.2 = (bf16[448,512]{1,0:T(8,128)(2,1)S(1)}, bf16[448,512]{1,0:T(8,128)(2,1)S(1)}, u32[]{:S(2)}, u32[]{:S(2)}) collective-permute-start(bf16[448,512]{1,0:T(8,128)(2,1)S(1)} %bitcast.18), channel_id=1, source_target_pairs={{0,2},{2,0},{4,6},{6,4},{8,10},{10,8},{12,14},{14,12},{1,3},{3,1},... | collective-permute-start | bytes 1376264 | tf_op jit(solution)/shard_map/ppermute | solution.py:48
  7.7 0.7 fusion.3
  8.4 3.6 %collective-permute-start.1 = (bf16[224,512]{1,0:T(8,128)(2,1)}, bf16[224,512]{1,0:T(8,128)(2,1)S(1)}, u32[]{:S(2)}, u32[]{:S(2)}) collective-permute-start(bf16[224,512]{1,0:T(8,128)(2,1)} %get-tuple-element.145), channel_id=1, source_target_pairs={{0,12},{2,14},{4,0},{6,2},{8,4},{10,6},{12,8},{14,10},{1,13},{3,15... | collective-permute-start | bytes 688136 | tf_op jit(solution)/shard_map/ppermute | solution.py:52
  12.2 6.2 %collective-permute-done.1.refs_2_.refs_8_ = bf16[224,512]{1,0:T(8,128)(2,1)S(1)} collective-permute-done((bf16[224,512]{1,0:T(8,128)(2,1)}, bf16[224,512]{1,0:T(8,128)(2,1)S(1)}, u32[]{:S(2)}, u32[]{:S(2)}) %collective-permute-start.1) | collective-permute-done | bytes 229408 | tf_op jit(solution)/shard_map/ppermute | solution.py:52
  18.4 4.0 %collective-permute-done.refs_0_.refs_7_ = bf16[224,512]{1,0:T(8,128)(2,1)S(1)} collective-permute-done((bf16[224,512]{1,0:T(8,128)(2,1)}, bf16[224,512]{1,0:T(8,128)(2,1)S(1)}, u32[]{:S(2)}, u32[]{:S(2)}) %collective-permute-start) | collective-permute-done | bytes 229408 | tf_op jit(solution)/shard_map/ppermute | solution.py:52
  22.4 0.7 pack.4
  23.1 1.7 %collective-permute-start.4 = (bf16[736,512]{1,0:T(8,128)(2,1)S(1)}, bf16[736,512]{1,0:T(8,128)(2,1)S(1)}, u32[]{:S(2)}, u32[]{:S(2)}) collective-permute-start(bf16[736,512]{1,0:T(8,128)(2,1)S(1)} %get-tuple-element.78), channel_id=1, source_target_pairs={{0,4},{2,6},{4,8},{6,10},{8,12},{10,14},{12,0},{14,2},{1,5},{3,7},... | collective-permute-start | bytes 2261000 | tf_op jit(solution)/shard_map/ppermute | solution.py:52
  24.8 0.5 collective-permute-start.5
  25.3 0.5 collective-permute-start.6
  25.8 1.2 %collective-permute-done.7.gp_ref = f32[2,512]{1,0:T(2,128)S(1)} collective-permute-done((f32[2,512]{1,0:T(2,128)S(1)}, f32[2,512]{1,0:T(2,128)S(1)}, u32[]{:S(2)}, u32[]{:S(2)}) %collective-permute-start.7) | collective-permute-done | bytes 4128 | tf_op jit(solution)/shard_map/ppermute | solution.py:40
  27.0 13.2 %collective-permute-done.5.refs_1_.refs_12_.refs_3_ = bf16[672,512]{1,0:T(8,128)(2,1)S(1)} collective-permute-done((bf16[672,512]{1,0:T(8,128)(2,1)S(1)}, bf16[672,512]{1,0:T(8,128)(2,1)S(1)}, u32[]{:S(2)}, u32[]{:S(2)}) %collective-permute-start.5) | collective-permute-done | bytes 688160 | tf_op jit(solution)/shard_map/ppermute | solution.py:48
  40.2 0.3 collective-permute-done.6.refs_13_
  40.5 1.6 %collective-permute-done.4.refs_2_.refs_11_ = bf16[736,512]{1,0:T(8,128)(2,1)S(1)} collective-permute-done((bf16[736,512]{1,0:T(8,128)(2,1)S(1)}, bf16[736,512]{1,0:T(8,128)(2,1)S(1)}, u32[]{:S(2)}, u32[]{:S(2)}) %collective-permute-start.4) | collective-permute-done | bytes 753696 | tf_op jit(solution)/shard_map/ppermute | solution.py:52
  42.0 0.8 pack.5
  42.8 0.6 collective-permute-start.10
  43.4 0.5 collective-permute-start.11
  43.9 3.8 %collective-permute-start.9 = (bf16[224,512]{1,0:T(8,128)(2,1)S(1)}, bf16[224,512]{1,0:T(8,128)(2,1)S(1)}, u32[]{:S(2)}, u32[]{:S(2)}) collective-permute-start(bf16[224,512]{1,0:T(8,128)(2,1)S(1)} %get-tuple-element.87), channel_id=1, source_target_pairs={{0,12},{2,14},{4,0},{6,2},{8,4},{10,6},{12,8},{14,10},{1,13},{3,15... | collective-permute-start | bytes 688136 | tf_op jit(solution)/shard_map/ppermute | solution.py:52
  47.7 10.4 %collective-permute-done.9.refs_2_.refs_5_ = bf16[224,512]{1,0:T(8,128)(2,1)S(1)} collective-permute-done((bf16[224,512]{1,0:T(8,128)(2,1)S(1)}, bf16[224,512]{1,0:T(8,128)(2,1)S(1)}, u32[]{:S(2)}, u32[]{:S(2)}) %collective-permute-start.9) | collective-permute-done | bytes 229408 | tf_op jit(solution)/shard_map/ppermute | solution.py:52
  58.1 0.9 collective-permute-done.10.refs_1_.refs_14_
  59.0 0.7 pack.6
  59.8 0.8 collective-permute-start.13
  60.6 1.5 %collective-permute-start.14 = (bf16[112,512]{1,0:T(8,128)(2,1)S(1)}, bf16[112,512]{1,0:T(8,128)(2,1)S(1)}, u32[]{:S(2)}, u32[]{:S(2)}) collective-permute-start(bf16[112,512]{1,0:T(8,128)(2,1)S(1)} %get-tuple-element.97), channel_id=1, source_target_pairs={{0,16},{16,0},{1,17},{17,1},{2,18},{18,2},{3,19},{19,3},{4,20},{20... | collective-permute-start | bytes 344072 | tf_op jit(solution)/shard_map/ppermute | solution.py:44
  62.1 2.5 %collective-permute-done.13.refs_0_ = bf16[112,512]{1,0:T(8,128)(2,1)S(1)} collective-permute-done((bf16[112,512]{1,0:T(8,128)(2,1)S(1)}, bf16[112,512]{1,0:T(8,128)(2,1)S(1)}, u32[]{:S(2)}, u32[]{:S(2)}) %collective-permute-start.13) | collective-permute-done | bytes 114720 | tf_op jit(solution)/shard_map/ppermute | solution.py:48
  64.7 0.7 collective-permute-done.14.refs_1_
  65.4 1.5 %collective-permute-start.16 = (bf16[448,512]{1,0:T(8,128)(2,1)S(1)}, bf16[448,512]{1,0:T(8,128)(2,1)S(1)}, u32[]{:S(2)}, u32[]{:S(2)}) collective-permute-start(bf16[448,512]{1,0:T(8,128)(2,1)S(1)} %get-tuple-element.98), channel_id=1, source_target_pairs={{0,16},{16,0},{1,17},{17,1},{2,18},{18,2},{3,19},{19,3},{4,20},{20... | collective-permute-start | bytes 1376264 | tf_op jit(solution)/shard_map/ppermute | solution.py:44
  66.9 0.5 collective-permute-start.15
  67.5 2.8 %ready.1 = (bf16[3072,512]{1,0:T(8,128)(2,1)S(1)}, bf16[512,512]{1,0:T(8,128)(2,1)S(1)}, bf16[2,1024,512]{2,1,0:T(8,128)(2,1)S(1)}, bf16[2,1024,512]{2,1,0:T(8,128)(2,1)S(1)}) custom-call(s32[3]{0:T(128)S(1)} %pad_add_fusion.place_ref.place, f32[2,512]{1,0:T(2,128)S(1)} %copy-done.1, f32[2,512]{1,0:T(2,128)S(1)} %collective-permute-done.7.gp_ref, ...), custom_call_target="tpu_custom_call" | custom-call | bytes 65536 | tf_op jit(solution)/shard_map/ready/pallas_call | solution.py:467
  70.3 4.0 %conv0_near.1 = (bf16[2,512,256]{2,1,0:T(8,128)(2,1)S(1)}, bf16[3072,512]{1,0:T(8,128)(2,1)S(1)}, bf16[512,512]{1,0:T(8,128)(2,1)S(1)}) custom-call(s32[3]{0:T(128)S(1)} %pad_add_fusion.place_ref.place, bf16[2,1024,512]{2,1,0:T(8,128)(2,1)S(1)} %get-tuple-element.118.hm._, ...), custom_call_target="tpu_custom_call", output_to_operand_aliasing={{1}: (5, {}), {2}: (6, {})} | custom-call | bytes 65536 | tf_op jit(solution)/shard_map/conv0_near/pallas_call | solution.py:491
  74.3 3.3 %collective-permute-done.16.refs_2_.refs_8_ = bf16[448,512]{1,0:T(8,128)(2,1)S(1)} collective-permute-done((bf16[448,512]{1,0:T(8,128)(2,1)S(1)}, bf16[448,512]{1,0:T(8,128)(2,1)S(1)}, u32[]{:S(2)}, u32[]{:S(2)}) %collective-permute-start.16) | collective-permute-done | bytes 458784 | tf_op jit(solution)/shard_map/ppermute | solution.py:44
  77.6 0.5 collective-permute-done.15.refs_3_.refs_7_
  78.1 0.5 collective-permute-start.22
  78.6 0.7 pack.7
  79.4 3.7 %collective-permute-start.24 = (bf16[336,512]{1,0:T(8,128)(2,1)S(1)}, bf16[336,512]{1,0:T(8,128)(2,1)S(1)}, u32[]{:S(2)}, u32[]{:S(2)}) collective-permute-start(bf16[336,512]{1,0:T(8,128)(2,1)S(1)} %get-tuple-element.124), channel_id=1, source_target_pairs={{0,4},{2,6},{4,8},{6,10},{8,12},{10,14},{12,0},{14,2},{1,5},{3,7},... | collective-permute-start | bytes 1032200 | tf_op jit(solution)/shard_map/ppermute | solution.py:52
  83.1 1.7 %collective-permute-start.25 = (bf16[336,512]{1,0:T(8,128)(2,1)S(1)}, bf16[336,512]{1,0:T(8,128)(2,1)S(1)}, u32[]{:S(2)}, u32[]{:S(2)}) collective-permute-start(bf16[336,512]{1,0:T(8,128)(2,1)S(1)} %get-tuple-element.125), channel_id=1, source_target_pairs={{0,2},{2,0},{4,6},{6,4},{8,10},{10,8},{12,14},{14,12},{1,3},{3,1},... | collective-permute-start | bytes 1032200 | tf_op jit(solution)/shard_map/ppermute | solution.py:48
  84.8 0.3 collective-permute-start.26
  85.2 3.0 %conv0_far.1 = (bf16[2,256,256]{2,1,0:T(8,128)(2,1)S(1)}, bf16[2,1024,512]{2,1,0:T(8,128)(2,1)S(1)}, bf16[2,1024,512]{2,1,0:T(8,128)(2,1)S(1)}) custom-call(s32[3]{0:T(128)S(1)} %pad_add_fusion.place_ref.place, f32[2,512]{1,0:T(2,128)S(1)} %copy-done.1, f32[2,512]{1,0:T(2,128)S(1)} %collective-permute-done.7.gp_ref, ...), custom_call_target="tpu_custom_call", output_to_operand_aliasing={{1}: (6, {}), {2}: (7, {})} | custom-call | bytes 65536 | tf_op jit(solution)/shard_map/conv0_far/pallas_call | solution.py:526
  88.3 1.5 %collective-permute-done.23.zpb = bf16[2,256,256]{2,1,0:T(8,128)(2,1)S(1)} collective-permute-done((bf16[2,256,256]{2,1,0:T(8,128)(2,1)S(1)}, bf16[2,256,256]{2,1,0:T(8,128)(2,1)S(1)}, u32[]{:S(2)}, u32[]{:S(2)}) %collective-permute-start.23) | collective-permute-done | bytes 262176 | tf_op jit(solution)/shard_map/ppermute | solution.py:40
  89.8 3.5 %mix0.1 = (bf16[3,2,256,512]{3,2,1,0:T(8,128)(2,1)S(1)}, bf16[3,2,256,512]{3,2,1,0:T(8,128)(2,1)S(1)}, bf16[2,256,512]{2,1,0:T(8,128)(2,1)S(1)}) custom-call(s32[3]{0:T(128)S(1)} %pad_add_fusion.place_ref.place, f32[2,512]{1,0:T(2,128)S(1)} %copy-done.1, f32[2,512]{1,0:T(2,128)S(1)} %collective-permute-done.7.gp_ref, ...), custom_call_target="tpu_custom_call" | custom-call | bytes 65536 | tf_op jit(solution)/shard_map/mix0/pallas_call | solution.py:542
  93.3 1.4 %collective-permute-done.26.refs_11_ = bf16[336,512]{1,0:T(8,128)(2,1)S(1)} collective-permute-done((bf16[336,512]{1,0:T(8,128)(2,1)S(1)}, bf16[336,512]{1,0:T(8,128)(2,1)S(1)}, u32[]{:S(2)}, u32[]{:S(2)}) %collective-permute-start.26) | collective-permute-done | bytes 344096 | tf_op jit(solution)/shard_map/ppermute | solution.py:44
  94.7 0.8 place.1
  95.5 2.3 %conv1.1.zm_ref = bf16[2,256,256]{2,1,0:T(8,128)(2,1)S(1)} custom-call(s32[3]{0:T(128)S(1)} %pad_add_fusion.place_ref.place, bf16[3,2,256,512]{3,2,1,0:T(8,128)(2,1)S(1)} %get-tuple-element.127.hm, bf16[3,2,256,512]{3,2,1,0:T(8,128)(2,1)S(1)} %get-tuple-element.128.hp, bf16[3072,512]{1,0:T(8,128)(2,1)S(1)} %get-tuple-element.141.wide), custom_call_target="tpu_custom_call" | custom-call | tf_op jit(solution)/shard_map/conv1/pallas_call | solution.py:577
  97.9 1.5 %collective-permute-done.27.zp_ref = bf16[2,256,256]{2,1,0:T(8,128)(2,1)S(1)} collective-permute-done((bf16[2,256,256]{2,1,0:T(8,128)(2,1)S(1)}, bf16[2,256,256]{2,1,0:T(8,128)(2,1)S(1)}, u32[]{:S(2)}, u32[]{:S(2)}) %collective-permute-start.27) | collective-permute-done | bytes 262176 | tf_op jit(solution)/shard_map/ppermute | solution.py:40
  99.4 1.7 %mix1.1 = (bf16[256,512]{1,0:T(8,128)(2,1)}, bf16[256,512]{1,0:T(8,128)(2,1)}) custom-call(s32[3]{0:T(128)S(1)} %pad_add_fusion.place_ref.place, bf16[2,256,256]{2,1,0:T(8,128)(2,1)S(1)} %conv1.1.zm_ref, bf16[2,256,256]{2,1,0:T(8,128)(2,1)S(1)} %collective-permute-done.27.zp_ref, bf16[512,512]{1,0:T(8,128)(2,1)S(1)} %get-tuple-element.142.mix_ref, ...), custom_call_target="tpu_custom_call" | custom-call | tf_op jit(solution)/shard_map/mix1/pallas_call | solution.py:587
  (34 shorter events, 0.5 us)
Async XLA Ops:
  0.6 1.1 %copy-start = (bf16[2,384,2,256]{3,2,1,0:T(2,128)(2,1)S(1)}, bf16[2,384,2,256]{3,2,1,0:T(2,128)(2,1)}, u32[]{:S(2)}) copy-start(bf16[2,384,2,256]{3,2,1,0:T(2,128)(2,1)} %param.8) | copy-start | bytes 2359300
  0.6 11.5 %copy-start.2 = (bf16[256,512]{1,0:T(8,128)(2,1)S(1)}, bf16[256,512]{1,0:T(8,128)(2,1)}, u32[]{:S(2)}) copy-start(bf16[256,512]{1,0:T(8,128)(2,1)} %param.6) | copy-start | bytes 786436
  0.7 11.5 %copy-start.3 = (bf16[256,512]{1,0:T(8,128)(2,1)S(1)}, bf16[256,512]{1,0:T(8,128)(2,1)}, u32[]{:S(2)}) copy-start(bf16[256,512]{1,0:T(8,128)(2,1)} %param.5) | copy-start | bytes 786436
  3.2 22.6 %copy-start.1 = (f32[2,512]{1,0:T(2,128)S(1)}, f32[2,512]{1,0:T(2,128)}, u32[]{:S(2)}) copy-start(f32[2,512]{1,0:T(2,128)} %gm_ref.5) | copy-start | bytes 12292
  3.2 19.2 %collective-permute-start.3 = (bf16[448,512]{1,0:T(8,128)(2,1)S(1)}, bf16[448,512]{1,0:T(8,128)(2,1)S(1)}, u32[]{:S(2)}, u32[]{:S(2)}) collective-permute-start(bf16[448,512]{1,0:T(8,128)(2,1)S(1)} %bitcast.17), channel_id=1, source_target_pairs={{0,16},{16,0},{1,17},{17,1},{2,18},{18,2},{3,19},{19,3},{4,20},{20... | collective-permute-start | bytes 1376264 | tf_op jit(solution)/shard_map/ppermute | solution.py:44
  6.2 16.2 %collective-permute-start.2 = (bf16[448,512]{1,0:T(8,128)(2,1)S(1)}, bf16[448,512]{1,0:T(8,128)(2,1)S(1)}, u32[]{:S(2)}, u32[]{:S(2)}) collective-permute-start(bf16[448,512]{1,0:T(8,128)(2,1)S(1)} %bitcast.18), channel_id=1, source_target_pairs={{0,2},{2,0},{4,6},{6,4},{8,10},{10,8},{12,14},{14,12},{1,3},{3,1},... | collective-permute-start | bytes 1376264 | tf_op jit(solution)/shard_map/ppermute | solution.py:48
  8.4 10.0 %collective-permute-start.1 = (bf16[224,512]{1,0:T(8,128)(2,1)}, bf16[224,512]{1,0:T(8,128)(2,1)S(1)}, u32[]{:S(2)}, u32[]{:S(2)}) collective-permute-start(bf16[224,512]{1,0:T(8,128)(2,1)} %get-tuple-element.145), channel_id=1, source_target_pairs={{0,12},{2,14},{4,0},{6,2},{8,4},{10,6},{12,8},{14,10},{1,13},{3,15... | collective-permute-start | bytes 688136 | tf_op jit(solution)/shard_map/ppermute | solution.py:52
  12.0 10.3 %collective-permute-start = (bf16[224,512]{1,0:T(8,128)(2,1)}, bf16[224,512]{1,0:T(8,128)(2,1)S(1)}, u32[]{:S(2)}, u32[]{:S(2)}) collective-permute-start(bf16[224,512]{1,0:T(8,128)(2,1)} %get-tuple-element.145), channel_id=1, source_target_pairs={{0,4},{2,6},{4,8},{6,10},{8,12},{10,14},{12,0},{14,2},{1,5},{3,7},... | collective-permute-start | bytes 688136 | tf_op jit(solution)/shard_map/ppermute | solution.py:52
  23.1 18.9 %collective-permute-start.4 = (bf16[736,512]{1,0:T(8,128)(2,1)S(1)}, bf16[736,512]{1,0:T(8,128)(2,1)S(1)}, u32[]{:S(2)}, u32[]{:S(2)}) collective-permute-start(bf16[736,512]{1,0:T(8,128)(2,1)S(1)} %get-tuple-element.78), channel_id=1, source_target_pairs={{0,4},{2,6},{4,8},{6,10},{8,12},{10,14},{12,0},{14,2},{1,5},{3,7},... | collective-permute-start | bytes 2261000 | tf_op jit(solution)/shard_map/ppermute | solution.py:52
  24.8 15.5 %collective-permute-start.5 = (bf16[672,512]{1,0:T(8,128)(2,1)S(1)}, bf16[672,512]{1,0:T(8,128)(2,1)S(1)}, u32[]{:S(2)}, u32[]{:S(2)}) collective-permute-start(bf16[672,512]{1,0:T(8,128)(2,1)S(1)} %get-tuple-element.79), channel_id=1, source_target_pairs={{0,2},{2,0},{4,6},{6,4},{8,10},{10,8},{12,14},{14,12},{1,3},{3,1},... | collective-permute-start | bytes 2064392 | tf_op jit(solution)/shard_map/ppermute | solution.py:48
  25.3 15.2 %collective-permute-start.6 = (bf16[672,512]{1,0:T(8,128)(2,1)S(1)}, bf16[672,512]{1,0:T(8,128)(2,1)S(1)}, u32[]{:S(2)}, u32[]{:S(2)}) collective-permute-start(bf16[672,512]{1,0:T(8,128)(2,1)S(1)} %get-tuple-element.80), channel_id=1, source_target_pairs={{0,16},{16,0},{1,17},{17,1},{2,18},{18,2},{3,19},{19,3},{4,20},{20... | collective-permute-start | bytes 2064392 | tf_op jit(solution)/shard_map/ppermute | solution.py:44
  25.8 1.2 %collective-permute-start.7 = (f32[2,512]{1,0:T(2,128)S(1)}, f32[2,512]{1,0:T(2,128)S(1)}, u32[]{:S(2)}, u32[]{:S(2)}) collective-permute-start(f32[2,512]{1,0:T(2,128)S(1)} %copy-done.1), channel_id=1, source_target_pairs={{0,1},{1,0},{2,3},{3,2},{4,5},{5,4},{6,7},{7,6},{8,9},{9,8},{10,11... | collective-permute-start | bytes 12296 | tf_op jit(solution)/shard_map/ppermute | solution.py:40
  42.8 16.2 %collective-permute-start.10 = (bf16[736,512]{1,0:T(8,128)(2,1)S(1)}, bf16[736,512]{1,0:T(8,128)(2,1)S(1)}, u32[]{:S(2)}, u32[]{:S(2)}) collective-permute-start(bf16[736,512]{1,0:T(8,128)(2,1)S(1)} %get-tuple-element.88), channel_id=1, source_target_pairs={{0,2},{2,0},{4,6},{6,4},{8,10},{10,8},{12,14},{14,12},{1,3},{3,1},... | collective-permute-start | bytes 2261000 | tf_op jit(solution)/shard_map/ppermute | solution.py:48
  43.4 14.7 %collective-permute-start.11 = (bf16[672,512]{1,0:T(8,128)(2,1)S(1)}, bf16[672,512]{1,0:T(8,128)(2,1)S(1)}, u32[]{:S(2)}, u32[]{:S(2)}) collective-permute-start(bf16[672,512]{1,0:T(8,128)(2,1)S(1)} %get-tuple-element.89), channel_id=1, source_target_pairs={{0,16},{16,0},{1,17},{17,1},{2,18},{18,2},{3,19},{19,3},{4,20},{20... | collective-permute-start | bytes 2064392 | tf_op jit(solution)/shard_map/ppermute | solution.py:44
  43.9 14.2 %collective-permute-start.8 = (bf16[448,512]{1,0:T(8,128)(2,1)S(1)}, bf16[448,512]{1,0:T(8,128)(2,1)S(1)}, u32[]{:S(2)}, u32[]{:S(2)}) collective-permute-start(bf16[448,512]{1,0:T(8,128)(2,1)S(1)} %get-tuple-element.86), channel_id=1, source_target_pairs={{0,4},{2,6},{4,8},{6,10},{8,12},{10,14},{12,0},{14,2},{1,5},{3,7},... | collective-permute-start | bytes 1376264 | tf_op jit(solution)/shard_map/ppermute | solution.py:52
  43.9 14.2 %collective-permute-start.9 = (bf16[224,512]{1,0:T(8,128)(2,1)S(1)}, bf16[224,512]{1,0:T(8,128)(2,1)S(1)}, u32[]{:S(2)}, u32[]{:S(2)}) collective-permute-start(bf16[224,512]{1,0:T(8,128)(2,1)S(1)} %get-tuple-element.87), channel_id=1, source_target_pairs={{0,12},{2,14},{4,0},{6,2},{8,4},{10,6},{12,8},{14,10},{1,13},{3,15... | collective-permute-start | bytes 688136 | tf_op jit(solution)/shard_map/ppermute | solution.py:52
  47.7 19.2 %collective-permute-start.17 = (bf16[2,256,512]{2,1,0:T(8,128)(2,1)S(1)}, bf16[2,256,512]{2,1,0:T(8,128)(2,1)S(1)}, u32[]{:S(2)}, u32[]{:S(2)}) collective-permute-start(bf16[2,256,512]{2,1,0:T(8,128)(2,1)S(1)} %pad_maximum_fusion.1), channel_id=1, source_target_pairs={{0,1},{1,0},{2,3},{3,2},{4,5},{5,4},{6,7},{7,6},{8,9},{9,8},{10,11... | collective-permute-start | bytes 1572872 | tf_op jit(solution)/shard_map/ppermute | solution.py:40
  59.8 18.3 %collective-permute-start.12 = (bf16[736,512]{1,0:T(8,128)(2,1)S(1)}, bf16[736,512]{1,0:T(8,128)(2,1)S(1)}, u32[]{:S(2)}, u32[]{:S(2)}) collective-permute-start(bf16[736,512]{1,0:T(8,128)(2,1)S(1)} %get-tuple-element.94), channel_id=1, source_target_pairs={{0,4},{2,6},{4,8},{6,10},{8,12},{10,14},{12,0},{14,2},{1,5},{3,7},... | collective-permute-start | bytes 2261000 | tf_op jit(solution)/shard_map/ppermute | solution.py:52
  59.8 4.9 %collective-permute-start.13 = (bf16[112,512]{1,0:T(8,128)(2,1)S(1)}, bf16[112,512]{1,0:T(8,128)(2,1)S(1)}, u32[]{:S(2)}, u32[]{:S(2)}) collective-permute-start(bf16[112,512]{1,0:T(8,128)(2,1)S(1)} %get-tuple-element.96), channel_id=1, source_target_pairs={{0,2},{2,0},{4,6},{6,4},{8,10},{10,8},{12,14},{14,12},{1,3},{3,1},... | collective-permute-start | bytes 344072 | tf_op jit(solution)/shard_map/ppermute | solution.py:48
  60.6 4.8 %collective-permute-start.14 = (bf16[112,512]{1,0:T(8,128)(2,1)S(1)}, bf16[112,512]{1,0:T(8,128)(2,1)S(1)}, u32[]{:S(2)}, u32[]{:S(2)}) collective-permute-start(bf16[112,512]{1,0:T(8,128)(2,1)S(1)} %get-tuple-element.97), channel_id=1, source_target_pairs={{0,16},{16,0},{1,17},{17,1},{2,18},{18,2},{3,19},{19,3},{4,20},{20... | collective-permute-start | bytes 344072 | tf_op jit(solution)/shard_map/ppermute | solution.py:44
  62.1 5.3 %collective-permute-start.19 = (bf16[2,256,512]{2,1,0:T(8,128)(2,1)S(1)}, bf16[2,256,512]{2,1,0:T(8,128)(2,1)S(1)}, u32[]{:S(2)}, u32[]{:S(2)}) collective-permute-start(bf16[2,256,512]{2,1,0:T(8,128)(2,1)S(1)} %bitcast.22), channel_id=1, source_target_pairs={{0,1},{1,0},{2,3},{3,2},{4,5},{5,4},{6,7},{7,6},{8,9},{9,8},{10,11... | collective-permute-start | bytes 1572872 | tf_op jit(solution)/shard_map/ppermute | solution.py:40
  64.7 2.8 %collective-permute-start.18 = (bf16[2,256,512]{2,1,0:T(8,128)(2,1)S(1)}, bf16[2,256,512]{2,1,0:T(8,128)(2,1)S(1)}, u32[]{:S(2)}, u32[]{:S(2)}) collective-permute-start(bf16[2,256,512]{2,1,0:T(8,128)(2,1)S(1)} %bitcast.25), channel_id=1, source_target_pairs={{0,1},{1,0},{2,3},{3,2},{4,5},{5,4},{6,7},{7,6},{8,9},{9,8},{10,11... | collective-permute-start | bytes 1572872 | tf_op jit(solution)/shard_map/ppermute | solution.py:40
  65.4 12.2 %collective-permute-start.16 = (bf16[448,512]{1,0:T(8,128)(2,1)S(1)}, bf16[448,512]{1,0:T(8,128)(2,1)S(1)}, u32[]{:S(2)}, u32[]{:S(2)}) collective-permute-start(bf16[448,512]{1,0:T(8,128)(2,1)S(1)} %get-tuple-element.98), channel_id=1, source_target_pairs={{0,16},{16,0},{1,17},{17,1},{2,18},{18,2},{3,19},{19,3},{4,20},{20... | collective-permute-start | bytes 1376264 | tf_op jit(solution)/shard_map/ppermute | solution.py:44
  66.9 11.2 %collective-permute-start.15 = (bf16[448,512]{1,0:T(8,128)(2,1)S(1)}, bf16[448,512]{1,0:T(8,128)(2,1)S(1)}, u32[]{:S(2)}, u32[]{:S(2)}) collective-permute-start(bf16[448,512]{1,0:T(8,128)(2,1)S(1)} %get-tuple-element.98), channel_id=1, source_target_pairs={{0,2},{2,0},{4,6},{6,4},{8,10},{10,8},{12,14},{14,12},{1,3},{3,1},... | collective-permute-start | bytes 1376264 | tf_op jit(solution)/shard_map/ppermute | solution.py:48
  78.1 6.7 %collective-permute-start.21 = (bf16[2,512,256]{2,1,0:T(8,128)(2,1)S(1)}, bf16[2,512,256]{2,1,0:T(8,128)(2,1)S(1)}, u32[]{:S(2)}, u32[]{:S(2)}) collective-permute-start(bf16[2,512,256]{2,1,0:T(8,128)(2,1)S(1)} %get-tuple-element.109.zma), channel_id=1, source_target_pairs={{0,1},{1,0},{2,3},{3,2},{4,5},{5,4},{6,7},{7,6},{8,9},{9,8},{10,11... | collective-permute-start | bytes 1572872 | tf_op jit(solution)/shard_map/ppermute | solution.py:40
  78.1 7.1 %collective-permute-start.22 = (bf16[512,512]{1,0:T(8,128)(2,1)S(1)}, bf16[512,512]{1,0:T(8,128)(2,1)S(1)}, u32[]{:S(2)}, u32[]{:S(2)}) collective-permute-start(bf16[512,512]{1,0:T(8,128)(2,1)S(1)} %get-tuple-element.114.mixm_ref), channel_id=1, source_target_pairs={{0,1},{1,0},{2,3},{3,2},{4,5},{5,4},{6,7},{7,6},{8,9},{9,8},{10,11... | collective-permute-start | bytes 1572872 | tf_op jit(solution)/shard_map/ppermute | solution.py:40
  79.3 5.9 %collective-permute-start.20 = (bf16[2,256,512]{2,1,0:T(8,128)(2,1)S(1)}, bf16[2,256,512]{2,1,0:T(8,128)(2,1)S(1)}, u32[]{:S(2)}, u32[]{:S(2)}) collective-permute-start(bf16[2,256,512]{2,1,0:T(8,128)(2,1)S(1)} %bitcast.28), channel_id=1, source_target_pairs={{0,1},{1,0},{2,3},{3,2},{4,5},{5,4},{6,7},{7,6},{8,9},{9,8},{10,11... | collective-permute-start | bytes 1572872 | tf_op jit(solution)/shard_map/ppermute | solution.py:40
  79.4 13.9 %collective-permute-start.24 = (bf16[336,512]{1,0:T(8,128)(2,1)S(1)}, bf16[336,512]{1,0:T(8,128)(2,1)S(1)}, u32[]{:S(2)}, u32[]{:S(2)}) collective-permute-start(bf16[336,512]{1,0:T(8,128)(2,1)S(1)} %get-tuple-element.124), channel_id=1, source_target_pairs={{0,4},{2,6},{4,8},{6,10},{8,12},{10,14},{12,0},{14,2},{1,5},{3,7},... | collective-permute-start | bytes 1032200 | tf_op jit(solution)/shard_map/ppermute | solution.py:52
  83.1 10.2 %collective-permute-start.25 = (bf16[336,512]{1,0:T(8,128)(2,1)S(1)}, bf16[336,512]{1,0:T(8,128)(2,1)S(1)}, u32[]{:S(2)}, u32[]{:S(2)}) collective-permute-start(bf16[336,512]{1,0:T(8,128)(2,1)S(1)} %get-tuple-element.125), channel_id=1, source_target_pairs={{0,2},{2,0},{4,6},{6,4},{8,10},{10,8},{12,14},{14,12},{1,3},{3,1},... | collective-permute-start | bytes 1032200 | tf_op jit(solution)/shard_map/ppermute | solution.py:48
  84.8 9.9 %collective-permute-start.26 = (bf16[336,512]{1,0:T(8,128)(2,1)S(1)}, bf16[336,512]{1,0:T(8,128)(2,1)S(1)}, u32[]{:S(2)}, u32[]{:S(2)}) collective-permute-start(bf16[336,512]{1,0:T(8,128)(2,1)S(1)} %get-tuple-element.126), channel_id=1, source_target_pairs={{0,16},{16,0},{1,17},{17,1},{2,18},{18,2},{3,19},{19,3},{4,20},{20... | collective-permute-start | bytes 1032200 | tf_op jit(solution)/shard_map/ppermute | solution.py:44
  88.2 1.6 %collective-permute-start.23 = (bf16[2,256,256]{2,1,0:T(8,128)(2,1)S(1)}, bf16[2,256,256]{2,1,0:T(8,128)(2,1)S(1)}, u32[]{:S(2)}, u32[]{:S(2)}) collective-permute-start(bf16[2,256,256]{2,1,0:T(8,128)(2,1)S(1)} %get-tuple-element.120.zmb), channel_id=1, source_target_pairs={{0,1},{1,0},{2,3},{3,2},{4,5},{5,4},{6,7},{7,6},{8,9},{9,8},{10,11... | collective-permute-start | bytes 786440 | tf_op jit(solution)/shard_map/ppermute | solution.py:40
  97.8 1.6 %collective-permute-start.27 = (bf16[2,256,256]{2,1,0:T(8,128)(2,1)S(1)}, bf16[2,256,256]{2,1,0:T(8,128)(2,1)S(1)}, u32[]{:S(2)}, u32[]{:S(2)}) collective-permute-start(bf16[2,256,256]{2,1,0:T(8,128)(2,1)S(1)} %conv1.1.zm_ref), channel_id=1, source_target_pairs={{0,1},{1,0},{2,3},{3,2},{4,5},{5,4},{6,7},{7,6},{8,9},{9,8},{10,11... | collective-permute-start | bytes 786440 | tf_op jit(solution)/shard_map/ppermute | solution.py:40

commit v5 on v4

--- a/solution.py
+++ b/solution.py
@@ -147,7 +147,7 @@
         dst[...] = src[...]
 
 
-def conv_slabs(cfg, place, hm, hp, wide, z_ref, acc):
+def conv_slabs(cfg, place, hm, hp, wide, z_refs, acc):
     rows, half, branch, slabs = cfg
     c = place[2]
     at_m = pl.multiple_of(c * half, half)
@@ -170,10 +170,7 @@
                     acc[v, 0:size, :] += part
         for r in range(0, size, rows):
             gate_into(
-                (
-                    z_ref.at[0, begin + r : begin + r + rows, :],
-                    z_ref.at[1, begin + r : begin + r + rows, :],
-                ),
+                [z_ref.at[begin + r : begin + r + rows, :] for z_ref in z_refs],
                 acc[0, r : r + rows, :],
                 acc[1, r : r + rows, :],
                 branch,
@@ -185,65 +182,60 @@
     if weight_cfg[2] is not None:
         for src, dst in weight_moves(place, refs[:-6], *weight_cfg, wide, mix):
             dst[...] = src[...]
-    conv_slabs(cfg, place, hm, hp, wide, z_ref, acc)
-
-
-def conv0_far_kernel(cfg, place, gm_ref, gp_ref, mine, theirs, wide, _, __, z_ref, hm, hp, acc):
+    conv_slabs(cfg, place, hm, hp, wide, (z_ref.at[0], z_ref.at[1]), acc)
+
+
+def conv0_far_kernel(cfg, place, gm_ref, gp_ref, mine, theirs, wide, _, __, *refs):
+    z_ref, dz_ref, hm, hp, acc = refs
     norm_rows(gm_ref[0:1, :], gp_ref[0:1, :], mine, theirs, hm, hp, 0)
-    conv_slabs(cfg, place, hm, hp, wide, z_ref, acc)
-
-
-def mix0_kernel(cfg, place, gm_ref, gp_ref, zma, zpa, zmb, zpb, mixm_ref, mixp_ref, *refs):
-    rows, half, branch, layer = cfg
-    mine = refs[:TAPS]
-    theirs = refs[TAPS : 2 * TAPS]
-    hm_ref, hp_ref, state_ref = refs[2 * TAPS :]
+    conv_slabs(cfg, place, hm, hp, wide, (z_ref, dz_ref), acc)
+
+
+def mix0_kernel(cfg, place, gm_ref, gp_ref, mixm_ref, mixp_ref, *refs):
+    rows, half, branch, layer, count, n_z = cfg
+    if n_z == 1:
+        zm_refs, zp_refs = ([ref.at[0], ref.at[1]] for ref in refs[:2])
+    else:
+        zm_refs, zp_refs = refs[:2], refs[2:4]
+    refs = refs[2 * n_z :]
+    mine, theirs = refs[:count], refs[count : 2 * count]
+    hm_ref, hp_ref, *state_refs = refs[2 * count :]
     c = place[2]
     at_m = pl.ds(pl.multiple_of(c * branch, branch), branch)
     at_p = pl.ds(pl.multiple_of((1 - c) * branch, branch), branch)
     gm = gm_ref[layer : layer + 1, :]
     gp = gp_ref[layer : layer + 1, :]
-    step = min(256, rows)
-    for j in range(TAPS):
-        zm_ref, zp_ref, base = (zma, zpa, (1 - j) * rows) if j < 2 else (zmb, zpb, 0)
-
-        def body(i, carry, j=j, base=base, zm_ref=zm_ref, zp_ref=zp_ref):
-            at = pl.multiple_of(i * step, step)
-            to = pl.multiple_of(base + i * step, step)
-            new = []
-            for v in range(2):
-                zm = zm_ref[v, pl.ds(to, step), :]
-                zp = zp_ref[v, pl.ds(to, step), :]
-                for x_ref, mix in ((mine[j], mixm_ref), (theirs[j], mixp_ref)):
-                    y = jnp.dot(zm, mix[at_m, :], preferred_element_type=F32)
-                    y = y + jnp.dot(zp, mix[at_p, :], preferred_element_type=F32)
-                    new.append((x_ref[v, pl.ds(at, step), :].astype(F32) + y).astype(BF16))
-            if j == 0:
-                state_ref[0, pl.ds(at, step), :] = new[0]
-                state_ref[1, pl.ds(at, step), :] = new[2]
-            xm, xp, dxm, dxp = (t.astype(F32) for t in new)
-            a, b, d, e = normalise(xm, xp, dxm, dxp, gm, gp, 2 * half)
-            hm_ref[j, 0, pl.ds(at, step), :] = a
-            hp_ref[j, 0, pl.ds(at, step), :] = b
-            hm_ref[j, 1, pl.ds(at, step), :] = d
-            hp_ref[j, 1, pl.ds(at, step), :] = e
-            return carry
-
-        lax.fori_loop(0, rows // step, body, 0)
-
-
-def conv1_kernel(cfg, place, hm, hp, wide, z_ref, acc):
+    for j in range(count):
+        at = slice((count - 1 - j) * rows, (count - j) * rows)
+        new = []
+        for v in range(2):
+            zm = zm_refs[v][at, :]
+            zp = zp_refs[v][at, :]
+            for x_ref, mix in ((mine[j], mixm_ref), (theirs[j], mixp_ref)):
+                y = jnp.dot(zm, mix[at_m, :], preferred_element_type=F32)
+                y = y + jnp.dot(zp, mix[at_p, :], preferred_element_type=F32)
+                new.append((x_ref[v].astype(F32) + y).astype(BF16))
+        if j == 0 and state_refs:
+            state_refs[0][0] = new[0]
+            state_refs[0][1] = new[2]
+        xm, xp, dxm, dxp = (t.astype(F32) for t in new)
+        hm_ref[j, 0], hp_ref[j, 0], hm_ref[j, 1], hp_ref[j, 1] = normalise(
+            xm, xp, dxm, dxp, gm, gp, 2 * half
+        )
+
+
+def conv1_kernel(cfg, place, hm_near, hp_near, hm_far, hp_far, wide, z_ref, acc):
     rows, half, branch = cfg
     c = place[2]
     at_m = pl.multiple_of(c * half, half)
     at_p = pl.multiple_of((1 - c) * half, half)
     for k in range(TAPS):
         part = jnp.dot(
-            hm[k].reshape(2 * rows, half),
+            (hm_near[k] if k < 2 else hm_far[0]).reshape(2 * rows, half),
             wide[pl.ds(2 * half * k + at_m, half), :],
             preferred_element_type=F32,
         ) + jnp.dot(
-            hp[k].reshape(2 * rows, half),
+            (hp_near[k] if k < 2 else hp_far[0]).reshape(2 * rows, half),
             wide[pl.ds(2 * half * k + at_p, half), :],
             preferred_element_type=F32,
         )
@@ -396,13 +388,13 @@
     to_z, to_x, to_y, three = pack(
         seq,
         place,
-        [(z3a, cut, 2 * unit - cut)],
+        [(z3a, unit, unit)],
         [(z4, 0, unit), (y4, unit, cut)],
         [(z4, 0, unit), (x4, unit + cut, unit - cut)],
         [(z4, unit, tall, 1)],
     )
     x5, y5, z5 = x(to_x), y(to_y), z(to_z)
-    keep(1, z5, (unit - cut, 0, unit, 2, 1, 1))
+    whole(1, z5, (2, 1, 1))
     keep(1, x5, (0, 0, unit, 2, 1, 0), (unit, 0, cut, 3, 1, 1))
     keep(1, y5, (0, 0, unit, 2, 0, 1), (unit, cut, unit - cut, 3, 1, 1))
     return gains_p, (one, two, three), made, (x5, y5, z5), pieces[1], (seq, tuple(order[1]))
@@ -523,48 +515,49 @@
         (swap_chan(last), swap_chan(za_mine), swap_chan(mix_mine))
     )
 
-    z_mine = pl.pallas_call(
+    z = pl.pallas_call(
         functools.partial(conv0_far_kernel, (rows, half, branch, far_slabs)),
         out_shape=(
-            near_out(2, rows, branch),
+            near_out(rows, branch),
+            near_out(rows, branch),
             near_out(2, tall, half),
             near_out(2, tall, half),
         ),
         in_specs=[SMEM] + [VMEM] * 7,
-        out_specs=(VMEM,) * 3,
-        input_output_aliases={6: 1, 7: 2},
+        out_specs=(VMEM,) * 4,
+        input_output_aliases={6: 2, 7: 3},
         scratch_shapes=[pltpu.VMEM((2, rows, 2 * branch), F32)],
         compiler_params=scoped(8),
         cost_estimate=cost(0, 2**16),
         name="conv0_far",
-    )(place, near(gains), near(gains_p), near(last), near(last_theirs), wide, hm, hp)[0]
-    z_theirs = swap_chan(z_mine)
-    hm, hp, state = pl.pallas_call(
-        functools.partial(mix0_kernel, (rows, half, branch, 1)),
-        out_shape=(
-            near_out(TAPS, 2, rows, half),
-            near_out(TAPS, 2, rows, half),
-            near_out(2, rows, half),
-        ),
-        in_specs=[SMEM] + [VMEM] * (8 + 2 * TAPS),
-        out_specs=(VMEM, VMEM, VMEM),
-        compiler_params=scoped(6),
-        cost_estimate=cost(0, 2**16),
-        name="mix0",
-    )(
-        place,
-        near(gains),
-        near(gains_p),
-        near(za_mine),
-        near(za_theirs),
-        z_mine,
-        near(z_theirs),
-        near(mix_mine),
-        near(mix_theirs),
-        *[near(mine[b]) for b in used],
-        *[near(theirs[b]) for b in used],
-    )
-    hm, hp, *weights1 = lax.optimization_barrier((hm, hp, *weights1))
+    )(place, near(gains), near(gains_p), near(last), near(last_theirs), wide, hm, hp)[:2]
+
+    def mix0(z, z_theirs, blocks_used, name):
+        n = len(blocks_used)
+        states = [near_out(2, rows, half)] if blocks_used[0] == 0 else []
+        return pl.pallas_call(
+            functools.partial(mix0_kernel, (rows, half, branch, 1, n, len(z))),
+            out_shape=(near_out(n, 2, rows, half), near_out(n, 2, rows, half), *states),
+            in_specs=[SMEM] + [VMEM] * (4 + 2 * len(z) + 2 * n),
+            out_specs=(VMEM,) * (2 + len(states)),
+            compiler_params=scoped(12),
+            cost_estimate=cost(0, 2**16),
+            name=name,
+        )(
+            place,
+            near(gains),
+            near(gains_p),
+            near(mix_mine),
+            near(mix_theirs),
+            *[near(t) for t in (*z, *z_theirs)],
+            *[near(mine[b]) for b in blocks_used],
+            *[near(theirs[b]) for b in blocks_used],
+        )
+
+    za_mine, *z = lax.optimization_barrier((za_mine, *z))
+    hm1, hp1, state = mix0([za_mine], [za_theirs], used[:2], "mix0_near")
+    hm, hp = mix0(z, [swap_chan(t) for t in z], used[2:], "mix0_far")
+    hm, hp, hm1, hp1, *weights1 = lax.optimization_barrier((hm, hp, hm1, hp1, *weights1))
     placed = pl.pallas_call(
         functools.partial(place_kernel, (conv_rows, mix_rows, pairs1)),
         out_shape=(near_out(wide_rows, 2 * branch), near_out(mix_whole, half)),
@@ -577,12 +570,12 @@
     z_mine = pl.pallas_call(
         functools.partial(conv1_kernel, (rows, half, branch)),
         out_shape=near_out(2, rows, branch),
-        in_specs=[SMEM] + [VMEM] * 3,
+        in_specs=[SMEM] + [VMEM] * 5,
         out_specs=VMEM,
         scratch_shapes=[pltpu.VMEM((2 * rows, 2 * branch), F32)],
         compiler_params=scoped(8),
         name="conv1",
-    )(place, hm, hp, wide)
+    )(place, hm1, hp1, hm, hp, wide)
     z_theirs = swap_chan(z_mine)
     return pl.pallas_call(
         functools.partial(mix1_kernel, (branch,)),

time: 101 us -> 99.6 us (0.986)
  waiting for transfers between devices: 49.2 us -> 46.2 us
    ppermute x9 -> x10, waiting for transfers between devices: 4.22 us -> 2.64 us  [swap_chan(): return lax.ppermute(block, 'chan', [(0, 1), (1, 0)])]
    ppermute x6, waiting for transfers between devices: 5.65 us -> 4.27 us  [swap_groups(): return lax.ppermute(block, 'groups', [(0, 1), (1, 0)])]
    pallas_call x1 -> x2, Pallas kernels: 3.46 us -> 4.12 us  [mix0(): pl.pallas_call(functools.partial(mix0_kernel, (rows, half, branch, 1, n,...]
  transfers between devices with their start and end apart: 28 -> 29, of which waited for: 15 -> 13; matrix products, arithmetic and copies ran while one was open for 1% -> 1% of each run, Pallas kernels for 15% -> 15%
where the time goes in v5:
time: 99.6 us; the launch traced here: 99.4 us
  waiting for transfers between devices  46.2 us (46%)
  starting transfers between devices  27.3 us (27%)
  Pallas kernels  21.7 us (22%)
  local copies, waits for them, and re-layouts  2.5 us (3%)
    ppermute x7, waiting for transfers between devices, ring(): return lax.ppermute(block, 'seq', [(s, (s + by) % seq) for s in range(seq)])  22.1 us
    ppermute x6, waiting for transfers between devices, swap_pair(): return lax.ppermute(block, 'seq', [(s, s ^ 1) for s in range(seq)])  17.2 us
    ppermute x7, starting transfers between devices, ring(): return lax.ppermute(block, 'seq', [(s, (s + by) % seq) for s in range(seq)])  12.9 us
    ppermute x6, starting transfers between devices, swap_groups(): return lax.ppermute(block, 'groups', [(0, 1), (1, 0)])  7.59 us
    ppermute x6, starting transfers between devices, swap_pair(): return lax.ppermute(block, 'seq', [(s, s ^ 1) for s in range(seq)])  5.51 us
    ppermute x6, waiting for transfers between devices, swap_groups(): return lax.ppermute(block, 'groups', [(0, 1), (1, 0)])  4.27 us
    pallas_call x2, Pallas kernels, mix0(): pl.pallas_call(functools.partial(mix0_kernel, (rows, half, branch, 1, n,...  4.12 us
    pallas_call x1, Pallas kernels, newest(): pl.pallas_call(functools.partial(conv0_near_kernel, (rows, half, branch,...  4.02 us
  transfers between devices with their start and end apart: 29, of which 13 were waited for; matrix products, arithmetic and copies ran while one was open for 1% of the time, Pallas kernels for 15%

profile of v5, /device:TPU:0, one launch (start us, length us, event | category | flops | bytes accessed | tf_op | source)
XLA Modules:
  0.0 99.4 jit_solution(16617080908808671528)
XLA Ops:
  0.7 1.1 %copy-done = bf16[2,384,2,256]{3,2,1,0:T(2,128)(2,1)S(1)} copy-done((bf16[2,384,2,256]{3,2,1,0:T(2,128)(2,1)S(1)}, bf16[2,384,2,256]{3,2,1,0:T(2,128)(2,1)}, u32[]{:S(2)}) %copy-start) | copy-done | bytes 786456
  1.8 0.3 constant_dynamic-slice_fusion.1
  2.0 0.3 reshape.27
  2.3 0.9 constant_dynamic-slice_fusion
  3.2 3.0 %collective-permute-start.3 = (bf16[448,512]{1,0:T(8,128)(2,1)S(1)}, bf16[448,512]{1,0:T(8,128)(2,1)S(1)}, u32[]{:S(2)}, u32[]{:S(2)}) collective-permute-start(bf16[448,512]{1,0:T(8,128)(2,1)S(1)} %bitcast.17), channel_id=1, source_target_pairs={{0,16},{16,0},{1,17},{17,1},{2,18},{18,2},{3,19},{19,3},{4,20},{20... | collective-permute-start | bytes 1376264 | tf_op jit(solution)/shard_map/ppermute | solution.py:44
  6.2 1.5 %collective-permute-start.2 = (bf16[448,512]{1,0:T(8,128)(2,1)S(1)}, bf16[448,512]{1,0:T(8,128)(2,1)S(1)}, u32[]{:S(2)}, u32[]{:S(2)}) collective-permute-start(bf16[448,512]{1,0:T(8,128)(2,1)S(1)} %bitcast.18), channel_id=1, source_target_pairs={{0,2},{2,0},{4,6},{6,4},{8,10},{10,8},{12,14},{14,12},{1,3},{3,1},... | collective-permute-start | bytes 1376264 | tf_op jit(solution)/shard_map/ppermute | solution.py:48
  7.7 0.7 fusion.3
  8.4 3.6 %collective-permute-start.1 = (bf16[224,512]{1,0:T(8,128)(2,1)}, bf16[224,512]{1,0:T(8,128)(2,1)S(1)}, u32[]{:S(2)}, u32[]{:S(2)}) collective-permute-start(bf16[224,512]{1,0:T(8,128)(2,1)} %get-tuple-element.161), channel_id=1, source_target_pairs={{0,12},{2,14},{4,0},{6,2},{8,4},{10,6},{12,8},{14,10},{1,13},{3,15... | collective-permute-start | bytes 688136 | tf_op jit(solution)/shard_map/ppermute | solution.py:52
  12.2 6.2 %collective-permute-done.1.refs_2_.refs_8_ = bf16[224,512]{1,0:T(8,128)(2,1)S(1)} collective-permute-done((bf16[224,512]{1,0:T(8,128)(2,1)}, bf16[224,512]{1,0:T(8,128)(2,1)S(1)}, u32[]{:S(2)}, u32[]{:S(2)}) %collective-permute-start.1) | collective-permute-done | bytes 229408 | tf_op jit(solution)/shard_map/ppermute | solution.py:52
  18.4 4.0 %collective-permute-done.refs_0_.refs_7_ = bf16[224,512]{1,0:T(8,128)(2,1)S(1)} collective-permute-done((bf16[224,512]{1,0:T(8,128)(2,1)}, bf16[224,512]{1,0:T(8,128)(2,1)S(1)}, u32[]{:S(2)}, u32[]{:S(2)}) %collective-permute-start) | collective-permute-done | bytes 229408 | tf_op jit(solution)/shard_map/ppermute | solution.py:52
  22.4 0.7 pack.4
  23.1 1.7 %collective-permute-start.4 = (bf16[736,512]{1,0:T(8,128)(2,1)S(1)}, bf16[736,512]{1,0:T(8,128)(2,1)S(1)}, u32[]{:S(2)}, u32[]{:S(2)}) collective-permute-start(bf16[736,512]{1,0:T(8,128)(2,1)S(1)} %get-tuple-element.86), channel_id=1, source_target_pairs={{0,4},{2,6},{4,8},{6,10},{8,12},{10,14},{12,0},{14,2},{1,5},{3,7},... | collective-permute-start | bytes 2261000 | tf_op jit(solution)/shard_map/ppermute | solution.py:52
  24.8 0.5 collective-permute-start.5
  25.3 0.5 collective-permute-start.6
  25.8 1.2 %collective-permute-done.7.gp_ref = f32[2,512]{1,0:T(2,128)S(1)} collective-permute-done((f32[2,512]{1,0:T(2,128)S(1)}, f32[2,512]{1,0:T(2,128)S(1)}, u32[]{:S(2)}, u32[]{:S(2)}) %collective-permute-start.7) | collective-permute-done | bytes 4128 | tf_op jit(solution)/shard_map/ppermute | solution.py:40
  27.0 13.2 %collective-permute-done.5.refs_1_.refs_12_.refs_3_ = bf16[672,512]{1,0:T(8,128)(2,1)S(1)} collective-permute-done((bf16[672,512]{1,0:T(8,128)(2,1)S(1)}, bf16[672,512]{1,0:T(8,128)(2,1)S(1)}, u32[]{:S(2)}, u32[]{:S(2)}) %collective-permute-start.5) | collective-permute-done | bytes 688160 | tf_op jit(solution)/shard_map/ppermute | solution.py:48
  40.2 0.3 collective-permute-done.6.refs_13_
  40.5 1.6 %collective-permute-done.4.refs_2_.refs_11_ = bf16[736,512]{1,0:T(8,128)(2,1)S(1)} collective-permute-done((bf16[736,512]{1,0:T(8,128)(2,1)S(1)}, bf16[736,512]{1,0:T(8,128)(2,1)S(1)}, u32[]{:S(2)}, u32[]{:S(2)}) %collective-permute-start.4) | collective-permute-done | bytes 753696 | tf_op jit(solution)/shard_map/ppermute | solution.py:52
  42.0 0.8 pack.5
  42.8 0.6 collective-permute-start.10
  43.4 0.5 collective-permute-start.11
  43.9 3.8 %collective-permute-start.9 = (bf16[224,512]{1,0:T(8,128)(2,1)S(1)}, bf16[224,512]{1,0:T(8,128)(2,1)S(1)}, u32[]{:S(2)}, u32[]{:S(2)}) collective-permute-start(bf16[224,512]{1,0:T(8,128)(2,1)S(1)} %get-tuple-element.95), channel_id=1, source_target_pairs={{0,12},{2,14},{4,0},{6,2},{8,4},{10,6},{12,8},{14,10},{1,13},{3,15... | collective-permute-start | bytes 688136 | tf_op jit(solution)/shard_map/ppermute | solution.py:52
  47.7 10.4 %collective-permute-done.9.refs_2_.refs_5_ = bf16[224,512]{1,0:T(8,128)(2,1)S(1)} collective-permute-done((bf16[224,512]{1,0:T(8,128)(2,1)S(1)}, bf16[224,512]{1,0:T(8,128)(2,1)S(1)}, u32[]{:S(2)}, u32[]{:S(2)}) %collective-permute-start.9) | collective-permute-done | bytes 229408 | tf_op jit(solution)/shard_map/ppermute | solution.py:52
  58.1 0.9 collective-permute-done.10.refs_1_.refs_14_
  59.0 0.7 pack.6
  59.8 0.8 collective-permute-start.13
  60.6 1.5 %collective-permute-start.14 = (bf16[112,512]{1,0:T(8,128)(2,1)S(1)}, bf16[112,512]{1,0:T(8,128)(2,1)S(1)}, u32[]{:S(2)}, u32[]{:S(2)}) collective-permute-start(bf16[112,512]{1,0:T(8,128)(2,1)S(1)} %get-tuple-element.105), channel_id=1, source_target_pairs={{0,16},{16,0},{1,17},{17,1},{2,18},{18,2},{3,19},{19,3},{4,20},{20... | collective-permute-start | bytes 344072 | tf_op jit(solution)/shard_map/ppermute | solution.py:44
  62.1 2.5 %collective-permute-done.13.refs_0_ = bf16[112,512]{1,0:T(8,128)(2,1)S(1)} collective-permute-done((bf16[112,512]{1,0:T(8,128)(2,1)S(1)}, bf16[112,512]{1,0:T(8,128)(2,1)S(1)}, u32[]{:S(2)}, u32[]{:S(2)}) %collective-permute-start.13) | collective-permute-done | bytes 114720 | tf_op jit(solution)/shard_map/ppermute | solution.py:48
  64.7 0.7 collective-permute-done.14.refs_1_
  65.4 1.5 %collective-permute-start.16 = (bf16[448,512]{1,0:T(8,128)(2,1)S(1)}, bf16[448,512]{1,0:T(8,128)(2,1)S(1)}, u32[]{:S(2)}, u32[]{:S(2)}) collective-permute-start(bf16[448,512]{1,0:T(8,128)(2,1)S(1)} %get-tuple-element.106), channel_id=1, source_target_pairs={{0,16},{16,0},{1,17},{17,1},{2,18},{18,2},{3,19},{19,3},{4,20},{20... | collective-permute-start | bytes 1376264 | tf_op jit(solution)/shard_map/ppermute | solution.py:44
  66.9 0.5 collective-permute-start.15
  67.5 2.8 %ready.1 = (bf16[3072,512]{1,0:T(8,128)(2,1)S(1)}, bf16[512,512]{1,0:T(8,128)(2,1)S(1)}, bf16[2,1024,512]{2,1,0:T(8,128)(2,1)S(1)}, bf16[2,1024,512]{2,1,0:T(8,128)(2,1)S(1)}) custom-call(s32[3]{0:T(128)S(1)} %pad_add_fusion.place_ref.place, f32[2,512]{1,0:T(2,128)S(1)} %copy-done.1, f32[2,512]{1,0:T(2,128)S(1)} %collective-permute-done.7.gp_ref, ...), custom_call_target="tpu_custom_call" | custom-call | bytes 65536 | tf_op jit(solution)/shard_map/ready/pallas_call | solution.py:459
  70.3 4.0 %conv0_near.1 = (bf16[2,512,256]{2,1,0:T(8,128)(2,1)S(1)}, bf16[3072,512]{1,0:T(8,128)(2,1)S(1)}, bf16[512,512]{1,0:T(8,128)(2,1)S(1)}) custom-call(s32[3]{0:T(128)S(1)} %pad_add_fusion.place_ref.place, bf16[2,1024,512]{2,1,0:T(8,128)(2,1)S(1)} %get-tuple-element.126.hm._, ...), custom_call_target="tpu_custom_call", output_to_operand_aliasing={{1}: (5, {}), {2}: (6, {})} | custom-call | bytes 65536 | tf_op jit(solution)/shard_map/conv0_near/pallas_call | solution.py:483
  74.3 3.3 %collective-permute-done.16.refs_2_.refs_8_ = bf16[448,512]{1,0:T(8,128)(2,1)S(1)} collective-permute-done((bf16[448,512]{1,0:T(8,128)(2,1)S(1)}, bf16[448,512]{1,0:T(8,128)(2,1)S(1)}, u32[]{:S(2)}, u32[]{:S(2)}) %collective-permute-start.16) | collective-permute-done | bytes 458784 | tf_op jit(solution)/shard_map/ppermute | solution.py:44
  77.6 0.5 collective-permute-done.15.refs_3_.refs_7_
  78.1 0.5 collective-permute-start.22
  78.6 0.7 pack.7
  79.4 1.6 %collective-permute-start.26 = (bf16[336,512]{1,0:T(8,128)(2,1)S(1)}, bf16[336,512]{1,0:T(8,128)(2,1)S(1)}, u32[]{:S(2)}, u32[]{:S(2)}) collective-permute-start(bf16[336,512]{1,0:T(8,128)(2,1)S(1)} %get-tuple-element.139), channel_id=1, source_target_pairs={{0,2},{2,0},{4,6},{6,4},{8,10},{10,8},{12,14},{14,12},{1,3},{3,1},... | collective-permute-start | bytes 1032200 | tf_op jit(solution)/shard_map/ppermute | solution.py:48
  80.9 0.5 collective-permute-start.27
  81.4 3.7 %collective-permute-start.25 = (bf16[224,512]{1,0:T(8,128)(2,1)S(1)}, bf16[224,512]{1,0:T(8,128)(2,1)S(1)}, u32[]{:S(2)}, u32[]{:S(2)}) collective-permute-start(bf16[224,512]{1,0:T(8,128)(2,1)S(1)} %get-tuple-element.138), channel_id=1, source_target_pairs={{0,4},{2,6},{4,8},{6,10},{8,12},{10,14},{12,0},{14,2},{1,5},{3,7},... | collective-permute-start | bytes 688136 | tf_op jit(solution)/shard_map/ppermute | solution.py:52
  85.2 3.0 %conv0_far.1 = (bf16[256,256]{1,0:T(8,128)(2,1)S(1)}, bf16[256,256]{1,0:T(8,128)(2,1)S(1)}, bf16[2,1024,512]{2,1,0:T(8,128)(2,1)S(1)}, bf16[2,1024,512]{2,1,0:T(8,128)(2,1)S(1)}) custom-call(s32[3]{0:T(128)S(1)} %pad_add_fusion.place_ref.place, f32[2,512]{1,0:T(2,128)S(1)} %copy-done.1, ...), custom_call_target="tpu_custom_call", output_to_operand_aliasing={{2}: (6, {}), {3}: (7, {})} | custom-call | bytes 65536 | tf_op jit(solution)/shard_map/conv0_far/pallas_call | solution.py:518
  88.3 0.5 collective-permute-start.24
  88.8 2.5 %mix0_near.1 = (bf16[2,2,256,512]{3,2,1,0:T(8,128)(2,1)S(1)}, bf16[2,2,256,512]{3,2,1,0:T(8,128)(2,1)S(1)}, bf16[2,256,512]{2,1,0:T(8,128)(2,1)S(1)}) custom-call(s32[3]{0:T(128)S(1)} %pad_add_fusion.place_ref.place, f32[2,512]{1,0:T(2,128)S(1)} %copy-done.1, f32[2,512]{1,0:T(2,128)S(1)} %collective-permute-done.7.gp_ref, ...), custom_call_target="tpu_custom_call" | custom-call | bytes 65536 | tf_op jit(solution)/shard_map/mix0_near/pallas_call | solution.py:538
  91.3 1.6 %mix0_far.1 = (bf16[1,2,256,512]{3,2,1,0:T(8,128)(2,1)S(1)}, bf16[1,2,256,512]{3,2,1,0:T(8,128)(2,1)S(1)}) custom-call(s32[3]{0:T(128)S(1)} %pad_add_fusion.place_ref.place, f32[2,512]{1,0:T(2,128)S(1)} %copy-done.1, f32[2,512]{1,0:T(2,128)S(1)} %collective-permute-done.7.gp_ref, bf16[512,512]{1,0:T(8,128)(2,1)S(1)} %get-tuple-element.117.mixm_ref, ...), custom_call_target="tpu_custom_call" | custom-call | bytes 65536 | tf_op jit(solution)/shard_map/mix0_far/pallas_call | solution.py:538
  93.0 0.8 place.1
  93.8 2.3 %conv1.1.zm_ref = bf16[2,256,256]{2,1,0:T(8,128)(2,1)S(1)} custom-call(s32[3]{0:T(128)S(1)} %pad_add_fusion.place_ref.place, bf16[2,2,256,512]{3,2,1,0:T(8,128)(2,1)S(1)} %get-tuple-element.141.hm_near, bf16[2,2,256,512]{3,2,1,0:T(8,128)(2,1)S(1)} %get-tuple-element.142.hp_near, bf16[1,2,256,512]{3,2,1,0:T(8,128)(2,1)S(1)} %get-tuple-element.143.hm_far, ...), custom_call_target="tpu_custom_call" | custom-call | tf_op jit(solution)/shard_map/conv1/pallas_call | solution.py:570
  96.3 1.5 %collective-permute-done.28.zp_ref = bf16[2,256,256]{2,1,0:T(8,128)(2,1)S(1)} collective-permute-done((bf16[2,256,256]{2,1,0:T(8,128)(2,1)S(1)}, bf16[2,256,256]{2,1,0:T(8,128)(2,1)S(1)}, u32[]{:S(2)}, u32[]{:S(2)}) %collective-permute-start.28) | collective-permute-done | bytes 262176 | tf_op jit(solution)/shard_map/ppermute | solution.py:40
  97.7 1.7 %mix1.1 = (bf16[256,512]{1,0:T(8,128)(2,1)}, bf16[256,512]{1,0:T(8,128)(2,1)}) custom-call(s32[3]{0:T(128)S(1)} %pad_add_fusion.place_ref.place, bf16[2,256,256]{2,1,0:T(8,128)(2,1)S(1)} %conv1.1.zm_ref, bf16[2,256,256]{2,1,0:T(8,128)(2,1)S(1)} %collective-permute-done.28.zp_ref, bf16[512,512]{1,0:T(8,128)(2,1)S(1)} %get-tuple-element.158.mix_ref, ...), custom_call_target="tpu_custom_call" | custom-call | tf_op jit(solution)/shard_map/mix1/pallas_call | solution.py:580
  (37 shorter events, 0.6 us)
Async XLA Ops:
  0.6 1.1 %copy-start = (bf16[2,384,2,256]{3,2,1,0:T(2,128)(2,1)S(1)}, bf16[2,384,2,256]{3,2,1,0:T(2,128)(2,1)}, u32[]{:S(2)}) copy-start(bf16[2,384,2,256]{3,2,1,0:T(2,128)(2,1)} %param.8) | copy-start | bytes 2359300
  0.6 11.5 %copy-start.2 = (bf16[256,512]{1,0:T(8,128)(2,1)S(1)}, bf16[256,512]{1,0:T(8,128)(2,1)}, u32[]{:S(2)}) copy-start(bf16[256,512]{1,0:T(8,128)(2,1)} %param.6) | copy-start | bytes 786436
  0.7 11.5 %copy-start.3 = (bf16[256,512]{1,0:T(8,128)(2,1)S(1)}, bf16[256,512]{1,0:T(8,128)(2,1)}, u32[]{:S(2)}) copy-start(bf16[256,512]{1,0:T(8,128)(2,1)} %param.5) | copy-start | bytes 786436
  3.2 22.6 %copy-start.1 = (f32[2,512]{1,0:T(2,128)S(1)}, f32[2,512]{1,0:T(2,128)}, u32[]{:S(2)}) copy-start(f32[2,512]{1,0:T(2,128)} %gm_ref.7) | copy-start | bytes 12292
  3.2 19.2 %collective-permute-start.3 = (bf16[448,512]{1,0:T(8,128)(2,1)S(1)}, bf16[448,512]{1,0:T(8,128)(2,1)S(1)}, u32[]{:S(2)}, u32[]{:S(2)}) collective-permute-start(bf16[448,512]{1,0:T(8,128)(2,1)S(1)} %bitcast.17), channel_id=1, source_target_pairs={{0,16},{16,0},{1,17},{17,1},{2,18},{18,2},{3,19},{19,3},{4,20},{20... | collective-permute-start | bytes 1376264 | tf_op jit(solution)/shard_map/ppermute | solution.py:44
  6.2 16.2 %collective-permute-start.2 = (bf16[448,512]{1,0:T(8,128)(2,1)S(1)}, bf16[448,512]{1,0:T(8,128)(2,1)S(1)}, u32[]{:S(2)}, u32[]{:S(2)}) collective-permute-start(bf16[448,512]{1,0:T(8,128)(2,1)S(1)} %bitcast.18), channel_id=1, source_target_pairs={{0,2},{2,0},{4,6},{6,4},{8,10},{10,8},{12,14},{14,12},{1,3},{3,1},... | collective-permute-start | bytes 1376264 | tf_op jit(solution)/shard_map/ppermute | solution.py:48
  8.4 10.0 %collective-permute-start.1 = (bf16[224,512]{1,0:T(8,128)(2,1)}, bf16[224,512]{1,0:T(8,128)(2,1)S(1)}, u32[]{:S(2)}, u32[]{:S(2)}) collective-permute-start(bf16[224,512]{1,0:T(8,128)(2,1)} %get-tuple-element.161), channel_id=1, source_target_pairs={{0,12},{2,14},{4,0},{6,2},{8,4},{10,6},{12,8},{14,10},{1,13},{3,15... | collective-permute-start | bytes 688136 | tf_op jit(solution)/shard_map/ppermute | solution.py:52
  12.0 10.3 %collective-permute-start = (bf16[224,512]{1,0:T(8,128)(2,1)}, bf16[224,512]{1,0:T(8,128)(2,1)S(1)}, u32[]{:S(2)}, u32[]{:S(2)}) collective-permute-start(bf16[224,512]{1,0:T(8,128)(2,1)} %get-tuple-element.161), channel_id=1, source_target_pairs={{0,4},{2,6},{4,8},{6,10},{8,12},{10,14},{12,0},{14,2},{1,5},{3,7},... | collective-permute-start | bytes 688136 | tf_op jit(solution)/shard_map/ppermute | solution.py:52
  23.1 18.9 %collective-permute-start.4 = (bf16[736,512]{1,0:T(8,128)(2,1)S(1)}, bf16[736,512]{1,0:T(8,128)(2,1)S(1)}, u32[]{:S(2)}, u32[]{:S(2)}) collective-permute-start(bf16[736,512]{1,0:T(8,128)(2,1)S(1)} %get-tuple-element.86), channel_id=1, source_target_pairs={{0,4},{2,6},{4,8},{6,10},{8,12},{10,14},{12,0},{14,2},{1,5},{3,7},... | collective-permute-start | bytes 2261000 | tf_op jit(solution)/shard_map/ppermute | solution.py:52
  24.8 15.5 %collective-permute-start.5 = (bf16[672,512]{1,0:T(8,128)(2,1)S(1)}, bf16[672,512]{1,0:T(8,128)(2,1)S(1)}, u32[]{:S(2)}, u32[]{:S(2)}) collective-permute-start(bf16[672,512]{1,0:T(8,128)(2,1)S(1)} %get-tuple-element.87), channel_id=1, source_target_pairs={{0,2},{2,0},{4,6},{6,4},{8,10},{10,8},{12,14},{14,12},{1,3},{3,1},... | collective-permute-start | bytes 2064392 | tf_op jit(solution)/shard_map/ppermute | solution.py:48
  25.3 15.2 %collective-permute-start.6 = (bf16[672,512]{1,0:T(8,128)(2,1)S(1)}, bf16[672,512]{1,0:T(8,128)(2,1)S(1)}, u32[]{:S(2)}, u32[]{:S(2)}) collective-permute-start(bf16[672,512]{1,0:T(8,128)(2,1)S(1)} %get-tuple-element.88), channel_id=1, source_target_pairs={{0,16},{16,0},{1,17},{17,1},{2,18},{18,2},{3,19},{19,3},{4,20},{20... | collective-permute-start | bytes 2064392 | tf_op jit(solution)/shard_map/ppermute | solution.py:44
  25.8 1.2 %collective-permute-start.7 = (f32[2,512]{1,0:T(2,128)S(1)}, f32[2,512]{1,0:T(2,128)S(1)}, u32[]{:S(2)}, u32[]{:S(2)}) collective-permute-start(f32[2,512]{1,0:T(2,128)S(1)} %copy-done.1), channel_id=1, source_target_pairs={{0,1},{1,0},{2,3},{3,2},{4,5},{5,4},{6,7},{7,6},{8,9},{9,8},{10,11... | collective-permute-start | bytes 12296 | tf_op jit(solution)/shard_map/ppermute | solution.py:40
  42.8 16.2 %collective-permute-start.10 = (bf16[736,512]{1,0:T(8,128)(2,1)S(1)}, bf16[736,512]{1,0:T(8,128)(2,1)S(1)}, u32[]{:S(2)}, u32[]{:S(2)}) collective-permute-start(bf16[736,512]{1,0:T(8,128)(2,1)S(1)} %get-tuple-element.96), channel_id=1, source_target_pairs={{0,2},{2,0},{4,6},{6,4},{8,10},{10,8},{12,14},{14,12},{1,3},{3,1},... | collective-permute-start | bytes 2261000 | tf_op jit(solution)/shard_map/ppermute | solution.py:48
  43.4 14.7 %collective-permute-start.11 = (bf16[672,512]{1,0:T(8,128)(2,1)S(1)}, bf16[672,512]{1,0:T(8,128)(2,1)S(1)}, u32[]{:S(2)}, u32[]{:S(2)}) collective-permute-start(bf16[672,512]{1,0:T(8,128)(2,1)S(1)} %get-tuple-element.97), channel_id=1, source_target_pairs={{0,16},{16,0},{1,17},{17,1},{2,18},{18,2},{3,19},{19,3},{4,20},{20... | collective-permute-start | bytes 2064392 | tf_op jit(solution)/shard_map/ppermute | solution.py:44
  43.9 14.2 %collective-permute-start.8 = (bf16[448,512]{1,0:T(8,128)(2,1)S(1)}, bf16[448,512]{1,0:T(8,128)(2,1)S(1)}, u32[]{:S(2)}, u32[]{:S(2)}) collective-permute-start(bf16[448,512]{1,0:T(8,128)(2,1)S(1)} %get-tuple-element.94), channel_id=1, source_target_pairs={{0,4},{2,6},{4,8},{6,10},{8,12},{10,14},{12,0},{14,2},{1,5},{3,7},... | collective-permute-start | bytes 1376264 | tf_op jit(solution)/shard_map/ppermute | solution.py:52
  43.9 14.2 %collective-permute-start.9 = (bf16[224,512]{1,0:T(8,128)(2,1)S(1)}, bf16[224,512]{1,0:T(8,128)(2,1)S(1)}, u32[]{:S(2)}, u32[]{:S(2)}) collective-permute-start(bf16[224,512]{1,0:T(8,128)(2,1)S(1)} %get-tuple-element.95), channel_id=1, source_target_pairs={{0,12},{2,14},{4,0},{6,2},{8,4},{10,6},{12,8},{14,10},{1,13},{3,15... | collective-permute-start | bytes 688136 | tf_op jit(solution)/shard_map/ppermute | solution.py:52
  47.7 19.2 %collective-permute-start.17 = (bf16[2,256,512]{2,1,0:T(8,128)(2,1)S(1)}, bf16[2,256,512]{2,1,0:T(8,128)(2,1)S(1)}, u32[]{:S(2)}, u32[]{:S(2)}) collective-permute-start(bf16[2,256,512]{2,1,0:T(8,128)(2,1)S(1)} %pad_maximum_fusion.1), channel_id=1, source_target_pairs={{0,1},{1,0},{2,3},{3,2},{4,5},{5,4},{6,7},{7,6},{8,9},{9,8},{10,11... | collective-permute-start | bytes 1572872 | tf_op jit(solution)/shard_map/ppermute | solution.py:40
  59.8 18.3 %collective-permute-start.12 = (bf16[736,512]{1,0:T(8,128)(2,1)S(1)}, bf16[736,512]{1,0:T(8,128)(2,1)S(1)}, u32[]{:S(2)}, u32[]{:S(2)}) collective-permute-start(bf16[736,512]{1,0:T(8,128)(2,1)S(1)} %get-tuple-element.102), channel_id=1, source_target_pairs={{0,4},{2,6},{4,8},{6,10},{8,12},{10,14},{12,0},{14,2},{1,5},{3,7},... | collective-permute-start | bytes 2261000 | tf_op jit(solution)/shard_map/ppermute | solution.py:52
  59.8 4.9 %collective-permute-start.13 = (bf16[112,512]{1,0:T(8,128)(2,1)S(1)}, bf16[112,512]{1,0:T(8,128)(2,1)S(1)}, u32[]{:S(2)}, u32[]{:S(2)}) collective-permute-start(bf16[112,512]{1,0:T(8,128)(2,1)S(1)} %get-tuple-element.104), channel_id=1, source_target_pairs={{0,2},{2,0},{4,6},{6,4},{8,10},{10,8},{12,14},{14,12},{1,3},{3,1},... | collective-permute-start | bytes 344072 | tf_op jit(solution)/shard_map/ppermute | solution.py:48
  60.6 4.8 %collective-permute-start.14 = (bf16[112,512]{1,0:T(8,128)(2,1)S(1)}, bf16[112,512]{1,0:T(8,128)(2,1)S(1)}, u32[]{:S(2)}, u32[]{:S(2)}) collective-permute-start(bf16[112,512]{1,0:T(8,128)(2,1)S(1)} %get-tuple-element.105), channel_id=1, source_target_pairs={{0,16},{16,0},{1,17},{17,1},{2,18},{18,2},{3,19},{19,3},{4,20},{20... | collective-permute-start | bytes 344072 | tf_op jit(solution)/shard_map/ppermute | solution.py:44
  62.1 5.3 %collective-permute-start.19 = (bf16[2,256,512]{2,1,0:T(8,128)(2,1)S(1)}, bf16[2,256,512]{2,1,0:T(8,128)(2,1)S(1)}, u32[]{:S(2)}, u32[]{:S(2)}) collective-permute-start(bf16[2,256,512]{2,1,0:T(8,128)(2,1)S(1)} %bitcast.25), channel_id=1, source_target_pairs={{0,1},{1,0},{2,3},{3,2},{4,5},{5,4},{6,7},{7,6},{8,9},{9,8},{10,11... | collective-permute-start | bytes 1572872 | tf_op jit(solution)/shard_map/ppermute | solution.py:40
  64.7 2.8 %collective-permute-start.18 = (bf16[2,256,512]{2,1,0:T(8,128)(2,1)S(1)}, bf16[2,256,512]{2,1,0:T(8,128)(2,1)S(1)}, u32[]{:S(2)}, u32[]{:S(2)}) collective-permute-start(bf16[2,256,512]{2,1,0:T(8,128)(2,1)S(1)} %bitcast.22), channel_id=1, source_target_pairs={{0,1},{1,0},{2,3},{3,2},{4,5},{5,4},{6,7},{7,6},{8,9},{9,8},{10,11... | collective-permute-start | bytes 1572872 | tf_op jit(solution)/shard_map/ppermute | solution.py:40
  65.4 12.2 %collective-permute-start.16 = (bf16[448,512]{1,0:T(8,128)(2,1)S(1)}, bf16[448,512]{1,0:T(8,128)(2,1)S(1)}, u32[]{:S(2)}, u32[]{:S(2)}) collective-permute-start(bf16[448,512]{1,0:T(8,128)(2,1)S(1)} %get-tuple-element.106), channel_id=1, source_target_pairs={{0,16},{16,0},{1,17},{17,1},{2,18},{18,2},{3,19},{19,3},{4,20},{20... | collective-permute-start | bytes 1376264 | tf_op jit(solution)/shard_map/ppermute | solution.py:44
  66.9 11.2 %collective-permute-start.15 = (bf16[448,512]{1,0:T(8,128)(2,1)S(1)}, bf16[448,512]{1,0:T(8,128)(2,1)S(1)}, u32[]{:S(2)}, u32[]{:S(2)}) collective-permute-start(bf16[448,512]{1,0:T(8,128)(2,1)S(1)} %get-tuple-element.106), channel_id=1, source_target_pairs={{0,2},{2,0},{4,6},{6,4},{8,10},{10,8},{12,14},{14,12},{1,3},{3,1},... | collective-permute-start | bytes 1376264 | tf_op jit(solution)/shard_map/ppermute | solution.py:48
  78.1 3.3 %collective-permute-start.21 = (bf16[2,512,256]{2,1,0:T(8,128)(2,1)S(1)}, bf16[2,512,256]{2,1,0:T(8,128)(2,1)S(1)}, u32[]{:S(2)}, u32[]{:S(2)}) collective-permute-start(bf16[2,512,256]{2,1,0:T(8,128)(2,1)S(1)} %get-tuple-element.134.refs_0_), channel_id=1, source_target_pairs={{0,1},{1,0},{2,3},{3,2},{4,5},{5,4},{6,7},{7,6},{8,9},{9,8},{10,11... | collective-permute-start | bytes 1572872 | tf_op jit(solution)/shard_map/ppermute | solution.py:40
  78.1 7.1 %collective-permute-start.22 = (bf16[512,512]{1,0:T(8,128)(2,1)S(1)}, bf16[512,512]{1,0:T(8,128)(2,1)S(1)}, u32[]{:S(2)}, u32[]{:S(2)}) collective-permute-start(bf16[512,512]{1,0:T(8,128)(2,1)S(1)} %get-tuple-element.117.mixm_ref), channel_id=1, source_target_pairs={{0,1},{1,0},{2,3},{3,2},{4,5},{5,4},{6,7},{7,6},{8,9},{9,8},{10,11... | collective-permute-start | bytes 1572872 | tf_op jit(solution)/shard_map/ppermute | solution.py:40
  79.3 5.9 %collective-permute-start.20 = (bf16[2,256,512]{2,1,0:T(8,128)(2,1)S(1)}, bf16[2,256,512]{2,1,0:T(8,128)(2,1)S(1)}, u32[]{:S(2)}, u32[]{:S(2)}) collective-permute-start(bf16[2,256,512]{2,1,0:T(8,128)(2,1)S(1)} %bitcast.28), channel_id=1, source_target_pairs={{0,1},{1,0},{2,3},{3,2},{4,5},{5,4},{6,7},{7,6},{8,9},{9,8},{10,11... | collective-permute-start | bytes 1572872 | tf_op jit(solution)/shard_map/ppermute | solution.py:40
  79.4 13.6 %collective-permute-start.26 = (bf16[336,512]{1,0:T(8,128)(2,1)S(1)}, bf16[336,512]{1,0:T(8,128)(2,1)S(1)}, u32[]{:S(2)}, u32[]{:S(2)}) collective-permute-start(bf16[336,512]{1,0:T(8,128)(2,1)S(1)} %get-tuple-element.139), channel_id=1, source_target_pairs={{0,2},{2,0},{4,6},{6,4},{8,10},{10,8},{12,14},{14,12},{1,3},{3,1},... | collective-permute-start | bytes 1032200 | tf_op jit(solution)/shard_map/ppermute | solution.py:48
  80.9 12.0 %collective-permute-start.27 = (bf16[336,512]{1,0:T(8,128)(2,1)S(1)}, bf16[336,512]{1,0:T(8,128)(2,1)S(1)}, u32[]{:S(2)}, u32[]{:S(2)}) collective-permute-start(bf16[336,512]{1,0:T(8,128)(2,1)S(1)} %get-tuple-element.140), channel_id=1, source_target_pairs={{0,16},{16,0},{1,17},{17,1},{2,18},{18,2},{3,19},{19,3},{4,20},{20... | collective-permute-start | bytes 1032200 | tf_op jit(solution)/shard_map/ppermute | solution.py:44
  81.4 11.5 %collective-permute-start.25 = (bf16[224,512]{1,0:T(8,128)(2,1)S(1)}, bf16[224,512]{1,0:T(8,128)(2,1)S(1)}, u32[]{:S(2)}, u32[]{:S(2)}) collective-permute-start(bf16[224,512]{1,0:T(8,128)(2,1)S(1)} %get-tuple-element.138), channel_id=1, source_target_pairs={{0,4},{2,6},{4,8},{6,10},{8,12},{10,14},{12,0},{14,2},{1,5},{3,7},... | collective-permute-start | bytes 688136 | tf_op jit(solution)/shard_map/ppermute | solution.py:52
  88.2 3.1 %collective-permute-start.23 = (bf16[256,256]{1,0:T(8,128)(2,1)S(1)}, bf16[256,256]{1,0:T(8,128)(2,1)S(1)}, u32[]{:S(2)}, u32[]{:S(2)}) collective-permute-start(bf16[256,256]{1,0:T(8,128)(2,1)S(1)} %get-tuple-element.130.refs_0_), channel_id=1, source_target_pairs={{0,1},{1,0},{2,3},{3,2},{4,5},{5,4},{6,7},{7,6},{8,9},{9,8},{10,11... | collective-permute-start | bytes 393224 | tf_op jit(solution)/shard_map/ppermute | solution.py:40
  88.3 3.0 %collective-permute-start.24 = (bf16[256,256]{1,0:T(8,128)(2,1)S(1)}, bf16[256,256]{1,0:T(8,128)(2,1)S(1)}, u32[]{:S(2)}, u32[]{:S(2)}) collective-permute-start(bf16[256,256]{1,0:T(8,128)(2,1)S(1)} %get-tuple-element.131.refs_1_), channel_id=1, source_target_pairs={{0,1},{1,0},{2,3},{3,2},{4,5},{5,4},{6,7},{7,6},{8,9},{9,8},{10,11... | collective-permute-start | bytes 393224 | tf_op jit(solution)/shard_map/ppermute | solution.py:40
  96.1 1.6 %collective-permute-start.28 = (bf16[2,256,256]{2,1,0:T(8,128)(2,1)S(1)}, bf16[2,256,256]{2,1,0:T(8,128)(2,1)S(1)}, u32[]{:S(2)}, u32[]{:S(2)}) collective-permute-start(bf16[2,256,256]{2,1,0:T(8,128)(2,1)S(1)} %conv1.1.zm_ref), channel_id=1, source_target_pairs={{0,1},{1,0},{2,3},{3,2},{4,5},{5,4},{6,7},{7,6},{8,9},{9,8},{10,11... | collective-permute-start | bytes 786440 | tf_op jit(solution)/shard_map/ppermute | solution.py:40

commit v6 on v5

--- a/solution.py
+++ b/solution.py
@@ -140,34 +140,23 @@
         )
 
 
-def place_kernel(cfg, place, *refs):
-    conv_rows, mix_rows, pairs = cfg
-    wide, mix = refs[-2:]
-    for src, dst in weight_moves(place, refs[:-2], conv_rows, mix_rows, pairs, wide, mix):
-        dst[...] = src[...]
-
-
 def conv_slabs(cfg, place, hm, hp, wide, z_refs, acc):
     rows, half, branch, slabs = cfg
     c = place[2]
     at_m = pl.multiple_of(c * half, half)
     at_p = pl.multiple_of((1 - c) * half, half)
     for begin, size, taps in slabs:
-        for k, row in enumerate(taps):
-            for v in range(2):
-                part = jnp.dot(
-                    hm[v, row : row + size, :],
-                    wide[pl.ds(2 * half * k + at_m, half), :],
-                    preferred_element_type=F32,
-                ) + jnp.dot(
-                    hp[v, row : row + size, :],
-                    wide[pl.ds(2 * half * k + at_p, half), :],
-                    preferred_element_type=F32,
-                )
-                if k == 0:
-                    acc[v, 0:size, :] = part
-                else:
-                    acc[v, 0:size, :] += part
+        for v in range(2):
+            full = None
+            for k, row in enumerate(taps):
+                for h, at in ((hm, at_m), (hp, at_p)):
+                    part = jnp.dot(
+                        h[v, row : row + size, :],
+                        wide[pl.ds(2 * half * k + at, half), :],
+                        preferred_element_type=F32,
+                    )
+                    full = part if full is None else full + part
+            acc[v, 0:size, :] = full
         for r in range(0, size, rows):
             gate_into(
                 [z_ref.at[begin + r : begin + r + rows, :] for z_ref in z_refs],
@@ -224,25 +213,24 @@
         )
 
 
-def conv1_kernel(cfg, place, hm_near, hp_near, hm_far, hp_far, wide, z_ref, acc):
+def conv1_kernel(cfg, weight_cfg, place, hm_near, hp_near, hm_far, hp_far, *refs):
     rows, half, branch = cfg
+    z_ref, mix, wide, acc = refs[-4:]
+    for src, dst in weight_moves(place, refs[:-4], *weight_cfg, wide, mix):
+        dst[...] = src[...]
     c = place[2]
     at_m = pl.multiple_of(c * half, half)
     at_p = pl.multiple_of((1 - c) * half, half)
+    full = None
     for k in range(TAPS):
-        part = jnp.dot(
-            (hm_near[k] if k < 2 else hm_far[0]).reshape(2 * rows, half),
-            wide[pl.ds(2 * half * k + at_m, half), :],
-            preferred_element_type=F32,
-        ) + jnp.dot(
-            (hp_near[k] if k < 2 else hp_far[0]).reshape(2 * rows, half),
-            wide[pl.ds(2 * half * k + at_p, half), :],
-            preferred_element_type=F32,
-        )
-        if k == 0:
-            acc[...] = part
-        else:
-            acc[...] += part
+        for near_ref, far_ref, at in ((hm_near, hm_far, at_m), (hp_near, hp_far, at_p)):
+            part = jnp.dot(
+                (near_ref[k] if k < 2 else far_ref[0]).reshape(2 * rows, half),
+                wide[pl.ds(2 * half * k + at, half), :],
+                preferred_element_type=F32,
+            )
+            full = part if full is None else full + part
+    acc[...] = full
     gate_into((z_ref.at[0], z_ref.at[1]), acc[0:rows, :], acc[rows : 2 * rows, :], branch)
 
 
@@ -558,24 +546,20 @@
     hm1, hp1, state = mix0([za_mine], [za_theirs], used[:2], "mix0_near")
     hm, hp = mix0(z, [swap_chan(t) for t in z], used[2:], "mix0_far")
     hm, hp, hm1, hp1, *weights1 = lax.optimization_barrier((hm, hp, hm1, hp1, *weights1))
-    placed = pl.pallas_call(
-        functools.partial(place_kernel, (conv_rows, mix_rows, pairs1)),
-        out_shape=(near_out(wide_rows, 2 * branch), near_out(mix_whole, half)),
-        in_specs=[SMEM] + [VMEM] * len(weights1),
+    z_mine, mix_last = pl.pallas_call(
+        functools.partial(
+            conv1_kernel, (rows, half, branch), (conv_rows, mix_rows, pairs1)
+        ),
+        out_shape=(near_out(2, rows, branch), near_out(mix_whole, half)),
+        in_specs=[SMEM] + [VMEM] * (4 + len(weights1)),
         out_specs=(VMEM, VMEM),
-        compiler_params=scoped(2),
-        name="place",
-    )(place, *[near(w) for w in weights1])
-    wide, mix_last = placed
-    z_mine = pl.pallas_call(
-        functools.partial(conv1_kernel, (rows, half, branch)),
-        out_shape=near_out(2, rows, branch),
-        in_specs=[SMEM] + [VMEM] * 5,
-        out_specs=VMEM,
-        scratch_shapes=[pltpu.VMEM((2 * rows, 2 * branch), F32)],
-        compiler_params=scoped(8),
+        scratch_shapes=[
+            pltpu.VMEM((wide_rows, 2 * branch), BF16),
+            pltpu.VMEM((2 * rows, 2 * branch), F32),
+        ],
+        compiler_params=scoped(12),
         name="conv1",
-    )(place, hm1, hp1, hm, hp, wide)
+    )(place, hm1, hp1, hm, hp, *[near(w) for w in weights1])
     z_theirs = swap_chan(z_mine)
     return pl.pallas_call(
         functools.partial(mix1_kernel, (branch,)),

time: 99.6 us -> 99.1 us (level)
    pallas_call x2 -> x1, Pallas kernels: 3.16 us -> 2.62 us  [on_device(): pl.pallas_call(functools.partial(conv1_kernel, (rows, half, branch), (con...]
  transfers between devices with their start and end apart: 29 -> 29, of which waited for: 13 -> 13; matrix products, arithmetic and copies ran while one was open for 1% -> 1% of each run, Pallas kernels for 15% -> 16%
where the time goes in v6:
time: 99.1 us; the launch traced here: 98.9 us
  waiting for transfers between devices  46.2 us (47%)
  starting transfers between devices  27.3 us (28%)
  Pallas kernels  21.1 us (21%)
  local copies, waits for them, and re-layouts  2.5 us (3%)
    ppermute x7, waiting for transfers between devices, ring(): return lax.ppermute(block, 'seq', [(s, (s + by) % seq) for s in range(seq)])  22.1 us
    ppermute x6, waiting for transfers between devices, swap_pair(): return lax.ppermute(block, 'seq', [(s, s ^ 1) for s in range(seq)])  17.2 us
    ppermute x7, starting transfers between devices, ring(): return lax.ppermute(block, 'seq', [(s, (s + by) % seq) for s in range(seq)])  12.9 us
    ppermute x6, starting transfers between devices, swap_groups(): return lax.ppermute(block, 'groups', [(0, 1), (1, 0)])  7.59 us
    ppermute x6, starting transfers between devices, swap_pair(): return lax.ppermute(block, 'seq', [(s, s ^ 1) for s in range(seq)])  5.51 us
    ppermute x6, waiting for transfers between devices, swap_groups(): return lax.ppermute(block, 'groups', [(0, 1), (1, 0)])  4.27 us
    pallas_call x2, Pallas kernels, mix0(): pl.pallas_call(functools.partial(mix0_kernel, (rows, half, branch, 1, n,...  4.12 us
    pallas_call x1, Pallas kernels, newest(): pl.pallas_call(functools.partial(conv0_near_kernel, (rows, half, branch,...  4.02 us
  transfers between devices with their start and end apart: 29, of which 13 were waited for; matrix products, arithmetic and copies ran while one was open for 1% of the time, Pallas kernels for 16%

profile of v6, /device:TPU:0, one launch (start us, length us, event | category | flops | bytes accessed | tf_op | source)
XLA Modules:
  0.0 98.9 jit_solution(8663062567662273113)
XLA Ops:
  0.7 1.1 %copy-done = bf16[2,384,2,256]{3,2,1,0:T(2,128)(2,1)S(1)} copy-done((bf16[2,384,2,256]{3,2,1,0:T(2,128)(2,1)S(1)}, bf16[2,384,2,256]{3,2,1,0:T(2,128)(2,1)}, u32[]{:S(2)}) %copy-start) | copy-done | bytes 786456
  1.8 0.3 constant_dynamic-slice_fusion.1
  2.0 0.3 reshape.27
  2.3 0.9 constant_dynamic-slice_fusion
  3.2 3.0 %collective-permute-start.3 = (bf16[448,512]{1,0:T(8,128)(2,1)S(1)}, bf16[448,512]{1,0:T(8,128)(2,1)S(1)}, u32[]{:S(2)}, u32[]{:S(2)}) collective-permute-start(bf16[448,512]{1,0:T(8,128)(2,1)S(1)} %bitcast.17), channel_id=1, source_target_pairs={{0,16},{16,0},{1,17},{17,1},{2,18},{18,2},{3,19},{19,3},{4,20},{20... | collective-permute-start | bytes 1376264 | tf_op jit(solution)/shard_map/ppermute | solution.py:44
  6.2 1.5 %collective-permute-start.2 = (bf16[448,512]{1,0:T(8,128)(2,1)S(1)}, bf16[448,512]{1,0:T(8,128)(2,1)S(1)}, u32[]{:S(2)}, u32[]{:S(2)}) collective-permute-start(bf16[448,512]{1,0:T(8,128)(2,1)S(1)} %bitcast.18), channel_id=1, source_target_pairs={{0,2},{2,0},{4,6},{6,4},{8,10},{10,8},{12,14},{14,12},{1,3},{3,1},... | collective-permute-start | bytes 1376264 | tf_op jit(solution)/shard_map/ppermute | solution.py:48
  7.7 0.7 fusion.3
  8.4 3.6 %collective-permute-start.1 = (bf16[224,512]{1,0:T(8,128)(2,1)}, bf16[224,512]{1,0:T(8,128)(2,1)S(1)}, u32[]{:S(2)}, u32[]{:S(2)}) collective-permute-start(bf16[224,512]{1,0:T(8,128)(2,1)} %get-tuple-element.161), channel_id=1, source_target_pairs={{0,12},{2,14},{4,0},{6,2},{8,4},{10,6},{12,8},{14,10},{1,13},{3,15... | collective-permute-start | bytes 688136 | tf_op jit(solution)/shard_map/ppermute | solution.py:52
  12.2 6.2 %collective-permute-done.1.refs_2_.refs_8_ = bf16[224,512]{1,0:T(8,128)(2,1)S(1)} collective-permute-done((bf16[224,512]{1,0:T(8,128)(2,1)}, bf16[224,512]{1,0:T(8,128)(2,1)S(1)}, u32[]{:S(2)}, u32[]{:S(2)}) %collective-permute-start.1) | collective-permute-done | bytes 229408 | tf_op jit(solution)/shard_map/ppermute | solution.py:52
  18.4 4.0 %collective-permute-done.refs_0_.refs_7_ = bf16[224,512]{1,0:T(8,128)(2,1)S(1)} collective-permute-done((bf16[224,512]{1,0:T(8,128)(2,1)}, bf16[224,512]{1,0:T(8,128)(2,1)S(1)}, u32[]{:S(2)}, u32[]{:S(2)}) %collective-permute-start) | collective-permute-done | bytes 229408 | tf_op jit(solution)/shard_map/ppermute | solution.py:52
  22.4 0.7 pack.4
  23.1 1.7 %collective-permute-start.4 = (bf16[736,512]{1,0:T(8,128)(2,1)S(1)}, bf16[736,512]{1,0:T(8,128)(2,1)S(1)}, u32[]{:S(2)}, u32[]{:S(2)}) collective-permute-start(bf16[736,512]{1,0:T(8,128)(2,1)S(1)} %get-tuple-element.86), channel_id=1, source_target_pairs={{0,4},{2,6},{4,8},{6,10},{8,12},{10,14},{12,0},{14,2},{1,5},{3,7},... | collective-permute-start | bytes 2261000 | tf_op jit(solution)/shard_map/ppermute | solution.py:52
  24.8 0.5 collective-permute-start.5
  25.3 0.5 collective-permute-start.6
  25.8 1.2 %collective-permute-done.7.gp_ref = f32[2,512]{1,0:T(2,128)S(1)} collective-permute-done((f32[2,512]{1,0:T(2,128)S(1)}, f32[2,512]{1,0:T(2,128)S(1)}, u32[]{:S(2)}, u32[]{:S(2)}) %collective-permute-start.7) | collective-permute-done | bytes 4128 | tf_op jit(solution)/shard_map/ppermute | solution.py:40
  27.0 13.2 %collective-permute-done.5.refs_1_.refs_12_.refs_3_ = bf16[672,512]{1,0:T(8,128)(2,1)S(1)} collective-permute-done((bf16[672,512]{1,0:T(8,128)(2,1)S(1)}, bf16[672,512]{1,0:T(8,128)(2,1)S(1)}, u32[]{:S(2)}, u32[]{:S(2)}) %collective-permute-start.5) | collective-permute-done | bytes 688160 | tf_op jit(solution)/shard_map/ppermute | solution.py:48
  40.2 0.3 collective-permute-done.6.refs_13_
  40.5 1.6 %collective-permute-done.4.refs_2_.refs_11_ = bf16[736,512]{1,0:T(8,128)(2,1)S(1)} collective-permute-done((bf16[736,512]{1,0:T(8,128)(2,1)S(1)}, bf16[736,512]{1,0:T(8,128)(2,1)S(1)}, u32[]{:S(2)}, u32[]{:S(2)}) %collective-permute-start.4) | collective-permute-done | bytes 753696 | tf_op jit(solution)/shard_map/ppermute | solution.py:52
  42.0 0.8 pack.5
  42.8 0.6 collective-permute-start.10
  43.4 0.5 collective-permute-start.11
  43.9 3.8 %collective-permute-start.9 = (bf16[224,512]{1,0:T(8,128)(2,1)S(1)}, bf16[224,512]{1,0:T(8,128)(2,1)S(1)}, u32[]{:S(2)}, u32[]{:S(2)}) collective-permute-start(bf16[224,512]{1,0:T(8,128)(2,1)S(1)} %get-tuple-element.95), channel_id=1, source_target_pairs={{0,12},{2,14},{4,0},{6,2},{8,4},{10,6},{12,8},{14,10},{1,13},{3,15... | collective-permute-start | bytes 688136 | tf_op jit(solution)/shard_map/ppermute | solution.py:52
  47.7 10.4 %collective-permute-done.9.refs_2_.refs_5_ = bf16[224,512]{1,0:T(8,128)(2,1)S(1)} collective-permute-done((bf16[224,512]{1,0:T(8,128)(2,1)S(1)}, bf16[224,512]{1,0:T(8,128)(2,1)S(1)}, u32[]{:S(2)}, u32[]{:S(2)}) %collective-permute-start.9) | collective-permute-done | bytes 229408 | tf_op jit(solution)/shard_map/ppermute | solution.py:52
  58.1 0.9 collective-permute-done.10.refs_1_.refs_14_
  59.0 0.7 pack.6
  59.8 0.8 collective-permute-start.13
  60.6 1.5 %collective-permute-start.14 = (bf16[112,512]{1,0:T(8,128)(2,1)S(1)}, bf16[112,512]{1,0:T(8,128)(2,1)S(1)}, u32[]{:S(2)}, u32[]{:S(2)}) collective-permute-start(bf16[112,512]{1,0:T(8,128)(2,1)S(1)} %get-tuple-element.105), channel_id=1, source_target_pairs={{0,16},{16,0},{1,17},{17,1},{2,18},{18,2},{3,19},{19,3},{4,20},{20... | collective-permute-start | bytes 344072 | tf_op jit(solution)/shard_map/ppermute | solution.py:44
  62.1 2.5 %collective-permute-done.13.refs_0_ = bf16[112,512]{1,0:T(8,128)(2,1)S(1)} collective-permute-done((bf16[112,512]{1,0:T(8,128)(2,1)S(1)}, bf16[112,512]{1,0:T(8,128)(2,1)S(1)}, u32[]{:S(2)}, u32[]{:S(2)}) %collective-permute-start.13) | collective-permute-done | bytes 114720 | tf_op jit(solution)/shard_map/ppermute | solution.py:48
  64.7 0.7 collective-permute-done.14.refs_1_
  65.4 1.5 %collective-permute-start.16 = (bf16[448,512]{1,0:T(8,128)(2,1)S(1)}, bf16[448,512]{1,0:T(8,128)(2,1)S(1)}, u32[]{:S(2)}, u32[]{:S(2)}) collective-permute-start(bf16[448,512]{1,0:T(8,128)(2,1)S(1)} %get-tuple-element.106), channel_id=1, source_target_pairs={{0,16},{16,0},{1,17},{17,1},{2,18},{18,2},{3,19},{19,3},{4,20},{20... | collective-permute-start | bytes 1376264 | tf_op jit(solution)/shard_map/ppermute | solution.py:44
  66.9 0.5 collective-permute-start.15
  67.5 2.8 %ready.1 = (bf16[3072,512]{1,0:T(8,128)(2,1)S(1)}, bf16[512,512]{1,0:T(8,128)(2,1)S(1)}, bf16[2,1024,512]{2,1,0:T(8,128)(2,1)S(1)}, bf16[2,1024,512]{2,1,0:T(8,128)(2,1)S(1)}) custom-call(s32[3]{0:T(128)S(1)} %pad_add_fusion.place_ref.place, f32[2,512]{1,0:T(2,128)S(1)} %copy-done.1, f32[2,512]{1,0:T(2,128)S(1)} %collective-permute-done.7.gp_ref, ...), custom_call_target="tpu_custom_call" | custom-call | bytes 65536 | tf_op jit(solution)/shard_map/ready/pallas_call | solution.py:447
  70.3 4.0 %conv0_near.1 = (bf16[2,512,256]{2,1,0:T(8,128)(2,1)S(1)}, bf16[3072,512]{1,0:T(8,128)(2,1)S(1)}, bf16[512,512]{1,0:T(8,128)(2,1)S(1)}) custom-call(s32[3]{0:T(128)S(1)} %pad_add_fusion.place_ref.place, bf16[2,1024,512]{2,1,0:T(8,128)(2,1)S(1)} %get-tuple-element.126.hm._, ...), custom_call_target="tpu_custom_call", output_to_operand_aliasing={{1}: (5, {}), {2}: (6, {})} | custom-call | bytes 65536 | tf_op jit(solution)/shard_map/conv0_near/pallas_call | solution.py:471
  74.3 3.3 %collective-permute-done.16.refs_2_.refs_8_ = bf16[448,512]{1,0:T(8,128)(2,1)S(1)} collective-permute-done((bf16[448,512]{1,0:T(8,128)(2,1)S(1)}, bf16[448,512]{1,0:T(8,128)(2,1)S(1)}, u32[]{:S(2)}, u32[]{:S(2)}) %collective-permute-start.16) | collective-permute-done | bytes 458784 | tf_op jit(solution)/shard_map/ppermute | solution.py:44
  77.6 0.5 collective-permute-done.15.refs_3_.refs_7_
  78.1 0.5 collective-permute-start.22
  78.6 0.7 pack.7
  79.3 1.6 %collective-permute-start.26 = (bf16[336,512]{1,0:T(8,128)(2,1)S(1)}, bf16[336,512]{1,0:T(8,128)(2,1)S(1)}, u32[]{:S(2)}, u32[]{:S(2)}) collective-permute-start(bf16[336,512]{1,0:T(8,128)(2,1)S(1)} %get-tuple-element.139), channel_id=1, source_target_pairs={{0,2},{2,0},{4,6},{6,4},{8,10},{10,8},{12,14},{14,12},{1,3},{3,1},... | collective-permute-start | bytes 1032200 | tf_op jit(solution)/shard_map/ppermute | solution.py:48
  80.9 0.5 collective-permute-start.27
  81.4 3.7 %collective-permute-start.25 = (bf16[224,512]{1,0:T(8,128)(2,1)S(1)}, bf16[224,512]{1,0:T(8,128)(2,1)S(1)}, u32[]{:S(2)}, u32[]{:S(2)}) collective-permute-start(bf16[224,512]{1,0:T(8,128)(2,1)S(1)} %get-tuple-element.138), channel_id=1, source_target_pairs={{0,4},{2,6},{4,8},{6,10},{8,12},{10,14},{12,0},{14,2},{1,5},{3,7},... | collective-permute-start | bytes 688136 | tf_op jit(solution)/shard_map/ppermute | solution.py:52
  85.2 3.0 %conv0_far.1 = (bf16[256,256]{1,0:T(8,128)(2,1)S(1)}, bf16[256,256]{1,0:T(8,128)(2,1)S(1)}, bf16[2,1024,512]{2,1,0:T(8,128)(2,1)S(1)}, bf16[2,1024,512]{2,1,0:T(8,128)(2,1)S(1)}) custom-call(s32[3]{0:T(128)S(1)} %pad_add_fusion.place_ref.place, f32[2,512]{1,0:T(2,128)S(1)} %copy-done.1, ...), custom_call_target="tpu_custom_call", output_to_operand_aliasing={{2}: (6, {}), {3}: (7, {})} | custom-call | bytes 65536 | tf_op jit(solution)/shard_map/conv0_far/pallas_call | solution.py:506
  88.3 0.5 collective-permute-start.24
  88.8 2.5 %mix0_near.1 = (bf16[2,2,256,512]{3,2,1,0:T(8,128)(2,1)S(1)}, bf16[2,2,256,512]{3,2,1,0:T(8,128)(2,1)S(1)}, bf16[2,256,512]{2,1,0:T(8,128)(2,1)S(1)}) custom-call(s32[3]{0:T(128)S(1)} %pad_add_fusion.place_ref.place, f32[2,512]{1,0:T(2,128)S(1)} %copy-done.1, f32[2,512]{1,0:T(2,128)S(1)} %collective-permute-done.7.gp_ref, ...), custom_call_target="tpu_custom_call" | custom-call | bytes 65536 | tf_op jit(solution)/shard_map/mix0_near/pallas_call | solution.py:526
  91.3 1.6 %mix0_far.1 = (bf16[1,2,256,512]{3,2,1,0:T(8,128)(2,1)S(1)}, bf16[1,2,256,512]{3,2,1,0:T(8,128)(2,1)S(1)}) custom-call(s32[3]{0:T(128)S(1)} %pad_add_fusion.place_ref.place, f32[2,512]{1,0:T(2,128)S(1)} %copy-done.1, f32[2,512]{1,0:T(2,128)S(1)} %collective-permute-done.7.gp_ref, bf16[512,512]{1,0:T(8,128)(2,1)S(1)} %get-tuple-element.117.mixm_ref, ...), custom_call_target="tpu_custom_call" | custom-call | bytes 65536 | tf_op jit(solution)/shard_map/mix0_far/pallas_call | solution.py:526
  92.9 2.6 %conv1.1 = (bf16[2,256,256]{2,1,0:T(8,128)(2,1)S(1)}, bf16[512,512]{1,0:T(8,128)(2,1)S(1)}) custom-call(s32[3]{0:T(128)S(1)} %pad_add_fusion.place_ref.place, bf16[2,2,256,512]{3,2,1,0:T(8,128)(2,1)S(1)} %get-tuple-element.141.hm_near, bf16[2,2,256,512]{3,2,1,0:T(8,128)(2,1)S(1)} %get-tuple-element.142.hp_near, ...), custom_call_target="tpu_custom_call" | custom-call | tf_op jit(solution)/shard_map/conv1/pallas_call | solution.py:549
  95.6 0.1 collective-permute-start.28
  95.7 1.5 %collective-permute-done.28.zp_ref = bf16[2,256,256]{2,1,0:T(8,128)(2,1)S(1)} collective-permute-done((bf16[2,256,256]{2,1,0:T(8,128)(2,1)S(1)}, bf16[2,256,256]{2,1,0:T(8,128)(2,1)S(1)}, u32[]{:S(2)}, u32[]{:S(2)}) %collective-permute-start.28) | collective-permute-done | bytes 262176 | tf_op jit(solution)/shard_map/ppermute | solution.py:40
  97.2 1.7 %mix1.1 = (bf16[256,512]{1,0:T(8,128)(2,1)}, bf16[256,512]{1,0:T(8,128)(2,1)}) custom-call(s32[3]{0:T(128)S(1)} %pad_add_fusion.place_ref.place, bf16[2,256,256]{2,1,0:T(8,128)(2,1)S(1)} %get-tuple-element.157.zm_ref, bf16[2,256,256]{2,1,0:T(8,128)(2,1)S(1)} %collective-permute-done.28.zp_ref, bf16[512,512]{1,0:T(8,128)(2,1)S(1)} %get-tuple-element.158.mix_ref, ...), custom_call_target="tpu_custom_call" | custom-call | tf_op jit(solution)/shard_map/mix1/pallas_call | solution.py:564
  (36 shorter events, 0.4 us)
Async XLA Ops:
  0.6 1.1 %copy-start = (bf16[2,384,2,256]{3,2,1,0:T(2,128)(2,1)S(1)}, bf16[2,384,2,256]{3,2,1,0:T(2,128)(2,1)}, u32[]{:S(2)}) copy-start(bf16[2,384,2,256]{3,2,1,0:T(2,128)(2,1)} %param.8) | copy-start | bytes 2359300
  0.6 11.5 %copy-start.2 = (bf16[256,512]{1,0:T(8,128)(2,1)S(1)}, bf16[256,512]{1,0:T(8,128)(2,1)}, u32[]{:S(2)}) copy-start(bf16[256,512]{1,0:T(8,128)(2,1)} %param.6) | copy-start | bytes 786436
  0.7 11.5 %copy-start.3 = (bf16[256,512]{1,0:T(8,128)(2,1)S(1)}, bf16[256,512]{1,0:T(8,128)(2,1)}, u32[]{:S(2)}) copy-start(bf16[256,512]{1,0:T(8,128)(2,1)} %param.5) | copy-start | bytes 786436
  3.2 22.6 %copy-start.1 = (f32[2,512]{1,0:T(2,128)S(1)}, f32[2,512]{1,0:T(2,128)}, u32[]{:S(2)}) copy-start(f32[2,512]{1,0:T(2,128)} %gm_ref.7) | copy-start | bytes 12292
  3.2 19.2 %collective-permute-start.3 = (bf16[448,512]{1,0:T(8,128)(2,1)S(1)}, bf16[448,512]{1,0:T(8,128)(2,1)S(1)}, u32[]{:S(2)}, u32[]{:S(2)}) collective-permute-start(bf16[448,512]{1,0:T(8,128)(2,1)S(1)} %bitcast.17), channel_id=1, source_target_pairs={{0,16},{16,0},{1,17},{17,1},{2,18},{18,2},{3,19},{19,3},{4,20},{20... | collective-permute-start | bytes 1376264 | tf_op jit(solution)/shard_map/ppermute | solution.py:44
  6.2 16.2 %collective-permute-start.2 = (bf16[448,512]{1,0:T(8,128)(2,1)S(1)}, bf16[448,512]{1,0:T(8,128)(2,1)S(1)}, u32[]{:S(2)}, u32[]{:S(2)}) collective-permute-start(bf16[448,512]{1,0:T(8,128)(2,1)S(1)} %bitcast.18), channel_id=1, source_target_pairs={{0,2},{2,0},{4,6},{6,4},{8,10},{10,8},{12,14},{14,12},{1,3},{3,1},... | collective-permute-start | bytes 1376264 | tf_op jit(solution)/shard_map/ppermute | solution.py:48
  8.4 10.0 %collective-permute-start.1 = (bf16[224,512]{1,0:T(8,128)(2,1)}, bf16[224,512]{1,0:T(8,128)(2,1)S(1)}, u32[]{:S(2)}, u32[]{:S(2)}) collective-permute-start(bf16[224,512]{1,0:T(8,128)(2,1)} %get-tuple-element.161), channel_id=1, source_target_pairs={{0,12},{2,14},{4,0},{6,2},{8,4},{10,6},{12,8},{14,10},{1,13},{3,15... | collective-permute-start | bytes 688136 | tf_op jit(solution)/shard_map/ppermute | solution.py:52
  12.0 10.3 %collective-permute-start = (bf16[224,512]{1,0:T(8,128)(2,1)}, bf16[224,512]{1,0:T(8,128)(2,1)S(1)}, u32[]{:S(2)}, u32[]{:S(2)}) collective-permute-start(bf16[224,512]{1,0:T(8,128)(2,1)} %get-tuple-element.161), channel_id=1, source_target_pairs={{0,4},{2,6},{4,8},{6,10},{8,12},{10,14},{12,0},{14,2},{1,5},{3,7},... | collective-permute-start | bytes 688136 | tf_op jit(solution)/shard_map/ppermute | solution.py:52
  23.1 18.9 %collective-permute-start.4 = (bf16[736,512]{1,0:T(8,128)(2,1)S(1)}, bf16[736,512]{1,0:T(8,128)(2,1)S(1)}, u32[]{:S(2)}, u32[]{:S(2)}) collective-permute-start(bf16[736,512]{1,0:T(8,128)(2,1)S(1)} %get-tuple-element.86), channel_id=1, source_target_pairs={{0,4},{2,6},{4,8},{6,10},{8,12},{10,14},{12,0},{14,2},{1,5},{3,7},... | collective-permute-start | bytes 2261000 | tf_op jit(solution)/shard_map/ppermute | solution.py:52
  24.8 15.5 %collective-permute-start.5 = (bf16[672,512]{1,0:T(8,128)(2,1)S(1)}, bf16[672,512]{1,0:T(8,128)(2,1)S(1)}, u32[]{:S(2)}, u32[]{:S(2)}) collective-permute-start(bf16[672,512]{1,0:T(8,128)(2,1)S(1)} %get-tuple-element.87), channel_id=1, source_target_pairs={{0,2},{2,0},{4,6},{6,4},{8,10},{10,8},{12,14},{14,12},{1,3},{3,1},... | collective-permute-start | bytes 2064392 | tf_op jit(solution)/shard_map/ppermute | solution.py:48
  25.3 15.2 %collective-permute-start.6 = (bf16[672,512]{1,0:T(8,128)(2,1)S(1)}, bf16[672,512]{1,0:T(8,128)(2,1)S(1)}, u32[]{:S(2)}, u32[]{:S(2)}) collective-permute-start(bf16[672,512]{1,0:T(8,128)(2,1)S(1)} %get-tuple-element.88), channel_id=1, source_target_pairs={{0,16},{16,0},{1,17},{17,1},{2,18},{18,2},{3,19},{19,3},{4,20},{20... | collective-permute-start | bytes 2064392 | tf_op jit(solution)/shard_map/ppermute | solution.py:44
  25.8 1.2 %collective-permute-start.7 = (f32[2,512]{1,0:T(2,128)S(1)}, f32[2,512]{1,0:T(2,128)S(1)}, u32[]{:S(2)}, u32[]{:S(2)}) collective-permute-start(f32[2,512]{1,0:T(2,128)S(1)} %copy-done.1), channel_id=1, source_target_pairs={{0,1},{1,0},{2,3},{3,2},{4,5},{5,4},{6,7},{7,6},{8,9},{9,8},{10,11... | collective-permute-start | bytes 12296 | tf_op jit(solution)/shard_map/ppermute | solution.py:40
  42.8 16.2 %collective-permute-start.10 = (bf16[736,512]{1,0:T(8,128)(2,1)S(1)}, bf16[736,512]{1,0:T(8,128)(2,1)S(1)}, u32[]{:S(2)}, u32[]{:S(2)}) collective-permute-start(bf16[736,512]{1,0:T(8,128)(2,1)S(1)} %get-tuple-element.96), channel_id=1, source_target_pairs={{0,2},{2,0},{4,6},{6,4},{8,10},{10,8},{12,14},{14,12},{1,3},{3,1},... | collective-permute-start | bytes 2261000 | tf_op jit(solution)/shard_map/ppermute | solution.py:48
  43.4 14.7 %collective-permute-start.11 = (bf16[672,512]{1,0:T(8,128)(2,1)S(1)}, bf16[672,512]{1,0:T(8,128)(2,1)S(1)}, u32[]{:S(2)}, u32[]{:S(2)}) collective-permute-start(bf16[672,512]{1,0:T(8,128)(2,1)S(1)} %get-tuple-element.97), channel_id=1, source_target_pairs={{0,16},{16,0},{1,17},{17,1},{2,18},{18,2},{3,19},{19,3},{4,20},{20... | collective-permute-start | bytes 2064392 | tf_op jit(solution)/shard_map/ppermute | solution.py:44
  43.9 14.2 %collective-permute-start.8 = (bf16[448,512]{1,0:T(8,128)(2,1)S(1)}, bf16[448,512]{1,0:T(8,128)(2,1)S(1)}, u32[]{:S(2)}, u32[]{:S(2)}) collective-permute-start(bf16[448,512]{1,0:T(8,128)(2,1)S(1)} %get-tuple-element.94), channel_id=1, source_target_pairs={{0,4},{2,6},{4,8},{6,10},{8,12},{10,14},{12,0},{14,2},{1,5},{3,7},... | collective-permute-start | bytes 1376264 | tf_op jit(solution)/shard_map/ppermute | solution.py:52
  43.9 14.2 %collective-permute-start.9 = (bf16[224,512]{1,0:T(8,128)(2,1)S(1)}, bf16[224,512]{1,0:T(8,128)(2,1)S(1)}, u32[]{:S(2)}, u32[]{:S(2)}) collective-permute-start(bf16[224,512]{1,0:T(8,128)(2,1)S(1)} %get-tuple-element.95), channel_id=1, source_target_pairs={{0,12},{2,14},{4,0},{6,2},{8,4},{10,6},{12,8},{14,10},{1,13},{3,15... | collective-permute-start | bytes 688136 | tf_op jit(solution)/shard_map/ppermute | solution.py:52
  47.7 19.2 %collective-permute-start.17 = (bf16[2,256,512]{2,1,0:T(8,128)(2,1)S(1)}, bf16[2,256,512]{2,1,0:T(8,128)(2,1)S(1)}, u32[]{:S(2)}, u32[]{:S(2)}) collective-permute-start(bf16[2,256,512]{2,1,0:T(8,128)(2,1)S(1)} %pad_maximum_fusion.1), channel_id=1, source_target_pairs={{0,1},{1,0},{2,3},{3,2},{4,5},{5,4},{6,7},{7,6},{8,9},{9,8},{10,11... | collective-permute-start | bytes 1572872 | tf_op jit(solution)/shard_map/ppermute | solution.py:40
  59.8 18.3 %collective-permute-start.12 = (bf16[736,512]{1,0:T(8,128)(2,1)S(1)}, bf16[736,512]{1,0:T(8,128)(2,1)S(1)}, u32[]{:S(2)}, u32[]{:S(2)}) collective-permute-start(bf16[736,512]{1,0:T(8,128)(2,1)S(1)} %get-tuple-element.102), channel_id=1, source_target_pairs={{0,4},{2,6},{4,8},{6,10},{8,12},{10,14},{12,0},{14,2},{1,5},{3,7},... | collective-permute-start | bytes 2261000 | tf_op jit(solution)/shard_map/ppermute | solution.py:52
  59.8 4.9 %collective-permute-start.13 = (bf16[112,512]{1,0:T(8,128)(2,1)S(1)}, bf16[112,512]{1,0:T(8,128)(2,1)S(1)}, u32[]{:S(2)}, u32[]{:S(2)}) collective-permute-start(bf16[112,512]{1,0:T(8,128)(2,1)S(1)} %get-tuple-element.104), channel_id=1, source_target_pairs={{0,2},{2,0},{4,6},{6,4},{8,10},{10,8},{12,14},{14,12},{1,3},{3,1},... | collective-permute-start | bytes 344072 | tf_op jit(solution)/shard_map/ppermute | solution.py:48
  60.6 4.8 %collective-permute-start.14 = (bf16[112,512]{1,0:T(8,128)(2,1)S(1)}, bf16[112,512]{1,0:T(8,128)(2,1)S(1)}, u32[]{:S(2)}, u32[]{:S(2)}) collective-permute-start(bf16[112,512]{1,0:T(8,128)(2,1)S(1)} %get-tuple-element.105), channel_id=1, source_target_pairs={{0,16},{16,0},{1,17},{17,1},{2,18},{18,2},{3,19},{19,3},{4,20},{20... | collective-permute-start | bytes 344072 | tf_op jit(solution)/shard_map/ppermute | solution.py:44
  62.1 5.3 %collective-permute-start.19 = (bf16[2,256,512]{2,1,0:T(8,128)(2,1)S(1)}, bf16[2,256,512]{2,1,0:T(8,128)(2,1)S(1)}, u32[]{:S(2)}, u32[]{:S(2)}) collective-permute-start(bf16[2,256,512]{2,1,0:T(8,128)(2,1)S(1)} %bitcast.25), channel_id=1, source_target_pairs={{0,1},{1,0},{2,3},{3,2},{4,5},{5,4},{6,7},{7,6},{8,9},{9,8},{10,11... | collective-permute-start | bytes 1572872 | tf_op jit(solution)/shard_map/ppermute | solution.py:40
  64.7 2.8 %collective-permute-start.18 = (bf16[2,256,512]{2,1,0:T(8,128)(2,1)S(1)}, bf16[2,256,512]{2,1,0:T(8,128)(2,1)S(1)}, u32[]{:S(2)}, u32[]{:S(2)}) collective-permute-start(bf16[2,256,512]{2,1,0:T(8,128)(2,1)S(1)} %bitcast.22), channel_id=1, source_target_pairs={{0,1},{1,0},{2,3},{3,2},{4,5},{5,4},{6,7},{7,6},{8,9},{9,8},{10,11... | collective-permute-start | bytes 1572872 | tf_op jit(solution)/shard_map/ppermute | solution.py:40
  65.4 12.2 %collective-permute-start.16 = (bf16[448,512]{1,0:T(8,128)(2,1)S(1)}, bf16[448,512]{1,0:T(8,128)(2,1)S(1)}, u32[]{:S(2)}, u32[]{:S(2)}) collective-permute-start(bf16[448,512]{1,0:T(8,128)(2,1)S(1)} %get-tuple-element.106), channel_id=1, source_target_pairs={{0,16},{16,0},{1,17},{17,1},{2,18},{18,2},{3,19},{19,3},{4,20},{20... | collective-permute-start | bytes 1376264 | tf_op jit(solution)/shard_map/ppermute | solution.py:44
  66.9 11.2 %collective-permute-start.15 = (bf16[448,512]{1,0:T(8,128)(2,1)S(1)}, bf16[448,512]{1,0:T(8,128)(2,1)S(1)}, u32[]{:S(2)}, u32[]{:S(2)}) collective-permute-start(bf16[448,512]{1,0:T(8,128)(2,1)S(1)} %get-tuple-element.106), channel_id=1, source_target_pairs={{0,2},{2,0},{4,6},{6,4},{8,10},{10,8},{12,14},{14,12},{1,3},{3,1},... | collective-permute-start | bytes 1376264 | tf_op jit(solution)/shard_map/ppermute | solution.py:48
  78.1 3.3 %collective-permute-start.21 = (bf16[2,512,256]{2,1,0:T(8,128)(2,1)S(1)}, bf16[2,512,256]{2,1,0:T(8,128)(2,1)S(1)}, u32[]{:S(2)}, u32[]{:S(2)}) collective-permute-start(bf16[2,512,256]{2,1,0:T(8,128)(2,1)S(1)} %get-tuple-element.134.refs_0_), channel_id=1, source_target_pairs={{0,1},{1,0},{2,3},{3,2},{4,5},{5,4},{6,7},{7,6},{8,9},{9,8},{10,11... | collective-permute-start | bytes 1572872 | tf_op jit(solution)/shard_map/ppermute | solution.py:40
  78.1 7.1 %collective-permute-start.22 = (bf16[512,512]{1,0:T(8,128)(2,1)S(1)}, bf16[512,512]{1,0:T(8,128)(2,1)S(1)}, u32[]{:S(2)}, u32[]{:S(2)}) collective-permute-start(bf16[512,512]{1,0:T(8,128)(2,1)S(1)} %get-tuple-element.117.mixm_ref), channel_id=1, source_target_pairs={{0,1},{1,0},{2,3},{3,2},{4,5},{5,4},{6,7},{7,6},{8,9},{9,8},{10,11... | collective-permute-start | bytes 1572872 | tf_op jit(solution)/shard_map/ppermute | solution.py:40
  79.3 5.9 %collective-permute-start.20 = (bf16[2,256,512]{2,1,0:T(8,128)(2,1)S(1)}, bf16[2,256,512]{2,1,0:T(8,128)(2,1)S(1)}, u32[]{:S(2)}, u32[]{:S(2)}) collective-permute-start(bf16[2,256,512]{2,1,0:T(8,128)(2,1)S(1)} %bitcast.28), channel_id=1, source_target_pairs={{0,1},{1,0},{2,3},{3,2},{4,5},{5,4},{6,7},{7,6},{8,9},{9,8},{10,11... | collective-permute-start | bytes 1572872 | tf_op jit(solution)/shard_map/ppermute | solution.py:40
  79.3 13.6 %collective-permute-start.26 = (bf16[336,512]{1,0:T(8,128)(2,1)S(1)}, bf16[336,512]{1,0:T(8,128)(2,1)S(1)}, u32[]{:S(2)}, u32[]{:S(2)}) collective-permute-start(bf16[336,512]{1,0:T(8,128)(2,1)S(1)} %get-tuple-element.139), channel_id=1, source_target_pairs={{0,2},{2,0},{4,6},{6,4},{8,10},{10,8},{12,14},{14,12},{1,3},{3,1},... | collective-permute-start | bytes 1032200 | tf_op jit(solution)/shard_map/ppermute | solution.py:48
  80.9 12.0 %collective-permute-start.27 = (bf16[336,512]{1,0:T(8,128)(2,1)S(1)}, bf16[336,512]{1,0:T(8,128)(2,1)S(1)}, u32[]{:S(2)}, u32[]{:S(2)}) collective-permute-start(bf16[336,512]{1,0:T(8,128)(2,1)S(1)} %get-tuple-element.140), channel_id=1, source_target_pairs={{0,16},{16,0},{1,17},{17,1},{2,18},{18,2},{3,19},{19,3},{4,20},{20... | collective-permute-start | bytes 1032200 | tf_op jit(solution)/shard_map/ppermute | solution.py:44
  81.4 11.5 %collective-permute-start.25 = (bf16[224,512]{1,0:T(8,128)(2,1)S(1)}, bf16[224,512]{1,0:T(8,128)(2,1)S(1)}, u32[]{:S(2)}, u32[]{:S(2)}) collective-permute-start(bf16[224,512]{1,0:T(8,128)(2,1)S(1)} %get-tuple-element.138), channel_id=1, source_target_pairs={{0,4},{2,6},{4,8},{6,10},{8,12},{10,14},{12,0},{14,2},{1,5},{3,7},... | collective-permute-start | bytes 688136 | tf_op jit(solution)/shard_map/ppermute | solution.py:52
  88.2 3.1 %collective-permute-start.23 = (bf16[256,256]{1,0:T(8,128)(2,1)S(1)}, bf16[256,256]{1,0:T(8,128)(2,1)S(1)}, u32[]{:S(2)}, u32[]{:S(2)}) collective-permute-start(bf16[256,256]{1,0:T(8,128)(2,1)S(1)} %get-tuple-element.130.refs_0_), channel_id=1, source_target_pairs={{0,1},{1,0},{2,3},{3,2},{4,5},{5,4},{6,7},{7,6},{8,9},{9,8},{10,11... | collective-permute-start | bytes 393224 | tf_op jit(solution)/shard_map/ppermute | solution.py:40
  88.3 3.0 %collective-permute-start.24 = (bf16[256,256]{1,0:T(8,128)(2,1)S(1)}, bf16[256,256]{1,0:T(8,128)(2,1)S(1)}, u32[]{:S(2)}, u32[]{:S(2)}) collective-permute-start(bf16[256,256]{1,0:T(8,128)(2,1)S(1)} %get-tuple-element.131.refs_1_), channel_id=1, source_target_pairs={{0,1},{1,0},{2,3},{3,2},{4,5},{5,4},{6,7},{7,6},{8,9},{9,8},{10,11... | collective-permute-start | bytes 393224 | tf_op jit(solution)/shard_map/ppermute | solution.py:40
  95.6 1.6 %collective-permute-start.28 = (bf16[2,256,256]{2,1,0:T(8,128)(2,1)S(1)}, bf16[2,256,256]{2,1,0:T(8,128)(2,1)S(1)}, u32[]{:S(2)}, u32[]{:S(2)}) collective-permute-start(bf16[2,256,256]{2,1,0:T(8,128)(2,1)S(1)} %get-tuple-element.157.zm_ref), channel_id=1, source_target_pairs={{0,1},{1,0},{2,3},{3,2},{4,5},{5,4},{6,7},{7,6},{8,9},{9,8},{10,11... | collective-permute-start | bytes 786440 | tf_op jit(solution)/shard_map/ppermute | solution.py:40

commit v7 on v6

--- a/solution.py
+++ b/solution.py
@@ -333,7 +333,9 @@
         [(z1a, 0, unit), (z1b, 0, unit), (y1, unit, unit)],
         [(z1a, 0, unit), (z1b, 0, unit), (x1, 0, unit)],
     )
-    z2, x2, y2, own, c1, gains_p = together(z(to_z), x(to_x), y(to_y), own, c1, swap_chan(gains))
+    z2, x2, y2, own, c1, gains_p, own_p = together(
+        z(to_z), x(to_x), y(to_y), own, c1, swap_chan(gains), swap_chan(own)
+    )
     keep(0, z2, (0, 0, unit, 2, 0, 0))
     whole(0, x2, (1, 1, 0), (3, 1, 0))
     keep(1, x2, (2 * unit, 0, unit, 0, 1, 1))
@@ -361,10 +363,11 @@
         [(x3, cut, unit - cut)],
         [(x3, unit, tall, 0)],
     )
-    first = ready(gains_p, (own, one, two), pieces[0], (seq, tuple(order[0])))
+    x4a, y4a = x(w_x), y(w_y)
+    halo = (own, one, two), (own_p, swap_chan(one), swap_chan(two))
+    first = ready(gains_p, halo, pieces[0], (seq, tuple(order[0])))
     pieces[0].clear()
     order[0].clear()
-    x4a, y4a = x(w_x), y(w_y)
     keep(0, x4a, (0, 0, cut, 2, 1, 1))
     keep(0, y4a, (0, cut, unit - cut, 2, 1, 1))
     made = newest(first, pieces[0], (seq, tuple(order[0])))
@@ -440,10 +443,9 @@
     mine, theirs = [], []
 
     def ready(gains_p, halo, pieces, pairs):
-        for block in halo:
-            mine.append(block.reshape(own.shape))
-            theirs.append(swap_chan(mine[-1]))
-        cfg = (rows, tall, len(halo), conv_rows, mix_rows, pairs)
+        mine.extend(block.reshape(own.shape) for block in halo[0])
+        theirs.extend(block.reshape(own.shape) for block in halo[1])
+        cfg = (rows, tall, len(mine), conv_rows, mix_rows, pairs)
         return pl.pallas_call(
             functools.partial(ready_kernel, cfg),
             out_shape=(
@@ -452,7 +454,7 @@
                 near_out(2, tall, half),
                 near_out(2, tall, half),
             ),
-            in_specs=[SMEM] + [VMEM] * (2 + 2 * len(halo) + len(pieces)),
+            in_specs=[SMEM] + [VMEM] * (2 + 2 * len(mine) + len(pieces)),
             out_specs=(VMEM,) * 4,
             compiler_params=scoped(4),
             cost_estimate=cost(0, 2**16),
@@ -496,7 +498,9 @@
     else:
         gains_p = swap_chan(gains)
         halo = [from_behind(own, seq, k * (lag // rows)) for k in range(1, 7)]
-        made = newest(ready(gains_p, (own, *halo[:-1]), weights[0], None), [], None)
+        newer = (own, *halo[:-1])
+        newer = newer, tuple(swap_chan(block) for block in newer)
+        made = newest(ready(gains_p, newer, weights[0], None), [], None)
         last, beside, weights1, pairs1 = halo[-1], (), weights[1], None
     za_mine, mix_mine, wide, hm, hp = made
     last_theirs, za_theirs, mix_theirs = lax.optimization_barrier(

time: 99.1 us -> 96.3 us (0.972)
  waiting for transfers between devices: 46.2 us -> 43.5 us
    ppermute x6, waiting for transfers between devices: 4.27 us -> 1.44 us  [swap_groups(): return lax.ppermute(block, 'groups', [(0, 1), (1, 0)])]
    ppermute x6, starting transfers between devices: 7.59 us -> 9.56 us  [swap_groups(): return lax.ppermute(block, 'groups', [(0, 1), (1, 0)])]
    ppermute x7, starting transfers between devices: 12.9 us -> 11.2 us  [ring(): return lax.ppermute(block, 'seq', [(s, (s + by) % seq) for s in range(seq)])]
    ppermute x6, starting transfers between devices: 5.51 us -> 4.22 us  [swap_pair(): return lax.ppermute(block, 'seq', [(s, s ^ 1) for s in range(seq)])]
    ppermute x10, starting transfers between devices: 1.31 us -> 2.31 us  [swap_chan(): return lax.ppermute(block, 'chan', [(0, 1), (1, 0)])]
  transfers between devices with their start and end apart: 29 -> 29, of which waited for: 13 -> 14; matrix products, arithmetic and copies ran while one was open for 1% -> 1% of each run, Pallas kernels for 16% -> 15%
where the time goes in v7:
time: 96.3 us; the launch traced here: 96.2 us
  waiting for transfers between devices  43.5 us (45%)
  starting transfers between devices  27.3 us (28%)
  Pallas kernels  21.1 us (22%)
  local copies, waits for them, and re-layouts  2.5 us (3%)
    ppermute x7, waiting for transfers between devices, ring(): return lax.ppermute(block, 'seq', [(s, (s + by) % seq) for s in range(seq)])  22.5 us
    ppermute x6, waiting for transfers between devices, swap_pair(): return lax.ppermute(block, 'seq', [(s, s ^ 1) for s in range(seq)])  16.7 us
    ppermute x7, starting transfers between devices, ring(): return lax.ppermute(block, 'seq', [(s, (s + by) % seq) for s in range(seq)])  11.2 us
    ppermute x6, starting transfers between devices, swap_groups(): return lax.ppermute(block, 'groups', [(0, 1), (1, 0)])  9.56 us
    ppermute x6, starting transfers between devices, swap_pair(): return lax.ppermute(block, 'seq', [(s, s ^ 1) for s in range(seq)])  4.22 us
    pallas_call x2, Pallas kernels, mix0(): pl.pallas_call(functools.partial(mix0_kernel, (rows, half, branch, 1, n,...  4.12 us
    pallas_call x1, Pallas kernels, newest(): pl.pallas_call(functools.partial(conv0_near_kernel, (rows, half, branch,...  4.02 us
    pallas_call x1, Pallas kernels, on_device(): pl.pallas_call(functools.partial(conv0_far_kernel, (rows, half, branch, f...  3.01 us
  transfers between devices with their start and end apart: 29, of which 14 were waited for; matrix products, arithmetic and copies ran while one was open for 1% of the time, Pallas kernels for 15%

profile of v7, /device:TPU:0, one launch (start us, length us, event | category | flops | bytes accessed | tf_op | source)
XLA Modules:
  0.0 96.2 jit_solution(15552514786029251095)
XLA Ops:
  0.7 1.1 %copy-done = bf16[2,384,2,256]{3,2,1,0:T(2,128)(2,1)S(1)} copy-done((bf16[2,384,2,256]{3,2,1,0:T(2,128)(2,1)S(1)}, bf16[2,384,2,256]{3,2,1,0:T(2,128)(2,1)}, u32[]{:S(2)}) %copy-start) | copy-done | bytes 786456
  1.8 0.3 constant_dynamic-slice_fusion.1
  2.3 0.9 constant_dynamic-slice_fusion
  3.2 3.0 %collective-permute-start.3 = (bf16[448,512]{1,0:T(8,128)(2,1)S(1)}, bf16[448,512]{1,0:T(8,128)(2,1)S(1)}, u32[]{:S(2)}, u32[]{:S(2)}) collective-permute-start(bf16[448,512]{1,0:T(8,128)(2,1)S(1)} %bitcast.21), channel_id=1, source_target_pairs={{0,16},{16,0},{1,17},{17,1},{2,18},{18,2},{3,19},{19,3},{4,20},{20... | collective-permute-start | bytes 1376264 | tf_op jit(solution)/shard_map/ppermute | solution.py:44
  6.2 1.5 %collective-permute-start.2 = (bf16[448,512]{1,0:T(8,128)(2,1)S(1)}, bf16[448,512]{1,0:T(8,128)(2,1)S(1)}, u32[]{:S(2)}, u32[]{:S(2)}) collective-permute-start(bf16[448,512]{1,0:T(8,128)(2,1)S(1)} %bitcast.22), channel_id=1, source_target_pairs={{0,2},{2,0},{4,6},{6,4},{8,10},{10,8},{12,14},{14,12},{1,3},{3,1},... | collective-permute-start | bytes 1376264 | tf_op jit(solution)/shard_map/ppermute | solution.py:48
  7.7 0.7 fusion.3
  8.4 3.6 %collective-permute-start.1 = (bf16[224,512]{1,0:T(8,128)(2,1)}, bf16[224,512]{1,0:T(8,128)(2,1)S(1)}, u32[]{:S(2)}, u32[]{:S(2)}) collective-permute-start(bf16[224,512]{1,0:T(8,128)(2,1)} %get-tuple-element.163), channel_id=1, source_target_pairs={{0,12},{2,14},{4,0},{6,2},{8,4},{10,6},{12,8},{14,10},{1,13},{3,15... | collective-permute-start | bytes 688136 | tf_op jit(solution)/shard_map/ppermute | solution.py:52
  12.2 6.2 %collective-permute-done.1.refs_2_.refs_8_ = bf16[224,512]{1,0:T(8,128)(2,1)S(1)} collective-permute-done((bf16[224,512]{1,0:T(8,128)(2,1)}, bf16[224,512]{1,0:T(8,128)(2,1)S(1)}, u32[]{:S(2)}, u32[]{:S(2)}) %collective-permute-start.1) | collective-permute-done | bytes 229408 | tf_op jit(solution)/shard_map/ppermute | solution.py:52
  18.4 4.0 %collective-permute-done.refs_0_.refs_7_ = bf16[224,512]{1,0:T(8,128)(2,1)S(1)} collective-permute-done((bf16[224,512]{1,0:T(8,128)(2,1)}, bf16[224,512]{1,0:T(8,128)(2,1)S(1)}, u32[]{:S(2)}, u32[]{:S(2)}) %collective-permute-start) | collective-permute-done | bytes 229408 | tf_op jit(solution)/shard_map/ppermute | solution.py:52
  22.4 0.7 pack.4
  23.1 1.7 %collective-permute-start.4 = (bf16[736,512]{1,0:T(8,128)(2,1)S(1)}, bf16[736,512]{1,0:T(8,128)(2,1)S(1)}, u32[]{:S(2)}, u32[]{:S(2)}) collective-permute-start(bf16[736,512]{1,0:T(8,128)(2,1)S(1)} %get-tuple-element.87), channel_id=1, source_target_pairs={{0,4},{2,6},{4,8},{6,10},{8,12},{10,14},{12,0},{14,2},{1,5},{3,7},... | collective-permute-start | bytes 2261000 | tf_op jit(solution)/shard_map/ppermute | solution.py:52
  24.8 0.5 collective-permute-start.5
  25.3 0.5 collective-permute-start.6
  25.8 0.5 collective-permute-start.7
  26.3 1.4 %collective-permute-done.7.gp_ref = f32[2,512]{1,0:T(2,128)S(1)} collective-permute-done((f32[2,512]{1,0:T(2,128)S(1)}, f32[2,512]{1,0:T(2,128)S(1)}, u32[]{:S(2)}, u32[]{:S(2)}) %collective-permute-start.7) | collective-permute-done | bytes 4128 | tf_op jit(solution)/shard_map/ppermute | solution.py:40
  27.7 12.5 %collective-permute-done.5.refs_1_.refs_12_.refs_3_ = bf16[672,512]{1,0:T(8,128)(2,1)S(1)} collective-permute-done((bf16[672,512]{1,0:T(8,128)(2,1)S(1)}, bf16[672,512]{1,0:T(8,128)(2,1)S(1)}, u32[]{:S(2)}, u32[]{:S(2)}) %collective-permute-start.5) | collective-permute-done | bytes 688160 | tf_op jit(solution)/shard_map/ppermute | solution.py:48
  40.2 0.3 collective-permute-done.6.refs_13_
  40.5 1.6 %collective-permute-done.4.refs_2_.refs_11_ = bf16[736,512]{1,0:T(8,128)(2,1)S(1)} collective-permute-done((bf16[736,512]{1,0:T(8,128)(2,1)S(1)}, bf16[736,512]{1,0:T(8,128)(2,1)S(1)}, u32[]{:S(2)}, u32[]{:S(2)}) %collective-permute-start.4) | collective-permute-done | bytes 753696 | tf_op jit(solution)/shard_map/ppermute | solution.py:52
  42.0 0.8 pack.5
  42.8 0.6 collective-permute-start.11
  43.4 0.5 collective-permute-start.12
  43.9 3.8 %collective-permute-start.10 = (bf16[224,512]{1,0:T(8,128)(2,1)S(1)}, bf16[224,512]{1,0:T(8,128)(2,1)S(1)}, u32[]{:S(2)}, u32[]{:S(2)}) collective-permute-start(bf16[224,512]{1,0:T(8,128)(2,1)S(1)} %get-tuple-element.96), channel_id=1, source_target_pairs={{0,12},{2,14},{4,0},{6,2},{8,4},{10,6},{12,8},{14,10},{1,13},{3,15... | collective-permute-start | bytes 688136 | tf_op jit(solution)/shard_map/ppermute | solution.py:52
  47.7 10.4 %collective-permute-done.10.refs_2_.refs_5_ = bf16[224,512]{1,0:T(8,128)(2,1)S(1)} collective-permute-done((bf16[224,512]{1,0:T(8,128)(2,1)S(1)}, bf16[224,512]{1,0:T(8,128)(2,1)S(1)}, u32[]{:S(2)}, u32[]{:S(2)}) %collective-permute-start.10) | collective-permute-done | bytes 229408 | tf_op jit(solution)/shard_map/ppermute | solution.py:52
  58.1 0.9 collective-permute-done.11.refs_1_.refs_14_
  59.0 0.7 pack.6
  59.8 0.8 collective-permute-start.14
  60.6 1.5 %collective-permute-start.15 = (bf16[112,512]{1,0:T(8,128)(2,1)S(1)}, bf16[112,512]{1,0:T(8,128)(2,1)S(1)}, u32[]{:S(2)}, u32[]{:S(2)}) collective-permute-start(bf16[112,512]{1,0:T(8,128)(2,1)S(1)} %get-tuple-element.106), channel_id=1, source_target_pairs={{0,16},{16,0},{1,17},{17,1},{2,18},{18,2},{3,19},{19,3},{4,20},{20... | collective-permute-start | bytes 344072 | tf_op jit(solution)/shard_map/ppermute | solution.py:44
  62.1 0.5 collective-permute-start.18
  62.6 2.0 %collective-permute-done.14.refs_0_ = bf16[112,512]{1,0:T(8,128)(2,1)S(1)} collective-permute-done((bf16[112,512]{1,0:T(8,128)(2,1)S(1)}, bf16[112,512]{1,0:T(8,128)(2,1)S(1)}, u32[]{:S(2)}, u32[]{:S(2)}) %collective-permute-start.14) | collective-permute-done | bytes 114720 | tf_op jit(solution)/shard_map/ppermute | solution.py:48
  64.7 0.9 collective-permute-done.15.refs_1_
  65.5 2.5 %collective-permute-start.17 = (bf16[448,512]{1,0:T(8,128)(2,1)S(1)}, bf16[448,512]{1,0:T(8,128)(2,1)S(1)}, u32[]{:S(2)}, u32[]{:S(2)}) collective-permute-start(bf16[448,512]{1,0:T(8,128)(2,1)S(1)} %get-tuple-element.107), channel_id=1, source_target_pairs={{0,16},{16,0},{1,17},{17,1},{2,18},{18,2},{3,19},{19,3},{4,20},{20... | collective-permute-start | bytes 1376264 | tf_op jit(solution)/shard_map/ppermute | solution.py:44
  68.0 2.9 %ready.1 = (bf16[3072,512]{1,0:T(8,128)(2,1)S(1)}, bf16[512,512]{1,0:T(8,128)(2,1)S(1)}, bf16[2,1024,512]{2,1,0:T(8,128)(2,1)S(1)}, bf16[2,1024,512]{2,1,0:T(8,128)(2,1)S(1)}) custom-call(s32[3]{0:T(128)S(1)} %pad_add_fusion.place_ref.place, f32[2,512]{1,0:T(2,128)S(1)} %copy-done.1, f32[2,512]{1,0:T(2,128)S(1)} %collective-permute-done.7.gp_ref, ...), custom_call_target="tpu_custom_call" | custom-call | bytes 65536 | tf_op jit(solution)/shard_map/ready/pallas_call | solution.py:449
  70.9 4.0 %conv0_near.1 = (bf16[2,512,256]{2,1,0:T(8,128)(2,1)S(1)}, bf16[3072,512]{1,0:T(8,128)(2,1)S(1)}, bf16[512,512]{1,0:T(8,128)(2,1)S(1)}) custom-call(s32[3]{0:T(128)S(1)} %pad_add_fusion.place_ref.place, bf16[2,1024,512]{2,1,0:T(8,128)(2,1)S(1)} %get-tuple-element.128.hm._, ...), custom_call_target="tpu_custom_call", output_to_operand_aliasing={{1}: (5, {}), {2}: (6, {})} | custom-call | bytes 65536 | tf_op jit(solution)/shard_map/conv0_near/pallas_call | solution.py:473
  74.9 0.3 collective-permute-done.17.refs_2_.refs_8_
  75.2 1.3 %collective-permute-done.16.refs_3_.refs_7_ = bf16[448,512]{1,0:T(8,128)(2,1)S(1)} collective-permute-done((bf16[448,512]{1,0:T(8,128)(2,1)S(1)}, bf16[448,512]{1,0:T(8,128)(2,1)S(1)}, u32[]{:S(2)}, u32[]{:S(2)}) %collective-permute-start.16) | collective-permute-done | bytes 458784 | tf_op jit(solution)/shard_map/ppermute | solution.py:48
  76.5 0.3 collective-permute-done.13.refs_1_.refs_6_
  76.9 0.5 collective-permute-start.22
  77.4 0.7 pack.7
  78.1 0.8 collective-permute-start.26
  78.9 1.5 %collective-permute-start.27 = (bf16[336,512]{1,0:T(8,128)(2,1)S(1)}, bf16[336,512]{1,0:T(8,128)(2,1)S(1)}, u32[]{:S(2)}, u32[]{:S(2)}) collective-permute-start(bf16[336,512]{1,0:T(8,128)(2,1)S(1)} %get-tuple-element.142), channel_id=1, source_target_pairs={{0,16},{16,0},{1,17},{17,1},{2,18},{18,2},{3,19},{19,3},{4,20},{20... | collective-permute-start | bytes 1032200 | tf_op jit(solution)/shard_map/ppermute | solution.py:44
  80.4 2.0 %collective-permute-start.25 = (bf16[224,512]{1,0:T(8,128)(2,1)S(1)}, bf16[224,512]{1,0:T(8,128)(2,1)S(1)}, u32[]{:S(2)}, u32[]{:S(2)}) collective-permute-start(bf16[224,512]{1,0:T(8,128)(2,1)S(1)} %get-tuple-element.140), channel_id=1, source_target_pairs={{0,4},{2,6},{4,8},{6,10},{8,12},{10,14},{12,0},{14,2},{1,5},{3,7},... | collective-permute-start | bytes 688136 | tf_op jit(solution)/shard_map/ppermute | solution.py:52
  82.5 3.0 %conv0_far.1 = (bf16[256,256]{1,0:T(8,128)(2,1)S(1)}, bf16[256,256]{1,0:T(8,128)(2,1)S(1)}, bf16[2,1024,512]{2,1,0:T(8,128)(2,1)S(1)}, bf16[2,1024,512]{2,1,0:T(8,128)(2,1)S(1)}) custom-call(s32[3]{0:T(128)S(1)} %pad_add_fusion.place_ref.place, f32[2,512]{1,0:T(2,128)S(1)} %copy-done.1, ...), custom_call_target="tpu_custom_call", output_to_operand_aliasing={{2}: (6, {}), {3}: (7, {})} | custom-call | bytes 65536 | tf_op jit(solution)/shard_map/conv0_far/pallas_call | solution.py:510
  85.5 0.5 collective-permute-start.24
  86.0 2.5 %mix0_near.1 = (bf16[2,2,256,512]{3,2,1,0:T(8,128)(2,1)S(1)}, bf16[2,2,256,512]{3,2,1,0:T(8,128)(2,1)S(1)}, bf16[2,256,512]{2,1,0:T(8,128)(2,1)S(1)}) custom-call(s32[3]{0:T(128)S(1)} %pad_add_fusion.place_ref.place, f32[2,512]{1,0:T(2,128)S(1)} %copy-done.1, f32[2,512]{1,0:T(2,128)S(1)} %collective-permute-done.7.gp_ref, ...), custom_call_target="tpu_custom_call" | custom-call | bytes 65536 | tf_op jit(solution)/shard_map/mix0_near/pallas_call | solution.py:530
  88.6 1.6 %mix0_far.1 = (bf16[1,2,256,512]{3,2,1,0:T(8,128)(2,1)S(1)}, bf16[1,2,256,512]{3,2,1,0:T(8,128)(2,1)S(1)}) custom-call(s32[3]{0:T(128)S(1)} %pad_add_fusion.place_ref.place, f32[2,512]{1,0:T(2,128)S(1)} %copy-done.1, f32[2,512]{1,0:T(2,128)S(1)} %collective-permute-done.7.gp_ref, bf16[512,512]{1,0:T(8,128)(2,1)S(1)} %get-tuple-element.119.mixm_ref, ...), custom_call_target="tpu_custom_call" | custom-call | bytes 65536 | tf_op jit(solution)/shard_map/mix0_far/pallas_call | solution.py:530
  90.2 2.6 %conv1.1 = (bf16[2,256,256]{2,1,0:T(8,128)(2,1)S(1)}, bf16[512,512]{1,0:T(8,128)(2,1)S(1)}) custom-call(s32[3]{0:T(128)S(1)} %pad_add_fusion.place_ref.place, bf16[2,2,256,512]{3,2,1,0:T(8,128)(2,1)S(1)} %get-tuple-element.143.hm_near, bf16[2,2,256,512]{3,2,1,0:T(8,128)(2,1)S(1)} %get-tuple-element.144.hp_near, ...), custom_call_target="tpu_custom_call" | custom-call | tf_op jit(solution)/shard_map/conv1/pallas_call | solution.py:553
  93.0 1.5 %collective-permute-done.28.zp_ref = bf16[2,256,256]{2,1,0:T(8,128)(2,1)S(1)} collective-permute-done((bf16[2,256,256]{2,1,0:T(8,128)(2,1)S(1)}, bf16[2,256,256]{2,1,0:T(8,128)(2,1)S(1)}, u32[]{:S(2)}, u32[]{:S(2)}) %collective-permute-start.28) | collective-permute-done | bytes 262176 | tf_op jit(solution)/shard_map/ppermute | solution.py:40
  94.5 1.7 %mix1.1 = (bf16[256,512]{1,0:T(8,128)(2,1)}, bf16[256,512]{1,0:T(8,128)(2,1)}) custom-call(s32[3]{0:T(128)S(1)} %pad_add_fusion.place_ref.place, bf16[2,256,256]{2,1,0:T(8,128)(2,1)S(1)} %get-tuple-element.159.zm_ref, bf16[2,256,256]{2,1,0:T(8,128)(2,1)S(1)} %collective-permute-done.28.zp_ref, bf16[512,512]{1,0:T(8,128)(2,1)S(1)} %get-tuple-element.160.mix_ref, ...), custom_call_target="tpu_custom_call" | custom-call | tf_op jit(solution)/shard_map/mix1/pallas_call | solution.py:568
  (36 shorter events, 0.8 us)
Async XLA Ops:
  0.6 1.1 %copy-start = (bf16[2,384,2,256]{3,2,1,0:T(2,128)(2,1)S(1)}, bf16[2,384,2,256]{3,2,1,0:T(2,128)(2,1)}, u32[]{:S(2)}) copy-start(bf16[2,384,2,256]{3,2,1,0:T(2,128)(2,1)} %param.8) | copy-start | bytes 2359300
  0.6 11.5 %copy-start.2 = (bf16[256,512]{1,0:T(8,128)(2,1)S(1)}, bf16[256,512]{1,0:T(8,128)(2,1)}, u32[]{:S(2)}) copy-start(bf16[256,512]{1,0:T(8,128)(2,1)} %param.6) | copy-start | bytes 786436
  0.7 11.5 %copy-start.3 = (bf16[256,512]{1,0:T(8,128)(2,1)S(1)}, bf16[256,512]{1,0:T(8,128)(2,1)}, u32[]{:S(2)}) copy-start(bf16[256,512]{1,0:T(8,128)(2,1)} %param.5) | copy-start | bytes 786436
  3.2 22.6 %copy-start.1 = (f32[2,512]{1,0:T(2,128)S(1)}, f32[2,512]{1,0:T(2,128)}, u32[]{:S(2)}) copy-start(f32[2,512]{1,0:T(2,128)} %gm_ref.7) | copy-start | bytes 12292
  3.2 19.2 %collective-permute-start.3 = (bf16[448,512]{1,0:T(8,128)(2,1)S(1)}, bf16[448,512]{1,0:T(8,128)(2,1)S(1)}, u32[]{:S(2)}, u32[]{:S(2)}) collective-permute-start(bf16[448,512]{1,0:T(8,128)(2,1)S(1)} %bitcast.21), channel_id=1, source_target_pairs={{0,16},{16,0},{1,17},{17,1},{2,18},{18,2},{3,19},{19,3},{4,20},{20... | collective-permute-start | bytes 1376264 | tf_op jit(solution)/shard_map/ppermute | solution.py:44
  6.2 16.2 %collective-permute-start.2 = (bf16[448,512]{1,0:T(8,128)(2,1)S(1)}, bf16[448,512]{1,0:T(8,128)(2,1)S(1)}, u32[]{:S(2)}, u32[]{:S(2)}) collective-permute-start(bf16[448,512]{1,0:T(8,128)(2,1)S(1)} %bitcast.22), channel_id=1, source_target_pairs={{0,2},{2,0},{4,6},{6,4},{8,10},{10,8},{12,14},{14,12},{1,3},{3,1},... | collective-permute-start | bytes 1376264 | tf_op jit(solution)/shard_map/ppermute | solution.py:48
  8.4 10.0 %collective-permute-start.1 = (bf16[224,512]{1,0:T(8,128)(2,1)}, bf16[224,512]{1,0:T(8,128)(2,1)S(1)}, u32[]{:S(2)}, u32[]{:S(2)}) collective-permute-start(bf16[224,512]{1,0:T(8,128)(2,1)} %get-tuple-element.163), channel_id=1, source_target_pairs={{0,12},{2,14},{4,0},{6,2},{8,4},{10,6},{12,8},{14,10},{1,13},{3,15... | collective-permute-start | bytes 688136 | tf_op jit(solution)/shard_map/ppermute | solution.py:52
  12.0 10.3 %collective-permute-start = (bf16[224,512]{1,0:T(8,128)(2,1)}, bf16[224,512]{1,0:T(8,128)(2,1)S(1)}, u32[]{:S(2)}, u32[]{:S(2)}) collective-permute-start(bf16[224,512]{1,0:T(8,128)(2,1)} %get-tuple-element.163), channel_id=1, source_target_pairs={{0,4},{2,6},{4,8},{6,10},{8,12},{10,14},{12,0},{14,2},{1,5},{3,7},... | collective-permute-start | bytes 688136 | tf_op jit(solution)/shard_map/ppermute | solution.py:52
  23.1 18.9 %collective-permute-start.4 = (bf16[736,512]{1,0:T(8,128)(2,1)S(1)}, bf16[736,512]{1,0:T(8,128)(2,1)S(1)}, u32[]{:S(2)}, u32[]{:S(2)}) collective-permute-start(bf16[736,512]{1,0:T(8,128)(2,1)S(1)} %get-tuple-element.87), channel_id=1, source_target_pairs={{0,4},{2,6},{4,8},{6,10},{8,12},{10,14},{12,0},{14,2},{1,5},{3,7},... | collective-permute-start | bytes 2261000 | tf_op jit(solution)/shard_map/ppermute | solution.py:52
  24.8 15.5 %collective-permute-start.5 = (bf16[672,512]{1,0:T(8,128)(2,1)S(1)}, bf16[672,512]{1,0:T(8,128)(2,1)S(1)}, u32[]{:S(2)}, u32[]{:S(2)}) collective-permute-start(bf16[672,512]{1,0:T(8,128)(2,1)S(1)} %get-tuple-element.88), channel_id=1, source_target_pairs={{0,2},{2,0},{4,6},{6,4},{8,10},{10,8},{12,14},{14,12},{1,3},{3,1},... | collective-permute-start | bytes 2064392 | tf_op jit(solution)/shard_map/ppermute | solution.py:48
  25.3 15.2 %collective-permute-start.6 = (bf16[672,512]{1,0:T(8,128)(2,1)S(1)}, bf16[672,512]{1,0:T(8,128)(2,1)S(1)}, u32[]{:S(2)}, u32[]{:S(2)}) collective-permute-start(bf16[672,512]{1,0:T(8,128)(2,1)S(1)} %get-tuple-element.89), channel_id=1, source_target_pairs={{0,16},{16,0},{1,17},{17,1},{2,18},{18,2},{3,19},{19,3},{4,20},{20... | collective-permute-start | bytes 2064392 | tf_op jit(solution)/shard_map/ppermute | solution.py:44
  25.8 1.9 %collective-permute-start.8 = (bf16[512,512]{1,0:T(8,128)(2,1)S(1)}, bf16[512,512]{1,0:T(8,128)(2,1)S(1)}, u32[]{:S(2)}, u32[]{:S(2)}) collective-permute-start(bf16[512,512]{1,0:T(8,128)(2,1)S(1)} %bitcast.19), channel_id=1, source_target_pairs={{0,1},{1,0},{2,3},{3,2},{4,5},{5,4},{6,7},{7,6},{8,9},{9,8},{10,11... | collective-permute-start | bytes 1572872 | tf_op jit(solution)/shard_map/ppermute | solution.py:40
  25.8 1.9 %collective-permute-start.7 = (f32[2,512]{1,0:T(2,128)S(1)}, f32[2,512]{1,0:T(2,128)S(1)}, u32[]{:S(2)}, u32[]{:S(2)}) collective-permute-start(f32[2,512]{1,0:T(2,128)S(1)} %copy-done.1), channel_id=1, source_target_pairs={{0,1},{1,0},{2,3},{3,2},{4,5},{5,4},{6,7},{7,6},{8,9},{9,8},{10,11... | collective-permute-start | bytes 12296 | tf_op jit(solution)/shard_map/ppermute | solution.py:40
  42.8 16.2 %collective-permute-start.11 = (bf16[736,512]{1,0:T(8,128)(2,1)S(1)}, bf16[736,512]{1,0:T(8,128)(2,1)S(1)}, u32[]{:S(2)}, u32[]{:S(2)}) collective-permute-start(bf16[736,512]{1,0:T(8,128)(2,1)S(1)} %get-tuple-element.97), channel_id=1, source_target_pairs={{0,2},{2,0},{4,6},{6,4},{8,10},{10,8},{12,14},{14,12},{1,3},{3,1},... | collective-permute-start | bytes 2261000 | tf_op jit(solution)/shard_map/ppermute | solution.py:48
  43.4 14.7 %collective-permute-start.12 = (bf16[672,512]{1,0:T(8,128)(2,1)S(1)}, bf16[672,512]{1,0:T(8,128)(2,1)S(1)}, u32[]{:S(2)}, u32[]{:S(2)}) collective-permute-start(bf16[672,512]{1,0:T(8,128)(2,1)S(1)} %get-tuple-element.98), channel_id=1, source_target_pairs={{0,16},{16,0},{1,17},{17,1},{2,18},{18,2},{3,19},{19,3},{4,20},{20... | collective-permute-start | bytes 2064392 | tf_op jit(solution)/shard_map/ppermute | solution.py:44
  43.9 14.2 %collective-permute-start.9 = (bf16[448,512]{1,0:T(8,128)(2,1)S(1)}, bf16[448,512]{1,0:T(8,128)(2,1)S(1)}, u32[]{:S(2)}, u32[]{:S(2)}) collective-permute-start(bf16[448,512]{1,0:T(8,128)(2,1)S(1)} %get-tuple-element.95), channel_id=1, source_target_pairs={{0,4},{2,6},{4,8},{6,10},{8,12},{10,14},{12,0},{14,2},{1,5},{3,7},... | collective-permute-start | bytes 1376264 | tf_op jit(solution)/shard_map/ppermute | solution.py:52
  43.9 14.2 %collective-permute-start.10 = (bf16[224,512]{1,0:T(8,128)(2,1)S(1)}, bf16[224,512]{1,0:T(8,128)(2,1)S(1)}, u32[]{:S(2)}, u32[]{:S(2)}) collective-permute-start(bf16[224,512]{1,0:T(8,128)(2,1)S(1)} %get-tuple-element.96), channel_id=1, source_target_pairs={{0,12},{2,14},{4,0},{6,2},{8,4},{10,6},{12,8},{14,10},{1,13},{3,15... | collective-permute-start | bytes 688136 | tf_op jit(solution)/shard_map/ppermute | solution.py:52
  59.8 17.1 %collective-permute-start.13 = (bf16[736,512]{1,0:T(8,128)(2,1)S(1)}, bf16[736,512]{1,0:T(8,128)(2,1)S(1)}, u32[]{:S(2)}, u32[]{:S(2)}) collective-permute-start(bf16[736,512]{1,0:T(8,128)(2,1)S(1)} %get-tuple-element.103), channel_id=1, source_target_pairs={{0,4},{2,6},{4,8},{6,10},{8,12},{10,14},{12,0},{14,2},{1,5},{3,7},... | collective-permute-start | bytes 2261000 | tf_op jit(solution)/shard_map/ppermute | solution.py:52
  59.8 4.9 %collective-permute-start.14 = (bf16[112,512]{1,0:T(8,128)(2,1)S(1)}, bf16[112,512]{1,0:T(8,128)(2,1)S(1)}, u32[]{:S(2)}, u32[]{:S(2)}) collective-permute-start(bf16[112,512]{1,0:T(8,128)(2,1)S(1)} %get-tuple-element.105), channel_id=1, source_target_pairs={{0,2},{2,0},{4,6},{6,4},{8,10},{10,8},{12,14},{14,12},{1,3},{3,1},... | collective-permute-start | bytes 344072 | tf_op jit(solution)/shard_map/ppermute | solution.py:48
  60.6 4.9 %collective-permute-start.15 = (bf16[112,512]{1,0:T(8,128)(2,1)S(1)}, bf16[112,512]{1,0:T(8,128)(2,1)S(1)}, u32[]{:S(2)}, u32[]{:S(2)}) collective-permute-start(bf16[112,512]{1,0:T(8,128)(2,1)S(1)} %get-tuple-element.106), channel_id=1, source_target_pairs={{0,16},{16,0},{1,17},{17,1},{2,18},{18,2},{3,19},{19,3},{4,20},{20... | collective-permute-start | bytes 344072 | tf_op jit(solution)/shard_map/ppermute | solution.py:44
  62.1 5.9 %collective-permute-start.19 = (bf16[512,512]{1,0:T(8,128)(2,1)S(1)}, bf16[512,512]{1,0:T(8,128)(2,1)S(1)}, u32[]{:S(2)}, u32[]{:S(2)}) collective-permute-start(bf16[512,512]{1,0:T(8,128)(2,1)S(1)} %get-tuple-element.109), channel_id=1, source_target_pairs={{0,1},{1,0},{2,3},{3,2},{4,5},{5,4},{6,7},{7,6},{8,9},{9,8},{10,11... | collective-permute-start | bytes 1572872 | tf_op jit(solution)/shard_map/ppermute | solution.py:40
  62.1 5.9 %collective-permute-start.18 = (bf16[512,512]{1,0:T(8,128)(2,1)S(1)}, bf16[512,512]{1,0:T(8,128)(2,1)S(1)}, u32[]{:S(2)}, u32[]{:S(2)}) collective-permute-start(bf16[512,512]{1,0:T(8,128)(2,1)S(1)} %get-tuple-element.108), channel_id=1, source_target_pairs={{0,1},{1,0},{2,3},{3,2},{4,5},{5,4},{6,7},{7,6},{8,9},{9,8},{10,11... | collective-permute-start | bytes 1572872 | tf_op jit(solution)/shard_map/ppermute | solution.py:40
  65.5 9.7 %collective-permute-start.17 = (bf16[448,512]{1,0:T(8,128)(2,1)S(1)}, bf16[448,512]{1,0:T(8,128)(2,1)S(1)}, u32[]{:S(2)}, u32[]{:S(2)}) collective-permute-start(bf16[448,512]{1,0:T(8,128)(2,1)S(1)} %get-tuple-element.107), channel_id=1, source_target_pairs={{0,16},{16,0},{1,17},{17,1},{2,18},{18,2},{3,19},{19,3},{4,20},{20... | collective-permute-start | bytes 1376264 | tf_op jit(solution)/shard_map/ppermute | solution.py:44
  68.0 8.5 %collective-permute-start.16 = (bf16[448,512]{1,0:T(8,128)(2,1)S(1)}, bf16[448,512]{1,0:T(8,128)(2,1)S(1)}, u32[]{:S(2)}, u32[]{:S(2)}) collective-permute-start(bf16[448,512]{1,0:T(8,128)(2,1)S(1)} %get-tuple-element.107), channel_id=1, source_target_pairs={{0,2},{2,0},{4,6},{6,4},{8,10},{10,8},{12,14},{14,12},{1,3},{3,1},... | collective-permute-start | bytes 1376264 | tf_op jit(solution)/shard_map/ppermute | solution.py:48
  76.9 3.6 %collective-permute-start.21 = (bf16[2,512,256]{2,1,0:T(8,128)(2,1)S(1)}, bf16[2,512,256]{2,1,0:T(8,128)(2,1)S(1)}, u32[]{:S(2)}, u32[]{:S(2)}) collective-permute-start(bf16[2,512,256]{2,1,0:T(8,128)(2,1)S(1)} %get-tuple-element.136.refs_0_), channel_id=1, source_target_pairs={{0,1},{1,0},{2,3},{3,2},{4,5},{5,4},{6,7},{7,6},{8,9},{9,8},{10,11... | collective-permute-start | bytes 1572872 | tf_op jit(solution)/shard_map/ppermute | solution.py:40
  76.9 5.6 %collective-permute-start.22 = (bf16[512,512]{1,0:T(8,128)(2,1)S(1)}, bf16[512,512]{1,0:T(8,128)(2,1)S(1)}, u32[]{:S(2)}, u32[]{:S(2)}) collective-permute-start(bf16[512,512]{1,0:T(8,128)(2,1)S(1)} %get-tuple-element.119.mixm_ref), channel_id=1, source_target_pairs={{0,1},{1,0},{2,3},{3,2},{4,5},{5,4},{6,7},{7,6},{8,9},{9,8},{10,11... | collective-permute-start | bytes 1572872 | tf_op jit(solution)/shard_map/ppermute | solution.py:40
  78.0 4.4 %collective-permute-start.20 = (bf16[2,256,512]{2,1,0:T(8,128)(2,1)S(1)}, bf16[2,256,512]{2,1,0:T(8,128)(2,1)S(1)}, u32[]{:S(2)}, u32[]{:S(2)}) collective-permute-start(bf16[2,256,512]{2,1,0:T(8,128)(2,1)S(1)} %bitcast.36), channel_id=1, source_target_pairs={{0,1},{1,0},{2,3},{3,2},{4,5},{5,4},{6,7},{7,6},{8,9},{9,8},{10,11... | collective-permute-start | bytes 1572872 | tf_op jit(solution)/shard_map/ppermute | solution.py:40
  78.1 12.1 %collective-permute-start.26 = (bf16[336,512]{1,0:T(8,128)(2,1)S(1)}, bf16[336,512]{1,0:T(8,128)(2,1)S(1)}, u32[]{:S(2)}, u32[]{:S(2)}) collective-permute-start(bf16[336,512]{1,0:T(8,128)(2,1)S(1)} %get-tuple-element.141), channel_id=1, source_target_pairs={{0,2},{2,0},{4,6},{6,4},{8,10},{10,8},{12,14},{14,12},{1,3},{3,1},... | collective-permute-start | bytes 1032200 | tf_op jit(solution)/shard_map/ppermute | solution.py:48
  78.9 11.3 %collective-permute-start.27 = (bf16[336,512]{1,0:T(8,128)(2,1)S(1)}, bf16[336,512]{1,0:T(8,128)(2,1)S(1)}, u32[]{:S(2)}, u32[]{:S(2)}) collective-permute-start(bf16[336,512]{1,0:T(8,128)(2,1)S(1)} %get-tuple-element.142), channel_id=1, source_target_pairs={{0,16},{16,0},{1,17},{17,1},{2,18},{18,2},{3,19},{19,3},{4,20},{20... | collective-permute-start | bytes 1032200 | tf_op jit(solution)/shard_map/ppermute | solution.py:44
  80.4 9.8 %collective-permute-start.25 = (bf16[224,512]{1,0:T(8,128)(2,1)S(1)}, bf16[224,512]{1,0:T(8,128)(2,1)S(1)}, u32[]{:S(2)}, u32[]{:S(2)}) collective-permute-start(bf16[224,512]{1,0:T(8,128)(2,1)S(1)} %get-tuple-element.140), channel_id=1, source_target_pairs={{0,4},{2,6},{4,8},{6,10},{8,12},{10,14},{12,0},{14,2},{1,5},{3,7},... | collective-permute-start | bytes 688136 | tf_op jit(solution)/shard_map/ppermute | solution.py:52
  85.5 3.1 %collective-permute-start.23 = (bf16[256,256]{1,0:T(8,128)(2,1)S(1)}, bf16[256,256]{1,0:T(8,128)(2,1)S(1)}, u32[]{:S(2)}, u32[]{:S(2)}) collective-permute-start(bf16[256,256]{1,0:T(8,128)(2,1)S(1)} %get-tuple-element.132.refs_0_), channel_id=1, source_target_pairs={{0,1},{1,0},{2,3},{3,2},{4,5},{5,4},{6,7},{7,6},{8,9},{9,8},{10,11... | collective-permute-start | bytes 393224 | tf_op jit(solution)/shard_map/ppermute | solution.py:40
  85.5 3.0 %collective-permute-start.24 = (bf16[256,256]{1,0:T(8,128)(2,1)S(1)}, bf16[256,256]{1,0:T(8,128)(2,1)S(1)}, u32[]{:S(2)}, u32[]{:S(2)}) collective-permute-start(bf16[256,256]{1,0:T(8,128)(2,1)S(1)} %get-tuple-element.133.refs_1_), channel_id=1, source_target_pairs={{0,1},{1,0},{2,3},{3,2},{4,5},{5,4},{6,7},{7,6},{8,9},{9,8},{10,11... | collective-permute-start | bytes 393224 | tf_op jit(solution)/shard_map/ppermute | solution.py:40
  92.9 1.6 %collective-permute-start.28 = (bf16[2,256,256]{2,1,0:T(8,128)(2,1)S(1)}, bf16[2,256,256]{2,1,0:T(8,128)(2,1)S(1)}, u32[]{:S(2)}, u32[]{:S(2)}) collective-permute-start(bf16[2,256,256]{2,1,0:T(8,128)(2,1)S(1)} %get-tuple-element.159.zm_ref), channel_id=1, source_target_pairs={{0,1},{1,0},{2,3},{3,2},{4,5},{5,4},{6,7},{7,6},{8,9},{9,8},{10,11... | collective-permute-start | bytes 786440 | tf_op jit(solution)/shard_map/ppermute | solution.py:40

commit v8 on v7

--- a/solution.py
+++ b/solution.py
@@ -245,6 +245,14 @@
         out[...] = (state_ref[v].astype(F32) + y).astype(BF16)
 
 
+def chunk_kernel(conv, mix, both, *chunks):
+    for layer, chunk in enumerate(chunks):
+        chunk[0 : conv.shape[1], :] = conv[layer]
+        chunk[conv.shape[1] :, :] = mix[layer]
+        begin = layer * chunk.shape[0]
+        both[begin : begin + chunk.shape[0], :] = chunk[...]
+
+
 def pack(seq, place, *buffers):
     arrays = []
 
@@ -290,7 +298,7 @@
 
 
 def exchange(place, own, chunks, gains, seq, ready, newest):
-    both = chunks
+    both, c0, c1 = chunks
     unit = both.shape[0] // 2
     tall = own.shape[0]
     pieces = ([], [])
@@ -316,7 +324,6 @@
     def z(block, by=1):
         return ring(block, seq, 2 * by)
 
-    c0, c1 = both[:unit], both[unit:]
     whole(0, both, (0, 0, 0))
     keep(1, both, (unit, 0, unit, 0, 0, 0))
     z1a, z1b, x1, y1, own, c1 = together(z(c0), z(c0, 3), x(both), y(both), own, c1)
@@ -407,15 +414,22 @@
     if 2 * lag == rows:
         conv_rows, mix_rows = shard // 2, mix_shard // 2
         g = lax.axis_index("groups")
-        chunks = jnp.concatenate(
-            [
-                lax.dynamic_slice_in_dim(
-                    convolution_kernel, g * conv_rows, conv_rows, 1
-                ).reshape(layers, conv_rows, 2 * branch),
-                lax.dynamic_slice_in_dim(mixing_kernel, g * mix_rows, mix_rows, 1),
-            ],
-            1,
-        ).reshape(layers * (conv_rows + mix_rows), 2 * branch)
+        conv_part = lax.dynamic_slice_in_dim(
+            convolution_kernel, g * conv_rows, conv_rows, 1
+        ).reshape(layers, conv_rows, 2 * branch)
+        mix_part = lax.dynamic_slice_in_dim(mixing_kernel, g * mix_rows, mix_rows, 1)
+        unit = conv_rows + mix_rows
+        chunks = pl.pallas_call(
+            chunk_kernel,
+            out_shape=(
+                near_out(layers * unit, 2 * branch),
+                *[near_out(unit, 2 * branch) for _ in range(layers)],
+            ),
+            in_specs=[VMEM, VMEM],
+            out_specs=(VMEM,) * (1 + layers),
+            compiler_params=scoped(2),
+            name="chunk",
+        )(near(conv_part), near(mix_part))
         step, used = lag, (0, 1, 2)
         blocks = 4
     else:

time: 96.3 us -> 95.5 us (level)
  waiting for transfers between devices: 43.5 us -> 42.4 us
    ppermute x7, waiting for transfers between devices: 22.5 us -> 21.3 us  [ring(): return lax.ppermute(block, 'seq', [(s, (s + by) % seq) for s in range(seq)])]
where the time goes in v8:
time: 95.5 us; the launch traced here: 95.3 us
  waiting for transfers between devices  42.4 us (44%)
  starting transfers between devices  27.3 us (29%)
  Pallas kernels  21.2 us (22%)
  local copies, waits for them, and re-layouts  2.51 us (3%)
  other arithmetic  1.08 us (1%)
    ppermute x7, waiting for transfers between devices, ring(): return lax.ppermute(block, 'seq', [(s, (s + by) % seq) for s in range(seq)])  21.3 us
    ppermute x6, waiting for transfers between devices, swap_pair(): return lax.ppermute(block, 'seq', [(s, s ^ 1) for s in range(seq)])  16.7 us
    ppermute x7, starting transfers between devices, ring(): return lax.ppermute(block, 'seq', [(s, (s + by) % seq) for s in range(seq)])  11.2 us
    ppermute x6, starting transfers between devices, swap_groups(): return lax.ppermute(block, 'groups', [(0, 1), (1, 0)])  9.56 us
    ppermute x6, starting transfers between devices, swap_pair(): return lax.ppermute(block, 'seq', [(s, s ^ 1) for s in range(seq)])  4.22 us
    pallas_call x2, Pallas kernels, mix0(): pl.pallas_call(functools.partial(mix0_kernel, (rows, half, branch, 1, n,...  4.12 us
    pallas_call x1, Pallas kernels, newest(): pl.pallas_call(functools.partial(conv0_near_kernel, (rows, half, branch,...  4.02 us
    pallas_call x1, Pallas kernels, on_device(): pl.pallas_call(functools.partial(conv0_far_kernel, (rows, half, branch, f...  3.01 us
  transfers between devices with their start and end apart: 29, of which 14 were waited for; matrix products, arithmetic and copies ran while one was open for 1% of the time, Pallas kernels for 15%

profile of v8, /device:TPU:0, one launch (start us, length us, event | category | flops | bytes accessed | tf_op | source)
XLA Modules:
  0.0 95.3 jit_solution(16481735659512771301)
XLA Ops:
  0.7 1.1 %copy-done = bf16[2,384,2,256]{3,2,1,0:T(2,128)(2,1)S(1)} copy-done((bf16[2,384,2,256]{3,2,1,0:T(2,128)(2,1)S(1)}, bf16[2,384,2,256]{3,2,1,0:T(2,128)(2,1)}, u32[]{:S(2)}) %copy-start) | copy-done | bytes 786456
  1.8 0.3 constant_dynamic-slice_fusion.1
  2.3 0.9 constant_dynamic-slice_fusion.mix
  3.2 3.0 %collective-permute-start.3 = (bf16[448,512]{1,0:T(8,128)(2,1)S(1)}, bf16[448,512]{1,0:T(8,128)(2,1)S(1)}, u32[]{:S(2)}, u32[]{:S(2)}) collective-permute-start(bf16[448,512]{1,0:T(8,128)(2,1)S(1)} %get-tuple-element.153.refs_0_.refs_6_), channel_id=1, source_target_pairs={{0,16},{16,0},{1,17},{17,1},{2,18},{18,2},{3,19},{19,3},{4,20},{20... | collective-permute-start | bytes 1376264 | tf_op jit(solution)/shard_map/ppermute | solution.py:44
  6.3 1.5 %collective-permute-start.2 = (bf16[448,512]{1,0:T(8,128)(2,1)S(1)}, bf16[448,512]{1,0:T(8,128)(2,1)S(1)}, u32[]{:S(2)}, u32[]{:S(2)}) collective-permute-start(bf16[448,512]{1,0:T(8,128)(2,1)S(1)} %get-tuple-element.153.refs_0_.refs_6_), channel_id=1, source_target_pairs={{0,2},{2,0},{4,6},{6,4},{8,10},{10,8},{12,14},{14,12},{1,3},{3,1},... | collective-permute-start | bytes 1376264 | tf_op jit(solution)/shard_map/ppermute | solution.py:48
  7.8 3.6 %collective-permute-start.1 = (bf16[224,512]{1,0:T(8,128)(2,1)S(1)}, bf16[224,512]{1,0:T(8,128)(2,1)S(1)}, u32[]{:S(2)}, u32[]{:S(2)}) collective-permute-start(bf16[224,512]{1,0:T(8,128)(2,1)S(1)} %get-tuple-element.85), channel_id=1, source_target_pairs={{0,12},{2,14},{4,0},{6,2},{8,4},{10,6},{12,8},{14,10},{1,13},{3,15... | collective-permute-start | bytes 688136 | tf_op jit(solution)/shard_map/ppermute | solution.py:52
  11.4 1.0 %pad_maximum_fusion = bf16[2,256,512]{2,1,0:T(8,128)(2,1)S(1)} fusion(bf16[1,256,512]{2,1,0:T(8,128)(2,1)S(1)} %bitcast.28, bf16[1,256,512]{2,1,0:T(8,128)(2,1)} %bitcast.29), kind=kLoop, calls=%fused_computation | loop fusion | flops 262144 | bytes 1048576 | tf_op jit(solution)/shard_map/stack | solution.py:413
  12.4 5.0 %collective-permute-done.1.refs_2_.refs_8_ = bf16[224,512]{1,0:T(8,128)(2,1)S(1)} collective-permute-done((bf16[224,512]{1,0:T(8,128)(2,1)S(1)}, bf16[224,512]{1,0:T(8,128)(2,1)S(1)}, u32[]{:S(2)}, u32[]{:S(2)}) %collective-permute-start.1) | collective-permute-done | bytes 229408 | tf_op jit(solution)/shard_map/ppermute | solution.py:52
  17.4 4.1 %collective-permute-done.refs_0_.refs_7_ = bf16[224,512]{1,0:T(8,128)(2,1)S(1)} collective-permute-done((bf16[224,512]{1,0:T(8,128)(2,1)S(1)}, bf16[224,512]{1,0:T(8,128)(2,1)S(1)}, u32[]{:S(2)}, u32[]{:S(2)}) %collective-permute-start) | collective-permute-done | bytes 229408 | tf_op jit(solution)/shard_map/ppermute | solution.py:52
  21.5 0.7 pack.4
  22.2 1.7 %collective-permute-start.4 = (bf16[736,512]{1,0:T(8,128)(2,1)S(1)}, bf16[736,512]{1,0:T(8,128)(2,1)S(1)}, u32[]{:S(2)}, u32[]{:S(2)}) collective-permute-start(bf16[736,512]{1,0:T(8,128)(2,1)S(1)} %get-tuple-element.93), channel_id=1, source_target_pairs={{0,4},{2,6},{4,8},{6,10},{8,12},{10,14},{12,0},{14,2},{1,5},{3,7},... | collective-permute-start | bytes 2261000 | tf_op jit(solution)/shard_map/ppermute | solution.py:52
  23.9 0.5 collective-permute-start.5
  24.4 0.5 collective-permute-start.6
  24.9 0.5 collective-permute-start.7
  25.4 1.4 %collective-permute-done.7.gp_ref = f32[2,512]{1,0:T(2,128)S(1)} collective-permute-done((f32[2,512]{1,0:T(2,128)S(1)}, f32[2,512]{1,0:T(2,128)S(1)}, u32[]{:S(2)}, u32[]{:S(2)}) %collective-permute-start.7) | collective-permute-done | bytes 4128 | tf_op jit(solution)/shard_map/ppermute | solution.py:40
  26.8 12.5 %collective-permute-done.5.refs_1_.refs_12_.refs_3_ = bf16[672,512]{1,0:T(8,128)(2,1)S(1)} collective-permute-done((bf16[672,512]{1,0:T(8,128)(2,1)S(1)}, bf16[672,512]{1,0:T(8,128)(2,1)S(1)}, u32[]{:S(2)}, u32[]{:S(2)}) %collective-permute-start.5) | collective-permute-done | bytes 688160 | tf_op jit(solution)/shard_map/ppermute | solution.py:48
  39.3 0.3 collective-permute-done.6.refs_13_
  39.6 1.6 %collective-permute-done.4.refs_2_.refs_11_ = bf16[736,512]{1,0:T(8,128)(2,1)S(1)} collective-permute-done((bf16[736,512]{1,0:T(8,128)(2,1)S(1)}, bf16[736,512]{1,0:T(8,128)(2,1)S(1)}, u32[]{:S(2)}, u32[]{:S(2)}) %collective-permute-start.4) | collective-permute-done | bytes 753696 | tf_op jit(solution)/shard_map/ppermute | solution.py:52
  41.1 0.8 pack.5
  41.9 0.6 collective-permute-start.11
  42.5 0.5 collective-permute-start.12
  43.0 3.8 %collective-permute-start.10 = (bf16[224,512]{1,0:T(8,128)(2,1)S(1)}, bf16[224,512]{1,0:T(8,128)(2,1)S(1)}, u32[]{:S(2)}, u32[]{:S(2)}) collective-permute-start(bf16[224,512]{1,0:T(8,128)(2,1)S(1)} %get-tuple-element.102), channel_id=1, source_target_pairs={{0,12},{2,14},{4,0},{6,2},{8,4},{10,6},{12,8},{14,10},{1,13},{3,15... | collective-permute-start | bytes 688136 | tf_op jit(solution)/shard_map/ppermute | solution.py:52
  46.8 10.4 %collective-permute-done.10.refs_2_.refs_5_ = bf16[224,512]{1,0:T(8,128)(2,1)S(1)} collective-permute-done((bf16[224,512]{1,0:T(8,128)(2,1)S(1)}, bf16[224,512]{1,0:T(8,128)(2,1)S(1)}, u32[]{:S(2)}, u32[]{:S(2)}) %collective-permute-start.10) | collective-permute-done | bytes 229408 | tf_op jit(solution)/shard_map/ppermute | solution.py:52
  57.2 0.9 collective-permute-done.11.refs_1_.refs_14_
  58.1 0.7 pack.6
  58.9 0.8 collective-permute-start.14
  59.7 1.5 %collective-permute-start.15 = (bf16[112,512]{1,0:T(8,128)(2,1)S(1)}, bf16[112,512]{1,0:T(8,128)(2,1)S(1)}, u32[]{:S(2)}, u32[]{:S(2)}) collective-permute-start(bf16[112,512]{1,0:T(8,128)(2,1)S(1)} %get-tuple-element.112), channel_id=1, source_target_pairs={{0,16},{16,0},{1,17},{17,1},{2,18},{18,2},{3,19},{19,3},{4,20},{20... | collective-permute-start | bytes 344072 | tf_op jit(solution)/shard_map/ppermute | solution.py:44
  61.2 0.5 collective-permute-start.18
  61.7 2.0 %collective-permute-done.14.refs_0_ = bf16[112,512]{1,0:T(8,128)(2,1)S(1)} collective-permute-done((bf16[112,512]{1,0:T(8,128)(2,1)S(1)}, bf16[112,512]{1,0:T(8,128)(2,1)S(1)}, u32[]{:S(2)}, u32[]{:S(2)}) %collective-permute-start.14) | collective-permute-done | bytes 114720 | tf_op jit(solution)/shard_map/ppermute | solution.py:48
  63.8 0.9 collective-permute-done.15.refs_1_
  64.6 2.5 %collective-permute-start.17 = (bf16[448,512]{1,0:T(8,128)(2,1)S(1)}, bf16[448,512]{1,0:T(8,128)(2,1)S(1)}, u32[]{:S(2)}, u32[]{:S(2)}) collective-permute-start(bf16[448,512]{1,0:T(8,128)(2,1)S(1)} %get-tuple-element.113), channel_id=1, source_target_pairs={{0,16},{16,0},{1,17},{17,1},{2,18},{18,2},{3,19},{19,3},{4,20},{20... | collective-permute-start | bytes 1376264 | tf_op jit(solution)/shard_map/ppermute | solution.py:44
  67.1 2.9 %ready.1 = (bf16[3072,512]{1,0:T(8,128)(2,1)S(1)}, bf16[512,512]{1,0:T(8,128)(2,1)S(1)}, bf16[2,1024,512]{2,1,0:T(8,128)(2,1)S(1)}, bf16[2,1024,512]{2,1,0:T(8,128)(2,1)S(1)}) custom-call(s32[3]{0:T(128)S(1)} %pad_add_fusion.place_ref.place, f32[2,512]{1,0:T(2,128)S(1)} %copy-done.1, f32[2,512]{1,0:T(2,128)S(1)} %collective-permute-done.7.gp_ref, ...), custom_call_target="tpu_custom_call" | custom-call | bytes 65536 | tf_op jit(solution)/shard_map/ready/pallas_call | solution.py:463
  70.0 4.0 %conv0_near.1 = (bf16[2,512,256]{2,1,0:T(8,128)(2,1)S(1)}, bf16[3072,512]{1,0:T(8,128)(2,1)S(1)}, bf16[512,512]{1,0:T(8,128)(2,1)S(1)}) custom-call(s32[3]{0:T(128)S(1)} %pad_add_fusion.place_ref.place, bf16[2,1024,512]{2,1,0:T(8,128)(2,1)S(1)} %get-tuple-element.134.hm._, ...), custom_call_target="tpu_custom_call", output_to_operand_aliasing={{1}: (5, {}), {2}: (6, {})} | custom-call | bytes 65536 | tf_op jit(solution)/shard_map/conv0_near/pallas_call | solution.py:487
  74.0 0.3 collective-permute-done.17.refs_2_.refs_8_
  74.3 1.3 %collective-permute-done.16.refs_3_.refs_7_ = bf16[448,512]{1,0:T(8,128)(2,1)S(1)} collective-permute-done((bf16[448,512]{1,0:T(8,128)(2,1)S(1)}, bf16[448,512]{1,0:T(8,128)(2,1)S(1)}, u32[]{:S(2)}, u32[]{:S(2)}) %collective-permute-start.16) | collective-permute-done | bytes 458784 | tf_op jit(solution)/shard_map/ppermute | solution.py:48
  75.6 0.3 collective-permute-done.13.refs_1_.refs_6_
  76.0 0.5 collective-permute-start.22
  76.5 0.7 pack.7
  77.2 0.8 collective-permute-start.26
  78.0 1.5 %collective-permute-start.27 = (bf16[336,512]{1,0:T(8,128)(2,1)S(1)}, bf16[336,512]{1,0:T(8,128)(2,1)S(1)}, u32[]{:S(2)}, u32[]{:S(2)}) collective-permute-start(bf16[336,512]{1,0:T(8,128)(2,1)S(1)} %get-tuple-element.148), channel_id=1, source_target_pairs={{0,16},{16,0},{1,17},{17,1},{2,18},{18,2},{3,19},{19,3},{4,20},{20... | collective-permute-start | bytes 1032200 | tf_op jit(solution)/shard_map/ppermute | solution.py:44
  79.5 2.0 %collective-permute-start.25 = (bf16[224,512]{1,0:T(8,128)(2,1)S(1)}, bf16[224,512]{1,0:T(8,128)(2,1)S(1)}, u32[]{:S(2)}, u32[]{:S(2)}) collective-permute-start(bf16[224,512]{1,0:T(8,128)(2,1)S(1)} %get-tuple-element.146), channel_id=1, source_target_pairs={{0,4},{2,6},{4,8},{6,10},{8,12},{10,14},{12,0},{14,2},{1,5},{3,7},... | collective-permute-start | bytes 688136 | tf_op jit(solution)/shard_map/ppermute | solution.py:52
  81.6 3.0 %conv0_far.1 = (bf16[256,256]{1,0:T(8,128)(2,1)S(1)}, bf16[256,256]{1,0:T(8,128)(2,1)S(1)}, bf16[2,1024,512]{2,1,0:T(8,128)(2,1)S(1)}, bf16[2,1024,512]{2,1,0:T(8,128)(2,1)S(1)}) custom-call(s32[3]{0:T(128)S(1)} %pad_add_fusion.place_ref.place, f32[2,512]{1,0:T(2,128)S(1)} %copy-done.1, ...), custom_call_target="tpu_custom_call", output_to_operand_aliasing={{2}: (6, {}), {3}: (7, {})} | custom-call | bytes 65536 | tf_op jit(solution)/shard_map/conv0_far/pallas_call | solution.py:524
  84.7 0.5 collective-permute-start.24
  85.1 2.5 %mix0_near.1 = (bf16[2,2,256,512]{3,2,1,0:T(8,128)(2,1)S(1)}, bf16[2,2,256,512]{3,2,1,0:T(8,128)(2,1)S(1)}, bf16[2,256,512]{2,1,0:T(8,128)(2,1)S(1)}) custom-call(s32[3]{0:T(128)S(1)} %pad_add_fusion.place_ref.place, f32[2,512]{1,0:T(2,128)S(1)} %copy-done.1, f32[2,512]{1,0:T(2,128)S(1)} %collective-permute-done.7.gp_ref, ...), custom_call_target="tpu_custom_call" | custom-call | bytes 65536 | tf_op jit(solution)/shard_map/mix0_near/pallas_call | solution.py:544
  87.7 1.6 %mix0_far.1 = (bf16[1,2,256,512]{3,2,1,0:T(8,128)(2,1)S(1)}, bf16[1,2,256,512]{3,2,1,0:T(8,128)(2,1)S(1)}) custom-call(s32[3]{0:T(128)S(1)} %pad_add_fusion.place_ref.place, f32[2,512]{1,0:T(2,128)S(1)} %copy-done.1, f32[2,512]{1,0:T(2,128)S(1)} %collective-permute-done.7.gp_ref, bf16[512,512]{1,0:T(8,128)(2,1)S(1)} %get-tuple-element.125.mixm_ref, ...), custom_call_target="tpu_custom_call" | custom-call | bytes 65536 | tf_op jit(solution)/shard_map/mix0_far/pallas_call | solution.py:544
  89.3 2.6 %conv1.1 = (bf16[2,256,256]{2,1,0:T(8,128)(2,1)S(1)}, bf16[512,512]{1,0:T(8,128)(2,1)S(1)}) custom-call(s32[3]{0:T(128)S(1)} %pad_add_fusion.place_ref.place, bf16[2,2,256,512]{3,2,1,0:T(8,128)(2,1)S(1)} %get-tuple-element.149.hm_near, bf16[2,2,256,512]{3,2,1,0:T(8,128)(2,1)S(1)} %get-tuple-element.150.hp_near, ...), custom_call_target="tpu_custom_call" | custom-call | tf_op jit(solution)/shard_map/conv1/pallas_call | solution.py:567
  92.1 1.5 %collective-permute-done.28.zp_ref = bf16[2,256,256]{2,1,0:T(8,128)(2,1)S(1)} collective-permute-done((bf16[2,256,256]{2,1,0:T(8,128)(2,1)S(1)}, bf16[2,256,256]{2,1,0:T(8,128)(2,1)S(1)}, u32[]{:S(2)}, u32[]{:S(2)}) %collective-permute-start.28) | collective-permute-done | bytes 262176 | tf_op jit(solution)/shard_map/ppermute | solution.py:40
  93.6 1.7 %mix1.1 = (bf16[256,512]{1,0:T(8,128)(2,1)}, bf16[256,512]{1,0:T(8,128)(2,1)}) custom-call(s32[3]{0:T(128)S(1)} %pad_add_fusion.place_ref.place, bf16[2,256,256]{2,1,0:T(8,128)(2,1)S(1)} %get-tuple-element.165.zm_ref, bf16[2,256,256]{2,1,0:T(8,128)(2,1)S(1)} %collective-permute-done.28.zp_ref, bf16[512,512]{1,0:T(8,128)(2,1)S(1)} %get-tuple-element.166.mix_ref, ...), custom_call_target="tpu_custom_call" | custom-call | tf_op jit(solution)/shard_map/mix1/pallas_call | solution.py:582
  (33 shorter events, 0.8 us)
Async XLA Ops:
  0.6 1.1 %copy-start = (bf16[2,384,2,256]{3,2,1,0:T(2,128)(2,1)S(1)}, bf16[2,384,2,256]{3,2,1,0:T(2,128)(2,1)}, u32[]{:S(2)}) copy-start(bf16[2,384,2,256]{3,2,1,0:T(2,128)(2,1)} %param.8) | copy-start | bytes 2359300
  0.6 10.8 %copy-start.2 = (bf16[256,512]{1,0:T(8,128)(2,1)S(1)}, bf16[256,512]{1,0:T(8,128)(2,1)}, u32[]{:S(2)}) copy-start(bf16[256,512]{1,0:T(8,128)(2,1)} %param.6) | copy-start | bytes 786436
  2.0 22.9 %copy-start.1 = (f32[2,512]{1,0:T(2,128)S(1)}, f32[2,512]{1,0:T(2,128)}, u32[]{:S(2)}) copy-start(f32[2,512]{1,0:T(2,128)} %gm_ref.7) | copy-start | bytes 12292
  3.2 18.3 %collective-permute-start.3 = (bf16[448,512]{1,0:T(8,128)(2,1)S(1)}, bf16[448,512]{1,0:T(8,128)(2,1)S(1)}, u32[]{:S(2)}, u32[]{:S(2)}) collective-permute-start(bf16[448,512]{1,0:T(8,128)(2,1)S(1)} %get-tuple-element.153.refs_0_.refs_6_), channel_id=1, source_target_pairs={{0,16},{16,0},{1,17},{17,1},{2,18},{18,2},{3,19},{19,3},{4,20},{20... | collective-permute-start | bytes 1376264 | tf_op jit(solution)/shard_map/ppermute | solution.py:44
  6.3 15.2 %collective-permute-start.2 = (bf16[448,512]{1,0:T(8,128)(2,1)S(1)}, bf16[448,512]{1,0:T(8,128)(2,1)S(1)}, u32[]{:S(2)}, u32[]{:S(2)}) collective-permute-start(bf16[448,512]{1,0:T(8,128)(2,1)S(1)} %get-tuple-element.153.refs_0_.refs_6_), channel_id=1, source_target_pairs={{0,2},{2,0},{4,6},{6,4},{8,10},{10,8},{12,14},{14,12},{1,3},{3,1},... | collective-permute-start | bytes 1376264 | tf_op jit(solution)/shard_map/ppermute | solution.py:48
  7.8 9.7 %collective-permute-start.1 = (bf16[224,512]{1,0:T(8,128)(2,1)S(1)}, bf16[224,512]{1,0:T(8,128)(2,1)S(1)}, u32[]{:S(2)}, u32[]{:S(2)}) collective-permute-start(bf16[224,512]{1,0:T(8,128)(2,1)S(1)} %get-tuple-element.85), channel_id=1, source_target_pairs={{0,12},{2,14},{4,0},{6,2},{8,4},{10,6},{12,8},{14,10},{1,13},{3,15... | collective-permute-start | bytes 688136 | tf_op jit(solution)/shard_map/ppermute | solution.py:52
  11.4 10.1 %collective-permute-start = (bf16[224,512]{1,0:T(8,128)(2,1)S(1)}, bf16[224,512]{1,0:T(8,128)(2,1)S(1)}, u32[]{:S(2)}, u32[]{:S(2)}) collective-permute-start(bf16[224,512]{1,0:T(8,128)(2,1)S(1)} %get-tuple-element.85), channel_id=1, source_target_pairs={{0,4},{2,6},{4,8},{6,10},{8,12},{10,14},{12,0},{14,2},{1,5},{3,7},... | collective-permute-start | bytes 688136 | tf_op jit(solution)/shard_map/ppermute | solution.py:52
  22.2 18.9 %collective-permute-start.4 = (bf16[736,512]{1,0:T(8,128)(2,1)S(1)}, bf16[736,512]{1,0:T(8,128)(2,1)S(1)}, u32[]{:S(2)}, u32[]{:S(2)}) collective-permute-start(bf16[736,512]{1,0:T(8,128)(2,1)S(1)} %get-tuple-element.93), channel_id=1, source_target_pairs={{0,4},{2,6},{4,8},{6,10},{8,12},{10,14},{12,0},{14,2},{1,5},{3,7},... | collective-permute-start | bytes 2261000 | tf_op jit(solution)/shard_map/ppermute | solution.py:52
  23.9 15.5 %collective-permute-start.5 = (bf16[672,512]{1,0:T(8,128)(2,1)S(1)}, bf16[672,512]{1,0:T(8,128)(2,1)S(1)}, u32[]{:S(2)}, u32[]{:S(2)}) collective-permute-start(bf16[672,512]{1,0:T(8,128)(2,1)S(1)} %get-tuple-element.94), channel_id=1, source_target_pairs={{0,2},{2,0},{4,6},{6,4},{8,10},{10,8},{12,14},{14,12},{1,3},{3,1},... | collective-permute-start | bytes 2064392 | tf_op jit(solution)/shard_map/ppermute | solution.py:48
  24.4 15.2 %collective-permute-start.6 = (bf16[672,512]{1,0:T(8,128)(2,1)S(1)}, bf16[672,512]{1,0:T(8,128)(2,1)S(1)}, u32[]{:S(2)}, u32[]{:S(2)}) collective-permute-start(bf16[672,512]{1,0:T(8,128)(2,1)S(1)} %get-tuple-element.95), channel_id=1, source_target_pairs={{0,16},{16,0},{1,17},{17,1},{2,18},{18,2},{3,19},{19,3},{4,20},{20... | collective-permute-start | bytes 2064392 | tf_op jit(solution)/shard_map/ppermute | solution.py:44
  24.9 1.9 %collective-permute-start.8 = (bf16[512,512]{1,0:T(8,128)(2,1)S(1)}, bf16[512,512]{1,0:T(8,128)(2,1)S(1)}, u32[]{:S(2)}, u32[]{:S(2)}) collective-permute-start(bf16[512,512]{1,0:T(8,128)(2,1)S(1)} %bitcast.14), channel_id=1, source_target_pairs={{0,1},{1,0},{2,3},{3,2},{4,5},{5,4},{6,7},{7,6},{8,9},{9,8},{10,11... | collective-permute-start | bytes 1572872 | tf_op jit(solution)/shard_map/ppermute | solution.py:40
  24.9 1.9 %collective-permute-start.7 = (f32[2,512]{1,0:T(2,128)S(1)}, f32[2,512]{1,0:T(2,128)S(1)}, u32[]{:S(2)}, u32[]{:S(2)}) collective-permute-start(f32[2,512]{1,0:T(2,128)S(1)} %copy-done.1), channel_id=1, source_target_pairs={{0,1},{1,0},{2,3},{3,2},{4,5},{5,4},{6,7},{7,6},{8,9},{9,8},{10,11... | collective-permute-start | bytes 12296 | tf_op jit(solution)/shard_map/ppermute | solution.py:40
  41.9 16.2 %collective-permute-start.11 = (bf16[736,512]{1,0:T(8,128)(2,1)S(1)}, bf16[736,512]{1,0:T(8,128)(2,1)S(1)}, u32[]{:S(2)}, u32[]{:S(2)}) collective-permute-start(bf16[736,512]{1,0:T(8,128)(2,1)S(1)} %get-tuple-element.103), channel_id=1, source_target_pairs={{0,2},{2,0},{4,6},{6,4},{8,10},{10,8},{12,14},{14,12},{1,3},{3,1},... | collective-permute-start | bytes 2261000 | tf_op jit(solution)/shard_map/ppermute | solution.py:48
  42.5 14.7 %collective-permute-start.12 = (bf16[672,512]{1,0:T(8,128)(2,1)S(1)}, bf16[672,512]{1,0:T(8,128)(2,1)S(1)}, u32[]{:S(2)}, u32[]{:S(2)}) collective-permute-start(bf16[672,512]{1,0:T(8,128)(2,1)S(1)} %get-tuple-element.104), channel_id=1, source_target_pairs={{0,16},{16,0},{1,17},{17,1},{2,18},{18,2},{3,19},{19,3},{4,20},{20... | collective-permute-start | bytes 2064392 | tf_op jit(solution)/shard_map/ppermute | solution.py:44
  43.0 14.2 %collective-permute-start.9 = (bf16[448,512]{1,0:T(8,128)(2,1)S(1)}, bf16[448,512]{1,0:T(8,128)(2,1)S(1)}, u32[]{:S(2)}, u32[]{:S(2)}) collective-permute-start(bf16[448,512]{1,0:T(8,128)(2,1)S(1)} %get-tuple-element.101), channel_id=1, source_target_pairs={{0,4},{2,6},{4,8},{6,10},{8,12},{10,14},{12,0},{14,2},{1,5},{3,7},... | collective-permute-start | bytes 1376264 | tf_op jit(solution)/shard_map/ppermute | solution.py:52
  43.0 14.2 %collective-permute-start.10 = (bf16[224,512]{1,0:T(8,128)(2,1)S(1)}, bf16[224,512]{1,0:T(8,128)(2,1)S(1)}, u32[]{:S(2)}, u32[]{:S(2)}) collective-permute-start(bf16[224,512]{1,0:T(8,128)(2,1)S(1)} %get-tuple-element.102), channel_id=1, source_target_pairs={{0,12},{2,14},{4,0},{6,2},{8,4},{10,6},{12,8},{14,10},{1,13},{3,15... | collective-permute-start | bytes 688136 | tf_op jit(solution)/shard_map/ppermute | solution.py:52
  58.9 17.1 %collective-permute-start.13 = (bf16[736,512]{1,0:T(8,128)(2,1)S(1)}, bf16[736,512]{1,0:T(8,128)(2,1)S(1)}, u32[]{:S(2)}, u32[]{:S(2)}) collective-permute-start(bf16[736,512]{1,0:T(8,128)(2,1)S(1)} %get-tuple-element.109), channel_id=1, source_target_pairs={{0,4},{2,6},{4,8},{6,10},{8,12},{10,14},{12,0},{14,2},{1,5},{3,7},... | collective-permute-start | bytes 2261000 | tf_op jit(solution)/shard_map/ppermute | solution.py:52
  58.9 4.9 %collective-permute-start.14 = (bf16[112,512]{1,0:T(8,128)(2,1)S(1)}, bf16[112,512]{1,0:T(8,128)(2,1)S(1)}, u32[]{:S(2)}, u32[]{:S(2)}) collective-permute-start(bf16[112,512]{1,0:T(8,128)(2,1)S(1)} %get-tuple-element.111), channel_id=1, source_target_pairs={{0,2},{2,0},{4,6},{6,4},{8,10},{10,8},{12,14},{14,12},{1,3},{3,1},... | collective-permute-start | bytes 344072 | tf_op jit(solution)/shard_map/ppermute | solution.py:48
  59.7 4.9 %collective-permute-start.15 = (bf16[112,512]{1,0:T(8,128)(2,1)S(1)}, bf16[112,512]{1,0:T(8,128)(2,1)S(1)}, u32[]{:S(2)}, u32[]{:S(2)}) collective-permute-start(bf16[112,512]{1,0:T(8,128)(2,1)S(1)} %get-tuple-element.112), channel_id=1, source_target_pairs={{0,16},{16,0},{1,17},{17,1},{2,18},{18,2},{3,19},{19,3},{4,20},{20... | collective-permute-start | bytes 344072 | tf_op jit(solution)/shard_map/ppermute | solution.py:44
  61.2 5.9 %collective-permute-start.19 = (bf16[512,512]{1,0:T(8,128)(2,1)S(1)}, bf16[512,512]{1,0:T(8,128)(2,1)S(1)}, u32[]{:S(2)}, u32[]{:S(2)}) collective-permute-start(bf16[512,512]{1,0:T(8,128)(2,1)S(1)} %get-tuple-element.115), channel_id=1, source_target_pairs={{0,1},{1,0},{2,3},{3,2},{4,5},{5,4},{6,7},{7,6},{8,9},{9,8},{10,11... | collective-permute-start | bytes 1572872 | tf_op jit(solution)/shard_map/ppermute | solution.py:40
  61.2 5.9 %collective-permute-start.18 = (bf16[512,512]{1,0:T(8,128)(2,1)S(1)}, bf16[512,512]{1,0:T(8,128)(2,1)S(1)}, u32[]{:S(2)}, u32[]{:S(2)}) collective-permute-start(bf16[512,512]{1,0:T(8,128)(2,1)S(1)} %get-tuple-element.114), channel_id=1, source_target_pairs={{0,1},{1,0},{2,3},{3,2},{4,5},{5,4},{6,7},{7,6},{8,9},{9,8},{10,11... | collective-permute-start | bytes 1572872 | tf_op jit(solution)/shard_map/ppermute | solution.py:40
  64.6 9.7 %collective-permute-start.17 = (bf16[448,512]{1,0:T(8,128)(2,1)S(1)}, bf16[448,512]{1,0:T(8,128)(2,1)S(1)}, u32[]{:S(2)}, u32[]{:S(2)}) collective-permute-start(bf16[448,512]{1,0:T(8,128)(2,1)S(1)} %get-tuple-element.113), channel_id=1, source_target_pairs={{0,16},{16,0},{1,17},{17,1},{2,18},{18,2},{3,19},{19,3},{4,20},{20... | collective-permute-start | bytes 1376264 | tf_op jit(solution)/shard_map/ppermute | solution.py:44
  67.1 8.5 %collective-permute-start.16 = (bf16[448,512]{1,0:T(8,128)(2,1)S(1)}, bf16[448,512]{1,0:T(8,128)(2,1)S(1)}, u32[]{:S(2)}, u32[]{:S(2)}) collective-permute-start(bf16[448,512]{1,0:T(8,128)(2,1)S(1)} %get-tuple-element.113), channel_id=1, source_target_pairs={{0,2},{2,0},{4,6},{6,4},{8,10},{10,8},{12,14},{14,12},{1,3},{3,1},... | collective-permute-start | bytes 1376264 | tf_op jit(solution)/shard_map/ppermute | solution.py:48
  76.0 3.6 %collective-permute-start.21 = (bf16[2,512,256]{2,1,0:T(8,128)(2,1)S(1)}, bf16[2,512,256]{2,1,0:T(8,128)(2,1)S(1)}, u32[]{:S(2)}, u32[]{:S(2)}) collective-permute-start(bf16[2,512,256]{2,1,0:T(8,128)(2,1)S(1)} %get-tuple-element.142.refs_0_), channel_id=1, source_target_pairs={{0,1},{1,0},{2,3},{3,2},{4,5},{5,4},{6,7},{7,6},{8,9},{9,8},{10,11... | collective-permute-start | bytes 1572872 | tf_op jit(solution)/shard_map/ppermute | solution.py:40
  76.0 5.6 %collective-permute-start.22 = (bf16[512,512]{1,0:T(8,128)(2,1)S(1)}, bf16[512,512]{1,0:T(8,128)(2,1)S(1)}, u32[]{:S(2)}, u32[]{:S(2)}) collective-permute-start(bf16[512,512]{1,0:T(8,128)(2,1)S(1)} %get-tuple-element.125.mixm_ref), channel_id=1, source_target_pairs={{0,1},{1,0},{2,3},{3,2},{4,5},{5,4},{6,7},{7,6},{8,9},{9,8},{10,11... | collective-permute-start | bytes 1572872 | tf_op jit(solution)/shard_map/ppermute | solution.py:40
  77.1 4.4 %collective-permute-start.20 = (bf16[2,256,512]{2,1,0:T(8,128)(2,1)S(1)}, bf16[2,256,512]{2,1,0:T(8,128)(2,1)S(1)}, u32[]{:S(2)}, u32[]{:S(2)}) collective-permute-start(bf16[2,256,512]{2,1,0:T(8,128)(2,1)S(1)} %bitcast.26), channel_id=1, source_target_pairs={{0,1},{1,0},{2,3},{3,2},{4,5},{5,4},{6,7},{7,6},{8,9},{9,8},{10,11... | collective-permute-start | bytes 1572872 | tf_op jit(solution)/shard_map/ppermute | solution.py:40
  77.2 12.1 %collective-permute-start.26 = (bf16[336,512]{1,0:T(8,128)(2,1)S(1)}, bf16[336,512]{1,0:T(8,128)(2,1)S(1)}, u32[]{:S(2)}, u32[]{:S(2)}) collective-permute-start(bf16[336,512]{1,0:T(8,128)(2,1)S(1)} %get-tuple-element.147), channel_id=1, source_target_pairs={{0,2},{2,0},{4,6},{6,4},{8,10},{10,8},{12,14},{14,12},{1,3},{3,1},... | collective-permute-start | bytes 1032200 | tf_op jit(solution)/shard_map/ppermute | solution.py:48
  78.0 11.3 %collective-permute-start.27 = (bf16[336,512]{1,0:T(8,128)(2,1)S(1)}, bf16[336,512]{1,0:T(8,128)(2,1)S(1)}, u32[]{:S(2)}, u32[]{:S(2)}) collective-permute-start(bf16[336,512]{1,0:T(8,128)(2,1)S(1)} %get-tuple-element.148), channel_id=1, source_target_pairs={{0,16},{16,0},{1,17},{17,1},{2,18},{18,2},{3,19},{19,3},{4,20},{20... | collective-permute-start | bytes 1032200 | tf_op jit(solution)/shard_map/ppermute | solution.py:44
  79.5 9.8 %collective-permute-start.25 = (bf16[224,512]{1,0:T(8,128)(2,1)S(1)}, bf16[224,512]{1,0:T(8,128)(2,1)S(1)}, u32[]{:S(2)}, u32[]{:S(2)}) collective-permute-start(bf16[224,512]{1,0:T(8,128)(2,1)S(1)} %get-tuple-element.146), channel_id=1, source_target_pairs={{0,4},{2,6},{4,8},{6,10},{8,12},{10,14},{12,0},{14,2},{1,5},{3,7},... | collective-permute-start | bytes 688136 | tf_op jit(solution)/shard_map/ppermute | solution.py:52
  84.6 3.1 %collective-permute-start.23 = (bf16[256,256]{1,0:T(8,128)(2,1)S(1)}, bf16[256,256]{1,0:T(8,128)(2,1)S(1)}, u32[]{:S(2)}, u32[]{:S(2)}) collective-permute-start(bf16[256,256]{1,0:T(8,128)(2,1)S(1)} %get-tuple-element.138.refs_0_), channel_id=1, source_target_pairs={{0,1},{1,0},{2,3},{3,2},{4,5},{5,4},{6,7},{7,6},{8,9},{9,8},{10,11... | collective-permute-start | bytes 393224 | tf_op jit(solution)/shard_map/ppermute | solution.py:40
  84.7 3.0 %collective-permute-start.24 = (bf16[256,256]{1,0:T(8,128)(2,1)S(1)}, bf16[256,256]{1,0:T(8,128)(2,1)S(1)}, u32[]{:S(2)}, u32[]{:S(2)}) collective-permute-start(bf16[256,256]{1,0:T(8,128)(2,1)S(1)} %get-tuple-element.139.refs_1_), channel_id=1, source_target_pairs={{0,1},{1,0},{2,3},{3,2},{4,5},{5,4},{6,7},{7,6},{8,9},{9,8},{10,11... | collective-permute-start | bytes 393224 | tf_op jit(solution)/shard_map/ppermute | solution.py:40
  92.0 1.6 %collective-permute-start.28 = (bf16[2,256,256]{2,1,0:T(8,128)(2,1)S(1)}, bf16[2,256,256]{2,1,0:T(8,128)(2,1)S(1)}, u32[]{:S(2)}, u32[]{:S(2)}) collective-permute-start(bf16[2,256,256]{2,1,0:T(8,128)(2,1)S(1)} %get-tuple-element.165.zm_ref), channel_id=1, source_target_pairs={{0,1},{1,0},{2,3},{3,2},{4,5},{5,4},{6,7},{7,6},{8,9},{9,8},{10,11... | collective-permute-start | bytes 786440 | tf_op jit(solution)/shard_map/ppermute | solution.py:40

commit v9 on v8

--- a/solution.py
+++ b/solution.py
@@ -105,7 +105,7 @@
 
 def norm_rows(gm, gp, mine, theirs, hm, hp, base):
     rows, half = mine.shape[1:]
-    step = 64
+    step = min(256, rows)
 
     def body(i, carry):
         at = pl.ds(pl.multiple_of(i * step, step), step)
@@ -470,7 +470,7 @@
             ),
             in_specs=[SMEM] + [VMEM] * (2 + 2 * len(mine) + len(pieces)),
             out_specs=(VMEM,) * 4,
-            compiler_params=scoped(4),
+            compiler_params=scoped(10),
             cost_estimate=cost(0, 2**16),
             name="ready",
         )(
@@ -533,7 +533,7 @@
         out_specs=(VMEM,) * 4,
         input_output_aliases={6: 2, 7: 3},
         scratch_shapes=[pltpu.VMEM((2, rows, 2 * branch), F32)],
-        compiler_params=scoped(8),
+        compiler_params=scoped(12),
         cost_estimate=cost(0, 2**16),
         name="conv0_far",
     )(place, near(gains), near(gains_p), near(last), near(last_theirs), wide, hm, hp)[:2]

time: 95.5 us -> 95.2 us (level)
  no operation moved by 1% of the time
where the time goes in v9:
time: 95.2 us; the launch traced here: 95 us
  waiting for transfers between devices  42.8 us (45%)
  starting transfers between devices  27.3 us (29%)
  Pallas kernels  20.5 us (22%)
  local copies, waits for them, and re-layouts  2.51 us (3%)
  other arithmetic  1.08 us (1%)
    ppermute x7, waiting for transfers between devices, ring(): return lax.ppermute(block, 'seq', [(s, (s + by) % seq) for s in range(seq)])  21.3 us
    ppermute x6, waiting for transfers between devices, swap_pair(): return lax.ppermute(block, 'seq', [(s, s ^ 1) for s in range(seq)])  16.7 us
    ppermute x7, starting transfers between devices, ring(): return lax.ppermute(block, 'seq', [(s, (s + by) % seq) for s in range(seq)])  11.2 us
    ppermute x6, starting transfers between devices, swap_groups(): return lax.ppermute(block, 'groups', [(0, 1), (1, 0)])  9.56 us
    ppermute x6, starting transfers between devices, swap_pair(): return lax.ppermute(block, 'seq', [(s, s ^ 1) for s in range(seq)])  4.22 us
    pallas_call x2, Pallas kernels, mix0(): pl.pallas_call(functools.partial(mix0_kernel, (rows, half, branch, 1, n,...  4.09 us
    pallas_call x1, Pallas kernels, newest(): pl.pallas_call(functools.partial(conv0_near_kernel, (rows, half, branch,...  4.01 us
    ppermute x10, waiting for transfers between devices, swap_chan(): return lax.ppermute(block, 'chan', [(0, 1), (1, 0)])  2.88 us
  transfers between devices with their start and end apart: 29, of which 14 were waited for; matrix products, arithmetic and copies ran while one was open for 1% of the time, Pallas kernels for 15%

profile of v9, /device:TPU:0, one launch (start us, length us, event | category | flops | bytes accessed | tf_op | source)
XLA Modules:
  0.0 95.0 jit_solution(6203353029460262941)
XLA Ops:
  0.7 1.1 %copy-done = bf16[2,384,2,256]{3,2,1,0:T(2,128)(2,1)S(1)} copy-done((bf16[2,384,2,256]{3,2,1,0:T(2,128)(2,1)S(1)}, bf16[2,384,2,256]{3,2,1,0:T(2,128)(2,1)}, u32[]{:S(2)}) %copy-start) | copy-done | bytes 786456
  1.8 0.3 constant_dynamic-slice_fusion.1
  2.3 0.9 constant_dynamic-slice_fusion.mix
  3.2 3.0 %collective-permute-start.3 = (bf16[448,512]{1,0:T(8,128)(2,1)S(1)}, bf16[448,512]{1,0:T(8,128)(2,1)S(1)}, u32[]{:S(2)}, u32[]{:S(2)}) collective-permute-start(bf16[448,512]{1,0:T(8,128)(2,1)S(1)} %get-tuple-element.153.refs_0_.refs_6_), channel_id=1, source_target_pairs={{0,16},{16,0},{1,17},{17,1},{2,18},{18,2},{3,19},{19,3},{4,20},{20... | collective-permute-start | bytes 1376264 | tf_op jit(solution)/shard_map/ppermute | solution.py:44
  6.3 1.5 %collective-permute-start.2 = (bf16[448,512]{1,0:T(8,128)(2,1)S(1)}, bf16[448,512]{1,0:T(8,128)(2,1)S(1)}, u32[]{:S(2)}, u32[]{:S(2)}) collective-permute-start(bf16[448,512]{1,0:T(8,128)(2,1)S(1)} %get-tuple-element.153.refs_0_.refs_6_), channel_id=1, source_target_pairs={{0,2},{2,0},{4,6},{6,4},{8,10},{10,8},{12,14},{14,12},{1,3},{3,1},... | collective-permute-start | bytes 1376264 | tf_op jit(solution)/shard_map/ppermute | solution.py:48
  7.8 3.6 %collective-permute-start.1 = (bf16[224,512]{1,0:T(8,128)(2,1)S(1)}, bf16[224,512]{1,0:T(8,128)(2,1)S(1)}, u32[]{:S(2)}, u32[]{:S(2)}) collective-permute-start(bf16[224,512]{1,0:T(8,128)(2,1)S(1)} %get-tuple-element.85), channel_id=1, source_target_pairs={{0,12},{2,14},{4,0},{6,2},{8,4},{10,6},{12,8},{14,10},{1,13},{3,15... | collective-permute-start | bytes 688136 | tf_op jit(solution)/shard_map/ppermute | solution.py:52
  11.4 1.0 %pad_maximum_fusion = bf16[2,256,512]{2,1,0:T(8,128)(2,1)S(1)} fusion(bf16[1,256,512]{2,1,0:T(8,128)(2,1)S(1)} %bitcast.28, bf16[1,256,512]{2,1,0:T(8,128)(2,1)} %bitcast.29), kind=kLoop, calls=%fused_computation | loop fusion | flops 262144 | bytes 1048576 | tf_op jit(solution)/shard_map/stack | solution.py:413
  12.4 5.0 %collective-permute-done.1.refs_2_.refs_8_ = bf16[224,512]{1,0:T(8,128)(2,1)S(1)} collective-permute-done((bf16[224,512]{1,0:T(8,128)(2,1)S(1)}, bf16[224,512]{1,0:T(8,128)(2,1)S(1)}, u32[]{:S(2)}, u32[]{:S(2)}) %collective-permute-start.1) | collective-permute-done | bytes 229408 | tf_op jit(solution)/shard_map/ppermute | solution.py:52
  17.4 4.1 %collective-permute-done.refs_0_.refs_7_ = bf16[224,512]{1,0:T(8,128)(2,1)S(1)} collective-permute-done((bf16[224,512]{1,0:T(8,128)(2,1)S(1)}, bf16[224,512]{1,0:T(8,128)(2,1)S(1)}, u32[]{:S(2)}, u32[]{:S(2)}) %collective-permute-start) | collective-permute-done | bytes 229408 | tf_op jit(solution)/shard_map/ppermute | solution.py:52
  21.5 0.7 pack.4
  22.2 1.7 %collective-permute-start.4 = (bf16[736,512]{1,0:T(8,128)(2,1)S(1)}, bf16[736,512]{1,0:T(8,128)(2,1)S(1)}, u32[]{:S(2)}, u32[]{:S(2)}) collective-permute-start(bf16[736,512]{1,0:T(8,128)(2,1)S(1)} %get-tuple-element.93), channel_id=1, source_target_pairs={{0,4},{2,6},{4,8},{6,10},{8,12},{10,14},{12,0},{14,2},{1,5},{3,7},... | collective-permute-start | bytes 2261000 | tf_op jit(solution)/shard_map/ppermute | solution.py:52
  23.9 0.5 collective-permute-start.5
  24.4 0.5 collective-permute-start.6
  24.9 0.5 collective-permute-start.7
  25.4 1.4 %collective-permute-done.7.gp_ref = f32[2,512]{1,0:T(2,128)S(1)} collective-permute-done((f32[2,512]{1,0:T(2,128)S(1)}, f32[2,512]{1,0:T(2,128)S(1)}, u32[]{:S(2)}, u32[]{:S(2)}) %collective-permute-start.7) | collective-permute-done | bytes 4128 | tf_op jit(solution)/shard_map/ppermute | solution.py:40
  26.8 12.5 %collective-permute-done.5.refs_1_.refs_12_.refs_3_ = bf16[672,512]{1,0:T(8,128)(2,1)S(1)} collective-permute-done((bf16[672,512]{1,0:T(8,128)(2,1)S(1)}, bf16[672,512]{1,0:T(8,128)(2,1)S(1)}, u32[]{:S(2)}, u32[]{:S(2)}) %collective-permute-start.5) | collective-permute-done | bytes 688160 | tf_op jit(solution)/shard_map/ppermute | solution.py:48
  39.3 0.3 collective-permute-done.6.refs_13_
  39.6 1.6 %collective-permute-done.4.refs_2_.refs_11_ = bf16[736,512]{1,0:T(8,128)(2,1)S(1)} collective-permute-done((bf16[736,512]{1,0:T(8,128)(2,1)S(1)}, bf16[736,512]{1,0:T(8,128)(2,1)S(1)}, u32[]{:S(2)}, u32[]{:S(2)}) %collective-permute-start.4) | collective-permute-done | bytes 753696 | tf_op jit(solution)/shard_map/ppermute | solution.py:52
  41.1 0.8 pack.5
  41.9 0.6 collective-permute-start.11
  42.5 0.5 collective-permute-start.12
  43.0 3.8 %collective-permute-start.10 = (bf16[224,512]{1,0:T(8,128)(2,1)S(1)}, bf16[224,512]{1,0:T(8,128)(2,1)S(1)}, u32[]{:S(2)}, u32[]{:S(2)}) collective-permute-start(bf16[224,512]{1,0:T(8,128)(2,1)S(1)} %get-tuple-element.102), channel_id=1, source_target_pairs={{0,12},{2,14},{4,0},{6,2},{8,4},{10,6},{12,8},{14,10},{1,13},{3,15... | collective-permute-start | bytes 688136 | tf_op jit(solution)/shard_map/ppermute | solution.py:52
  46.8 10.4 %collective-permute-done.10.refs_2_.refs_5_ = bf16[224,512]{1,0:T(8,128)(2,1)S(1)} collective-permute-done((bf16[224,512]{1,0:T(8,128)(2,1)S(1)}, bf16[224,512]{1,0:T(8,128)(2,1)S(1)}, u32[]{:S(2)}, u32[]{:S(2)}) %collective-permute-start.10) | collective-permute-done | bytes 229408 | tf_op jit(solution)/shard_map/ppermute | solution.py:52
  57.2 0.9 collective-permute-done.11.refs_1_.refs_14_
  58.1 0.7 pack.6
  58.9 0.8 collective-permute-start.14
  59.7 1.5 %collective-permute-start.15 = (bf16[112,512]{1,0:T(8,128)(2,1)S(1)}, bf16[112,512]{1,0:T(8,128)(2,1)S(1)}, u32[]{:S(2)}, u32[]{:S(2)}) collective-permute-start(bf16[112,512]{1,0:T(8,128)(2,1)S(1)} %get-tuple-element.112), channel_id=1, source_target_pairs={{0,16},{16,0},{1,17},{17,1},{2,18},{18,2},{3,19},{19,3},{4,20},{20... | collective-permute-start | bytes 344072 | tf_op jit(solution)/shard_map/ppermute | solution.py:44
  61.2 0.5 collective-permute-start.18
  61.7 2.0 %collective-permute-done.14.refs_0_ = bf16[112,512]{1,0:T(8,128)(2,1)S(1)} collective-permute-done((bf16[112,512]{1,0:T(8,128)(2,1)S(1)}, bf16[112,512]{1,0:T(8,128)(2,1)S(1)}, u32[]{:S(2)}, u32[]{:S(2)}) %collective-permute-start.14) | collective-permute-done | bytes 114720 | tf_op jit(solution)/shard_map/ppermute | solution.py:48
  63.8 0.9 collective-permute-done.15.refs_1_
  64.6 2.5 %collective-permute-start.17 = (bf16[448,512]{1,0:T(8,128)(2,1)S(1)}, bf16[448,512]{1,0:T(8,128)(2,1)S(1)}, u32[]{:S(2)}, u32[]{:S(2)}) collective-permute-start(bf16[448,512]{1,0:T(8,128)(2,1)S(1)} %get-tuple-element.113), channel_id=1, source_target_pairs={{0,16},{16,0},{1,17},{17,1},{2,18},{18,2},{3,19},{19,3},{4,20},{20... | collective-permute-start | bytes 1376264 | tf_op jit(solution)/shard_map/ppermute | solution.py:44
  67.1 2.4 %ready.1 = (bf16[3072,512]{1,0:T(8,128)(2,1)S(1)}, bf16[512,512]{1,0:T(8,128)(2,1)S(1)}, bf16[2,1024,512]{2,1,0:T(8,128)(2,1)S(1)}, bf16[2,1024,512]{2,1,0:T(8,128)(2,1)S(1)}) custom-call(s32[3]{0:T(128)S(1)} %pad_add_fusion.place_ref.place, f32[2,512]{1,0:T(2,128)S(1)} %copy-done.1, f32[2,512]{1,0:T(2,128)S(1)} %collective-permute-done.7.gp_ref, ...), custom_call_target="tpu_custom_call" | custom-call | bytes 65536 | tf_op jit(solution)/shard_map/ready/pallas_call | solution.py:463
  69.6 4.0 %conv0_near.1 = (bf16[2,512,256]{2,1,0:T(8,128)(2,1)S(1)}, bf16[3072,512]{1,0:T(8,128)(2,1)S(1)}, bf16[512,512]{1,0:T(8,128)(2,1)S(1)}) custom-call(s32[3]{0:T(128)S(1)} %pad_add_fusion.place_ref.place, bf16[2,1024,512]{2,1,0:T(8,128)(2,1)S(1)} %get-tuple-element.134.hm._, ...), custom_call_target="tpu_custom_call", output_to_operand_aliasing={{1}: (5, {}), {2}: (6, {})} | custom-call | bytes 65536 | tf_op jit(solution)/shard_map/conv0_near/pallas_call | solution.py:487
  73.6 0.7 collective-permute-done.17.refs_2_.refs_8_
  74.3 1.3 %collective-permute-done.16.refs_3_.refs_7_ = bf16[448,512]{1,0:T(8,128)(2,1)S(1)} collective-permute-done((bf16[448,512]{1,0:T(8,128)(2,1)S(1)}, bf16[448,512]{1,0:T(8,128)(2,1)S(1)}, u32[]{:S(2)}, u32[]{:S(2)}) %collective-permute-start.16) | collective-permute-done | bytes 458784 | tf_op jit(solution)/shard_map/ppermute | solution.py:48
  75.6 0.3 collective-permute-done.13.refs_1_.refs_6_
  76.0 0.5 collective-permute-start.22
  76.5 0.7 pack.7
  77.2 0.8 collective-permute-start.26
  78.0 1.5 %collective-permute-start.27 = (bf16[336,512]{1,0:T(8,128)(2,1)S(1)}, bf16[336,512]{1,0:T(8,128)(2,1)S(1)}, u32[]{:S(2)}, u32[]{:S(2)}) collective-permute-start(bf16[336,512]{1,0:T(8,128)(2,1)S(1)} %get-tuple-element.148), channel_id=1, source_target_pairs={{0,16},{16,0},{1,17},{17,1},{2,18},{18,2},{3,19},{19,3},{4,20},{20... | collective-permute-start | bytes 1032200 | tf_op jit(solution)/shard_map/ppermute | solution.py:44
  79.5 2.0 %collective-permute-start.25 = (bf16[224,512]{1,0:T(8,128)(2,1)S(1)}, bf16[224,512]{1,0:T(8,128)(2,1)S(1)}, u32[]{:S(2)}, u32[]{:S(2)}) collective-permute-start(bf16[224,512]{1,0:T(8,128)(2,1)S(1)} %get-tuple-element.146), channel_id=1, source_target_pairs={{0,4},{2,6},{4,8},{6,10},{8,12},{10,14},{12,0},{14,2},{1,5},{3,7},... | collective-permute-start | bytes 688136 | tf_op jit(solution)/shard_map/ppermute | solution.py:52
  81.6 2.8 %conv0_far.1 = (bf16[256,256]{1,0:T(8,128)(2,1)S(1)}, bf16[256,256]{1,0:T(8,128)(2,1)S(1)}, bf16[2,1024,512]{2,1,0:T(8,128)(2,1)S(1)}, bf16[2,1024,512]{2,1,0:T(8,128)(2,1)S(1)}) custom-call(s32[3]{0:T(128)S(1)} %pad_add_fusion.place_ref.place, f32[2,512]{1,0:T(2,128)S(1)} %copy-done.1, ...), custom_call_target="tpu_custom_call", output_to_operand_aliasing={{2}: (6, {}), {3}: (7, {})} | custom-call | bytes 65536 | tf_op jit(solution)/shard_map/conv0_far/pallas_call | solution.py:524
  84.4 0.5 collective-permute-start.24
  84.9 2.5 %mix0_near.1 = (bf16[2,2,256,512]{3,2,1,0:T(8,128)(2,1)S(1)}, bf16[2,2,256,512]{3,2,1,0:T(8,128)(2,1)S(1)}, bf16[2,256,512]{2,1,0:T(8,128)(2,1)S(1)}) custom-call(s32[3]{0:T(128)S(1)} %pad_add_fusion.place_ref.place, f32[2,512]{1,0:T(2,128)S(1)} %copy-done.1, f32[2,512]{1,0:T(2,128)S(1)} %collective-permute-done.7.gp_ref, ...), custom_call_target="tpu_custom_call" | custom-call | bytes 65536 | tf_op jit(solution)/shard_map/mix0_near/pallas_call | solution.py:544
  87.4 1.6 %mix0_far.1 = (bf16[1,2,256,512]{3,2,1,0:T(8,128)(2,1)S(1)}, bf16[1,2,256,512]{3,2,1,0:T(8,128)(2,1)S(1)}) custom-call(s32[3]{0:T(128)S(1)} %pad_add_fusion.place_ref.place, f32[2,512]{1,0:T(2,128)S(1)} %copy-done.1, f32[2,512]{1,0:T(2,128)S(1)} %collective-permute-done.7.gp_ref, bf16[512,512]{1,0:T(8,128)(2,1)S(1)} %get-tuple-element.125.mixm_ref, ...), custom_call_target="tpu_custom_call" | custom-call | bytes 65536 | tf_op jit(solution)/shard_map/mix0_far/pallas_call | solution.py:544
  89.1 2.6 %conv1.1 = (bf16[2,256,256]{2,1,0:T(8,128)(2,1)S(1)}, bf16[512,512]{1,0:T(8,128)(2,1)S(1)}) custom-call(s32[3]{0:T(128)S(1)} %pad_add_fusion.place_ref.place, bf16[2,2,256,512]{3,2,1,0:T(8,128)(2,1)S(1)} %get-tuple-element.149.hm_near, bf16[2,2,256,512]{3,2,1,0:T(8,128)(2,1)S(1)} %get-tuple-element.150.hp_near, ...), custom_call_target="tpu_custom_call" | custom-call | tf_op jit(solution)/shard_map/conv1/pallas_call | solution.py:567
  91.9 1.5 %collective-permute-done.28.zp_ref = bf16[2,256,256]{2,1,0:T(8,128)(2,1)S(1)} collective-permute-done((bf16[2,256,256]{2,1,0:T(8,128)(2,1)S(1)}, bf16[2,256,256]{2,1,0:T(8,128)(2,1)S(1)}, u32[]{:S(2)}, u32[]{:S(2)}) %collective-permute-start.28) | collective-permute-done | bytes 262176 | tf_op jit(solution)/shard_map/ppermute | solution.py:40
  93.3 1.7 %mix1.1 = (bf16[256,512]{1,0:T(8,128)(2,1)}, bf16[256,512]{1,0:T(8,128)(2,1)}) custom-call(s32[3]{0:T(128)S(1)} %pad_add_fusion.place_ref.place, bf16[2,256,256]{2,1,0:T(8,128)(2,1)S(1)} %get-tuple-element.165.zm_ref, bf16[2,256,256]{2,1,0:T(8,128)(2,1)S(1)} %collective-permute-done.28.zp_ref, bf16[512,512]{1,0:T(8,128)(2,1)S(1)} %get-tuple-element.166.mix_ref, ...), custom_call_target="tpu_custom_call" | custom-call | tf_op jit(solution)/shard_map/mix1/pallas_call | solution.py:582
  (33 shorter events, 0.8 us)
Async XLA Ops:
  0.6 1.1 %copy-start = (bf16[2,384,2,256]{3,2,1,0:T(2,128)(2,1)S(1)}, bf16[2,384,2,256]{3,2,1,0:T(2,128)(2,1)}, u32[]{:S(2)}) copy-start(bf16[2,384,2,256]{3,2,1,0:T(2,128)(2,1)} %param.8) | copy-start | bytes 2359300
  0.6 10.8 %copy-start.2 = (bf16[256,512]{1,0:T(8,128)(2,1)S(1)}, bf16[256,512]{1,0:T(8,128)(2,1)}, u32[]{:S(2)}) copy-start(bf16[256,512]{1,0:T(8,128)(2,1)} %param.6) | copy-start | bytes 786436
  2.0 22.9 %copy-start.1 = (f32[2,512]{1,0:T(2,128)S(1)}, f32[2,512]{1,0:T(2,128)}, u32[]{:S(2)}) copy-start(f32[2,512]{1,0:T(2,128)} %gm_ref.7) | copy-start | bytes 12292
  3.2 18.3 %collective-permute-start.3 = (bf16[448,512]{1,0:T(8,128)(2,1)S(1)}, bf16[448,512]{1,0:T(8,128)(2,1)S(1)}, u32[]{:S(2)}, u32[]{:S(2)}) collective-permute-start(bf16[448,512]{1,0:T(8,128)(2,1)S(1)} %get-tuple-element.153.refs_0_.refs_6_), channel_id=1, source_target_pairs={{0,16},{16,0},{1,17},{17,1},{2,18},{18,2},{3,19},{19,3},{4,20},{20... | collective-permute-start | bytes 1376264 | tf_op jit(solution)/shard_map/ppermute | solution.py:44
  6.3 15.2 %collective-permute-start.2 = (bf16[448,512]{1,0:T(8,128)(2,1)S(1)}, bf16[448,512]{1,0:T(8,128)(2,1)S(1)}, u32[]{:S(2)}, u32[]{:S(2)}) collective-permute-start(bf16[448,512]{1,0:T(8,128)(2,1)S(1)} %get-tuple-element.153.refs_0_.refs_6_), channel_id=1, source_target_pairs={{0,2},{2,0},{4,6},{6,4},{8,10},{10,8},{12,14},{14,12},{1,3},{3,1},... | collective-permute-start | bytes 1376264 | tf_op jit(solution)/shard_map/ppermute | solution.py:48
  7.8 9.7 %collective-permute-start.1 = (bf16[224,512]{1,0:T(8,128)(2,1)S(1)}, bf16[224,512]{1,0:T(8,128)(2,1)S(1)}, u32[]{:S(2)}, u32[]{:S(2)}) collective-permute-start(bf16[224,512]{1,0:T(8,128)(2,1)S(1)} %get-tuple-element.85), channel_id=1, source_target_pairs={{0,12},{2,14},{4,0},{6,2},{8,4},{10,6},{12,8},{14,10},{1,13},{3,15... | collective-permute-start | bytes 688136 | tf_op jit(solution)/shard_map/ppermute | solution.py:52
  11.4 10.1 %collective-permute-start = (bf16[224,512]{1,0:T(8,128)(2,1)S(1)}, bf16[224,512]{1,0:T(8,128)(2,1)S(1)}, u32[]{:S(2)}, u32[]{:S(2)}) collective-permute-start(bf16[224,512]{1,0:T(8,128)(2,1)S(1)} %get-tuple-element.85), channel_id=1, source_target_pairs={{0,4},{2,6},{4,8},{6,10},{8,12},{10,14},{12,0},{14,2},{1,5},{3,7},... | collective-permute-start | bytes 688136 | tf_op jit(solution)/shard_map/ppermute | solution.py:52
  22.2 18.9 %collective-permute-start.4 = (bf16[736,512]{1,0:T(8,128)(2,1)S(1)}, bf16[736,512]{1,0:T(8,128)(2,1)S(1)}, u32[]{:S(2)}, u32[]{:S(2)}) collective-permute-start(bf16[736,512]{1,0:T(8,128)(2,1)S(1)} %get-tuple-element.93), channel_id=1, source_target_pairs={{0,4},{2,6},{4,8},{6,10},{8,12},{10,14},{12,0},{14,2},{1,5},{3,7},... | collective-permute-start | bytes 2261000 | tf_op jit(solution)/shard_map/ppermute | solution.py:52
  23.9 15.5 %collective-permute-start.5 = (bf16[672,512]{1,0:T(8,128)(2,1)S(1)}, bf16[672,512]{1,0:T(8,128)(2,1)S(1)}, u32[]{:S(2)}, u32[]{:S(2)}) collective-permute-start(bf16[672,512]{1,0:T(8,128)(2,1)S(1)} %get-tuple-element.94), channel_id=1, source_target_pairs={{0,2},{2,0},{4,6},{6,4},{8,10},{10,8},{12,14},{14,12},{1,3},{3,1},... | collective-permute-start | bytes 2064392 | tf_op jit(solution)/shard_map/ppermute | solution.py:48
  24.4 15.2 %collective-permute-start.6 = (bf16[672,512]{1,0:T(8,128)(2,1)S(1)}, bf16[672,512]{1,0:T(8,128)(2,1)S(1)}, u32[]{:S(2)}, u32[]{:S(2)}) collective-permute-start(bf16[672,512]{1,0:T(8,128)(2,1)S(1)} %get-tuple-element.95), channel_id=1, source_target_pairs={{0,16},{16,0},{1,17},{17,1},{2,18},{18,2},{3,19},{19,3},{4,20},{20... | collective-permute-start | bytes 2064392 | tf_op jit(solution)/shard_map/ppermute | solution.py:44
  24.9 1.9 %collective-permute-start.8 = (bf16[512,512]{1,0:T(8,128)(2,1)S(1)}, bf16[512,512]{1,0:T(8,128)(2,1)S(1)}, u32[]{:S(2)}, u32[]{:S(2)}) collective-permute-start(bf16[512,512]{1,0:T(8,128)(2,1)S(1)} %bitcast.14), channel_id=1, source_target_pairs={{0,1},{1,0},{2,3},{3,2},{4,5},{5,4},{6,7},{7,6},{8,9},{9,8},{10,11... | collective-permute-start | bytes 1572872 | tf_op jit(solution)/shard_map/ppermute | solution.py:40
  24.9 1.9 %collective-permute-start.7 = (f32[2,512]{1,0:T(2,128)S(1)}, f32[2,512]{1,0:T(2,128)S(1)}, u32[]{:S(2)}, u32[]{:S(2)}) collective-permute-start(f32[2,512]{1,0:T(2,128)S(1)} %copy-done.1), channel_id=1, source_target_pairs={{0,1},{1,0},{2,3},{3,2},{4,5},{5,4},{6,7},{7,6},{8,9},{9,8},{10,11... | collective-permute-start | bytes 12296 | tf_op jit(solution)/shard_map/ppermute | solution.py:40
  41.9 16.2 %collective-permute-start.11 = (bf16[736,512]{1,0:T(8,128)(2,1)S(1)}, bf16[736,512]{1,0:T(8,128)(2,1)S(1)}, u32[]{:S(2)}, u32[]{:S(2)}) collective-permute-start(bf16[736,512]{1,0:T(8,128)(2,1)S(1)} %get-tuple-element.103), channel_id=1, source_target_pairs={{0,2},{2,0},{4,6},{6,4},{8,10},{10,8},{12,14},{14,12},{1,3},{3,1},... | collective-permute-start | bytes 2261000 | tf_op jit(solution)/shard_map/ppermute | solution.py:48
  42.5 14.7 %collective-permute-start.12 = (bf16[672,512]{1,0:T(8,128)(2,1)S(1)}, bf16[672,512]{1,0:T(8,128)(2,1)S(1)}, u32[]{:S(2)}, u32[]{:S(2)}) collective-permute-start(bf16[672,512]{1,0:T(8,128)(2,1)S(1)} %get-tuple-element.104), channel_id=1, source_target_pairs={{0,16},{16,0},{1,17},{17,1},{2,18},{18,2},{3,19},{19,3},{4,20},{20... | collective-permute-start | bytes 2064392 | tf_op jit(solution)/shard_map/ppermute | solution.py:44
  43.0 14.2 %collective-permute-start.9 = (bf16[448,512]{1,0:T(8,128)(2,1)S(1)}, bf16[448,512]{1,0:T(8,128)(2,1)S(1)}, u32[]{:S(2)}, u32[]{:S(2)}) collective-permute-start(bf16[448,512]{1,0:T(8,128)(2,1)S(1)} %get-tuple-element.101), channel_id=1, source_target_pairs={{0,4},{2,6},{4,8},{6,10},{8,12},{10,14},{12,0},{14,2},{1,5},{3,7},... | collective-permute-start | bytes 1376264 | tf_op jit(solution)/shard_map/ppermute | solution.py:52
  43.0 14.2 %collective-permute-start.10 = (bf16[224,512]{1,0:T(8,128)(2,1)S(1)}, bf16[224,512]{1,0:T(8,128)(2,1)S(1)}, u32[]{:S(2)}, u32[]{:S(2)}) collective-permute-start(bf16[224,512]{1,0:T(8,128)(2,1)S(1)} %get-tuple-element.102), channel_id=1, source_target_pairs={{0,12},{2,14},{4,0},{6,2},{8,4},{10,6},{12,8},{14,10},{1,13},{3,15... | collective-permute-start | bytes 688136 | tf_op jit(solution)/shard_map/ppermute | solution.py:52
  58.9 17.1 %collective-permute-start.13 = (bf16[736,512]{1,0:T(8,128)(2,1)S(1)}, bf16[736,512]{1,0:T(8,128)(2,1)S(1)}, u32[]{:S(2)}, u32[]{:S(2)}) collective-permute-start(bf16[736,512]{1,0:T(8,128)(2,1)S(1)} %get-tuple-element.109), channel_id=1, source_target_pairs={{0,4},{2,6},{4,8},{6,10},{8,12},{10,14},{12,0},{14,2},{1,5},{3,7},... | collective-permute-start | bytes 2261000 | tf_op jit(solution)/shard_map/ppermute | solution.py:52
  58.9 4.9 %collective-permute-start.14 = (bf16[112,512]{1,0:T(8,128)(2,1)S(1)}, bf16[112,512]{1,0:T(8,128)(2,1)S(1)}, u32[]{:S(2)}, u32[]{:S(2)}) collective-permute-start(bf16[112,512]{1,0:T(8,128)(2,1)S(1)} %get-tuple-element.111), channel_id=1, source_target_pairs={{0,2},{2,0},{4,6},{6,4},{8,10},{10,8},{12,14},{14,12},{1,3},{3,1},... | collective-permute-start | bytes 344072 | tf_op jit(solution)/shard_map/ppermute | solution.py:48
  59.7 4.9 %collective-permute-start.15 = (bf16[112,512]{1,0:T(8,128)(2,1)S(1)}, bf16[112,512]{1,0:T(8,128)(2,1)S(1)}, u32[]{:S(2)}, u32[]{:S(2)}) collective-permute-start(bf16[112,512]{1,0:T(8,128)(2,1)S(1)} %get-tuple-element.112), channel_id=1, source_target_pairs={{0,16},{16,0},{1,17},{17,1},{2,18},{18,2},{3,19},{19,3},{4,20},{20... | collective-permute-start | bytes 344072 | tf_op jit(solution)/shard_map/ppermute | solution.py:44
  61.2 5.9 %collective-permute-start.19 = (bf16[512,512]{1,0:T(8,128)(2,1)S(1)}, bf16[512,512]{1,0:T(8,128)(2,1)S(1)}, u32[]{:S(2)}, u32[]{:S(2)}) collective-permute-start(bf16[512,512]{1,0:T(8,128)(2,1)S(1)} %get-tuple-element.115), channel_id=1, source_target_pairs={{0,1},{1,0},{2,3},{3,2},{4,5},{5,4},{6,7},{7,6},{8,9},{9,8},{10,11... | collective-permute-start | bytes 1572872 | tf_op jit(solution)/shard_map/ppermute | solution.py:40
  61.2 5.9 %collective-permute-start.18 = (bf16[512,512]{1,0:T(8,128)(2,1)S(1)}, bf16[512,512]{1,0:T(8,128)(2,1)S(1)}, u32[]{:S(2)}, u32[]{:S(2)}) collective-permute-start(bf16[512,512]{1,0:T(8,128)(2,1)S(1)} %get-tuple-element.114), channel_id=1, source_target_pairs={{0,1},{1,0},{2,3},{3,2},{4,5},{5,4},{6,7},{7,6},{8,9},{9,8},{10,11... | collective-permute-start | bytes 1572872 | tf_op jit(solution)/shard_map/ppermute | solution.py:40
  64.6 9.7 %collective-permute-start.17 = (bf16[448,512]{1,0:T(8,128)(2,1)S(1)}, bf16[448,512]{1,0:T(8,128)(2,1)S(1)}, u32[]{:S(2)}, u32[]{:S(2)}) collective-permute-start(bf16[448,512]{1,0:T(8,128)(2,1)S(1)} %get-tuple-element.113), channel_id=1, source_target_pairs={{0,16},{16,0},{1,17},{17,1},{2,18},{18,2},{3,19},{19,3},{4,20},{20... | collective-permute-start | bytes 1376264 | tf_op jit(solution)/shard_map/ppermute | solution.py:44
  67.1 8.5 %collective-permute-start.16 = (bf16[448,512]{1,0:T(8,128)(2,1)S(1)}, bf16[448,512]{1,0:T(8,128)(2,1)S(1)}, u32[]{:S(2)}, u32[]{:S(2)}) collective-permute-start(bf16[448,512]{1,0:T(8,128)(2,1)S(1)} %get-tuple-element.113), channel_id=1, source_target_pairs={{0,2},{2,0},{4,6},{6,4},{8,10},{10,8},{12,14},{14,12},{1,3},{3,1},... | collective-permute-start | bytes 1376264 | tf_op jit(solution)/shard_map/ppermute | solution.py:48
  76.0 3.6 %collective-permute-start.21 = (bf16[2,512,256]{2,1,0:T(8,128)(2,1)S(1)}, bf16[2,512,256]{2,1,0:T(8,128)(2,1)S(1)}, u32[]{:S(2)}, u32[]{:S(2)}) collective-permute-start(bf16[2,512,256]{2,1,0:T(8,128)(2,1)S(1)} %get-tuple-element.142.refs_0_), channel_id=1, source_target_pairs={{0,1},{1,0},{2,3},{3,2},{4,5},{5,4},{6,7},{7,6},{8,9},{9,8},{10,11... | collective-permute-start | bytes 1572872 | tf_op jit(solution)/shard_map/ppermute | solution.py:40
  76.0 5.6 %collective-permute-start.22 = (bf16[512,512]{1,0:T(8,128)(2,1)S(1)}, bf16[512,512]{1,0:T(8,128)(2,1)S(1)}, u32[]{:S(2)}, u32[]{:S(2)}) collective-permute-start(bf16[512,512]{1,0:T(8,128)(2,1)S(1)} %get-tuple-element.125.mixm_ref), channel_id=1, source_target_pairs={{0,1},{1,0},{2,3},{3,2},{4,5},{5,4},{6,7},{7,6},{8,9},{9,8},{10,11... | collective-permute-start | bytes 1572872 | tf_op jit(solution)/shard_map/ppermute | solution.py:40
  77.1 4.4 %collective-permute-start.20 = (bf16[2,256,512]{2,1,0:T(8,128)(2,1)S(1)}, bf16[2,256,512]{2,1,0:T(8,128)(2,1)S(1)}, u32[]{:S(2)}, u32[]{:S(2)}) collective-permute-start(bf16[2,256,512]{2,1,0:T(8,128)(2,1)S(1)} %bitcast.26), channel_id=1, source_target_pairs={{0,1},{1,0},{2,3},{3,2},{4,5},{5,4},{6,7},{7,6},{8,9},{9,8},{10,11... | collective-permute-start | bytes 1572872 | tf_op jit(solution)/shard_map/ppermute | solution.py:40
  77.2 11.9 %collective-permute-start.26 = (bf16[336,512]{1,0:T(8,128)(2,1)S(1)}, bf16[336,512]{1,0:T(8,128)(2,1)S(1)}, u32[]{:S(2)}, u32[]{:S(2)}) collective-permute-start(bf16[336,512]{1,0:T(8,128)(2,1)S(1)} %get-tuple-element.147), channel_id=1, source_target_pairs={{0,2},{2,0},{4,6},{6,4},{8,10},{10,8},{12,14},{14,12},{1,3},{3,1},... | collective-permute-start | bytes 1032200 | tf_op jit(solution)/shard_map/ppermute | solution.py:48
  78.0 11.1 %collective-permute-start.27 = (bf16[336,512]{1,0:T(8,128)(2,1)S(1)}, bf16[336,512]{1,0:T(8,128)(2,1)S(1)}, u32[]{:S(2)}, u32[]{:S(2)}) collective-permute-start(bf16[336,512]{1,0:T(8,128)(2,1)S(1)} %get-tuple-element.148), channel_id=1, source_target_pairs={{0,16},{16,0},{1,17},{17,1},{2,18},{18,2},{3,19},{19,3},{4,20},{20... | collective-permute-start | bytes 1032200 | tf_op jit(solution)/shard_map/ppermute | solution.py:44
  79.5 9.5 %collective-permute-start.25 = (bf16[224,512]{1,0:T(8,128)(2,1)S(1)}, bf16[224,512]{1,0:T(8,128)(2,1)S(1)}, u32[]{:S(2)}, u32[]{:S(2)}) collective-permute-start(bf16[224,512]{1,0:T(8,128)(2,1)S(1)} %get-tuple-element.146), channel_id=1, source_target_pairs={{0,4},{2,6},{4,8},{6,10},{8,12},{10,14},{12,0},{14,2},{1,5},{3,7},... | collective-permute-start | bytes 688136 | tf_op jit(solution)/shard_map/ppermute | solution.py:52
  84.3 3.1 %collective-permute-start.23 = (bf16[256,256]{1,0:T(8,128)(2,1)S(1)}, bf16[256,256]{1,0:T(8,128)(2,1)S(1)}, u32[]{:S(2)}, u32[]{:S(2)}) collective-permute-start(bf16[256,256]{1,0:T(8,128)(2,1)S(1)} %get-tuple-element.138.refs_0_), channel_id=1, source_target_pairs={{0,1},{1,0},{2,3},{3,2},{4,5},{5,4},{6,7},{7,6},{8,9},{9,8},{10,11... | collective-permute-start | bytes 393224 | tf_op jit(solution)/shard_map/ppermute | solution.py:40
  84.4 3.0 %collective-permute-start.24 = (bf16[256,256]{1,0:T(8,128)(2,1)S(1)}, bf16[256,256]{1,0:T(8,128)(2,1)S(1)}, u32[]{:S(2)}, u32[]{:S(2)}) collective-permute-start(bf16[256,256]{1,0:T(8,128)(2,1)S(1)} %get-tuple-element.139.refs_1_), channel_id=1, source_target_pairs={{0,1},{1,0},{2,3},{3,2},{4,5},{5,4},{6,7},{7,6},{8,9},{9,8},{10,11... | collective-permute-start | bytes 393224 | tf_op jit(solution)/shard_map/ppermute | solution.py:40
  91.7 1.6 %collective-permute-start.28 = (bf16[2,256,256]{2,1,0:T(8,128)(2,1)S(1)}, bf16[2,256,256]{2,1,0:T(8,128)(2,1)S(1)}, u32[]{:S(2)}, u32[]{:S(2)}) collective-permute-start(bf16[2,256,256]{2,1,0:T(8,128)(2,1)S(1)} %get-tuple-element.165.zm_ref), channel_id=1, source_target_pairs={{0,1},{1,0},{2,3},{3,2},{4,5},{5,4},{6,7},{7,6},{8,9},{9,8},{10,11... | collective-permute-start | bytes 786440 | tf_op jit(solution)/shard_map/ppermute | solution.py:40

commit v10 on v8

--- a/solution.py
+++ b/solution.py
@@ -326,7 +326,9 @@
 
     whole(0, both, (0, 0, 0))
     keep(1, both, (unit, 0, unit, 0, 0, 0))
-    z1a, z1b, x1, y1, own, c1 = together(z(c0), z(c0, 3), x(both), y(both), own, c1)
+    z1a, z1b, x1, y1, own, c1, gains_p = together(
+        z(c0), z(c0, 3), x(both), y(both), own, c1, swap_chan(gains)
+    )
     whole(0, z1a, (1, 0, 0))
     whole(0, z1b, (3, 0, 0))
     whole(0, x1, (0, 1, 0))
@@ -340,9 +342,7 @@
         [(z1a, 0, unit), (z1b, 0, unit), (y1, unit, unit)],
         [(z1a, 0, unit), (z1b, 0, unit), (x1, 0, unit)],
     )
-    z2, x2, y2, own, c1, gains_p, own_p = together(
-        z(to_z), x(to_x), y(to_y), own, c1, swap_chan(gains), swap_chan(own)
-    )
+    z2, x2, y2, own, c1, own_p = together(z(to_z), x(to_x), y(to_y), own, c1, swap_chan(own))
     keep(0, z2, (0, 0, unit, 2, 0, 0))
     whole(0, x2, (1, 1, 0), (3, 1, 0))
     keep(1, x2, (2 * unit, 0, unit, 0, 1, 1))

time: 95.5 us -> 95.5 us (level)
  transfers between devices with their start and end apart: 29 -> 29, of which waited for: 14 -> 15; matrix products, arithmetic and copies ran while one was open for 1% -> 1% of each run, Pallas kernels for 15% -> 15%
where the time goes in v10:
time: 95.5 us; the launch traced here: 95.3 us
  waiting for transfers between devices  42.9 us (45%)
  starting transfers between devices  26.8 us (28%)
  Pallas kernels  21.2 us (22%)
  local copies, waits for them, and re-layouts  2.49 us (3%)
  other arithmetic  1.08 us (1%)
    ppermute x7, waiting for transfers between devices, ring(): return lax.ppermute(block, 'seq', [(s, (s + by) % seq) for s in range(seq)])  21.2 us
    ppermute x6, waiting for transfers between devices, swap_pair(): return lax.ppermute(block, 'seq', [(s, s ^ 1) for s in range(seq)])  16.7 us
    ppermute x7, starting transfers between devices, ring(): return lax.ppermute(block, 'seq', [(s, (s + by) % seq) for s in range(seq)])  11.2 us
    ppermute x6, starting transfers between devices, swap_groups(): return lax.ppermute(block, 'groups', [(0, 1), (1, 0)])  9.56 us
    ppermute x6, starting transfers between devices, swap_pair(): return lax.ppermute(block, 'seq', [(s, s ^ 1) for s in range(seq)])  4.22 us
    pallas_call x2, Pallas kernels, mix0(): pl.pallas_call(functools.partial(mix0_kernel, (rows, half, branch, 1, n,...  4.13 us
    pallas_call x1, Pallas kernels, newest(): pl.pallas_call(functools.partial(conv0_near_kernel, (rows, half, branch,...  4.01 us
    ppermute x10, waiting for transfers between devices, swap_chan(): return lax.ppermute(block, 'chan', [(0, 1), (1, 0)])  3.45 us
  transfers between devices with their start and end apart: 29, of which 15 were waited for; matrix products, arithmetic and copies ran while one was open for 1% of the time, Pallas kernels for 15%

profile of v10, /device:TPU:0, one launch (start us, length us, event | category | flops | bytes accessed | tf_op | source)
XLA Modules:
  0.0 95.3 jit_solution(7568442493498259362)
XLA Ops:
  0.7 1.1 %copy-done = bf16[2,384,2,256]{3,2,1,0:T(2,128)(2,1)S(1)} copy-done((bf16[2,384,2,256]{3,2,1,0:T(2,128)(2,1)S(1)}, bf16[2,384,2,256]{3,2,1,0:T(2,128)(2,1)}, u32[]{:S(2)}) %copy-start) | copy-done | bytes 786456
  1.8 0.3 constant_dynamic-slice_fusion.1
  2.0 0.3 reshape.31.conv
  2.3 0.9 constant_dynamic-slice_fusion.mix
  3.2 3.0 %collective-permute-start.3 = (bf16[448,512]{1,0:T(8,128)(2,1)S(1)}, bf16[448,512]{1,0:T(8,128)(2,1)S(1)}, u32[]{:S(2)}, u32[]{:S(2)}) collective-permute-start(bf16[448,512]{1,0:T(8,128)(2,1)S(1)} %get-tuple-element.153.refs_0_.refs_6_), channel_id=1, source_target_pairs={{0,16},{16,0},{1,17},{17,1},{2,18},{18,2},{3,19},{19,3},{4,20},{20... | collective-permute-start | bytes 1376264 | tf_op jit(solution)/shard_map/ppermute | solution.py:44
  6.3 1.5 %collective-permute-start.2 = (bf16[448,512]{1,0:T(8,128)(2,1)S(1)}, bf16[448,512]{1,0:T(8,128)(2,1)S(1)}, u32[]{:S(2)}, u32[]{:S(2)}) collective-permute-start(bf16[448,512]{1,0:T(8,128)(2,1)S(1)} %get-tuple-element.153.refs_0_.refs_6_), channel_id=1, source_target_pairs={{0,2},{2,0},{4,6},{6,4},{8,10},{10,8},{12,14},{14,12},{1,3},{3,1},... | collective-permute-start | bytes 1376264 | tf_op jit(solution)/shard_map/ppermute | solution.py:48
  7.7 3.6 %collective-permute-start.1 = (bf16[224,512]{1,0:T(8,128)(2,1)S(1)}, bf16[224,512]{1,0:T(8,128)(2,1)S(1)}, u32[]{:S(2)}, u32[]{:S(2)}) collective-permute-start(bf16[224,512]{1,0:T(8,128)(2,1)S(1)} %get-tuple-element.85), channel_id=1, source_target_pairs={{0,12},{2,14},{4,0},{6,2},{8,4},{10,6},{12,8},{14,10},{1,13},{3,15... | collective-permute-start | bytes 688136 | tf_op jit(solution)/shard_map/ppermute | solution.py:52
  11.4 1.0 %pad_maximum_fusion = bf16[2,256,512]{2,1,0:T(8,128)(2,1)S(1)} fusion(bf16[1,256,512]{2,1,0:T(8,128)(2,1)S(1)} %bitcast.28, bf16[1,256,512]{2,1,0:T(8,128)(2,1)} %bitcast.29), kind=kLoop, calls=%fused_computation | loop fusion | flops 262144 | bytes 1048576 | tf_op jit(solution)/shard_map/stack | solution.py:413
  12.5 4.9 %collective-permute-done.1.refs_2_.refs_8_ = bf16[224,512]{1,0:T(8,128)(2,1)S(1)} collective-permute-done((bf16[224,512]{1,0:T(8,128)(2,1)S(1)}, bf16[224,512]{1,0:T(8,128)(2,1)S(1)}, u32[]{:S(2)}, u32[]{:S(2)}) %collective-permute-start.1) | collective-permute-done | bytes 229408 | tf_op jit(solution)/shard_map/ppermute | solution.py:52
  17.4 4.1 %collective-permute-done.refs_0_.refs_7_ = bf16[224,512]{1,0:T(8,128)(2,1)S(1)} collective-permute-done((bf16[224,512]{1,0:T(8,128)(2,1)S(1)}, bf16[224,512]{1,0:T(8,128)(2,1)S(1)}, u32[]{:S(2)}, u32[]{:S(2)}) %collective-permute-start) | collective-permute-done | bytes 229408 | tf_op jit(solution)/shard_map/ppermute | solution.py:52
  21.5 0.7 pack.4
  22.2 1.7 %collective-permute-start.5 = (bf16[736,512]{1,0:T(8,128)(2,1)S(1)}, bf16[736,512]{1,0:T(8,128)(2,1)S(1)}, u32[]{:S(2)}, u32[]{:S(2)}) collective-permute-start(bf16[736,512]{1,0:T(8,128)(2,1)S(1)} %get-tuple-element.94), channel_id=1, source_target_pairs={{0,4},{2,6},{4,8},{6,10},{8,12},{10,14},{12,0},{14,2},{1,5},{3,7},... | collective-permute-start | bytes 2261000 | tf_op jit(solution)/shard_map/ppermute | solution.py:52
  23.8 0.5 collective-permute-start.6
  24.4 0.5 collective-permute-start.7
  24.9 1.9 %collective-permute-done.8 = bf16[512,512]{1,0:T(8,128)(2,1)S(1)} collective-permute-done((bf16[512,512]{1,0:T(8,128)(2,1)S(1)}, bf16[512,512]{1,0:T(8,128)(2,1)S(1)}, u32[]{:S(2)}, u32[]{:S(2)}) %collective-permute-start.8) | collective-permute-done | bytes 524320 | tf_op jit(solution)/shard_map/ppermute | solution.py:40
  26.8 12.5 %collective-permute-done.6.refs_1_.refs_12_.refs_3_ = bf16[672,512]{1,0:T(8,128)(2,1)S(1)} collective-permute-done((bf16[672,512]{1,0:T(8,128)(2,1)S(1)}, bf16[672,512]{1,0:T(8,128)(2,1)S(1)}, u32[]{:S(2)}, u32[]{:S(2)}) %collective-permute-start.6) | collective-permute-done | bytes 688160 | tf_op jit(solution)/shard_map/ppermute | solution.py:48
  39.3 0.3 collective-permute-done.7.refs_13_
  39.6 1.6 %collective-permute-done.5.refs_2_.refs_11_ = bf16[736,512]{1,0:T(8,128)(2,1)S(1)} collective-permute-done((bf16[736,512]{1,0:T(8,128)(2,1)S(1)}, bf16[736,512]{1,0:T(8,128)(2,1)S(1)}, u32[]{:S(2)}, u32[]{:S(2)}) %collective-permute-start.5) | collective-permute-done | bytes 753696 | tf_op jit(solution)/shard_map/ppermute | solution.py:52
  41.1 0.8 pack.5
  41.9 0.6 collective-permute-start.11
  42.5 0.5 collective-permute-start.12
  43.0 3.8 %collective-permute-start.10 = (bf16[224,512]{1,0:T(8,128)(2,1)S(1)}, bf16[224,512]{1,0:T(8,128)(2,1)S(1)}, u32[]{:S(2)}, u32[]{:S(2)}) collective-permute-start(bf16[224,512]{1,0:T(8,128)(2,1)S(1)} %get-tuple-element.102), channel_id=1, source_target_pairs={{0,12},{2,14},{4,0},{6,2},{8,4},{10,6},{12,8},{14,10},{1,13},{3,15... | collective-permute-start | bytes 688136 | tf_op jit(solution)/shard_map/ppermute | solution.py:52
  46.8 10.4 %collective-permute-done.10.refs_2_.refs_5_ = bf16[224,512]{1,0:T(8,128)(2,1)S(1)} collective-permute-done((bf16[224,512]{1,0:T(8,128)(2,1)S(1)}, bf16[224,512]{1,0:T(8,128)(2,1)S(1)}, u32[]{:S(2)}, u32[]{:S(2)}) %collective-permute-start.10) | collective-permute-done | bytes 229408 | tf_op jit(solution)/shard_map/ppermute | solution.py:52
  57.2 0.9 collective-permute-done.11.refs_1_.refs_14_
  58.1 0.7 pack.6
  58.9 0.8 collective-permute-start.14
  59.7 1.5 %collective-permute-start.15 = (bf16[112,512]{1,0:T(8,128)(2,1)S(1)}, bf16[112,512]{1,0:T(8,128)(2,1)S(1)}, u32[]{:S(2)}, u32[]{:S(2)}) collective-permute-start(bf16[112,512]{1,0:T(8,128)(2,1)S(1)} %get-tuple-element.112), channel_id=1, source_target_pairs={{0,16},{16,0},{1,17},{17,1},{2,18},{18,2},{3,19},{19,3},{4,20},{20... | collective-permute-start | bytes 344072 | tf_op jit(solution)/shard_map/ppermute | solution.py:44
  61.2 0.5 collective-permute-start.18
  61.7 2.0 %collective-permute-done.14.refs_0_ = bf16[112,512]{1,0:T(8,128)(2,1)S(1)} collective-permute-done((bf16[112,512]{1,0:T(8,128)(2,1)S(1)}, bf16[112,512]{1,0:T(8,128)(2,1)S(1)}, u32[]{:S(2)}, u32[]{:S(2)}) %collective-permute-start.14) | collective-permute-done | bytes 114720 | tf_op jit(solution)/shard_map/ppermute | solution.py:48
  63.8 0.9 collective-permute-done.15.refs_1_
  64.6 2.5 %collective-permute-start.17 = (bf16[448,512]{1,0:T(8,128)(2,1)S(1)}, bf16[448,512]{1,0:T(8,128)(2,1)S(1)}, u32[]{:S(2)}, u32[]{:S(2)}) collective-permute-start(bf16[448,512]{1,0:T(8,128)(2,1)S(1)} %get-tuple-element.113), channel_id=1, source_target_pairs={{0,16},{16,0},{1,17},{17,1},{2,18},{18,2},{3,19},{19,3},{4,20},{20... | collective-permute-start | bytes 1376264 | tf_op jit(solution)/shard_map/ppermute | solution.py:44
  67.1 2.9 %ready.1 = (bf16[3072,512]{1,0:T(8,128)(2,1)S(1)}, bf16[512,512]{1,0:T(8,128)(2,1)S(1)}, bf16[2,1024,512]{2,1,0:T(8,128)(2,1)S(1)}, bf16[2,1024,512]{2,1,0:T(8,128)(2,1)S(1)}) custom-call(s32[3]{0:T(128)S(1)} %pad_add_fusion.place_ref.place, f32[2,512]{1,0:T(2,128)S(1)} %copy-done.1, f32[2,512]{1,0:T(2,128)S(1)} %collective-permute-done.4.gp_ref, ...), custom_call_target="tpu_custom_call" | custom-call | bytes 65536 | tf_op jit(solution)/shard_map/ready/pallas_call | solution.py:463
  70.0 4.0 %conv0_near.1 = (bf16[2,512,256]{2,1,0:T(8,128)(2,1)S(1)}, bf16[3072,512]{1,0:T(8,128)(2,1)S(1)}, bf16[512,512]{1,0:T(8,128)(2,1)S(1)}) custom-call(s32[3]{0:T(128)S(1)} %pad_add_fusion.place_ref.place, bf16[2,1024,512]{2,1,0:T(8,128)(2,1)S(1)} %get-tuple-element.134.hm._, ...), custom_call_target="tpu_custom_call", output_to_operand_aliasing={{1}: (5, {}), {2}: (6, {})} | custom-call | bytes 65536 | tf_op jit(solution)/shard_map/conv0_near/pallas_call | solution.py:487
  74.0 0.3 collective-permute-done.17.refs_2_.refs_8_
  74.3 1.3 %collective-permute-done.16.refs_3_.refs_7_ = bf16[448,512]{1,0:T(8,128)(2,1)S(1)} collective-permute-done((bf16[448,512]{1,0:T(8,128)(2,1)S(1)}, bf16[448,512]{1,0:T(8,128)(2,1)S(1)}, u32[]{:S(2)}, u32[]{:S(2)}) %collective-permute-start.16) | collective-permute-done | bytes 458784 | tf_op jit(solution)/shard_map/ppermute | solution.py:48
  75.6 0.3 collective-permute-done.13.refs_1_.refs_6_
  75.9 0.5 collective-permute-start.22
  76.5 0.7 pack.7
  77.2 0.8 collective-permute-start.26
  78.0 1.5 %collective-permute-start.27 = (bf16[336,512]{1,0:T(8,128)(2,1)S(1)}, bf16[336,512]{1,0:T(8,128)(2,1)S(1)}, u32[]{:S(2)}, u32[]{:S(2)}) collective-permute-start(bf16[336,512]{1,0:T(8,128)(2,1)S(1)} %get-tuple-element.148), channel_id=1, source_target_pairs={{0,16},{16,0},{1,17},{17,1},{2,18},{18,2},{3,19},{19,3},{4,20},{20... | collective-permute-start | bytes 1032200 | tf_op jit(solution)/shard_map/ppermute | solution.py:44
  79.5 2.0 %collective-permute-start.25 = (bf16[224,512]{1,0:T(8,128)(2,1)S(1)}, bf16[224,512]{1,0:T(8,128)(2,1)S(1)}, u32[]{:S(2)}, u32[]{:S(2)}) collective-permute-start(bf16[224,512]{1,0:T(8,128)(2,1)S(1)} %get-tuple-element.146), channel_id=1, source_target_pairs={{0,4},{2,6},{4,8},{6,10},{8,12},{10,14},{12,0},{14,2},{1,5},{3,7},... | collective-permute-start | bytes 688136 | tf_op jit(solution)/shard_map/ppermute | solution.py:52
  81.5 3.0 %conv0_far.1 = (bf16[256,256]{1,0:T(8,128)(2,1)S(1)}, bf16[256,256]{1,0:T(8,128)(2,1)S(1)}, bf16[2,1024,512]{2,1,0:T(8,128)(2,1)S(1)}, bf16[2,1024,512]{2,1,0:T(8,128)(2,1)S(1)}) custom-call(s32[3]{0:T(128)S(1)} %pad_add_fusion.place_ref.place, f32[2,512]{1,0:T(2,128)S(1)} %copy-done.1, ...), custom_call_target="tpu_custom_call", output_to_operand_aliasing={{2}: (6, {}), {3}: (7, {})} | custom-call | bytes 65536 | tf_op jit(solution)/shard_map/conv0_far/pallas_call | solution.py:524
  84.6 0.5 collective-permute-start.24
  85.1 2.5 %mix0_near.1 = (bf16[2,2,256,512]{3,2,1,0:T(8,128)(2,1)S(1)}, bf16[2,2,256,512]{3,2,1,0:T(8,128)(2,1)S(1)}, bf16[2,256,512]{2,1,0:T(8,128)(2,1)S(1)}) custom-call(s32[3]{0:T(128)S(1)} %pad_add_fusion.place_ref.place, f32[2,512]{1,0:T(2,128)S(1)} %copy-done.1, f32[2,512]{1,0:T(2,128)S(1)} %collective-permute-done.4.gp_ref, ...), custom_call_target="tpu_custom_call" | custom-call | bytes 65536 | tf_op jit(solution)/shard_map/mix0_near/pallas_call | solution.py:544
  87.7 1.6 %mix0_far.1 = (bf16[1,2,256,512]{3,2,1,0:T(8,128)(2,1)S(1)}, bf16[1,2,256,512]{3,2,1,0:T(8,128)(2,1)S(1)}) custom-call(s32[3]{0:T(128)S(1)} %pad_add_fusion.place_ref.place, f32[2,512]{1,0:T(2,128)S(1)} %copy-done.1, f32[2,512]{1,0:T(2,128)S(1)} %collective-permute-done.4.gp_ref, bf16[512,512]{1,0:T(8,128)(2,1)S(1)} %get-tuple-element.125.mixm_ref, ...), custom_call_target="tpu_custom_call" | custom-call | bytes 65536 | tf_op jit(solution)/shard_map/mix0_far/pallas_call | solution.py:544
  89.3 2.6 %conv1.1 = (bf16[2,256,256]{2,1,0:T(8,128)(2,1)S(1)}, bf16[512,512]{1,0:T(8,128)(2,1)S(1)}) custom-call(s32[3]{0:T(128)S(1)} %pad_add_fusion.place_ref.place, bf16[2,2,256,512]{3,2,1,0:T(8,128)(2,1)S(1)} %get-tuple-element.149.hm_near, bf16[2,2,256,512]{3,2,1,0:T(8,128)(2,1)S(1)} %get-tuple-element.150.hp_near, ...), custom_call_target="tpu_custom_call" | custom-call | tf_op jit(solution)/shard_map/conv1/pallas_call | solution.py:567
  92.1 1.5 %collective-permute-done.28.zp_ref = bf16[2,256,256]{2,1,0:T(8,128)(2,1)S(1)} collective-permute-done((bf16[2,256,256]{2,1,0:T(8,128)(2,1)S(1)}, bf16[2,256,256]{2,1,0:T(8,128)(2,1)S(1)}, u32[]{:S(2)}, u32[]{:S(2)}) %collective-permute-start.28) | collective-permute-done | bytes 262176 | tf_op jit(solution)/shard_map/ppermute | solution.py:40
  93.6 1.7 %mix1.1 = (bf16[256,512]{1,0:T(8,128)(2,1)}, bf16[256,512]{1,0:T(8,128)(2,1)}) custom-call(s32[3]{0:T(128)S(1)} %pad_add_fusion.place_ref.place, bf16[2,256,256]{2,1,0:T(8,128)(2,1)S(1)} %get-tuple-element.165.zm_ref, bf16[2,256,256]{2,1,0:T(8,128)(2,1)S(1)} %collective-permute-done.28.zp_ref, bf16[512,512]{1,0:T(8,128)(2,1)S(1)} %get-tuple-element.166.mix_ref, ...), custom_call_target="tpu_custom_call" | custom-call | tf_op jit(solution)/shard_map/mix1/pallas_call | solution.py:582
  (33 shorter events, 0.6 us)
Async XLA Ops:
  0.6 1.1 %copy-start = (bf16[2,384,2,256]{3,2,1,0:T(2,128)(2,1)S(1)}, bf16[2,384,2,256]{3,2,1,0:T(2,128)(2,1)}, u32[]{:S(2)}) copy-start(bf16[2,384,2,256]{3,2,1,0:T(2,128)(2,1)} %param.8) | copy-start | bytes 2359300
  0.6 10.7 %copy-start.1 = (f32[2,512]{1,0:T(2,128)S(1)}, f32[2,512]{1,0:T(2,128)}, u32[]{:S(2)}) copy-start(f32[2,512]{1,0:T(2,128)} %gm_ref.7) | copy-start | bytes 12292
  0.7 10.7 %copy-start.2 = (bf16[256,512]{1,0:T(8,128)(2,1)S(1)}, bf16[256,512]{1,0:T(8,128)(2,1)}, u32[]{:S(2)}) copy-start(bf16[256,512]{1,0:T(8,128)(2,1)} %param.6) | copy-start | bytes 786436
  3.2 18.3 %collective-permute-start.3 = (bf16[448,512]{1,0:T(8,128)(2,1)S(1)}, bf16[448,512]{1,0:T(8,128)(2,1)S(1)}, u32[]{:S(2)}, u32[]{:S(2)}) collective-permute-start(bf16[448,512]{1,0:T(8,128)(2,1)S(1)} %get-tuple-element.153.refs_0_.refs_6_), channel_id=1, source_target_pairs={{0,16},{16,0},{1,17},{17,1},{2,18},{18,2},{3,19},{19,3},{4,20},{20... | collective-permute-start | bytes 1376264 | tf_op jit(solution)/shard_map/ppermute | solution.py:44
  6.3 15.2 %collective-permute-start.2 = (bf16[448,512]{1,0:T(8,128)(2,1)S(1)}, bf16[448,512]{1,0:T(8,128)(2,1)S(1)}, u32[]{:S(2)}, u32[]{:S(2)}) collective-permute-start(bf16[448,512]{1,0:T(8,128)(2,1)S(1)} %get-tuple-element.153.refs_0_.refs_6_), channel_id=1, source_target_pairs={{0,2},{2,0},{4,6},{6,4},{8,10},{10,8},{12,14},{14,12},{1,3},{3,1},... | collective-permute-start | bytes 1376264 | tf_op jit(solution)/shard_map/ppermute | solution.py:48
  7.7 9.7 %collective-permute-start.1 = (bf16[224,512]{1,0:T(8,128)(2,1)S(1)}, bf16[224,512]{1,0:T(8,128)(2,1)S(1)}, u32[]{:S(2)}, u32[]{:S(2)}) collective-permute-start(bf16[224,512]{1,0:T(8,128)(2,1)S(1)} %get-tuple-element.85), channel_id=1, source_target_pairs={{0,12},{2,14},{4,0},{6,2},{8,4},{10,6},{12,8},{14,10},{1,13},{3,15... | collective-permute-start | bytes 688136 | tf_op jit(solution)/shard_map/ppermute | solution.py:52
  11.3 10.1 %collective-permute-start = (bf16[224,512]{1,0:T(8,128)(2,1)S(1)}, bf16[224,512]{1,0:T(8,128)(2,1)S(1)}, u32[]{:S(2)}, u32[]{:S(2)}) collective-permute-start(bf16[224,512]{1,0:T(8,128)(2,1)S(1)} %get-tuple-element.85), channel_id=1, source_target_pairs={{0,4},{2,6},{4,8},{6,10},{8,12},{10,14},{12,0},{14,2},{1,5},{3,7},... | collective-permute-start | bytes 688136 | tf_op jit(solution)/shard_map/ppermute | solution.py:52
  11.4 1.2 %collective-permute-start.4 = (f32[2,512]{1,0:T(2,128)S(1)}, f32[2,512]{1,0:T(2,128)S(1)}, u32[]{:S(2)}, u32[]{:S(2)}) collective-permute-start(f32[2,512]{1,0:T(2,128)S(1)} %copy-done.1), channel_id=1, source_target_pairs={{0,1},{1,0},{2,3},{3,2},{4,5},{5,4},{6,7},{7,6},{8,9},{9,8},{10,11... | collective-permute-start | bytes 12296 | tf_op jit(solution)/shard_map/ppermute | solution.py:40
  22.2 18.9 %collective-permute-start.5 = (bf16[736,512]{1,0:T(8,128)(2,1)S(1)}, bf16[736,512]{1,0:T(8,128)(2,1)S(1)}, u32[]{:S(2)}, u32[]{:S(2)}) collective-permute-start(bf16[736,512]{1,0:T(8,128)(2,1)S(1)} %get-tuple-element.94), channel_id=1, source_target_pairs={{0,4},{2,6},{4,8},{6,10},{8,12},{10,14},{12,0},{14,2},{1,5},{3,7},... | collective-permute-start | bytes 2261000 | tf_op jit(solution)/shard_map/ppermute | solution.py:52
  23.8 15.5 %collective-permute-start.6 = (bf16[672,512]{1,0:T(8,128)(2,1)S(1)}, bf16[672,512]{1,0:T(8,128)(2,1)S(1)}, u32[]{:S(2)}, u32[]{:S(2)}) collective-permute-start(bf16[672,512]{1,0:T(8,128)(2,1)S(1)} %get-tuple-element.95), channel_id=1, source_target_pairs={{0,2},{2,0},{4,6},{6,4},{8,10},{10,8},{12,14},{14,12},{1,3},{3,1},... | collective-permute-start | bytes 2064392 | tf_op jit(solution)/shard_map/ppermute | solution.py:48
  24.4 15.2 %collective-permute-start.7 = (bf16[672,512]{1,0:T(8,128)(2,1)S(1)}, bf16[672,512]{1,0:T(8,128)(2,1)S(1)}, u32[]{:S(2)}, u32[]{:S(2)}) collective-permute-start(bf16[672,512]{1,0:T(8,128)(2,1)S(1)} %get-tuple-element.96), channel_id=1, source_target_pairs={{0,16},{16,0},{1,17},{17,1},{2,18},{18,2},{3,19},{19,3},{4,20},{20... | collective-permute-start | bytes 2064392 | tf_op jit(solution)/shard_map/ppermute | solution.py:44
  24.9 1.9 %collective-permute-start.8 = (bf16[512,512]{1,0:T(8,128)(2,1)S(1)}, bf16[512,512]{1,0:T(8,128)(2,1)S(1)}, u32[]{:S(2)}, u32[]{:S(2)}) collective-permute-start(bf16[512,512]{1,0:T(8,128)(2,1)S(1)} %bitcast.14), channel_id=1, source_target_pairs={{0,1},{1,0},{2,3},{3,2},{4,5},{5,4},{6,7},{7,6},{8,9},{9,8},{10,11... | collective-permute-start | bytes 1572872 | tf_op jit(solution)/shard_map/ppermute | solution.py:40
  41.9 16.2 %collective-permute-start.11 = (bf16[736,512]{1,0:T(8,128)(2,1)S(1)}, bf16[736,512]{1,0:T(8,128)(2,1)S(1)}, u32[]{:S(2)}, u32[]{:S(2)}) collective-permute-start(bf16[736,512]{1,0:T(8,128)(2,1)S(1)} %get-tuple-element.103), channel_id=1, source_target_pairs={{0,2},{2,0},{4,6},{6,4},{8,10},{10,8},{12,14},{14,12},{1,3},{3,1},... | collective-permute-start | bytes 2261000 | tf_op jit(solution)/shard_map/ppermute | solution.py:48
  42.5 14.7 %collective-permute-start.12 = (bf16[672,512]{1,0:T(8,128)(2,1)S(1)}, bf16[672,512]{1,0:T(8,128)(2,1)S(1)}, u32[]{:S(2)}, u32[]{:S(2)}) collective-permute-start(bf16[672,512]{1,0:T(8,128)(2,1)S(1)} %get-tuple-element.104), channel_id=1, source_target_pairs={{0,16},{16,0},{1,17},{17,1},{2,18},{18,2},{3,19},{19,3},{4,20},{20... | collective-permute-start | bytes 2064392 | tf_op jit(solution)/shard_map/ppermute | solution.py:44
  43.0 14.2 %collective-permute-start.9 = (bf16[448,512]{1,0:T(8,128)(2,1)S(1)}, bf16[448,512]{1,0:T(8,128)(2,1)S(1)}, u32[]{:S(2)}, u32[]{:S(2)}) collective-permute-start(bf16[448,512]{1,0:T(8,128)(2,1)S(1)} %get-tuple-element.101), channel_id=1, source_target_pairs={{0,4},{2,6},{4,8},{6,10},{8,12},{10,14},{12,0},{14,2},{1,5},{3,7},... | collective-permute-start | bytes 1376264 | tf_op jit(solution)/shard_map/ppermute | solution.py:52
  43.0 14.2 %collective-permute-start.10 = (bf16[224,512]{1,0:T(8,128)(2,1)S(1)}, bf16[224,512]{1,0:T(8,128)(2,1)S(1)}, u32[]{:S(2)}, u32[]{:S(2)}) collective-permute-start(bf16[224,512]{1,0:T(8,128)(2,1)S(1)} %get-tuple-element.102), channel_id=1, source_target_pairs={{0,12},{2,14},{4,0},{6,2},{8,4},{10,6},{12,8},{14,10},{1,13},{3,15... | collective-permute-start | bytes 688136 | tf_op jit(solution)/shard_map/ppermute | solution.py:52
  58.8 17.1 %collective-permute-start.13 = (bf16[736,512]{1,0:T(8,128)(2,1)S(1)}, bf16[736,512]{1,0:T(8,128)(2,1)S(1)}, u32[]{:S(2)}, u32[]{:S(2)}) collective-permute-start(bf16[736,512]{1,0:T(8,128)(2,1)S(1)} %get-tuple-element.109), channel_id=1, source_target_pairs={{0,4},{2,6},{4,8},{6,10},{8,12},{10,14},{12,0},{14,2},{1,5},{3,7},... | collective-permute-start | bytes 2261000 | tf_op jit(solution)/shard_map/ppermute | solution.py:52
  58.9 4.9 %collective-permute-start.14 = (bf16[112,512]{1,0:T(8,128)(2,1)S(1)}, bf16[112,512]{1,0:T(8,128)(2,1)S(1)}, u32[]{:S(2)}, u32[]{:S(2)}) collective-permute-start(bf16[112,512]{1,0:T(8,128)(2,1)S(1)} %get-tuple-element.111), channel_id=1, source_target_pairs={{0,2},{2,0},{4,6},{6,4},{8,10},{10,8},{12,14},{14,12},{1,3},{3,1},... | collective-permute-start | bytes 344072 | tf_op jit(solution)/shard_map/ppermute | solution.py:48
  59.7 4.9 %collective-permute-start.15 = (bf16[112,512]{1,0:T(8,128)(2,1)S(1)}, bf16[112,512]{1,0:T(8,128)(2,1)S(1)}, u32[]{:S(2)}, u32[]{:S(2)}) collective-permute-start(bf16[112,512]{1,0:T(8,128)(2,1)S(1)} %get-tuple-element.112), channel_id=1, source_target_pairs={{0,16},{16,0},{1,17},{17,1},{2,18},{18,2},{3,19},{19,3},{4,20},{20... | collective-permute-start | bytes 344072 | tf_op jit(solution)/shard_map/ppermute | solution.py:44
  61.2 5.9 %collective-permute-start.19 = (bf16[512,512]{1,0:T(8,128)(2,1)S(1)}, bf16[512,512]{1,0:T(8,128)(2,1)S(1)}, u32[]{:S(2)}, u32[]{:S(2)}) collective-permute-start(bf16[512,512]{1,0:T(8,128)(2,1)S(1)} %get-tuple-element.115), channel_id=1, source_target_pairs={{0,1},{1,0},{2,3},{3,2},{4,5},{5,4},{6,7},{7,6},{8,9},{9,8},{10,11... | collective-permute-start | bytes 1572872 | tf_op jit(solution)/shard_map/ppermute | solution.py:40
  61.2 5.9 %collective-permute-start.18 = (bf16[512,512]{1,0:T(8,128)(2,1)S(1)}, bf16[512,512]{1,0:T(8,128)(2,1)S(1)}, u32[]{:S(2)}, u32[]{:S(2)}) collective-permute-start(bf16[512,512]{1,0:T(8,128)(2,1)S(1)} %get-tuple-element.114), channel_id=1, source_target_pairs={{0,1},{1,0},{2,3},{3,2},{4,5},{5,4},{6,7},{7,6},{8,9},{9,8},{10,11... | collective-permute-start | bytes 1572872 | tf_op jit(solution)/shard_map/ppermute | solution.py:40
  64.6 9.7 %collective-permute-start.17 = (bf16[448,512]{1,0:T(8,128)(2,1)S(1)}, bf16[448,512]{1,0:T(8,128)(2,1)S(1)}, u32[]{:S(2)}, u32[]{:S(2)}) collective-permute-start(bf16[448,512]{1,0:T(8,128)(2,1)S(1)} %get-tuple-element.113), channel_id=1, source_target_pairs={{0,16},{16,0},{1,17},{17,1},{2,18},{18,2},{3,19},{19,3},{4,20},{20... | collective-permute-start | bytes 1376264 | tf_op jit(solution)/shard_map/ppermute | solution.py:44
  67.1 8.5 %collective-permute-start.16 = (bf16[448,512]{1,0:T(8,128)(2,1)S(1)}, bf16[448,512]{1,0:T(8,128)(2,1)S(1)}, u32[]{:S(2)}, u32[]{:S(2)}) collective-permute-start(bf16[448,512]{1,0:T(8,128)(2,1)S(1)} %get-tuple-element.113), channel_id=1, source_target_pairs={{0,2},{2,0},{4,6},{6,4},{8,10},{10,8},{12,14},{14,12},{1,3},{3,1},... | collective-permute-start | bytes 1376264 | tf_op jit(solution)/shard_map/ppermute | solution.py:48
  75.9 3.6 %collective-permute-start.21 = (bf16[2,512,256]{2,1,0:T(8,128)(2,1)S(1)}, bf16[2,512,256]{2,1,0:T(8,128)(2,1)S(1)}, u32[]{:S(2)}, u32[]{:S(2)}) collective-permute-start(bf16[2,512,256]{2,1,0:T(8,128)(2,1)S(1)} %get-tuple-element.142.refs_0_), channel_id=1, source_target_pairs={{0,1},{1,0},{2,3},{3,2},{4,5},{5,4},{6,7},{7,6},{8,9},{9,8},{10,11... | collective-permute-start | bytes 1572872 | tf_op jit(solution)/shard_map/ppermute | solution.py:40
  75.9 5.6 %collective-permute-start.22 = (bf16[512,512]{1,0:T(8,128)(2,1)S(1)}, bf16[512,512]{1,0:T(8,128)(2,1)S(1)}, u32[]{:S(2)}, u32[]{:S(2)}) collective-permute-start(bf16[512,512]{1,0:T(8,128)(2,1)S(1)} %get-tuple-element.125.mixm_ref), channel_id=1, source_target_pairs={{0,1},{1,0},{2,3},{3,2},{4,5},{5,4},{6,7},{7,6},{8,9},{9,8},{10,11... | collective-permute-start | bytes 1572872 | tf_op jit(solution)/shard_map/ppermute | solution.py:40
  77.1 4.4 %collective-permute-start.20 = (bf16[2,256,512]{2,1,0:T(8,128)(2,1)S(1)}, bf16[2,256,512]{2,1,0:T(8,128)(2,1)S(1)}, u32[]{:S(2)}, u32[]{:S(2)}) collective-permute-start(bf16[2,256,512]{2,1,0:T(8,128)(2,1)S(1)} %bitcast.26), channel_id=1, source_target_pairs={{0,1},{1,0},{2,3},{3,2},{4,5},{5,4},{6,7},{7,6},{8,9},{9,8},{10,11... | collective-permute-start | bytes 1572872 | tf_op jit(solution)/shard_map/ppermute | solution.py:40
  77.2 12.1 %collective-permute-start.26 = (bf16[336,512]{1,0:T(8,128)(2,1)S(1)}, bf16[336,512]{1,0:T(8,128)(2,1)S(1)}, u32[]{:S(2)}, u32[]{:S(2)}) collective-permute-start(bf16[336,512]{1,0:T(8,128)(2,1)S(1)} %get-tuple-element.147), channel_id=1, source_target_pairs={{0,2},{2,0},{4,6},{6,4},{8,10},{10,8},{12,14},{14,12},{1,3},{3,1},... | collective-permute-start | bytes 1032200 | tf_op jit(solution)/shard_map/ppermute | solution.py:48
  78.0 11.3 %collective-permute-start.27 = (bf16[336,512]{1,0:T(8,128)(2,1)S(1)}, bf16[336,512]{1,0:T(8,128)(2,1)S(1)}, u32[]{:S(2)}, u32[]{:S(2)}) collective-permute-start(bf16[336,512]{1,0:T(8,128)(2,1)S(1)} %get-tuple-element.148), channel_id=1, source_target_pairs={{0,16},{16,0},{1,17},{17,1},{2,18},{18,2},{3,19},{19,3},{4,20},{20... | collective-permute-start | bytes 1032200 | tf_op jit(solution)/shard_map/ppermute | solution.py:44
  79.5 9.8 %collective-permute-start.25 = (bf16[224,512]{1,0:T(8,128)(2,1)S(1)}, bf16[224,512]{1,0:T(8,128)(2,1)S(1)}, u32[]{:S(2)}, u32[]{:S(2)}) collective-permute-start(bf16[224,512]{1,0:T(8,128)(2,1)S(1)} %get-tuple-element.146), channel_id=1, source_target_pairs={{0,4},{2,6},{4,8},{6,10},{8,12},{10,14},{12,0},{14,2},{1,5},{3,7},... | collective-permute-start | bytes 688136 | tf_op jit(solution)/shard_map/ppermute | solution.py:52
  84.6 3.1 %collective-permute-start.23 = (bf16[256,256]{1,0:T(8,128)(2,1)S(1)}, bf16[256,256]{1,0:T(8,128)(2,1)S(1)}, u32[]{:S(2)}, u32[]{:S(2)}) collective-permute-start(bf16[256,256]{1,0:T(8,128)(2,1)S(1)} %get-tuple-element.138.refs_0_), channel_id=1, source_target_pairs={{0,1},{1,0},{2,3},{3,2},{4,5},{5,4},{6,7},{7,6},{8,9},{9,8},{10,11... | collective-permute-start | bytes 393224 | tf_op jit(solution)/shard_map/ppermute | solution.py:40
  84.6 3.0 %collective-permute-start.24 = (bf16[256,256]{1,0:T(8,128)(2,1)S(1)}, bf16[256,256]{1,0:T(8,128)(2,1)S(1)}, u32[]{:S(2)}, u32[]{:S(2)}) collective-permute-start(bf16[256,256]{1,0:T(8,128)(2,1)S(1)} %get-tuple-element.139.refs_1_), channel_id=1, source_target_pairs={{0,1},{1,0},{2,3},{3,2},{4,5},{5,4},{6,7},{7,6},{8,9},{9,8},{10,11... | collective-permute-start | bytes 393224 | tf_op jit(solution)/shard_map/ppermute | solution.py:40
  92.0 1.6 %collective-permute-start.28 = (bf16[2,256,256]{2,1,0:T(8,128)(2,1)S(1)}, bf16[2,256,256]{2,1,0:T(8,128)(2,1)S(1)}, u32[]{:S(2)}, u32[]{:S(2)}) collective-permute-start(bf16[2,256,256]{2,1,0:T(8,128)(2,1)S(1)} %get-tuple-element.165.zm_ref), channel_id=1, source_target_pairs={{0,1},{1,0},{2,3},{3,2},{4,5},{5,4},{6,7},{7,6},{8,9},{9,8},{10,11... | collective-permute-start | bytes 786440 | tf_op jit(solution)/shard_map/ppermute | solution.py:40
